TPU v7x, 32 devices: a whole 2x2x4 slice. The times are simulated.
32 devices in a mesh: ops: 8 (over z, x), sec: 4 (over y, core).
Axes of the slice: x: 2, y: 2, z: 4, core: 2. Of those that a mesh axis runs over, the one named last changes fastest.
Arguments:
- sector_states: int32 [4], P('sec'), may hold values from 85 to 256, as said below
- psi_guess: bfloat16 [4, 256, 256], P('sec'), may hold values from -6 to 6
- precond_diag: bfloat16 [4, 256, 256], P('sec'), may hold values from -12 to 12
- left_ops: float32 [16, 4, 256, 256], P('ops', 'sec'), may hold values from -0.375 to 0.375
- right_ops: float32 [16, 4, 256, 256], P('ops', 'sec'), may hold values from -0.375 to 0.375
- couple: int32 [16, 4], P('ops', 'sec'), may hold values from -1 to 3, as said below
- new_sector: int32 [4], P('sec'), may hold values from 0 to 3, as said below
Outputs:
- wavefunction: float32 [4, 256, 256], P('sec')
- rotated_ops: float32 [16, 4, 256, 256], P('ops', 'sec')
Inputs may be any that keep to these rules, and one draw needn't show every extreme that they name: `sector_states`: at least one sector has 256 states. couple[p, s] is s - 1, s or s + 1, or -1 where that lies outside the sectors. `new_sector`: each aligned pair of sectors 2k, 2k + 1 either keeps its labels or swaps them; the pair with 2k = 2 always swaps.
All inputs are finite; a program needn't handle non-finite values.
Results may differ from a plain program's by a relative error of at most 0.0003.
Values sent between devices are 32-bit elements; how exact they have to be, the bound alone decides.
No kernel may reach another device: no remote copies, remote signals or barrier semaphores. Data moves between devices by JAX's collectives and lax.ppermute only.
A program may use at most 64 MiB of HBM per device.

v0:
```python
import jax
import jax.numpy as jnp
from jax import lax
from jax.sharding import PartitionSpec as P

UPDATES = 2


HIGH = lax.Precision.HIGHEST


def extended(cells, sides, width):
    for axis, dim in sides:
        count = lax.axis_size(axis)
        ends = count - 1
        head = lax.slice_in_dim(cells, 0, width, axis=dim)
        tail = lax.slice_in_dim(cells, cells.shape[dim] - width, cells.shape[dim], axis=dim)
        cells = jnp.concatenate(
            [
                lax.ppermute(tail, axis, [(i, (i + 1) % count) for i in range(ends)]),
                cells,
                lax.ppermute(head, axis, [((i + 1) % count, i) for i in range(ends)]),
            ],
            axis=dim,
        )
    return cells


def swapped(block, axis, bit):
    count = lax.axis_size(axis)
    route = []
    for low in range(count):
        high = low | 1 << bit
        if high != low and high < count:
            route += [(low, high), (high, low)]
    return lax.ppermute(block, axis, route)


def local(sector_states, psi_guess, precond_diag, left_ops, right_ops, couple, new_sector):
    block = psi_guess.shape[1]
    here = lax.axis_index("sec")
    sectors = lax.axis_size("sec")
    index = jnp.arange(block, dtype=jnp.int32)
    size_here = sector_states[0]
    live = ((index[:, None] < size_here) & (index[None, :] < size_here)).astype(jnp.float32)[None]
    source = couple[:, 0]
    offset = source - here + 1
    picks = jnp.stack(
        [((offset == k) & (source >= 0)).astype(jnp.float32) for k in range(3)], axis=1
    )
    lefts = left_ops[:, 0]
    rights = right_ops[:, 0]
    diag_rows = precond_diag.astype(jnp.float32)

    def widen(full):
        return extended(full, (("sec", 0),), 1)

    def product(wide):
        chosen = jnp.einsum("pk,kij->pij", picks, wide, precision=HIGH)
        mixed = jnp.einsum("pij,pjk->pik", lefts, chosen, precision=HIGH)
        terms = jnp.einsum("pik,plk->il", mixed, rights, precision=HIGH)[None]
        summed = lax.psum(terms, "ops")
        return summed * live

    def totals(values):
        return lax.psum(values, "sec")

    start = psi_guess.astype(jnp.float32) * live
    start_wide = widen(start)
    h_start = product(start_wide)
    squares, energy = totals((jnp.sum(start * start), jnp.sum(start * h_start)))
    factor = lax.rsqrt(squares + 1e-06)
    vecx = start * factor
    hvec = h_start * factor
    wide_x = start_wide * factor
    theta = energy * factor * factor
    for update in range(UPDATES):
        corr = live * (hvec - theta * vecx) / (jnp.abs(diag_rows - theta) + 1.0)
        correlation, length = totals((jnp.sum(vecx * corr), jnp.sum(corr * corr)))
        corr = (corr - correlation * vecx) * lax.rsqrt(length - correlation * correlation + 1e-06)
        wide_c = widen(corr)
        hcorr = product(wide_c)
        cross_a, cross_b, last = totals(
            (jnp.sum(vecx * hcorr), jnp.sum(corr * hvec), jnp.sum(corr * hcorr))
        )
        middle = 0.5 * (cross_a + cross_b)
        angle = 0.5 * jnp.arctan2(-2.0 * middle, last - theta)
        cosine = jnp.cos(angle)
        sine = jnp.sin(angle)
        vecx = cosine * vecx + sine * corr
        hvec = cosine * hvec + sine * hcorr
        wide_x = cosine * wide_x + sine * wide_c
        theta = 0.5 * (theta + last) - 0.5 * jnp.sqrt((last - theta) ** 2 + 4.0 * middle * middle)
    scaled = wide_x * jnp.sqrt(jnp.float32(sectors * block * block))
    wavefunction = scaled[1:2]
    chosen = jnp.einsum("pk,kij->pij", picks, scaled, precision=HIGH)
    inner = jnp.einsum("pjk,pkl->pjl", lefts, chosen, precision=HIGH)
    turned = jnp.einsum("ji,pjl->pil", scaled[1], inner, precision=HIGH) / jnp.sqrt(
        jnp.float32(block)
    )
    partner = swapped(turned, "sec", 0)
    keep = new_sector[0] == here
    rotated_ops = jnp.where(keep, turned, partner)[:, None]
    return (wavefunction, rotated_ops)


def solution(mesh):
    in_specs = (
        P("sec"),
        P("sec", None, None),
        P("sec", None, None),
        P("ops", "sec", None, None),
        P("ops", "sec", None, None),
        P("ops", "sec"),
        P("sec"),
    )
    out_specs = (P("sec", None, None), P("ops", "sec", None, None))
    return jax.shard_map(local, mesh=mesh, in_specs=in_specs, out_specs=out_specs, check_vma=False)
```

profile of v0, /device:TPU:0, one launch (start us, length us, event | category | flops | bytes accessed | tf_op | source)
XLA Modules:
  0.0 334.9 jit_solution(3646627671179335005)
XLA Ops:
  7.9 1.0 and_select_fusion.5
  8.9 2.4 collective-permute-start
  11.4 1.3 collective-permute-start.1
  12.7 0.6 copy-done.9
  13.4 3.5 %collective-permute-done.1 = f32[1,256,256]{2,1,0:T(8,128)S(1)} collective-permute-done((f32[1,256,256]{2,1,0:T(8,128)S(1)}, f32[1,256,256]{2,1,0:T(8,128)S(1)}, u32[]{:S(2)}, u32[]{:S(2)}) %collective-permute-start.1) | collective-permute-done | bytes 262176 | tf_op jit(solution)/shard_map/ppermute | solution.py:22
  16.9 0.1 pad_maximum_fusion
  17.0 1.6 fusion.7
  18.6 0.7 convolution_bitcast_fusion.3
  19.3 0.4 copy-done.3
  19.7 1.3 convolution_bitcast_fusion.6
  21.1 75.8 %all-reduce.9.cloned.1.call-done = f32[1,256,256]{2,1,0:T(8,128)} async-done(((f32[1,256,256]{2,1,0:T(8,128)}), f32[1,256,256]{2,1,0:T(8,128)}) %all-reduce.9.cloned.1.call-update) | async-done | bytes 262160 | tf_op jit(solution)/shard_map/psum | solution.py:62
  96.9 1.8 multiply_reduce_fusion.11
  98.7 6.3 %all-reduce.4 = (f32[]{:T(128)}, f32[]{:T(128)}) all-reduce(f32[]{:T(128)} %get-tuple-element.15, f32[]{:T(128)} %get-tuple-element.14), channel_id=1, replica_groups=mesh['ops'=8,'sec'=4] {'sec'}, use_global_device_ids=true, to_apply=%region_4.0 | all-reduce | flops 2 | bytes 16 | tf_op jit(solution)/shard_map/psum | solution.py:66
  106.3 0.8 multiply_reduce_fusion.9
  107.1 7.2 %all-reduce.3 = (f32[]{:T(128)}, f32[]{:T(128)}) all-reduce(f32[]{:T(128)} %get-tuple-element.13, f32[]{:T(128)} %get-tuple-element.12), channel_id=1, replica_groups=mesh['ops'=8,'sec'=4] {'sec'}, use_global_device_ids=true, to_apply=%region_8.0 | all-reduce | flops 2 | bytes 16 | tf_op jit(solution)/shard_map/psum | solution.py:66
  116.3 0.8 subtract_multiply_fusion.1
  117.1 1.3 collective-permute-start.3
  118.4 3.0 collective-permute-start.2
  121.5 1.1 collective-permute-done.2
  122.6 0.1 pad_maximum_fusion.1
  122.7 1.6 fusion.5
  124.3 0.7 convolution_bitcast_fusion.2
  125.0 1.3 convolution_bitcast_fusion.5
  126.4 74.0 %all-reduce.11.cloned.1.call-done = f32[1,256,256]{2,1,0:T(8,128)} async-done(((f32[1,256,256]{2,1,0:T(8,128)}), f32[1,256,256]{2,1,0:T(8,128)}) %all-reduce.11.cloned.1.call-update) | async-done | bytes 262160 | tf_op jit(solution)/shard_map/psum | solution.py:62
  200.3 1.9 multiply_reduce_fusion.6
  203.5 6.4 %all-reduce.2 = (f32[]{:T(128)}, f32[]{:T(128)}) all-reduce(f32[]{:T(128)} %get-tuple-element.8, f32[]{:T(128)S(6)} %add.79), channel_id=1, replica_groups=mesh['ops'=8,'sec'=4] {'sec'}, use_global_device_ids=true, to_apply=%region_15.0 | all-reduce | flops 2 | bytes 16 | tf_op jit(solution)/shard_map/psum | solution.py:66
  213.3 1.7 multiply_reduce_fusion.4
  215.0 7.2 %all-reduce.1 = (f32[]{:T(128)}, f32[]{:T(128)}) all-reduce(f32[]{:T(128)} %get-tuple-element.11, f32[]{:T(128)} %get-tuple-element.10), channel_id=1, replica_groups=mesh['ops'=8,'sec'=4] {'sec'}, use_global_device_ids=true, to_apply=%region_19.0 | all-reduce | flops 2 | bytes 16 | tf_op jit(solution)/shard_map/psum | solution.py:66
  224.1 1.8 subtract_multiply_fusion
  225.8 1.3 collective-permute-start.5
  227.1 3.2 collective-permute-start.4
  230.4 0.9 collective-permute-done.4
  231.3 0.7 copy-done.7
  232.0 0.1 pad_maximum_fusion.2
  232.1 1.6 fusion.3
  233.7 0.7 convolution_bitcast_fusion.1
  234.4 1.3 convolution_bitcast_fusion.4
  235.7 74.0 %all-reduce.13.cloned.1.call-done = f32[1,256,256]{2,1,0:T(8,128)} async-done(((f32[1,256,256]{2,1,0:T(8,128)}), f32[1,256,256]{2,1,0:T(8,128)}) %all-reduce.13.cloned.1.call-update) | async-done | bytes 262160 | tf_op jit(solution)/shard_map/psum | solution.py:62
  309.7 1.9 multiply_reduce_fusion
  312.9 6.4 %all-reduce = (f32[]{:T(128)}, f32[]{:T(128)}) all-reduce(f32[]{:T(128)S(6)} %add.86, f32[]{:T(128)} %get-tuple-element.4), channel_id=1, replica_groups=mesh['ops'=8,'sec'=4] {'sec'}, use_global_device_ids=true, to_apply=%region_22.0 | all-reduce | flops 2 | bytes 16 | tf_op jit(solution)/shard_map/psum | solution.py:66
  320.7 1.2 add_multiply_fusion
  322.0 1.6 fusion.1
  323.7 1.0 convolution_bitcast_fusion
  324.7 0.6 fusion
  325.3 0.1 collective-permute-start.6
  326.0 1.2 collective-permute-done.6
  327.3 0.1 select_bitcast_fusion
  327.4 1.0 copy.9
  (30 shorter events, 0.3 us)
Async XLA Ops:
  7.2 11.5 %copy-start = (f32[2,1,256,256]{3,2,1,0:T(8,128)S(1)}, f32[2,1,256,256]{3,2,1,0:T(8,128)}, u32[]{:S(2)}) copy-start(f32[2,1,256,256]{3,2,1,0:T(8,128)} %param.10) | copy-start | bytes 1572868
  7.2 89.7 %all-reduce.9.cloned.1.call-start = ((), (), s32[]{:S(2)}) async-start(), calls=%async_computation | async-start | bytes 524288 | tf_op jit(solution)/shard_map/psum | solution.py:62
  8.9 4.4 %collective-permute-start = (f32[1,256,256]{2,1,0:T(8,128)S(1)}, f32[1,256,256]{2,1,0:T(8,128)S(1)}, u32[]{:S(2)}, u32[]{:S(2)}) collective-permute-start(f32[1,256,256]{2,1,0:T(8,128)S(1)} %and_select_fusion.5), channel_id=1, source_target_pairs={{0,1},{1,2},{2,3},{4,5},{5,6},{6,7},{8,9},{9,10},{10,11},{12,13},{... | collective-permute-start | bytes 786440 | tf_op jit(solution)/shard_map/ppermute | solution.py:20
  11.4 5.5 %collective-permute-start.1 = (f32[1,256,256]{2,1,0:T(8,128)S(1)}, f32[1,256,256]{2,1,0:T(8,128)S(1)}, u32[]{:S(2)}, u32[]{:S(2)}) collective-permute-start(f32[1,256,256]{2,1,0:T(8,128)S(1)} %and_select_fusion.5), channel_id=1, source_target_pairs={{1,0},{2,1},{3,2},{5,4},{6,5},{7,6},{9,8},{10,9},{11,10},{13,12},{... | collective-permute-start | bytes 786440 | tf_op jit(solution)/shard_map/ppermute | solution.py:22
  12.7 0.7 copy-start.9
  18.6 1.0 copy-start.3
  21.0 75.9 %copy-start.1 = (bf16[1,256,256]{2,1,0:T(8,128)(2,1)S(1)}, bf16[1,256,256]{2,1,0:T(8,128)(2,1)}, u32[]{:S(2)}) copy-start(bf16[1,256,256]{2,1,0:T(8,128)(2,1)} %param.8) | copy-start | bytes 393220
  21.0 85.3 %copy-start.8 = (bf16[1,256,256]{2,1,0:T(8,128)(2,1)S(1)}, bf16[1,256,256]{2,1,0:T(8,128)(2,1)}, u32[]{:S(2)}) copy-start(bf16[1,256,256]{2,1,0:T(8,128)(2,1)} %param.9) | copy-start | bytes 393220
  21.0 179.3 %all-reduce.11.cloned.1.call-start = ((), (), s32[]{:S(2)}) async-start(), calls=%async_computation.1 | async-start | bytes 524288 | tf_op jit(solution)/shard_map/psum | solution.py:62
  96.9 9.4 %copy-start.2 = (f32[1,256,256]{2,1,0:T(8,128)S(1)}, f32[1,256,256]{2,1,0:T(8,128)}, u32[]{:S(2)}) copy-start(f32[1,256,256]{2,1,0:T(8,128)} %all-reduce.9.cloned.1.call-done) | copy-start | bytes 786436
  117.1 4.4 %collective-permute-start.3 = (f32[1,256,256]{2,1,0:T(8,128)S(1)}, f32[1,256,256]{2,1,0:T(8,128)S(1)}, u32[]{:S(2)}, u32[]{:S(2)}) collective-permute-start(f32[1,256,256]{2,1,0:T(8,128)S(1)} %subtract_multiply_fusion.1), channel_id=1, source_target_pairs={{1,0},{2,1},{3,2},{5,4},{6,5},{7,6},{9,8},{10,9},{11,10},{13,12},{... | collective-permute-start | bytes 786440 | tf_op jit(solution)/shard_map/ppermute | solution.py:22
  118.4 4.2 %collective-permute-start.2 = (f32[1,256,256]{2,1,0:T(8,128)S(1)}, f32[1,256,256]{2,1,0:T(8,128)S(1)}, u32[]{:S(2)}, u32[]{:S(2)}) collective-permute-start(f32[1,256,256]{2,1,0:T(8,128)S(1)} %subtract_multiply_fusion.1), channel_id=1, source_target_pairs={{0,1},{1,2},{2,3},{4,5},{5,6},{6,7},{8,9},{9,10},{10,11},{12,13},{... | collective-permute-start | bytes 786440 | tf_op jit(solution)/shard_map/ppermute | solution.py:20
  126.3 183.4 %all-reduce.13.cloned.1.call-start = ((), (), s32[]{:S(2)}) async-start(), calls=%async_computation.2 | async-start | bytes 524288 | tf_op jit(solution)/shard_map/psum | solution.py:62
  200.3 13.0 %copy-start.4 = (f32[1,256,256]{2,1,0:T(8,128)S(1)}, f32[1,256,256]{2,1,0:T(8,128)}, u32[]{:S(2)}) copy-start(f32[1,256,256]{2,1,0:T(8,128)} %all-reduce.11.cloned.1.call-done) | copy-start | bytes 786436
  225.8 4.5 %collective-permute-start.5 = (f32[1,256,256]{2,1,0:T(8,128)S(1)}, f32[1,256,256]{2,1,0:T(8,128)S(1)}, u32[]{:S(2)}, u32[]{:S(2)}) collective-permute-start(f32[1,256,256]{2,1,0:T(8,128)S(1)} %subtract_multiply_fusion), channel_id=1, source_target_pairs={{1,0},{2,1},{3,2},{5,4},{6,5},{7,6},{9,8},{10,9},{11,10},{13,12},{... | collective-permute-start | bytes 786440 | tf_op jit(solution)/shard_map/ppermute | solution.py:22
  227.1 4.2 %collective-permute-start.4 = (f32[1,256,256]{2,1,0:T(8,128)S(1)}, f32[1,256,256]{2,1,0:T(8,128)S(1)}, u32[]{:S(2)}, u32[]{:S(2)}) collective-permute-start(f32[1,256,256]{2,1,0:T(8,128)S(1)} %subtract_multiply_fusion), channel_id=1, source_target_pairs={{0,1},{1,2},{2,3},{4,5},{5,6},{6,7},{8,9},{9,10},{10,11},{12,13},{... | collective-permute-start | bytes 786440 | tf_op jit(solution)/shard_map/ppermute | solution.py:20
  230.4 0.9 copy-start.6
  231.3 0.7 copy-start.7
  322.0 2.7 copy-start.5
  325.3 2.0 collective-permute-start.6
Sparse Core Ops, SparseCore 0:
  21.1 75.6 all-reduce.8
  126.5 73.8 all-reduce.10
  235.9 73.8 all-reduce.12
where the time goes:
time: 336 us; the launch traced here: 335 us
  waiting for transfers between devices  231 us (69%)
  blocking collectives  33.4 us (10%)
  between operations  28.1 us (8%)
  matrix products  14.2 us (4%)
  other arithmetic  13.1 us (4%)
  starting transfers between devices  12.8 us (4%)
    psum x3, waiting for transfers between devices, product(): summed = lax.psum(terms, 'ops')  224 us
    psum x5, blocking collectives, totals(): return lax.psum(values, 'sec')  33.4 us
    ppermute x3, starting transfers between devices, extended(): lax.ppermute(tail, axis, [(i, (i + 1) % count) for i in range(ends)])  8.69 us
  transfers between devices with their start and end apart: 10, of which 7 were waited for; matrix products, arithmetic and copies ran while one was open for 0% of the time, Pallas kernels for 0%

commit v1 on v0

v1 whole, which is shorter than its diff:
```python
import functools

import jax
import jax.numpy as jnp
from jax import lax
from jax.experimental import pallas as pl
from jax.experimental.pallas import tpu as pltpu
from jax.sharding import PartitionSpec as P

LANES = 128
F32 = jnp.float32
BF16 = jnp.bfloat16
VMEM = pl.BlockSpec(memory_space=pltpu.VMEM)
SMEM = pl.BlockSpec(memory_space=pltpu.SMEM)


def call(body, outs, in_specs, scratch, flops, *args):
    size = sum(a.size * a.dtype.itemsize for a in args)
    size += sum(o.size * o.dtype.itemsize for o in outs)
    return pl.pallas_call(
        body,
        out_shape=tuple(outs),
        in_specs=in_specs,
        out_specs=tuple(VMEM for _ in outs),
        scratch_shapes=scratch,
        compiler_params=pltpu.CompilerParams(vmem_limit_bytes=24 * 1024 * 1024),
        cost_estimate=pl.CostEstimate(flops=flops, bytes_accessed=size, transcendentals=0),
    )(*args)


def pack(ref, lead, block, value):
    rc = value.shape[0] // block[0]
    for o in range(block[0]):
        for j in range(value.shape[1] // LANES):
            ref[lead + (o, slice(j * rc, (j + 1) * rc))] = value[
                o * rc : (o + 1) * rc, j * LANES : (j + 1) * LANES
            ]


def unpack(ref, k, value):
    chunks, cw, _ = value.shape
    side = ref.shape[1]
    rc = side // chunks
    for o in range(chunks):
        for j in range(side // LANES):
            ref[k, o * rc : (o + 1) * rc, j * LANES : (j + 1) * LANES] = value[
                o, j * rc : (j + 1) * rc
            ]


def halves(value):
    high = value.astype(BF16)
    low = (value - high.astype(F32)).astype(BF16)
    return high, low


def dot(a, b):
    return jnp.dot(a, b, preferred_element_type=F32)


def mask(size, side):
    rows = lax.broadcasted_iota(jnp.int32, (side, side), 0)
    cols = lax.broadcasted_iota(jnp.int32, (side, side), 1)
    return (rows < size) & (cols < size)


def pick(couple_ref, p, here, ref):
    source = couple_ref[p, 0]
    slot = jnp.where(source == here, 0, jnp.where(source == here + 1 - 2 * (here % 2), 1, 2))
    return jnp.where(source >= 0, ref[slot], 0.0)


def apply(couple_ref, here, ref, lcat_ref, rcat_ref):
    total = None
    for p in range(lcat_ref.shape[0]):
        high, low = halves(pick(couple_ref, p, here, ref))
        mixed = dot(lcat_ref[p], jnp.concatenate([high, low, high], axis=0))
        high, low = halves(mixed)
        term = dot(jnp.concatenate([high, low, high], axis=1), rcat_ref[p])
        total = term if total is None else total + term
    return total


def rows(value):
    return jnp.sum(value.reshape(-1, LANES), axis=0, keepdims=True)


def tile(parts):
    parts = parts + [jnp.zeros((8 - len(parts), LANES), F32)]
    return jnp.concatenate(parts, axis=0)


def half_angle(middle, first, last):
    gap = last - first
    tilt = -2.0 * middle
    length = jnp.sqrt(gap * gap + tilt * tilt)
    safe = jnp.where(length > 0.0, length, 1.0)
    big = jnp.where(length > 0.0, jnp.sqrt(0.5 + 0.5 * jnp.abs(gap) / safe), 1.0)
    small = 0.5 * tilt / (safe * big)
    sign = jnp.where(tilt > 0.0, 1.0, -1.0)
    cosine = jnp.where(gap >= 0.0, big, jnp.abs(small))
    sine = jnp.where(gap >= 0.0, small, sign * big)
    return cosine, sine, 0.5 * (first + last) - 0.5 * length


def update(xx, first, xr, rr, rh, xhr, rhr):
    n = lax.rsqrt(rr - 2.0 * xr * xr + xr * xr * xx + 1e-06)
    middle = 0.5 * n * ((xhr - xr * first) + (rh - xr * first))
    last = n * n * (rhr - xr * rh - xr * xhr + xr * xr * first)
    cosine, sine, theta = half_angle(middle, first, last)
    on_r = sine * n
    on_x = cosine - on_r * xr
    xx = on_x * on_x * xx + 2.0 * on_x * on_r * xr + on_r * on_r * rr
    return on_x, on_r, theta, xx


def start_body(size_ref, psi_ref, diag_ref, x_ref, d_ref):
    block = x_ref.shape
    side = psi_ref.shape[1]
    live = mask(size_ref[0], side)
    pack(x_ref, (), block, jnp.where(live, psi_ref[0].astype(F32), 0.0))
    pack(d_ref, (), block, diag_ref[0].astype(F32))


def split_body(left_ref, right_ref, lcat_ref, rcat_ref):
    for p in range(left_ref.shape[0]):
        high, low = halves(left_ref[p, 0])
        lcat_ref[p] = jnp.concatenate([high, high, low], axis=1)
        high, low = halves(right_ref[p, 0].T)
        rcat_ref[p] = jnp.concatenate([high, high, low], axis=0)


def first_body(size_ref, couple_ref, x0, x1, x2, lcat_ref, rcat_ref, y_ref, v_ref):
    here = lax.axis_index("sec")
    side = v_ref.shape[1]
    for k, x in enumerate((x0, x1, x2)):
        unpack(v_ref, k, x[...])
    y = apply(couple_ref, here, v_ref, lcat_ref, rcat_ref)
    pack(y_ref, (), y_ref.shape, jnp.where(mask(size_ref[0], side), y, 0.0))


def fan(out_ref, cw, block, scalars):
    for o in range(out_ref.shape[0]):
        out_ref[o, :cw] = block
        out_ref[o, cw:] = scalars


def first_sum_body(part_ref, x_ref, out_ref):
    o = lax.axis_index("ops")
    cw = part_ref.shape[1]
    block = jnp.sum(part_ref[...], axis=0)
    x = x_ref[o]
    fan(out_ref, cw, block, tile([rows(x * x), rows(x * block)]))


def second_sum_body(part_ref, x_ref, r_ref, g_ref, out_ref):
    o = lax.axis_index("ops")
    cw = part_ref.shape[1]
    block = jnp.sum(part_ref[...], axis=0)
    x, r, h = x_ref[o], r_ref[0, o], g_ref[o][:cw]
    scalars = tile([rows(x * r), rows(r * r), rows(r * h), rows(x * block), rows(r * block)])
    fan(out_ref, cw, block, scalars)


def numbers(g_refs, others, cw, count):
    total = others[...]
    for g in g_refs:
        total = total + jnp.sum(g[:, cw:], axis=0)
    total = jnp.sum(total, axis=1, keepdims=True)
    return [total[i : i + 1] for i in range(count)]


def keep(out_ref, values):
    out_ref[...] = tile([jnp.broadcast_to(v, (1, LANES)) for v in values])


def second_body(
    size_ref, couple_ref, g0, g1, g2, others, x0, x1, x2, d0, d1, d2, lcat_ref, rcat_ref,
    y_ref, r_ref, c_ref, v_ref,
):
    here = lax.axis_index("sec")
    side = v_ref.shape[1]
    cw = x0.shape[1]
    squares, energy = numbers((g0, g1), others, cw, 2)
    factor = lax.rsqrt(squares + 1e-06)
    theta = energy * factor * factor
    keep(c_ref, [factor, theta, squares * factor * factor])
    for k, (g, x, d) in enumerate(((g0, x0, d0), (g1, x1, d1), (g2, x2, d2))):
        r = factor * (g[:, :cw] - theta * x[...]) / (jnp.abs(d[...] - theta) + 1.0)
        r_ref[k] = r
        unpack(v_ref, k, r)
    y = apply(couple_ref, here, v_ref, lcat_ref, rcat_ref)
    pack(y_ref, (), y_ref.shape, jnp.where(mask(size_ref[0], side), y, 0.0))


def third_body(
    size_ref, couple_ref, s0, s1, s2, others, g0, g1, g2, x0, x1, x2, d0, d1, d2, r_in, c_in,
    lcat_ref, rcat_ref, x_ref, r_ref, c_ref, part_ref, v_ref, y_ref,
):
    here = lax.axis_index("sec")
    o = lax.axis_index("ops")
    side = v_ref.shape[1]
    cw = x0.shape[1]
    xr, rr, rh, xhr, rhr = numbers((s0, s1), others, cw, 5)
    factor, first, xx = c_in[0:1, 0:1], c_in[1:2, 0:1], c_in[2:3, 0:1]
    on_x, on_r, theta, xx = update(
        xx, first, factor * xr, rr, factor * rh, factor * xhr, rhr
    )
    on_x = on_x * factor
    keep(c_ref, [theta, xx])
    for k, (s, g, x, d) in enumerate(((s0, g0, x0, d0), (s1, g1, x1, d1), (s2, g2, x2, d2))):
        x = on_x * x[...] + on_r * r_in[k]
        h = on_x * g[:, :cw] + on_r * s[:, :cw]
        r = (h - theta * x) / (jnp.abs(d[...] - theta) + 1.0)
        x_ref[k] = x
        r_ref[k] = r
        unpack(v_ref, k, r)
    y = apply(couple_ref, here, v_ref, lcat_ref, rcat_ref)
    pack(y_ref, (), y_ref.shape, jnp.where(mask(size_ref[0], side), y, 0.0))
    y = y_ref[...]
    x, r = x_ref[0, o], r_ref[0, o]
    h = on_x * g0[o][:cw] + on_r * s0[o][:cw]
    part_ref[...] = tile(
        [rows(x * r), rows(r * r), rows(r * h), rows(x_ref[0] * y), rows(r_ref[0] * y)]
    )


def last_body(
    scale, couple_ref, parts_ref, c_in, x_ref, r_ref, lcat_ref, wave_ref, turn_ref, v_ref
):
    here = lax.axis_index("sec")
    side = v_ref.shape[1]
    total = jnp.sum(jnp.sum(parts_ref[...], axis=0), axis=1, keepdims=True)
    xr, rr, rh, xhr, rhr = [total[i : i + 1] for i in range(5)]
    first, xx = c_in[0:1, 0:1], c_in[1:2, 0:1]
    on_x, on_r, _, _ = update(xx, first, xr, rr, rh, xhr, rhr)
    for k in range(3):
        unpack(v_ref, k, (on_x * scale) * x_ref[k] + (on_r * scale) * r_ref[k])
    wave = v_ref[0]
    wave_ref[0] = wave
    high, low = halves(wave.T * (1.0 / side**0.5))
    turning = jnp.concatenate([high, low, high], axis=1)
    for p in range(lcat_ref.shape[0]):
        high, low = halves(pick(couple_ref, p, here, v_ref))
        inner = dot(lcat_ref[p], jnp.concatenate([high, low, high], axis=0))
        high, low = halves(inner)
        turn_ref[p] = dot(turning, jnp.concatenate([high, high, low], axis=0))


def partner(value):
    count = lax.axis_size("sec")
    return lax.ppermute(value, "sec", [(i, i ^ 1) for i in range(count)])


def other(value):
    count = lax.axis_size("sec")
    route = []
    for i in range(1, count - 1, 2):
        route += [(i, i + 1), (i + 1, i)]
    return lax.ppermute(value, "sec", route)


def rest(value):
    count = lax.axis_size("sec")
    total = jnp.zeros_like(value)
    for d in range(2, count):
        total = total + lax.ppermute(value, "sec", [(i, i ^ d) for i in range(count)])
    return total


def exchange(value):
    return lax.all_to_all(value, "ops", 0, 0)


def local(sector_states, psi_guess, precond_diag, left_ops, right_ops, couple, new_sector):
    side = psi_guess.shape[1]
    pairs = left_ops.shape[0]
    here = lax.axis_index("sec")
    chunks = lax.axis_size("ops")
    sectors = lax.axis_size("sec")
    rc = side // chunks
    cw = rc * side // LANES
    block = jax.ShapeDtypeStruct((chunks, cw, LANES), F32)
    wide = jax.ShapeDtypeStruct((chunks, cw + 8, LANES), F32)
    three = jax.ShapeDtypeStruct((3, chunks, cw, LANES), F32)
    small = jax.ShapeDtypeStruct((8, LANES), F32)
    scratch = pltpu.VMEM((3, side, side), F32)
    work = 12 * pairs * side**3
    light = 20 * side**2

    x0, d0 = call(
        start_body, (block, block), [SMEM, VMEM, VMEM], [], light,
        sector_states, psi_guess, precond_diag,
    )
    x2, x1 = other(x0), partner(x0)
    d2, d1 = other(d0), partner(d0)
    lcat, rcat = call(
        split_body,
        (
            jax.ShapeDtypeStruct((pairs, side, 3 * side), BF16),
            jax.ShapeDtypeStruct((pairs, 3 * side, side), BF16),
        ),
        [VMEM, VMEM], [], light * pairs, left_ops, right_ops,
    )
    (y,) = call(
        first_body, (block,), [SMEM] * 2 + [VMEM] * 5, [scratch], work,
        sector_states, couple, x0, x1, x2, lcat, rcat,
    )
    (g0,) = call(
        first_sum_body, (wide,), [VMEM] * 2, [], light, exchange(y), x0
    )
    g0 = exchange(g0)
    others = rest(jnp.sum(g0[:, cw:], axis=0))
    g2, g1 = other(g0), partner(g0)
    y, r, c = call(
        second_body, (block, three, small), [SMEM] * 2 + [VMEM] * 12, [scratch], work,
        sector_states, couple, g0, g1, g2, others, x0, x1, x2, d0, d1, d2, lcat, rcat,
    )
    (s0,) = call(
        second_sum_body, (wide,), [VMEM] * 4, [], light, exchange(y), x0, r, g0
    )
    s0 = exchange(s0)
    others = rest(jnp.sum(s0[:, cw:], axis=0))
    s2, s1 = other(s0), partner(s0)
    x, r, c, part = call(
        third_body, (three, three, small, small), [SMEM] * 2 + [VMEM] * 17,
        [scratch, pltpu.VMEM(block.shape, F32)], work,
        sector_states, couple, s0, s1, s2, others, g0, g1, g2, x0, x1, x2, d0, d1, d2, r, c,
        lcat, rcat,
    )
    count = chunks * sectors
    parts = lax.all_to_all(
        jnp.broadcast_to(part[None], (count, 8, LANES)), ("ops", "sec"), 0, 0
    )
    wavefunction, turned = call(
        functools.partial(last_body, float((sectors * side * side) ** 0.5)),
        (
            jax.ShapeDtypeStruct((1, side, side), F32),
            jax.ShapeDtypeStruct((pairs, side, side), F32),
        ),
        [SMEM] + [VMEM] * 5, [scratch], work,
        couple, parts, c, x, r, lcat,
    )
    rotated_ops = jnp.where(new_sector[0] == here, turned, partner(turned))[:, None]
    return (wavefunction, rotated_ops)


def solution(mesh):
    in_specs = (
        P("sec"),
        P("sec", None, None),
        P("sec", None, None),
        P("ops", "sec", None, None),
        P("ops", "sec", None, None),
        P("ops", "sec"),
        P("sec"),
    )
    out_specs = (P("sec", None, None), P("ops", "sec", None, None))
    return jax.shard_map(local, mesh=mesh, in_specs=in_specs, out_specs=out_specs, check_vma=False)
```

time: 336 us -> 107 us (0.32)
  waiting for transfers between devices: 231 us -> 11.1 us
  blocking collectives: 33.4 us -> 59.9 us
  between operations: 28.1 us -> 2.1 us
  matrix products: 14.2 us -> 0 us
  other arithmetic: 13.1 us -> 0.89 us
  Pallas kernels: 0 us -> 8.05 us
  starting transfers between devices: 12.8 us -> 20.8 us
    psum x3 -> x0, waiting for transfers between devices: 224 us -> none  [product(): summed = lax.psum(terms, 'ops')]
    all_to_all x0 -> x5, blocking collectives: none -> 59.9 us  [the longest x4 49 us: exchange(): return lax.all_to_all(value, 'ops', 0, 0)]
    psum x5 -> x0, blocking collectives: 33.4 us -> none  [totals(): return lax.psum(values, 'sec')]
    dot_general x12 -> x0, matrix products: 14.2 us -> none  [the longest x3 4.93 us: product(): chosen = jnp.einsum('pk,kij->pij', picks, wide, precision=HIGH)]
    ppermute x7 -> x13, starting transfers between devices: 12.6 us -> 20.8 us  [the longest x4 9.92 us: rest(): lax.ppermute(value, 'sec', [(i, i ^ d) for i in range(count)])]
    reduce_sum x5 -> x2, other arithmetic: 8.08 us -> 0.02 us  [the longest x1 0.01 us: local(): others = rest(jnp.sum(g0[:, cw:], axis=0))]
    pallas_call x0 -> x8, Pallas kernels: none -> 8.05 us  [call(): pl.pallas_call(body, out_shape=tuple(outs), in_specs=in_specs, out_specs=...]
    mul x4 -> x0, other arithmetic: 4.78 us -> none  [the longest x2 2.53 us: local(): (corr - correlation * vecx) * lax.rsqrt(length - correlation * correlatio...]
  transfers between devices with their start and end apart: 10 -> 13, of which waited for: 7 -> 4; matrix products, arithmetic and copies ran while one was open for 0% -> 0% of each run, Pallas kernels for 0% -> 0%
where the time goes in v1:
time: 107 us
  blocking collectives  59.9 us (56%)
  starting transfers between devices  20.8 us (19%)
  waiting for transfers between devices  11.1 us (10%)
  Pallas kernels  8.05 us (8%)
  local copies, waits for them, and re-layouts  3.99 us (4%)
  between operations  2.1 us (2%)
    all_to_all x4, blocking collectives, exchange(): return lax.all_to_all(value, 'ops', 0, 0)  49 us
    all_to_all x1, blocking collectives, local(): lax.all_to_all(jnp.broadcast_to(part[None], (count, 8, LANES)), ('ops', '...  10.9 us
    ppermute x4, waiting for transfers between devices, rest(): lax.ppermute(value, 'sec', [(i, i ^ d) for i in range(count)])  10 us
    ppermute x4, starting transfers between devices, rest(): lax.ppermute(value, 'sec', [(i, i ^ d) for i in range(count)])  9.92 us
    ppermute x5, starting transfers between devices, partner(): return lax.ppermute(value, 'sec', [(i, i ^ 1) for i in range(count)])  8.23 us
    pallas_call x8, Pallas kernels, call(): pl.pallas_call(body, out_shape=tuple(outs), in_specs=in_specs, out_specs=...  8.05 us
    unnamed x11, local copies, waits for them, and re-layouts  3.98 us
    ppermute x4, starting transfers between devices, other(): return lax.ppermute(value, 'sec', route)  2.67 us
  transfers between devices with their start and end apart: 13, of which 4 were waited for; matrix products, arithmetic and copies ran while one was open for 0% of the time, Pallas kernels for 0%

profile of v1, /device:TPU:0, one launch (start us, length us, event | category | flops | bytes accessed | tf_op | source)
XLA Modules:
  0.0 106.8 jit_solution(6292329902200785109)
XLA Ops:
  1.3 0.0 copy-start.2
  1.3 0.9 copy-done.2
  2.2 0.0 copy-start.3
  2.2 0.9 copy-done.3
  3.1 0.1 shard_map.86
  3.1 0.0 copy-start.4
  3.2 0.6 collective-permute-start
  3.7 0.7 collective-permute-start.1
  4.4 0.0 copy-done.4
  4.4 0.1 copy.12.couple_ref
  4.5 0.0 copy-start
  4.5 1.0 copy-done
  5.5 1.0 copy-done.1
  6.6 0.3 shard_map.87
  6.9 0.0 collective-permute-done.x1
  6.9 0.0 collective-permute-done.1.x2
  6.9 1.6 %shard_map.88 = f32[8,64,128]{2,1,0:T(8,128)S(1)} custom-call(s32[1]{0:T(128)S(6)} %copy.14.size_ref, s32[2,1]{1,0:T(2,128)S(1)} %copy.12.couple_ref, f32[8,64,128]{2,1,0:T(8,128)S(1)} %get-tuple-element.15.x0.x_ref, f32[8,64,128]{2,1,0:T(8,128)S(1)} %collective-permute-done.x1, f32[8,64,128]{2,1,0:T(8,128)S(1)} %collective-permute-done.1.x2, ...), custom_call_target="tpu_custom_call" | custom-call | flops 402653184 | bytes 2621452 | tf_op jit(solution)/shard_map/pallas_call | solution.py:20
  8.5 14.8 %all_to_all.25.part_ref = f32[8,64,128]{2,1,0:T(8,128)S(1)} all-to-all(f32[8,64,128]{2,1,0:T(8,128)S(1)} %shard_map.88), channel_id=1, replica_groups=mesh['ops'=8,'sec'=4] {'ops'}, dimensions={0} | all-to-all | bytes 524288 | tf_op jit(solution)/shard_map/all_to_all | solution.py:272
  23.4 11.5 %all_to_all.26.g0.g_ref = f32[8,72,128]{2,1,0:T(8,128)S(1)} all-to-all(f32[8,72,128]{2,1,0:T(8,128)S(1)} %shard_map.89), channel_id=1, replica_groups=mesh['ops'=8,'sec'=4] {'ops'}, dimensions={0} | all-to-all | bytes 589824 | tf_op jit(solution)/shard_map/all_to_all | solution.py:272
  34.9 2.8 %collective-permute-start.2 = (f32[8,72,128]{2,1,0:T(8,128)S(1)}, f32[8,72,128]{2,1,0:T(8,128)S(1)}, u32[]{:S(2)}, u32[]{:S(2)}) collective-permute-start(f32[8,72,128]{2,1,0:T(8,128)S(1)} %all_to_all.26.g0.g_ref), channel_id=1, source_target_pairs={{0,1},{1,0},{2,3},{3,2},{4,5},{5,4},{6,7},{7,6},{8,9},{9,8},{10,11... | collective-permute-start | bytes 884744 | tf_op jit(solution)/shard_map/ppermute | solution.py:252
  37.7 0.7 collective-permute-start.3
  38.4 4.6 %collective-permute-start.6 = (f32[8,64,128]{2,1,0:T(8,128)S(1)}, f32[8,64,128]{2,1,0:T(8,128)S(1)}, u32[]{:S(2)}, u32[]{:S(2)}) collective-permute-start(f32[8,64,128]{2,1,0:T(8,128)S(1)} %get-tuple-element.18.d0), channel_id=1, source_target_pairs={{0,1},{1,0},{2,3},{3,2},{4,5},{5,4},{6,7},{7,6},{8,9},{9,8},{10,11... | collective-permute-start | bytes 786440 | tf_op jit(solution)/shard_map/ppermute | solution.py:252
  43.0 0.7 collective-permute-start.7
  43.7 3.0 %collective-permute-start.4 = (f32[8,128]{1,0:T(8,128)S(1)}, f32[8,128]{1,0:T(8,128)S(1)}, u32[]{:S(2)}, u32[]{:S(2)}) collective-permute-start(f32[8,128]{1,0:T(8,128)S(1)} %slice_reduce_fusion.1), channel_id=1, source_target_pairs={{0,2},{1,3},{2,0},{3,1},{4,6},{5,7},{6,4},{7,5},{8,10},{9,11},{10,... | collective-permute-start | bytes 12296 | tf_op jit(solution)/shard_map/ppermute | solution.py:267
  46.6 4.3 %collective-permute-done.4 = f32[8,128]{1,0:T(8,128)S(1)} collective-permute-done((f32[8,128]{1,0:T(8,128)S(1)}, f32[8,128]{1,0:T(8,128)S(1)}, u32[]{:S(2)}, u32[]{:S(2)}) %collective-permute-start.4) | collective-permute-done | bytes 4128 | tf_op jit(solution)/shard_map/ppermute | solution.py:267
  50.9 0.6 collective-permute-start.5
  51.5 2.4 %collective-permute-done.5 = f32[8,128]{1,0:T(8,128)S(1)} collective-permute-done((f32[8,128]{1,0:T(8,128)S(1)}, f32[8,128]{1,0:T(8,128)S(1)}, u32[]{:S(2)}, u32[]{:S(2)}) %collective-permute-start.5) | collective-permute-done | bytes 4128 | tf_op jit(solution)/shard_map/ppermute | solution.py:267
  54.0 0.0 collective-permute-done.6.d1
  54.0 0.0 collective-permute-done.7.d2
  54.0 0.0 collective-permute-done.2.g1
  54.0 0.0 collective-permute-done.3.g2
  54.0 2.0 %shard_map.90 = (f32[8,64,128]{2,1,0:T(8,128)S(1)}, f32[3,8,64,128]{3,2,1,0:T(8,128)S(1)}, f32[8,128]{1,0:T(8,128)S(1)}) custom-call(s32[1]{0:T(128)S(6)} %copy.14.size_ref, s32[2,1]{1,0:T(2,128)S(1)} %copy.12.couple_ref, f32[8,72,128]{2,1,0:T(8,128)S(1)} %all_to_all.26.g0.g_ref, f32[8,72,128]{2,1,0:T(8,128)S(1)} %collective-permute-done.2.g1, ...), custom_call_target="tpu_custom_call" | custom-call | flops 402653184 | bytes 5087244 | tf_op jit(solution)/shard_map/pallas_call | solution.py:20
  56.0 10.7 %all_to_all.27.part_ref = f32[8,64,128]{2,1,0:T(8,128)S(1)} all-to-all(f32[8,64,128]{2,1,0:T(8,128)S(1)} %get-tuple-element.19), channel_id=1, replica_groups=mesh['ops'=8,'sec'=4] {'ops'}, dimensions={0} | all-to-all | bytes 524288 | tf_op jit(solution)/shard_map/all_to_all | solution.py:272
  66.7 12.0 %all_to_all.28.s0 = f32[8,72,128]{2,1,0:T(8,128)S(1)} all-to-all(f32[8,72,128]{2,1,0:T(8,128)S(1)} %shard_map.91), channel_id=1, replica_groups=mesh['ops'=8,'sec'=4] {'ops'}, dimensions={0} | all-to-all | bytes 589824 | tf_op jit(solution)/shard_map/all_to_all | solution.py:272
  78.7 0.0 collective-permute-start.8
  78.7 0.7 collective-permute-start.9
  79.4 4.9 %collective-permute-start.10 = (f32[8,128]{1,0:T(8,128)S(1)}, f32[8,128]{1,0:T(8,128)S(1)}, u32[]{:S(2)}, u32[]{:S(2)}) collective-permute-start(f32[8,128]{1,0:T(8,128)S(1)} %slice_reduce_fusion), channel_id=1, source_target_pairs={{0,2},{1,3},{2,0},{3,1},{4,6},{5,7},{6,4},{7,5},{8,10},{9,11},{10,... | collective-permute-start | bytes 12296 | tf_op jit(solution)/shard_map/ppermute | solution.py:267
  84.3 1.5 %collective-permute-start.11 = (f32[8,128]{1,0:T(8,128)S(1)}, f32[8,128]{1,0:T(8,128)S(1)}, u32[]{:S(2)}, u32[]{:S(2)}) collective-permute-start(f32[8,128]{1,0:T(8,128)S(1)} %slice_reduce_fusion), channel_id=1, source_target_pairs={{0,3},{1,2},{2,1},{3,0},{4,7},{5,6},{6,5},{7,4},{8,11},{9,10},{10,... | collective-permute-start | bytes 12296 | tf_op jit(solution)/shard_map/ppermute | solution.py:267
  85.8 3.3 %collective-permute-done.10 = f32[8,128]{1,0:T(8,128)S(1)} collective-permute-done((f32[8,128]{1,0:T(8,128)S(1)}, f32[8,128]{1,0:T(8,128)S(1)}, u32[]{:S(2)}, u32[]{:S(2)}) %collective-permute-start.10) | collective-permute-done | bytes 4128 | tf_op jit(solution)/shard_map/ppermute | solution.py:267
  89.1 0.0 collective-permute-done.11
  89.1 0.0 collective-permute-done.8.s1
  89.1 0.0 collective-permute-done.9.s2
  89.1 2.2 %shard_map.92 = (f32[3,8,64,128]{3,2,1,0:T(8,128)S(1)}, f32[3,8,64,128]{3,2,1,0:T(8,128)S(1)}, f32[8,128]{1,0:T(8,128)S(1)}, f32[8,128]{1,0:T(8,128)S(1)}) custom-call(s32[1]{0:T(128)S(6)} %copy.14.size_ref, s32[2,1]{1,0:T(2,128)S(1)} %copy.12.couple_ref, f32[8,72,128]{2,1,0:T(8,128)S(1)} %all_to_all.28.s0, f32[8,72,128]{2,1,0:T(8,128)S(1)} %collective-permute-done.8.s1, ...), custom_call_target="tpu_custom_call" | custom-call | flops 402653184 | bytes 7290892 | tf_op jit(solution)/shard_map/pallas_call | solution.py:20
  91.3 10.9 %all_to_all.29.parts_ref = f32[32,8,128]{2,1,0:T(8,128)S(1)} all-to-all(f32[32,8,128]{2,1,0:T(8,128)S(1)} %broadcast_in_dim.4), channel_id=1, replica_groups=mesh['ops'=8,'sec'=4] {'ops','sec'}, dimensions={0} | all-to-all | bytes 262144 | tf_op jit(solution)/shard_map/all_to_all | solution.py:332
  102.2 1.8 %shard_map.93 = (f32[1,256,256]{2,1,0:T(8,128)}, f32[2,256,256]{2,1,0:T(8,128)S(1)}) custom-call(s32[2,1]{1,0:T(2,128)S(1)} %copy.12.couple_ref, f32[32,8,128]{2,1,0:T(8,128)S(1)} %all_to_all.29.parts_ref, f32[8,128]{1,0:T(8,128)S(1)} %get-tuple-element.23.c_in, f32[3,8,64,128]{3,2,1,0:T(8,128)S(1)} %get-tuple-element.24.x_ref, ...), custom_call_target="tpu_custom_call" | custom-call | flops 402653184 | bytes 3280904 | tf_op jit(solution)/shard_map/pallas_call | solution.py:20
  104.0 0.3 collective-permute-start.12
  104.9 1.0 collective-permute-done.12
  106.0 0.9 select_bitcast_fusion
  (8 shorter events, 0.1 us)
Async XLA Ops:
  1.3 0.9 copy-start.2
  2.2 0.9 copy-start.3
  3.1 1.2 %copy-start.4 = (s32[2,1]{0,1:T(1,128)S(1)}, s32[2,1]{0,1:T(1,128)}, u32[]{:S(2)}) copy-start(s32[2,1]{0,1:T(1,128)} %param.12) | copy-start | bytes 28
  3.2 3.7 %collective-permute-start = (f32[8,64,128]{2,1,0:T(8,128)S(1)}, f32[8,64,128]{2,1,0:T(8,128)S(1)}, u32[]{:S(2)}, u32[]{:S(2)}) collective-permute-start(f32[8,64,128]{2,1,0:T(8,128)S(1)} %get-tuple-element.15.x0.x_ref), channel_id=1, source_target_pairs={{0,1},{1,0},{2,3},{3,2},{4,5},{5,4},{6,7},{7,6},{8,9},{9,8},{10,11... | collective-permute-start | bytes 786440 | tf_op jit(solution)/shard_map/ppermute | solution.py:252
  3.7 3.2 %collective-permute-start.1 = (f32[8,64,128]{2,1,0:T(8,128)S(1)}, f32[8,64,128]{2,1,0:T(8,128)S(1)}, u32[]{:S(2)}, u32[]{:S(2)}) collective-permute-start(f32[8,64,128]{2,1,0:T(8,128)S(1)} %get-tuple-element.15.x0.x_ref), channel_id=1, source_target_pairs={{1,2},{2,1},{5,6},{6,5},{9,10},{10,9},{13,14},{14,13},{17,18},{18,... | collective-permute-start | bytes 786440 | tf_op jit(solution)/shard_map/ppermute | solution.py:260
  4.5 1.0 copy-start
  5.5 1.0 copy-start.1
  34.9 19.0 %collective-permute-start.2 = (f32[8,72,128]{2,1,0:T(8,128)S(1)}, f32[8,72,128]{2,1,0:T(8,128)S(1)}, u32[]{:S(2)}, u32[]{:S(2)}) collective-permute-start(f32[8,72,128]{2,1,0:T(8,128)S(1)} %all_to_all.26.g0.g_ref), channel_id=1, source_target_pairs={{0,1},{1,0},{2,3},{3,2},{4,5},{5,4},{6,7},{7,6},{8,9},{9,8},{10,11... | collective-permute-start | bytes 884744 | tf_op jit(solution)/shard_map/ppermute | solution.py:252
  37.7 16.3 %collective-permute-start.3 = (f32[8,72,128]{2,1,0:T(8,128)S(1)}, f32[8,72,128]{2,1,0:T(8,128)S(1)}, u32[]{:S(2)}, u32[]{:S(2)}) collective-permute-start(f32[8,72,128]{2,1,0:T(8,128)S(1)} %all_to_all.26.g0.g_ref), channel_id=1, source_target_pairs={{1,2},{2,1},{5,6},{6,5},{9,10},{10,9},{13,14},{14,13},{17,18},{18,... | collective-permute-start | bytes 884744 | tf_op jit(solution)/shard_map/ppermute | solution.py:260
  38.4 15.6 %collective-permute-start.6 = (f32[8,64,128]{2,1,0:T(8,128)S(1)}, f32[8,64,128]{2,1,0:T(8,128)S(1)}, u32[]{:S(2)}, u32[]{:S(2)}) collective-permute-start(f32[8,64,128]{2,1,0:T(8,128)S(1)} %get-tuple-element.18.d0), channel_id=1, source_target_pairs={{0,1},{1,0},{2,3},{3,2},{4,5},{5,4},{6,7},{7,6},{8,9},{9,8},{10,11... | collective-permute-start | bytes 786440 | tf_op jit(solution)/shard_map/ppermute | solution.py:252
  43.0 11.0 %collective-permute-start.7 = (f32[8,64,128]{2,1,0:T(8,128)S(1)}, f32[8,64,128]{2,1,0:T(8,128)S(1)}, u32[]{:S(2)}, u32[]{:S(2)}) collective-permute-start(f32[8,64,128]{2,1,0:T(8,128)S(1)} %get-tuple-element.18.d0), channel_id=1, source_target_pairs={{1,2},{2,1},{5,6},{6,5},{9,10},{10,9},{13,14},{14,13},{17,18},{18,... | collective-permute-start | bytes 786440 | tf_op jit(solution)/shard_map/ppermute | solution.py:260
  43.7 7.2 %collective-permute-start.4 = (f32[8,128]{1,0:T(8,128)S(1)}, f32[8,128]{1,0:T(8,128)S(1)}, u32[]{:S(2)}, u32[]{:S(2)}) collective-permute-start(f32[8,128]{1,0:T(8,128)S(1)} %slice_reduce_fusion.1), channel_id=1, source_target_pairs={{0,2},{1,3},{2,0},{3,1},{4,6},{5,7},{6,4},{7,5},{8,10},{9,11},{10,... | collective-permute-start | bytes 12296 | tf_op jit(solution)/shard_map/ppermute | solution.py:267
  50.9 3.0 %collective-permute-start.5 = (f32[8,128]{1,0:T(8,128)S(1)}, f32[8,128]{1,0:T(8,128)S(1)}, u32[]{:S(2)}, u32[]{:S(2)}) collective-permute-start(f32[8,128]{1,0:T(8,128)S(1)} %slice_reduce_fusion.1), channel_id=1, source_target_pairs={{0,3},{1,2},{2,1},{3,0},{4,7},{5,6},{6,5},{7,4},{8,11},{9,10},{10,... | collective-permute-start | bytes 12296 | tf_op jit(solution)/shard_map/ppermute | solution.py:267
  78.7 10.4 %collective-permute-start.8 = (f32[8,72,128]{2,1,0:T(8,128)S(1)}, f32[8,72,128]{2,1,0:T(8,128)S(1)}, u32[]{:S(2)}, u32[]{:S(2)}) collective-permute-start(f32[8,72,128]{2,1,0:T(8,128)S(1)} %all_to_all.28.s0), channel_id=1, source_target_pairs={{0,1},{1,0},{2,3},{3,2},{4,5},{5,4},{6,7},{7,6},{8,9},{9,8},{10,11... | collective-permute-start | bytes 884744 | tf_op jit(solution)/shard_map/ppermute | solution.py:252
  78.7 10.4 %collective-permute-start.9 = (f32[8,72,128]{2,1,0:T(8,128)S(1)}, f32[8,72,128]{2,1,0:T(8,128)S(1)}, u32[]{:S(2)}, u32[]{:S(2)}) collective-permute-start(f32[8,72,128]{2,1,0:T(8,128)S(1)} %all_to_all.28.s0), channel_id=1, source_target_pairs={{1,2},{2,1},{5,6},{6,5},{9,10},{10,9},{13,14},{14,13},{17,18},{18,... | collective-permute-start | bytes 884744 | tf_op jit(solution)/shard_map/ppermute | solution.py:260
  79.4 9.6 %collective-permute-start.10 = (f32[8,128]{1,0:T(8,128)S(1)}, f32[8,128]{1,0:T(8,128)S(1)}, u32[]{:S(2)}, u32[]{:S(2)}) collective-permute-start(f32[8,128]{1,0:T(8,128)S(1)} %slice_reduce_fusion), channel_id=1, source_target_pairs={{0,2},{1,3},{2,0},{3,1},{4,6},{5,7},{6,4},{7,5},{8,10},{9,11},{10,... | collective-permute-start | bytes 12296 | tf_op jit(solution)/shard_map/ppermute | solution.py:267
  84.3 4.7 %collective-permute-start.11 = (f32[8,128]{1,0:T(8,128)S(1)}, f32[8,128]{1,0:T(8,128)S(1)}, u32[]{:S(2)}, u32[]{:S(2)}) collective-permute-start(f32[8,128]{1,0:T(8,128)S(1)} %slice_reduce_fusion), channel_id=1, source_target_pairs={{0,3},{1,2},{2,1},{3,0},{4,7},{5,6},{6,5},{7,4},{8,11},{9,10},{10,... | collective-permute-start | bytes 12296 | tf_op jit(solution)/shard_map/ppermute | solution.py:267
  104.0 2.0 %collective-permute-start.12 = (f32[2,256,256]{2,1,0:T(8,128)S(1)}, f32[2,256,256]{2,1,0:T(8,128)S(1)}, u32[]{:S(2)}, u32[]{:S(2)}) collective-permute-start(f32[2,256,256]{2,1,0:T(8,128)S(1)} %get-tuple-element.27), channel_id=1, source_target_pairs={{0,1},{1,0},{2,3},{3,2},{4,5},{5,4},{6,7},{7,6},{8,9},{9,8},{10,11... | collective-permute-start | bytes 1572872 | tf_op jit(solution)/shard_map/ppermute | solution.py:252

commit v2 on v1

v2 whole, which is shorter than its diff:
```python
import functools

import jax
import jax.numpy as jnp
from jax import lax
from jax.experimental import pallas as pl
from jax.experimental.pallas import tpu as pltpu
from jax.sharding import PartitionSpec as P

LANES = 128
F32 = jnp.float32
BF16 = jnp.bfloat16
VMEM = pl.BlockSpec(memory_space=pltpu.VMEM)
SMEM = pl.BlockSpec(memory_space=pltpu.SMEM)


def call(body, outs, in_specs, scratch, flops, *args):
    size = sum(a.size * a.dtype.itemsize for a in args)
    size += sum(o.size * o.dtype.itemsize for o in outs)
    return pl.pallas_call(
        body,
        out_shape=tuple(outs),
        in_specs=in_specs,
        out_specs=tuple(VMEM for _ in outs),
        scratch_shapes=scratch,
        compiler_params=pltpu.CompilerParams(vmem_limit_bytes=24 * 1024 * 1024),
        cost_estimate=pl.CostEstimate(flops=flops, bytes_accessed=size, transcendentals=0),
    )(*args)


def pack(ref, lead, block, value):
    rc = value.shape[0] // block[0]
    for o in range(block[0]):
        for j in range(value.shape[1] // LANES):
            ref[lead + (o, slice(j * rc, (j + 1) * rc))] = value[
                o * rc : (o + 1) * rc, j * LANES : (j + 1) * LANES
            ]


def unpack(ref, k, value):
    chunks, cw, _ = value.shape
    side = ref.shape[1]
    rc = side // chunks
    for o in range(chunks):
        for j in range(side // LANES):
            ref[k, o * rc : (o + 1) * rc, j * LANES : (j + 1) * LANES] = value[
                o, j * rc : (j + 1) * rc
            ]


def halves(value):
    high = value.astype(BF16)
    low = (value - high.astype(F32)).astype(BF16)
    return high, low


def dot(a, b):
    return jnp.dot(a, b, preferred_element_type=F32)


def mask(size, side):
    rows = lax.broadcasted_iota(jnp.int32, (side, side), 0)
    cols = lax.broadcasted_iota(jnp.int32, (side, side), 1)
    return (rows < size) & (cols < size)


def pick(couple_ref, p, here, ref):
    source = couple_ref[p, 0]
    slot = jnp.where(source == here, 0, jnp.where(source == here + 1 - 2 * (here % 2), 1, 2))
    return jnp.where(source >= 0, ref[slot], 0.0)


def apply(couple_ref, here, ref, lcat_ref, rcat_ref):
    total = None
    for p in range(lcat_ref.shape[0]):
        high, low = halves(pick(couple_ref, p, here, ref))
        mixed = dot(lcat_ref[p], jnp.concatenate([high, low, high], axis=0))
        high, low = halves(mixed)
        term = dot(jnp.concatenate([high, low, high], axis=1), rcat_ref[p])
        total = term if total is None else total + term
    return total


def rows(value):
    return jnp.sum(value.reshape(-1, LANES), axis=0, keepdims=True)


def tile(parts):
    parts = parts + [jnp.zeros((8 - len(parts), LANES), F32)]
    return jnp.concatenate(parts, axis=0)


def half_angle(middle, first, last):
    gap = last - first
    tilt = -2.0 * middle
    length = jnp.sqrt(gap * gap + tilt * tilt)
    safe = jnp.where(length > 0.0, length, 1.0)
    big = jnp.where(length > 0.0, jnp.sqrt(0.5 + 0.5 * jnp.abs(gap) / safe), 1.0)
    small = 0.5 * tilt / (safe * big)
    sign = jnp.where(tilt > 0.0, 1.0, -1.0)
    cosine = jnp.where(gap >= 0.0, big, jnp.abs(small))
    sine = jnp.where(gap >= 0.0, small, sign * big)
    return cosine, sine, 0.5 * (first + last) - 0.5 * length


def update(xx, first, xr, rr, rh, xhr, rhr):
    n = lax.rsqrt(rr - 2.0 * xr * xr + xr * xr * xx + 1e-06)
    middle = 0.5 * n * ((xhr - xr * first) + (rh - xr * first))
    last = n * n * (rhr - xr * rh - xr * xhr + xr * xr * first)
    cosine, sine, theta = half_angle(middle, first, last)
    on_r = sine * n
    on_x = cosine - on_r * xr
    xx = on_x * on_x * xx + 2.0 * on_x * on_r * xr + on_r * on_r * rr
    return on_x, on_r, theta, xx


def start_body(size_ref, psi_ref, x_ref):
    live = mask(size_ref[0], psi_ref.shape[1])
    pack(x_ref, (), x_ref.shape, jnp.where(live, psi_ref[0].astype(F32), 0.0))


def split_body(left_ref, right_ref, diag_ref, lcat_ref, rcat_ref, d_ref):
    for p in range(left_ref.shape[0]):
        high, low = halves(left_ref[p, 0])
        lcat_ref[p] = jnp.concatenate([high, high, low], axis=1)
        high, low = halves(right_ref[p, 0].T)
        rcat_ref[p] = jnp.concatenate([high, high, low], axis=0)
    pack(d_ref, (), d_ref.shape, diag_ref[0].astype(F32))


def product(size_ref, couple_ref, blocks, lcat_ref, rcat_ref, y_ref, v_ref):
    here = lax.axis_index("sec")
    for k, block in enumerate(blocks):
        unpack(v_ref, k, block[...])
    y = apply(couple_ref, here, v_ref, lcat_ref, rcat_ref)
    y = jnp.where(mask(size_ref[0], v_ref.shape[1]), y, 0.0)
    pack(y_ref, (), y_ref.shape, y)


def first_body(size_ref, couple_ref, x0, x1, x2, lcat_ref, rcat_ref, y_ref, part_ref, v_ref):
    product(size_ref, couple_ref, (x0, x1, x2), lcat_ref, rcat_ref, y_ref, v_ref)
    x = x0[lax.axis_index("ops")]
    part_ref[...] = tile([rows(x * x), rows(x0[...] * y_ref[...])])


def second_body(
    size_ref, couple_ref, r0, r1, r2, x0, g0, lcat_ref, rcat_ref, y_ref, part_ref, v_ref
):
    product(size_ref, couple_ref, (r0, r1, r2), lcat_ref, rcat_ref, y_ref, v_ref)
    o = lax.axis_index("ops")
    x, r, h = x0[o], r0[o], g0[o][: x0.shape[1]]
    y = y_ref[...]
    part_ref[...] = tile(
        [rows(x * r), rows(r * r), rows(r * h), rows(x0[...] * y), rows(r0[...] * y)]
    )


def sum_body(terms_ref, mine, others, out_ref):
    cw = terms_ref.shape[1]
    block = jnp.sum(terms_ref[...], axis=0)
    scalars = mine[...] + others[...]
    for o in range(out_ref.shape[0]):
        out_ref[o, :cw] = block
        out_ref[o, cw:] = scalars


def numbers(tiles, count):
    total = jnp.sum(jnp.sum(tiles, axis=0), axis=1, keepdims=True)
    return [total[i : i + 1] for i in range(count)]


def store(out_ref, values):
    out_ref[...] = tile([jnp.broadcast_to(v, (1, LANES)) for v in values])


def first_residual_body(g_ref, x_ref, d_ref, r_ref, c_ref):
    cw = x_ref.shape[1]
    squares, energy = numbers(g_ref[:, cw:], 2)
    factor = lax.rsqrt(squares + 1e-06)
    theta = energy * factor * factor
    r = factor * (g_ref[:, :cw] - theta * x_ref[...]) / (jnp.abs(d_ref[...] - theta) + 1.0)
    r_ref[...] = r
    store(c_ref, [factor, theta, squares * factor * factor])


def second_residual_body(s_ref, g_ref, x_ref, d_ref, r_in, c_in, x_out, h_out, r_ref, c_ref):
    cw = x_ref.shape[1]
    xr, rr, rh, xhr, rhr = numbers(s_ref[:, cw:], 5)
    factor, first, xx = c_in[0:1, 0:1], c_in[1:2, 0:1], c_in[2:3, 0:1]
    on_x, on_r, theta, xx = update(
        xx, first, factor * xr, rr, factor * rh, factor * xhr, rhr
    )
    on_x = on_x * factor
    x = on_x * x_ref[...] + on_r * r_in[...]
    h = on_x * g_ref[:, :cw] + on_r * s_ref[:, :cw]
    x_out[...] = x
    h_out[...] = h
    r_ref[...] = (h - theta * x) / (jnp.abs(d_ref[...] - theta) + 1.0)
    store(c_ref, [theta, xx, on_x, on_r])


def last_body(
    scale, couple_ref, parts_ref, c_in, x0, x1, x2, r0, r1, r2, s0, s1, s2, lcat_ref,
    wave_ref, turn_ref, v_ref,
):
    here = lax.axis_index("sec")
    side = v_ref.shape[1]
    xr, rr, rh, xhr, rhr = numbers(parts_ref[...], 5)
    first, xx, x_part, r_part = [c_in[i : i + 1, 0:1] for i in range(4)]
    on_x, on_s, _, _ = update(xx, first, xr, rr, rh, xhr, rhr)
    on_r = on_x * r_part * scale
    on_x = on_x * x_part * scale
    on_s = on_s * scale
    for k, (x, r, s) in enumerate(((x0, r0, s0), (x1, r1, s1), (x2, r2, s2))):
        unpack(v_ref, k, on_x * x[...] + on_r * r[...] + on_s * s[...])
    wave = v_ref[0]
    wave_ref[0] = wave
    high, low = halves(wave.T * (1.0 / side**0.5))
    turning = jnp.concatenate([high, low, high], axis=1)
    for p in range(lcat_ref.shape[0]):
        high, low = halves(pick(couple_ref, p, here, v_ref))
        inner = dot(lcat_ref[p], jnp.concatenate([high, low, high], axis=0))
        high, low = halves(inner)
        turn_ref[p] = dot(turning, jnp.concatenate([high, high, low], axis=0))


def partner(value):
    count = lax.axis_size("sec")
    return lax.ppermute(value, "sec", [(i, i ^ 1) for i in range(count)])


def other(value):
    count = lax.axis_size("sec")
    route = []
    for i in range(1, count - 1, 2):
        route += [(i, i + 1), (i + 1, i)]
    return lax.ppermute(value, "sec", route)


def over_sectors(value):
    count = lax.axis_size("sec")
    total = jnp.zeros_like(value)
    for d in range(1, count):
        total = total + lax.ppermute(value, "sec", [(i, i ^ d) for i in range(count)])
    return total


def exchange(value):
    return lax.all_to_all(value, "ops", 0, 0)


def local(sector_states, psi_guess, precond_diag, left_ops, right_ops, couple, new_sector):
    side = psi_guess.shape[1]
    pairs = left_ops.shape[0]
    here = lax.axis_index("sec")
    chunks = lax.axis_size("ops")
    sectors = lax.axis_size("sec")
    cw = side // chunks * side // LANES
    block = jax.ShapeDtypeStruct((chunks, cw, LANES), F32)
    wide = jax.ShapeDtypeStruct((chunks, cw + 8, LANES), F32)
    small = jax.ShapeDtypeStruct((8, LANES), F32)
    scratch = pltpu.VMEM((3, side, side), F32)
    work = 12 * pairs * side**3
    light = 20 * side**2

    def gathered(y, part):
        others = over_sectors(part)
        (full,) = call(
            sum_body, (wide,), [VMEM] * 3, [], light, exchange(y), part, others
        )
        return exchange(full)

    (x0,) = call(start_body, (block,), [SMEM, VMEM], [], light, sector_states, psi_guess)
    x2, x1 = other(x0), partner(x0)
    lcat, rcat, d = call(
        split_body,
        (
            jax.ShapeDtypeStruct((pairs, side, 3 * side), BF16),
            jax.ShapeDtypeStruct((pairs, 3 * side, side), BF16),
            block,
        ),
        [VMEM] * 3, [], light * pairs, left_ops, right_ops, precond_diag,
    )
    y, part = call(
        first_body, (block, small), [SMEM] * 2 + [VMEM] * 5, [scratch], work,
        sector_states, couple, x0, x1, x2, lcat, rcat,
    )
    g = gathered(y, part)
    r0, c = call(first_residual_body, (block, small), [VMEM] * 3, [], light, g, x0, d)
    r2, r1 = other(r0), partner(r0)
    y, part = call(
        second_body, (block, small), [SMEM] * 2 + [VMEM] * 7, [scratch], work,
        sector_states, couple, r0, r1, r2, x0, g, lcat, rcat,
    )
    s = gathered(y, part)
    x, h, s0, c = call(
        second_residual_body, (block, block, block, small), [VMEM] * 6, [], light,
        s, g, x0, d, r0, c,
    )
    s2, s1 = other(s0), partner(s0)
    y, part = call(
        second_body, (block, small), [SMEM] * 2 + [VMEM] * 7, [scratch], work,
        sector_states, couple, s0, s1, s2, x, h, lcat, rcat,
    )
    count = chunks * sectors
    parts = lax.all_to_all(
        jnp.broadcast_to(part[None], (count, 8, LANES)), ("ops", "sec"), 0, 0
    )
    wavefunction, turned = call(
        functools.partial(last_body, float((sectors * side * side) ** 0.5)),
        (
            jax.ShapeDtypeStruct((1, side, side), F32),
            jax.ShapeDtypeStruct((pairs, side, side), F32),
        ),
        [SMEM] + [VMEM] * 12, [scratch], work,
        couple, parts, c, x0, x1, x2, r0, r1, r2, s0, s1, s2, lcat,
    )
    rotated_ops = jnp.where(new_sector[0] == here, turned, partner(turned))[:, None]
    return (wavefunction, rotated_ops)


def solution(mesh):
    in_specs = (
        P("sec"),
        P("sec", None, None),
        P("sec", None, None),
        P("ops", "sec", None, None),
        P("ops", "sec", None, None),
        P("ops", "sec"),
        P("sec"),
    )
    out_specs = (P("sec", None, None), P("ops", "sec", None, None))
    return jax.shard_map(local, mesh=mesh, in_specs=in_specs, out_specs=out_specs, check_vma=False)
```

time: 107 us -> 103 us (0.963)
  blocking collectives: 59.9 us -> 49.4 us
  starting transfers between devices: 20.8 us -> 28.1 us
  waiting for transfers between devices: 11.1 us -> 7.9 us
  Pallas kernels: 8.05 us -> 10.1 us
    all_to_all x4 -> x2, blocking collectives: 49 us -> 33.1 us  [exchange(): return lax.all_to_all(value, 'ops', 0, 0)]
    all_to_all x0 -> x2, starting transfers between devices: none -> 10.9 us  [exchange(): return lax.all_to_all(value, 'ops', 0, 0)]
    ppermute x5 -> x4, starting transfers between devices: 8.23 us -> 0.98 us  [partner(): return lax.ppermute(value, 'sec', [(i, i ^ 1) for i in range(count)])]
    all_to_all x1, blocking collectives: 10.9 us -> 16.3 us  [local(): lax.all_to_all(jnp.broadcast_to(part[None], (count, 8, LANES)), ('ops', '...]
    ppermute x4 -> x6, waiting for transfers between devices: 10 us -> 5.17 us  [over_sectors(): lax.ppermute(value, 'sec', [(i, i ^ d) for i in range(count)])]
    ppermute x4 -> x6, starting transfers between devices: 9.92 us -> 14.2 us  [over_sectors(): lax.ppermute(value, 'sec', [(i, i ^ d) for i in range(count)])]
    pallas_call x8 -> x10, Pallas kernels: 8.05 us -> 10.1 us  [call(): pl.pallas_call(body, out_shape=tuple(outs), in_specs=in_specs, out_specs=...]
    ppermute x5 -> x4, waiting for transfers between devices: 1.05 us -> 2.72 us  [partner(): return lax.ppermute(value, 'sec', [(i, i ^ 1) for i in range(count)])]
  transfers between devices with their start and end apart: 13 -> 15, of which waited for: 4 -> 6; matrix products, arithmetic and copies ran while one was open for 0% -> 0% of each run, Pallas kernels for 0% -> 0%
where the time goes in v2:
time: 103 us; the launch traced here: 102 us
  blocking collectives  49.4 us (48%)
  starting transfers between devices  28.1 us (27%)
  Pallas kernels  10.1 us (10%)
  waiting for transfers between devices  7.9 us (8%)
  local copies, waits for them, and re-layouts  3.8 us (4%)
  between operations  2.1 us (2%)
    all_to_all x2, blocking collectives, exchange(): return lax.all_to_all(value, 'ops', 0, 0)  33.1 us
    all_to_all x1, blocking collectives, local(): lax.all_to_all(jnp.broadcast_to(part[None], (count, 8, LANES)), ('ops', '...  16.3 us
    ppermute x6, starting transfers between devices, over_sectors(): lax.ppermute(value, 'sec', [(i, i ^ d) for i in range(count)])  14.2 us
    all_to_all x2, starting transfers between devices, exchange(): return lax.all_to_all(value, 'ops', 0, 0)  10.9 us
    pallas_call x10, Pallas kernels, call(): pl.pallas_call(body, out_shape=tuple(outs), in_specs=in_specs, out_specs=...  10.1 us
    ppermute x6, waiting for transfers between devices, over_sectors(): lax.ppermute(value, 'sec', [(i, i ^ d) for i in range(count)])  5.17 us
    unnamed x17, local copies, waits for them, and re-layouts  3.79 us
    ppermute x4, waiting for transfers between devices, partner(): return lax.ppermute(value, 'sec', [(i, i ^ 1) for i in range(count)])  2.72 us
  transfers between devices with their start and end apart: 15, of which 6 were waited for; matrix products, arithmetic and copies ran while one was open for 0% of the time, Pallas kernels for 0%

profile of v2, /device:TPU:0, one launch (start us, length us, event | category | flops | bytes accessed | tf_op | source)
XLA Modules:
  0.0 102.3 jit_solution(5057655995078722041)
XLA Ops:
  1.3 0.9 copy-done.6
  2.2 0.6 collective-permute-start
  2.8 0.7 collective-permute-start.1
  3.5 0.1 copy.12.couple_ref
  3.6 1.0 %copy-done.2 = f32[2,1,256,256]{3,2,1,0:T(8,128)S(1)} copy-done((f32[2,1,256,256]{3,2,1,0:T(8,128)S(1)}, f32[2,1,256,256]{3,2,1,0:T(8,128)}, u32[]{:S(2)}) %copy-start.2) | copy-done | bytes 524312
  4.6 1.0 %copy-done.3 = f32[2,1,256,256]{3,2,1,0:T(8,128)S(1)} copy-done((f32[2,1,256,256]{3,2,1,0:T(8,128)S(1)}, f32[2,1,256,256]{3,2,1,0:T(8,128)}, u32[]{:S(2)}) %copy-start.3) | copy-done | bytes 524312
  5.6 0.3 shard_map.87
  6.0 0.0 copy-start
  6.0 0.0 collective-permute-done.x1
  6.0 0.0 collective-permute-done.1.x2
  6.0 2.3 %shard_map.88 = (f32[8,64,128]{2,1,0:T(8,128)}, f32[8,128]{1,0:T(8,128)S(1)}) custom-call(s32[1]{0:T(128)S(6)} %copy.14.size_ref, s32[2,1]{1,0:T(2,128)S(1)} %copy.12.couple_ref, f32[8,64,128]{2,1,0:T(8,128)S(1)} %shard_map.86.x0.x_ref, f32[8,64,128]{2,1,0:T(8,128)S(1)} %collective-permute-done.x1, f32[8,64,128]{2,1,0:T(8,128)S(1)} %collective-permute-done.1.x2, ...), custom_call_target="tpu_custom_call" | custom-call | flops 402653184 | bytes 2625548 | tf_op jit(solution)/shard_map/pallas_call | solution.py:20
  8.3 6.8 %all-to-all-start = ((f32[8,64,128]{2,1,0:T(8,128)}), f32[8,64,128]{2,1,0:T(8,128)S(1)}, u32[]{:S(2)}, u32[]{:S(2)}) async-start(f32[8,64,128]{2,1,0:T(8,128)} %get-tuple-element.20), calls=%async_computation | async-start | bytes 524288 | tf_op jit(solution)/shard_map/all_to_all | solution.py:249
  15.2 4.7 %collective-permute-start.2 = (f32[8,128]{1,0:T(8,128)S(1)}, f32[8,128]{1,0:T(8,128)S(1)}, u32[]{:S(2)}, u32[]{:S(2)}) collective-permute-start(f32[8,128]{1,0:T(8,128)S(1)} %get-tuple-element.21.mine), channel_id=1, source_target_pairs={{0,1},{1,0},{2,3},{3,2},{4,5},{5,4},{6,7},{7,6},{8,9},{9,8},{10,11... | collective-permute-start | bytes 12296 | tf_op jit(solution)/shard_map/ppermute | solution.py:244
  19.8 1.4 %collective-permute-start.3 = (f32[8,128]{1,0:T(8,128)S(1)}, f32[8,128]{1,0:T(8,128)S(1)}, u32[]{:S(2)}, u32[]{:S(2)}) collective-permute-start(f32[8,128]{1,0:T(8,128)S(1)} %get-tuple-element.21.mine), channel_id=1, source_target_pairs={{0,2},{1,3},{2,0},{3,1},{4,6},{5,7},{6,4},{7,5},{8,10},{9,11},{10,... | collective-permute-start | bytes 12296 | tf_op jit(solution)/shard_map/ppermute | solution.py:244
  21.2 0.0 collective-permute-start.4
  21.2 2.2 %collective-permute-done.3 = f32[8,128]{1,0:T(8,128)S(1)} collective-permute-done((f32[8,128]{1,0:T(8,128)S(1)}, f32[8,128]{1,0:T(8,128)S(1)}, u32[]{:S(2)}, u32[]{:S(2)}) %collective-permute-start.3) | collective-permute-done | bytes 4128 | tf_op jit(solution)/shard_map/ppermute | solution.py:244
  23.4 0.8 collective-permute-done.4
  24.2 0.0 all-to-all-done.terms_ref
  24.3 16.5 %all_to_all.25.g_ref.g0 = f32[8,72,128]{2,1,0:T(8,128)S(1)} all-to-all(f32[8,72,128]{2,1,0:T(8,128)S(1)} %shard_map.89), channel_id=1, replica_groups=mesh['ops'=8,'sec'=4] {'ops'}, dimensions={0} | all-to-all | bytes 589824 | tf_op jit(solution)/shard_map/all_to_all | solution.py:249
  40.7 0.2 shard_map.90
  41.0 0.1 collective-permute-start.5
  41.1 0.7 collective-permute-start.6
  41.7 0.8 collective-permute-done.5.r1
  42.6 0.0 collective-permute-done.6.r2
  42.6 1.6 %shard_map.91 = (f32[8,64,128]{2,1,0:T(8,128)S(1)}, f32[8,128]{1,0:T(8,128)S(1)}) custom-call(s32[1]{0:T(128)S(6)} %copy.14.size_ref, s32[2,1]{1,0:T(2,128)S(1)} %copy.12.couple_ref, f32[8,64,128]{2,1,0:T(8,128)S(1)} %get-tuple-element.23.r0.r_in, f32[8,64,128]{2,1,0:T(8,128)S(1)} %collective-permute-done.5.r1, f32[8,64,128]{2,1,0:T(8,128)S(1)} %collective-permute-done.6.r2, ...), custom_call_target="tpu_custom_call" | custom-call | flops 402653184 | bytes 3182604 | tf_op jit(solution)/shard_map/pallas_call | solution.py:20
  44.2 0.0 copy-start.4
  44.2 0.7 copy-done.4
  44.9 4.0 %all-to-all-start.2 = ((f32[8,64,128]{2,1,0:T(8,128)}), f32[8,64,128]{2,1,0:T(8,128)}, u32[]{:S(2)}, u32[]{:S(2)}) async-start(f32[8,64,128]{2,1,0:T(8,128)} %copy-done.4), calls=%async_computation.2 | async-start | bytes 524288 | tf_op jit(solution)/shard_map/all_to_all | solution.py:249
  49.0 6.7 %collective-permute-start.7 = (f32[8,128]{1,0:T(8,128)S(1)}, f32[8,128]{1,0:T(8,128)S(1)}, u32[]{:S(2)}, u32[]{:S(2)}) collective-permute-start(f32[8,128]{1,0:T(8,128)S(1)} %get-tuple-element.25.mine), channel_id=1, source_target_pairs={{0,1},{1,0},{2,3},{3,2},{4,5},{5,4},{6,7},{7,6},{8,9},{9,8},{10,11... | collective-permute-start | bytes 12296 | tf_op jit(solution)/shard_map/ppermute | solution.py:244
  55.7 0.2 collective-permute-start.8
  55.9 1.2 %collective-permute-start.9 = (f32[8,128]{1,0:T(8,128)S(1)}, f32[8,128]{1,0:T(8,128)S(1)}, u32[]{:S(2)}, u32[]{:S(2)}) collective-permute-start(f32[8,128]{1,0:T(8,128)S(1)} %get-tuple-element.25.mine), channel_id=1, source_target_pairs={{0,3},{1,2},{2,1},{3,0},{4,7},{5,6},{6,5},{7,4},{8,11},{9,10},{10,... | collective-permute-start | bytes 12296 | tf_op jit(solution)/shard_map/ppermute | solution.py:244
  57.1 2.2 %collective-permute-done.8 = f32[8,128]{1,0:T(8,128)S(1)} collective-permute-done((f32[8,128]{1,0:T(8,128)S(1)}, f32[8,128]{1,0:T(8,128)S(1)}, u32[]{:S(2)}, u32[]{:S(2)}) %collective-permute-start.8) | collective-permute-done | bytes 4128 | tf_op jit(solution)/shard_map/ppermute | solution.py:244
  59.3 0.0 collective-permute-done.9
  59.3 0.0 all-to-all-done.2.terms_ref
  59.3 1.0 shard_map.92
  60.3 0.0 copy-start.1
  60.3 16.7 %all_to_all.26.s_ref = f32[8,72,128]{2,1,0:T(8,128)S(1)} all-to-all(f32[8,72,128]{2,1,0:T(8,128)S(1)} %shard_map.92), channel_id=1, replica_groups=mesh['ops'=8,'sec'=4] {'ops'}, dimensions={0} | all-to-all | bytes 589824 | tf_op jit(solution)/shard_map/all_to_all | solution.py:249
  77.0 0.4 shard_map.93
  77.4 0.1 collective-permute-start.10
  77.5 0.7 collective-permute-start.11
  78.1 0.8 collective-permute-done.10.r1.s1
  79.0 0.0 collective-permute-done.11.r2.s2
  79.0 2.3 %shard_map.94 = (f32[8,64,128]{2,1,0:T(8,128)}, f32[8,128]{1,0:T(8,128)S(1)}) custom-call(s32[1]{0:T(128)S(6)} %copy.14.size_ref, s32[2,1]{1,0:T(2,128)S(1)} %copy.12.couple_ref, f32[8,64,128]{2,1,0:T(8,128)S(1)} %get-tuple-element.27.r0.s0, f32[8,64,128]{2,1,0:T(8,128)S(1)} %collective-permute-done.10.r1.s1, ...), custom_call_target="tpu_custom_call" | custom-call | flops 402653184 | bytes 3149836 | tf_op jit(solution)/shard_map/pallas_call | solution.py:20
  81.3 16.3 %all_to_all.27.parts_ref = f32[32,8,128]{2,1,0:T(8,128)S(1)} all-to-all(f32[32,8,128]{2,1,0:T(8,128)S(1)} %broadcast_in_dim.4), channel_id=1, replica_groups=mesh['ops'=8,'sec'=4] {'ops','sec'}, dimensions={0} | all-to-all | bytes 262144 | tf_op jit(solution)/shard_map/all_to_all | solution.py:306
  97.6 1.8 %shard_map.95 = (f32[1,256,256]{2,1,0:T(8,128)}, f32[2,256,256]{2,1,0:T(8,128)S(1)}) custom-call(s32[2,1]{1,0:T(2,128)S(1)} %copy.12.couple_ref, f32[32,8,128]{2,1,0:T(8,128)S(1)} %all_to_all.27.parts_ref, f32[8,128]{1,0:T(8,128)S(1)} %get-tuple-element.31.c_in, f32[8,64,128]{2,1,0:T(8,128)S(1)} %shard_map.86.x0.x_ref, ...), custom_call_target="tpu_custom_call" | custom-call | flops 402653184 | bytes 4067336 | tf_op jit(solution)/shard_map/pallas_call | solution.py:20
  99.4 0.3 collective-permute-start.12
  100.3 1.0 %collective-permute-done.12 = f32[2,256,256]{2,1,0:T(8,128)S(1)} collective-permute-done((f32[2,256,256]{2,1,0:T(8,128)S(1)}, f32[2,256,256]{2,1,0:T(8,128)S(1)}, u32[]{:S(2)}, u32[]{:S(2)}) %collective-permute-start.12) | collective-permute-done | bytes 524320 | tf_op jit(solution)/shard_map/ppermute | solution.py:229
  101.4 0.9 select_bitcast_fusion
  (16 shorter events, 0.1 us)
Async XLA Ops:
  1.3 0.9 copy-start.6
  2.2 1.3 %copy-start.7 = (s32[2,1]{0,1:T(1,128)S(1)}, s32[2,1]{0,1:T(1,128)}, u32[]{:S(2)}) copy-start(s32[2,1]{0,1:T(1,128)} %param.12) | copy-start | bytes 28
  2.2 1.4 %copy-start.5 = (bf16[1,256,256]{2,1,0:T(8,128)(2,1)S(1)}, bf16[1,256,256]{2,1,0:T(8,128)(2,1)}, u32[]{:S(2)}) copy-start(bf16[1,256,256]{2,1,0:T(8,128)(2,1)} %diag_ref.1) | copy-start | bytes 393220
  2.2 3.8 %collective-permute-start = (f32[8,64,128]{2,1,0:T(8,128)S(1)}, f32[8,64,128]{2,1,0:T(8,128)S(1)}, u32[]{:S(2)}, u32[]{:S(2)}) collective-permute-start(f32[8,64,128]{2,1,0:T(8,128)S(1)} %shard_map.86.x0.x_ref), channel_id=1, source_target_pairs={{0,1},{1,0},{2,3},{3,2},{4,5},{5,4},{6,7},{7,6},{8,9},{9,8},{10,11... | collective-permute-start | bytes 786440 | tf_op jit(solution)/shard_map/ppermute | solution.py:229
  2.8 3.2 %collective-permute-start.1 = (f32[8,64,128]{2,1,0:T(8,128)S(1)}, f32[8,64,128]{2,1,0:T(8,128)S(1)}, u32[]{:S(2)}, u32[]{:S(2)}) collective-permute-start(f32[8,64,128]{2,1,0:T(8,128)S(1)} %shard_map.86.x0.x_ref), channel_id=1, source_target_pairs={{1,2},{2,1},{5,6},{6,5},{9,10},{10,9},{13,14},{14,13},{17,18},{18,... | collective-permute-start | bytes 786440 | tf_op jit(solution)/shard_map/ppermute | solution.py:237
  3.6 1.0 %copy-start.2 = (f32[2,1,256,256]{3,2,1,0:T(8,128)S(1)}, f32[2,1,256,256]{3,2,1,0:T(8,128)}, u32[]{:S(2)}) copy-start(f32[2,1,256,256]{3,2,1,0:T(8,128)} %left_ref.1) | copy-start | bytes 1572868
  4.6 1.0 %copy-start.3 = (f32[2,1,256,256]{3,2,1,0:T(8,128)S(1)}, f32[2,1,256,256]{3,2,1,0:T(8,128)}, u32[]{:S(2)}) copy-start(f32[2,1,256,256]{3,2,1,0:T(8,128)} %right_ref.1) | copy-start | bytes 1572868
  6.0 34.8 %copy-start = (f32[8,64,128]{2,1,0:T(8,128)}, f32[8,64,128]{2,1,0:T(8,128)S(1)}, u32[]{:S(2)}) copy-start(f32[8,64,128]{2,1,0:T(8,128)S(1)} %get-tuple-element.22.d_ref) | copy-start | bytes 786436
  8.3 15.9 %all-to-all-start = ((f32[8,64,128]{2,1,0:T(8,128)}), f32[8,64,128]{2,1,0:T(8,128)S(1)}, u32[]{:S(2)}, u32[]{:S(2)}) async-start(f32[8,64,128]{2,1,0:T(8,128)} %get-tuple-element.20), calls=%async_computation | async-start | bytes 524288 | tf_op jit(solution)/shard_map/all_to_all | solution.py:249
  15.2 6.1 %collective-permute-start.2 = (f32[8,128]{1,0:T(8,128)S(1)}, f32[8,128]{1,0:T(8,128)S(1)}, u32[]{:S(2)}, u32[]{:S(2)}) collective-permute-start(f32[8,128]{1,0:T(8,128)S(1)} %get-tuple-element.21.mine), channel_id=1, source_target_pairs={{0,1},{1,0},{2,3},{3,2},{4,5},{5,4},{6,7},{7,6},{8,9},{9,8},{10,11... | collective-permute-start | bytes 12296 | tf_op jit(solution)/shard_map/ppermute | solution.py:244
  19.8 3.6 %collective-permute-start.3 = (f32[8,128]{1,0:T(8,128)S(1)}, f32[8,128]{1,0:T(8,128)S(1)}, u32[]{:S(2)}, u32[]{:S(2)}) collective-permute-start(f32[8,128]{1,0:T(8,128)S(1)} %get-tuple-element.21.mine), channel_id=1, source_target_pairs={{0,2},{1,3},{2,0},{3,1},{4,6},{5,7},{6,4},{7,5},{8,10},{9,11},{10,... | collective-permute-start | bytes 12296 | tf_op jit(solution)/shard_map/ppermute | solution.py:244
  21.2 3.0 %collective-permute-start.4 = (f32[8,128]{1,0:T(8,128)S(1)}, f32[8,128]{1,0:T(8,128)S(1)}, u32[]{:S(2)}, u32[]{:S(2)}) collective-permute-start(f32[8,128]{1,0:T(8,128)S(1)} %get-tuple-element.21.mine), channel_id=1, source_target_pairs={{0,3},{1,2},{2,1},{3,0},{4,7},{5,6},{6,5},{7,4},{8,11},{9,10},{10,... | collective-permute-start | bytes 12296 | tf_op jit(solution)/shard_map/ppermute | solution.py:244
  41.0 1.6 %collective-permute-start.5 = (f32[8,64,128]{2,1,0:T(8,128)S(1)}, f32[8,64,128]{2,1,0:T(8,128)S(1)}, u32[]{:S(2)}, u32[]{:S(2)}) collective-permute-start(f32[8,64,128]{2,1,0:T(8,128)S(1)} %get-tuple-element.23.r0.r_in), channel_id=1, source_target_pairs={{0,1},{1,0},{2,3},{3,2},{4,5},{5,4},{6,7},{7,6},{8,9},{9,8},{10,11... | collective-permute-start | bytes 786440 | tf_op jit(solution)/shard_map/ppermute | solution.py:229
  41.1 1.5 %collective-permute-start.6 = (f32[8,64,128]{2,1,0:T(8,128)S(1)}, f32[8,64,128]{2,1,0:T(8,128)S(1)}, u32[]{:S(2)}, u32[]{:S(2)}) collective-permute-start(f32[8,64,128]{2,1,0:T(8,128)S(1)} %get-tuple-element.23.r0.r_in), channel_id=1, source_target_pairs={{1,2},{2,1},{5,6},{6,5},{9,10},{10,9},{13,14},{14,13},{17,18},{18,... | collective-permute-start | bytes 786440 | tf_op jit(solution)/shard_map/ppermute | solution.py:237
  44.2 0.7 copy-start.4
  44.9 14.4 %all-to-all-start.2 = ((f32[8,64,128]{2,1,0:T(8,128)}), f32[8,64,128]{2,1,0:T(8,128)}, u32[]{:S(2)}, u32[]{:S(2)}) async-start(f32[8,64,128]{2,1,0:T(8,128)} %copy-done.4), calls=%async_computation.2 | async-start | bytes 524288 | tf_op jit(solution)/shard_map/all_to_all | solution.py:249
  49.0 8.1 %collective-permute-start.7 = (f32[8,128]{1,0:T(8,128)S(1)}, f32[8,128]{1,0:T(8,128)S(1)}, u32[]{:S(2)}, u32[]{:S(2)}) collective-permute-start(f32[8,128]{1,0:T(8,128)S(1)} %get-tuple-element.25.mine), channel_id=1, source_target_pairs={{0,1},{1,0},{2,3},{3,2},{4,5},{5,4},{6,7},{7,6},{8,9},{9,8},{10,11... | collective-permute-start | bytes 12296 | tf_op jit(solution)/shard_map/ppermute | solution.py:244
  55.7 3.6 %collective-permute-start.8 = (f32[8,128]{1,0:T(8,128)S(1)}, f32[8,128]{1,0:T(8,128)S(1)}, u32[]{:S(2)}, u32[]{:S(2)}) collective-permute-start(f32[8,128]{1,0:T(8,128)S(1)} %get-tuple-element.25.mine), channel_id=1, source_target_pairs={{0,2},{1,3},{2,0},{3,1},{4,6},{5,7},{6,4},{7,5},{8,10},{9,11},{10,... | collective-permute-start | bytes 12296 | tf_op jit(solution)/shard_map/ppermute | solution.py:244
  55.9 3.4 %collective-permute-start.9 = (f32[8,128]{1,0:T(8,128)S(1)}, f32[8,128]{1,0:T(8,128)S(1)}, u32[]{:S(2)}, u32[]{:S(2)}) collective-permute-start(f32[8,128]{1,0:T(8,128)S(1)} %get-tuple-element.25.mine), channel_id=1, source_target_pairs={{0,3},{1,2},{2,1},{3,0},{4,7},{5,6},{6,5},{7,4},{8,11},{9,10},{10,... | collective-permute-start | bytes 12296 | tf_op jit(solution)/shard_map/ppermute | solution.py:244
  60.3 16.7 %copy-start.1 = (f32[8,64,128]{2,1,0:T(8,128)S(1)}, f32[8,64,128]{2,1,0:T(8,128)}, u32[]{:S(2)}) copy-start(f32[8,64,128]{2,1,0:T(8,128)} %copy-done) | copy-start | bytes 786436
  77.4 1.6 %collective-permute-start.10 = (f32[8,64,128]{2,1,0:T(8,128)S(1)}, f32[8,64,128]{2,1,0:T(8,128)S(1)}, u32[]{:S(2)}, u32[]{:S(2)}) collective-permute-start(f32[8,64,128]{2,1,0:T(8,128)S(1)} %get-tuple-element.27.r0.s0), channel_id=1, source_target_pairs={{0,1},{1,0},{2,3},{3,2},{4,5},{5,4},{6,7},{7,6},{8,9},{9,8},{10,11... | collective-permute-start | bytes 786440 | tf_op jit(solution)/shard_map/ppermute | solution.py:229
  77.5 1.5 %collective-permute-start.11 = (f32[8,64,128]{2,1,0:T(8,128)S(1)}, f32[8,64,128]{2,1,0:T(8,128)S(1)}, u32[]{:S(2)}, u32[]{:S(2)}) collective-permute-start(f32[8,64,128]{2,1,0:T(8,128)S(1)} %get-tuple-element.27.r0.s0), channel_id=1, source_target_pairs={{1,2},{2,1},{5,6},{6,5},{9,10},{10,9},{13,14},{14,13},{17,18},{18,... | collective-permute-start | bytes 786440 | tf_op jit(solution)/shard_map/ppermute | solution.py:237
  99.4 2.0 %collective-permute-start.12 = (f32[2,256,256]{2,1,0:T(8,128)S(1)}, f32[2,256,256]{2,1,0:T(8,128)S(1)}, u32[]{:S(2)}, u32[]{:S(2)}) collective-permute-start(f32[2,256,256]{2,1,0:T(8,128)S(1)} %get-tuple-element.33), channel_id=1, source_target_pairs={{0,1},{1,0},{2,3},{3,2},{4,5},{5,4},{6,7},{7,6},{8,9},{9,8},{10,11... | collective-permute-start | bytes 1572872 | tf_op jit(solution)/shard_map/ppermute | solution.py:229

commit v3 on v2

--- a/solution.py
+++ b/solution.py
@@ -6,6 +6,7 @@
 from jax.experimental import pallas as pl
 from jax.experimental.pallas import tpu as pltpu
 from jax.sharding import PartitionSpec as P
+
 
 LANES = 128
 F32 = jnp.float32
@@ -23,7 +24,7 @@
         in_specs=in_specs,
         out_specs=tuple(VMEM for _ in outs),
         scratch_shapes=scratch,
-        compiler_params=pltpu.CompilerParams(vmem_limit_bytes=24 * 1024 * 1024),
+        compiler_params=pltpu.CompilerParams(vmem_limit_bytes=8 * 1024 * 1024),
         cost_estimate=pl.CostEstimate(flops=flops, bytes_accessed=size, transcendentals=0),
     )(*args)
 
@@ -38,7 +39,7 @@
 
 
 def unpack(ref, k, value):
-    chunks, cw, _ = value.shape
+    chunks, _, _ = value.shape
     side = ref.shape[1]
     rc = side // chunks
     for o in range(chunks):
@@ -70,11 +71,12 @@
     return jnp.where(source >= 0, ref[slot], 0.0)
 
 
-def apply(couple_ref, here, ref, lcat_ref, rcat_ref):
+def apply(couple_ref, here, ref, lcat_ref, rcat_ref, m_ref):
     total = None
     for p in range(lcat_ref.shape[0]):
         high, low = halves(pick(couple_ref, p, here, ref))
         mixed = dot(lcat_ref[p], jnp.concatenate([high, low, high], axis=0))
+        m_ref[p] = mixed
         high, low = halves(mixed)
         term = dot(jnp.concatenate([high, low, high], axis=1), rcat_ref[p])
         total = term if total is None else total + term
@@ -128,25 +130,27 @@
     pack(d_ref, (), d_ref.shape, diag_ref[0].astype(F32))
 
 
-def product(size_ref, couple_ref, blocks, lcat_ref, rcat_ref, y_ref, v_ref):
+def product(size_ref, couple_ref, blocks, lcat_ref, rcat_ref, y_ref, m_ref, v_ref):
     here = lax.axis_index("sec")
     for k, block in enumerate(blocks):
         unpack(v_ref, k, block[...])
-    y = apply(couple_ref, here, v_ref, lcat_ref, rcat_ref)
+    y = apply(couple_ref, here, v_ref, lcat_ref, rcat_ref, m_ref)
     y = jnp.where(mask(size_ref[0], v_ref.shape[1]), y, 0.0)
     pack(y_ref, (), y_ref.shape, y)
 
 
-def first_body(size_ref, couple_ref, x0, x1, x2, lcat_ref, rcat_ref, y_ref, part_ref, v_ref):
-    product(size_ref, couple_ref, (x0, x1, x2), lcat_ref, rcat_ref, y_ref, v_ref)
+def first_body(
+    size_ref, couple_ref, x0, x1, x2, lcat_ref, rcat_ref, y_ref, m_ref, part_ref, v_ref
+):
+    product(size_ref, couple_ref, (x0, x1, x2), lcat_ref, rcat_ref, y_ref, m_ref, v_ref)
     x = x0[lax.axis_index("ops")]
     part_ref[...] = tile([rows(x * x), rows(x0[...] * y_ref[...])])
 
 
 def second_body(
-    size_ref, couple_ref, r0, r1, r2, x0, g0, lcat_ref, rcat_ref, y_ref, part_ref, v_ref
+    size_ref, couple_ref, r0, r1, r2, x0, g0, lcat_ref, rcat_ref, y_ref, m_ref, part_ref, v_ref
 ):
-    product(size_ref, couple_ref, (r0, r1, r2), lcat_ref, rcat_ref, y_ref, v_ref)
+    product(size_ref, couple_ref, (r0, r1, r2), lcat_ref, rcat_ref, y_ref, m_ref, v_ref)
     o = lax.axis_index("ops")
     x, r, h = x0[o], r0[o], g0[o][: x0.shape[1]]
     y = y_ref[...]
@@ -200,31 +204,33 @@
 
 
 def last_body(
-    scale, couple_ref, parts_ref, c_in, x0, x1, x2, r0, r1, r2, s0, s1, s2, lcat_ref,
+    scale, label_ref, parts_ref, c_in, x0, x1, r0, r1, s0, s1, mx, mr, ms, nx, nr, ns,
     wave_ref, turn_ref, v_ref,
 ):
-    here = lax.axis_index("sec")
     side = v_ref.shape[1]
+    stay = label_ref[0] == lax.axis_index("sec")
     xr, rr, rh, xhr, rhr = numbers(parts_ref[...], 5)
     first, xx, x_part, r_part = [c_in[i : i + 1, 0:1] for i in range(4)]
     on_x, on_s, _, _ = update(xx, first, xr, rr, rh, xhr, rhr)
     on_r = on_x * r_part * scale
     on_x = on_x * x_part * scale
     on_s = on_s * scale
-    for k, (x, r, s) in enumerate(((x0, r0, s0), (x1, r1, s1), (x2, r2, s2))):
+    for k, (x, r, s) in enumerate(((x0, r0, s0), (x1, r1, s1))):
         unpack(v_ref, k, on_x * x[...] + on_r * r[...] + on_s * s[...])
-    wave = v_ref[0]
-    wave_ref[0] = wave
-    high, low = halves(wave.T * (1.0 / side**0.5))
+    wave_ref[0] = v_ref[0]
+    high, low = halves(jnp.where(stay, v_ref[0], v_ref[1]).T * (1.0 / side**0.5))
     turning = jnp.concatenate([high, low, high], axis=1)
-    for p in range(lcat_ref.shape[0]):
-        high, low = halves(pick(couple_ref, p, here, v_ref))
-        inner = dot(lcat_ref[p], jnp.concatenate([high, low, high], axis=0))
+    for p in range(turn_ref.shape[0]):
+        inner = (
+            on_x * jnp.where(stay, mx[p], nx[p])
+            + on_r * jnp.where(stay, mr[p], nr[p])
+            + on_s * jnp.where(stay, ms[p], ns[p])
+        )
         high, low = halves(inner)
-        turn_ref[p] = dot(turning, jnp.concatenate([high, high, low], axis=0))
-
-
-def partner(value):
+        turn_ref[p, 0] = dot(turning, jnp.concatenate([high, high, low], axis=0))
+
+
+def paired(value):
     count = lax.axis_size("sec")
     return lax.ppermute(value, "sec", [(i, i ^ 1) for i in range(count)])
 
@@ -252,26 +258,24 @@
 def local(sector_states, psi_guess, precond_diag, left_ops, right_ops, couple, new_sector):
     side = psi_guess.shape[1]
     pairs = left_ops.shape[0]
-    here = lax.axis_index("sec")
     chunks = lax.axis_size("ops")
     sectors = lax.axis_size("sec")
     cw = side // chunks * side // LANES
     block = jax.ShapeDtypeStruct((chunks, cw, LANES), F32)
     wide = jax.ShapeDtypeStruct((chunks, cw + 8, LANES), F32)
     small = jax.ShapeDtypeStruct((8, LANES), F32)
+    inner = jax.ShapeDtypeStruct((pairs, side, side), F32)
     scratch = pltpu.VMEM((3, side, side), F32)
     work = 12 * pairs * side**3
     light = 20 * side**2
 
     def gathered(y, part):
         others = over_sectors(part)
-        (full,) = call(
-            sum_body, (wide,), [VMEM] * 3, [], light, exchange(y), part, others
-        )
+        (full,) = call(sum_body, (wide,), [VMEM] * 3, [], light, exchange(y), part, others)
         return exchange(full)
 
     (x0,) = call(start_body, (block,), [SMEM, VMEM], [], light, sector_states, psi_guess)
-    x2, x1 = other(x0), partner(x0)
+    x2, x1 = other(x0), paired(x0)
     lcat, rcat, d = call(
         split_body,
         (
@@ -281,15 +285,15 @@
         ),
         [VMEM] * 3, [], light * pairs, left_ops, right_ops, precond_diag,
     )
-    y, part = call(
-        first_body, (block, small), [SMEM] * 2 + [VMEM] * 5, [scratch], work,
+    y, mx, part = call(
+        first_body, (block, inner, small), [SMEM] * 2 + [VMEM] * 5, [scratch], work,
         sector_states, couple, x0, x1, x2, lcat, rcat,
     )
     g = gathered(y, part)
     r0, c = call(first_residual_body, (block, small), [VMEM] * 3, [], light, g, x0, d)
-    r2, r1 = other(r0), partner(r0)
-    y, part = call(
-        second_body, (block, small), [SMEM] * 2 + [VMEM] * 7, [scratch], work,
+    r2, r1 = other(r0), paired(r0)
+    y, mr, part = call(
+        second_body, (block, inner, small), [SMEM] * 2 + [VMEM] * 7, [scratch], work,
         sector_states, couple, r0, r1, r2, x0, g, lcat, rcat,
     )
     s = gathered(y, part)
@@ -297,26 +301,23 @@
         second_residual_body, (block, block, block, small), [VMEM] * 6, [], light,
         s, g, x0, d, r0, c,
     )
-    s2, s1 = other(s0), partner(s0)
-    y, part = call(
-        second_body, (block, small), [SMEM] * 2 + [VMEM] * 7, [scratch], work,
+    s2, s1 = other(s0), paired(s0)
+    y, ms, part = call(
+        second_body, (block, inner, small), [SMEM] * 2 + [VMEM] * 7, [scratch], work,
         sector_states, couple, s0, s1, s2, x, h, lcat, rcat,
     )
+    nx, nr, ns = paired(mx), paired(mr), paired(ms)
     count = chunks * sectors
-    parts = lax.all_to_all(
-        jnp.broadcast_to(part[None], (count, 8, LANES)), ("ops", "sec"), 0, 0
-    )
-    wavefunction, turned = call(
+    parts = lax.all_to_all(jnp.broadcast_to(part[None], (count, 8, LANES)), ("ops", "sec"), 0, 0)
+    return call(
         functools.partial(last_body, float((sectors * side * side) ** 0.5)),
         (
             jax.ShapeDtypeStruct((1, side, side), F32),
-            jax.ShapeDtypeStruct((pairs, side, side), F32),
+            jax.ShapeDtypeStruct((pairs, 1, side, side), F32),
         ),
-        [SMEM] + [VMEM] * 12, [scratch], work,
-        couple, parts, c, x0, x1, x2, r0, r1, r2, s0, s1, s2, lcat,
-    )
-    rotated_ops = jnp.where(new_sector[0] == here, turned, partner(turned))[:, None]
-    return (wavefunction, rotated_ops)
+        [SMEM] + [VMEM] * 14, [pltpu.VMEM((2, side, side), F32)], work,
+        new_sector, parts, c, x0, x1, r0, r1, s0, s1, mx, mr, ms, nx, nr, ns,
+    )
 
 
 def solution(mesh):

time: 103 us -> 102 us (level)
  blocking collectives: 49.4 us -> 32.9 us
  starting transfers between devices: 28.1 us -> 37.3 us
  waiting for transfers between devices: 7.9 us -> 13.6 us
  Pallas kernels: 10.1 us -> 11.3 us
    all_to_all x1 -> x0, blocking collectives: 16.3 us -> none  [local(): lax.all_to_all(jnp.broadcast_to(part[None], (count, 8, LANES)), ('ops', '...]
    all_to_all x0 -> x1, waiting for transfers between devices: none -> 7.54 us  [local(): lax.all_to_all(jnp.broadcast_to(part[None], (count, 8, LANES)), ('ops', '...]
    ppermute x4 -> x6, starting transfers between devices: 0.98 us -> 8.18 us  [paired(): return lax.ppermute(value, 'sec', [(i, i ^ 1) for i in range(count)])]
    all_to_all x0 -> x1, starting transfers between devices: none -> 2.58 us  [local(): lax.all_to_all(jnp.broadcast_to(part[None], (count, 8, LANES)), ('ops', '...]
    ppermute x4 -> x6, waiting for transfers between devices: 2.72 us -> 0.85 us  [paired(): return lax.ppermute(value, 'sec', [(i, i ^ 1) for i in range(count)])]
    pallas_call x10, Pallas kernels: 10.1 us -> 11.3 us  [call(): pl.pallas_call(body, out_shape=tuple(outs), in_specs=in_specs, out_specs=...]
    unnamed x17 -> x13, local copies, waits for them, and re-layouts: 3.79 us -> 3.78 us
  transfers between devices with their start and end apart: 15 -> 18, of which waited for: 6 -> 5; matrix products, arithmetic and copies ran while one was open for 0% -> 1% of each run, Pallas kernels for 0% -> 3%
where the time goes in v3:
time: 102 us
  starting transfers between devices  37.3 us (37%)
  blocking collectives  32.9 us (32%)
  waiting for transfers between devices  13.6 us (13%)
  Pallas kernels  11.3 us (11%)
  local copies, waits for them, and re-layouts  4.45 us (4%)
  between operations  2.09 us (2%)
    all_to_all x2, blocking collectives, exchange(): return lax.all_to_all(value, 'ops', 0, 0)  32.9 us
    ppermute x6, starting transfers between devices, over_sectors(): lax.ppermute(value, 'sec', [(i, i ^ d) for i in range(count)])  14.2 us
    pallas_call x10, Pallas kernels, call(): pl.pallas_call(body, out_shape=tuple(outs), in_specs=in_specs, out_specs=...  11.3 us
    all_to_all x2, starting transfers between devices, exchange(): return lax.all_to_all(value, 'ops', 0, 0)  10.2 us
    ppermute x6, starting transfers between devices, paired(): return lax.ppermute(value, 'sec', [(i, i ^ 1) for i in range(count)])  8.18 us
    all_to_all x1, waiting for transfers between devices, local(): lax.all_to_all(jnp.broadcast_to(part[None], (count, 8, LANES)), ('ops', '...  7.54 us
    ppermute x6, waiting for transfers between devices, over_sectors(): lax.ppermute(value, 'sec', [(i, i ^ d) for i in range(count)])  5.17 us
    unnamed x13, local copies, waits for them, and re-layouts  3.78 us
  transfers between devices with their start and end apart: 18, of which 5 were waited for; matrix products, arithmetic and copies ran while one was open for 1% of the time, Pallas kernels for 3%

profile of v3, /device:TPU:0, one launch (start us, length us, event | category | flops | bytes accessed | tf_op | source)
XLA Modules:
  0.0 101.6 jit_solution(932539272291205670)
XLA Ops:
  1.3 0.9 copy-done.4
  2.2 0.6 collective-permute-start
  2.8 0.7 collective-permute-start.1
  3.5 0.1 copy.11.couple_ref
  3.6 1.0 %copy-done = f32[2,1,256,256]{3,2,1,0:T(8,128)S(1)} copy-done((f32[2,1,256,256]{3,2,1,0:T(8,128)S(1)}, f32[2,1,256,256]{3,2,1,0:T(8,128)}, u32[]{:S(2)}) %copy-start) | copy-done | bytes 524312
  4.6 1.0 %copy-done.1 = f32[2,1,256,256]{3,2,1,0:T(8,128)S(1)} copy-done((f32[2,1,256,256]{3,2,1,0:T(8,128)S(1)}, f32[2,1,256,256]{3,2,1,0:T(8,128)}, u32[]{:S(2)}) %copy-start.1) | copy-done | bytes 524312
  5.6 0.3 shard_map.87
  6.0 0.0 collective-permute-done.x1
  6.0 0.0 collective-permute-done.1.x2
  6.0 2.3 %shard_map.88 = (f32[8,64,128]{2,1,0:T(8,128)}, f32[2,256,256]{2,1,0:T(8,128)}, f32[8,128]{1,0:T(8,128)S(1)}) custom-call(s32[1]{0:T(128)S(6)} %copy.12.size_ref, s32[2,1]{1,0:T(2,128)S(1)} %copy.11.couple_ref, f32[8,64,128]{2,1,0:T(8,128)S(1)} %shard_map.86.x0.x_ref, f32[8,64,128]{2,1,0:T(8,128)S(1)} %collective-permute-done.x1, ...), custom_call_target="tpu_custom_call" | custom-call | flops 402653184 | bytes 3149836 | tf_op jit(solution)/shard_map/pallas_call | solution.py:21
  8.3 6.8 %all-to-all-start = ((f32[8,64,128]{2,1,0:T(8,128)}), f32[8,64,128]{2,1,0:T(8,128)S(1)}, u32[]{:S(2)}, u32[]{:S(2)}) async-start(f32[8,64,128]{2,1,0:T(8,128)} %get-tuple-element.21), calls=%async_computation | async-start | bytes 524288 | tf_op jit(solution)/shard_map/all_to_all | solution.py:255
  15.1 4.7 %collective-permute-start.2 = (f32[8,128]{1,0:T(8,128)S(1)}, f32[8,128]{1,0:T(8,128)S(1)}, u32[]{:S(2)}, u32[]{:S(2)}) collective-permute-start(f32[8,128]{1,0:T(8,128)S(1)} %get-tuple-element.22.mine), channel_id=1, source_target_pairs={{0,1},{1,0},{2,3},{3,2},{4,5},{5,4},{6,7},{7,6},{8,9},{9,8},{10,11... | collective-permute-start | bytes 12296 | tf_op jit(solution)/shard_map/ppermute | solution.py:250
  19.8 1.4 %collective-permute-start.3 = (f32[8,128]{1,0:T(8,128)S(1)}, f32[8,128]{1,0:T(8,128)S(1)}, u32[]{:S(2)}, u32[]{:S(2)}) collective-permute-start(f32[8,128]{1,0:T(8,128)S(1)} %get-tuple-element.22.mine), channel_id=1, source_target_pairs={{0,2},{1,3},{2,0},{3,1},{4,6},{5,7},{6,4},{7,5},{8,10},{9,11},{10,... | collective-permute-start | bytes 12296 | tf_op jit(solution)/shard_map/ppermute | solution.py:250
  21.2 0.0 collective-permute-start.4
  21.2 0.0 collective-permute-done.2
  21.3 2.2 %collective-permute-done.3 = f32[8,128]{1,0:T(8,128)S(1)} collective-permute-done((f32[8,128]{1,0:T(8,128)S(1)}, f32[8,128]{1,0:T(8,128)S(1)}, u32[]{:S(2)}, u32[]{:S(2)}) %collective-permute-start.3) | collective-permute-done | bytes 4128 | tf_op jit(solution)/shard_map/ppermute | solution.py:250
  23.4 0.8 collective-permute-done.4
  24.2 0.0 all-to-all-done.terms_ref
  24.3 16.5 %all_to_all.25.g_ref.g0 = f32[8,72,128]{2,1,0:T(8,128)S(1)} all-to-all(f32[8,72,128]{2,1,0:T(8,128)S(1)} %shard_map.89), channel_id=1, replica_groups=mesh['ops'=8,'sec'=4] {'ops'}, dimensions={0} | all-to-all | bytes 589824 | tf_op jit(solution)/shard_map/all_to_all | solution.py:255
  40.7 0.2 shard_map.90
  41.0 0.1 collective-permute-start.5
  41.1 0.7 collective-permute-start.6
  41.7 0.8 collective-permute-done.5.r1
  42.6 0.0 collective-permute-done.6.r2
  42.6 2.3 %shard_map.91 = (f32[8,64,128]{2,1,0:T(8,128)S(1)}, f32[2,256,256]{2,1,0:T(8,128)}, f32[8,128]{1,0:T(8,128)S(1)}) custom-call(s32[1]{0:T(128)S(6)} %copy.12.size_ref, s32[2,1]{1,0:T(2,128)S(1)} %copy.11.couple_ref, f32[8,64,128]{2,1,0:T(8,128)S(1)} %get-tuple-element.24.r0.r_in, f32[8,64,128]{2,1,0:T(8,128)S(1)} %collective-permute-done.5.r1, ...), custom_call_target="tpu_custom_call" | custom-call | flops 402653184 | bytes 3706892 | tf_op jit(solution)/shard_map/pallas_call | solution.py:21
  44.8 0.7 copy-done.2
  45.5 3.4 %all-to-all-start.2 = ((f32[8,64,128]{2,1,0:T(8,128)}), f32[8,64,128]{2,1,0:T(8,128)S(1)}, u32[]{:S(2)}, u32[]{:S(2)}) async-start(f32[8,64,128]{2,1,0:T(8,128)} %copy-done.2), calls=%async_computation.2 | async-start | bytes 524288 | tf_op jit(solution)/shard_map/all_to_all | solution.py:255
  49.0 6.7 %collective-permute-start.7 = (f32[8,128]{1,0:T(8,128)S(1)}, f32[8,128]{1,0:T(8,128)S(1)}, u32[]{:S(2)}, u32[]{:S(2)}) collective-permute-start(f32[8,128]{1,0:T(8,128)S(1)} %get-tuple-element.26.mine), channel_id=1, source_target_pairs={{0,1},{1,0},{2,3},{3,2},{4,5},{5,4},{6,7},{7,6},{8,9},{9,8},{10,11... | collective-permute-start | bytes 12296 | tf_op jit(solution)/shard_map/ppermute | solution.py:250
  55.7 0.2 collective-permute-start.8
  55.9 1.2 %collective-permute-start.9 = (f32[8,128]{1,0:T(8,128)S(1)}, f32[8,128]{1,0:T(8,128)S(1)}, u32[]{:S(2)}, u32[]{:S(2)}) collective-permute-start(f32[8,128]{1,0:T(8,128)S(1)} %get-tuple-element.26.mine), channel_id=1, source_target_pairs={{0,3},{1,2},{2,1},{3,0},{4,7},{5,6},{6,5},{7,4},{8,11},{9,10},{10,... | collective-permute-start | bytes 12296 | tf_op jit(solution)/shard_map/ppermute | solution.py:250
  57.1 0.0 collective-permute-done.7
  57.1 2.2 %collective-permute-done.8 = f32[8,128]{1,0:T(8,128)S(1)} collective-permute-done((f32[8,128]{1,0:T(8,128)S(1)}, f32[8,128]{1,0:T(8,128)S(1)}, u32[]{:S(2)}, u32[]{:S(2)}) %collective-permute-start.8) | collective-permute-done | bytes 4128 | tf_op jit(solution)/shard_map/ppermute | solution.py:250
  59.3 0.0 collective-permute-done.9
  59.3 16.5 %all_to_all.26.s_ref = f32[8,72,128]{2,1,0:T(8,128)S(1)} all-to-all(f32[8,72,128]{2,1,0:T(8,128)S(1)} %shard_map.92), channel_id=1, replica_groups=mesh['ops'=8,'sec'=4] {'ops'}, dimensions={0} | all-to-all | bytes 589824 | tf_op jit(solution)/shard_map/all_to_all | solution.py:255
  75.8 0.4 shard_map.93
  76.2 0.1 collective-permute-start.10
  76.3 0.7 collective-permute-start.11
  77.0 2.1 %collective-permute-start.12 = (f32[2,256,256]{2,1,0:T(8,128)}, f32[2,256,256]{2,1,0:T(8,128)}, u32[]{:S(2)}, u32[]{:S(2)}) collective-permute-start(f32[2,256,256]{2,1,0:T(8,128)} %get-tuple-element.33.mx), channel_id=1, source_target_pairs={{0,1},{1,0},{2,3},{3,2},{4,5},{5,4},{6,7},{7,6},{8,9},{9,8},{10,11... | collective-permute-start | bytes 1572872 | tf_op jit(solution)/shard_map/ppermute | solution.py:235
  79.1 0.1 collective-permute-start.13
  79.2 0.0 collective-permute-done.10.r1.s1
  79.2 0.0 collective-permute-done.11.r2
  79.2 2.3 %shard_map.94 = (f32[8,64,128]{2,1,0:T(8,128)}, f32[2,256,256]{2,1,0:T(8,128)}, f32[8,128]{1,0:T(8,128)S(1)}) custom-call(s32[1]{0:T(128)S(6)} %copy.12.size_ref, s32[2,1]{1,0:T(2,128)S(1)} %copy.11.couple_ref, f32[8,64,128]{2,1,0:T(8,128)S(1)} %get-tuple-element.28.r0.s0, f32[8,64,128]{2,1,0:T(8,128)S(1)} %collective-permute-done.10.r1.s1, ...), custom_call_target="tpu_custom_call" | custom-call | flops 402653184 | bytes 3674124 | tf_op jit(solution)/shard_map/pallas_call | solution.py:21
  81.5 5.3 %collective-permute-start.14 = (f32[2,256,256]{2,1,0:T(8,128)}, f32[2,256,256]{2,1,0:T(8,128)S(1)}, u32[]{:S(2)}, u32[]{:S(2)}) collective-permute-start(f32[2,256,256]{2,1,0:T(8,128)} %get-tuple-element.35.ms), channel_id=1, source_target_pairs={{0,1},{1,0},{2,3},{3,2},{4,5},{5,4},{6,7},{7,6},{8,9},{9,8},{10,11... | collective-permute-start | bytes 1572872 | tf_op jit(solution)/shard_map/ppermute | solution.py:235
  86.8 0.7 broadcast_in_dim.2
  87.5 2.6 %all-to-all-start.4 = ((f32[32,8,128]{2,1,0:T(8,128)}), f32[32,8,128]{2,1,0:T(8,128)S(1)}, u32[]{:S(2)}, u32[]{:S(2)}) async-start(f32[32,8,128]{2,1,0:T(8,128)} %broadcast_in_dim.2), calls=%async_computation.4 | async-start | bytes 262144 | tf_op jit(solution)/shard_map/all_to_all | solution.py:311
  90.7 0.0 collective-permute-done.13.nr
  90.7 7.5 %all-to-all-done.4.parts_ref = f32[32,8,128]{2,1,0:T(8,128)S(1)} async-done(((f32[32,8,128]{2,1,0:T(8,128)}), f32[32,8,128]{2,1,0:T(8,128)S(1)}, u32[]{:S(2)}, u32[]{:S(2)}) %all-to-all-start.4) | async-done | bytes 131104 | tf_op jit(solution)/shard_map/all_to_all | solution.py:311
  98.2 3.3 %shard_map.95 = (f32[1,256,256]{2,1,0:T(8,128)}, f32[2,1,256,256]{3,2,1,0:T(8,128)}) custom-call(s32[1]{0:T(128)S(6)} %copy.13.label_ref, f32[32,8,128]{2,1,0:T(8,128)S(1)} %all-to-all-done.4.parts_ref, f32[8,128]{1,0:T(8,128)S(1)} %get-tuple-element.32.c_in, f32[8,64,128]{2,1,0:T(8,128)S(1)} %shard_map.86.x0.x_ref, ...), custom_call_target="tpu_custom_call" | custom-call | flops 402653184 | bytes 5640196 | tf_op jit(solution)/shard_map/pallas_call | solution.py:21
  (16 shorter events, 0.1 us)
Async XLA Ops:
  1.3 0.9 copy-start.4
  2.2 1.3 %copy-start.5 = (s32[2,1]{0,1:T(1,128)S(1)}, s32[2,1]{0,1:T(1,128)}, u32[]{:S(2)}) copy-start(s32[2,1]{0,1:T(1,128)} %param.12) | copy-start | bytes 28
  2.2 1.4 %copy-start.3 = (bf16[1,256,256]{2,1,0:T(8,128)(2,1)S(1)}, bf16[1,256,256]{2,1,0:T(8,128)(2,1)}, u32[]{:S(2)}) copy-start(bf16[1,256,256]{2,1,0:T(8,128)(2,1)} %diag_ref.1) | copy-start | bytes 393220
  2.2 3.7 %collective-permute-start = (f32[8,64,128]{2,1,0:T(8,128)S(1)}, f32[8,64,128]{2,1,0:T(8,128)S(1)}, u32[]{:S(2)}, u32[]{:S(2)}) collective-permute-start(f32[8,64,128]{2,1,0:T(8,128)S(1)} %shard_map.86.x0.x_ref), channel_id=1, source_target_pairs={{0,1},{1,0},{2,3},{3,2},{4,5},{5,4},{6,7},{7,6},{8,9},{9,8},{10,11... | collective-permute-start | bytes 786440 | tf_op jit(solution)/shard_map/ppermute | solution.py:235
  2.8 3.2 %collective-permute-start.1 = (f32[8,64,128]{2,1,0:T(8,128)S(1)}, f32[8,64,128]{2,1,0:T(8,128)S(1)}, u32[]{:S(2)}, u32[]{:S(2)}) collective-permute-start(f32[8,64,128]{2,1,0:T(8,128)S(1)} %shard_map.86.x0.x_ref), channel_id=1, source_target_pairs={{1,2},{2,1},{5,6},{6,5},{9,10},{10,9},{13,14},{14,13},{17,18},{18,... | collective-permute-start | bytes 786440 | tf_op jit(solution)/shard_map/ppermute | solution.py:243
  3.6 1.0 %copy-start = (f32[2,1,256,256]{3,2,1,0:T(8,128)S(1)}, f32[2,1,256,256]{3,2,1,0:T(8,128)}, u32[]{:S(2)}) copy-start(f32[2,1,256,256]{3,2,1,0:T(8,128)} %left_ref.1) | copy-start | bytes 1572868
  4.6 1.0 %copy-start.1 = (f32[2,1,256,256]{3,2,1,0:T(8,128)S(1)}, f32[2,1,256,256]{3,2,1,0:T(8,128)}, u32[]{:S(2)}) copy-start(f32[2,1,256,256]{3,2,1,0:T(8,128)} %right_ref.1) | copy-start | bytes 1572868
  8.3 15.9 %all-to-all-start = ((f32[8,64,128]{2,1,0:T(8,128)}), f32[8,64,128]{2,1,0:T(8,128)S(1)}, u32[]{:S(2)}, u32[]{:S(2)}) async-start(f32[8,64,128]{2,1,0:T(8,128)} %get-tuple-element.21), calls=%async_computation | async-start | bytes 524288 | tf_op jit(solution)/shard_map/all_to_all | solution.py:255
  15.1 6.1 %collective-permute-start.2 = (f32[8,128]{1,0:T(8,128)S(1)}, f32[8,128]{1,0:T(8,128)S(1)}, u32[]{:S(2)}, u32[]{:S(2)}) collective-permute-start(f32[8,128]{1,0:T(8,128)S(1)} %get-tuple-element.22.mine), channel_id=1, source_target_pairs={{0,1},{1,0},{2,3},{3,2},{4,5},{5,4},{6,7},{7,6},{8,9},{9,8},{10,11... | collective-permute-start | bytes 12296 | tf_op jit(solution)/shard_map/ppermute | solution.py:250
  19.8 3.6 %collective-permute-start.3 = (f32[8,128]{1,0:T(8,128)S(1)}, f32[8,128]{1,0:T(8,128)S(1)}, u32[]{:S(2)}, u32[]{:S(2)}) collective-permute-start(f32[8,128]{1,0:T(8,128)S(1)} %get-tuple-element.22.mine), channel_id=1, source_target_pairs={{0,2},{1,3},{2,0},{3,1},{4,6},{5,7},{6,4},{7,5},{8,10},{9,11},{10,... | collective-permute-start | bytes 12296 | tf_op jit(solution)/shard_map/ppermute | solution.py:250
  21.2 3.0 %collective-permute-start.4 = (f32[8,128]{1,0:T(8,128)S(1)}, f32[8,128]{1,0:T(8,128)S(1)}, u32[]{:S(2)}, u32[]{:S(2)}) collective-permute-start(f32[8,128]{1,0:T(8,128)S(1)} %get-tuple-element.22.mine), channel_id=1, source_target_pairs={{0,3},{1,2},{2,1},{3,0},{4,7},{5,6},{6,5},{7,4},{8,11},{9,10},{10,... | collective-permute-start | bytes 12296 | tf_op jit(solution)/shard_map/ppermute | solution.py:250
  41.0 1.6 %collective-permute-start.5 = (f32[8,64,128]{2,1,0:T(8,128)S(1)}, f32[8,64,128]{2,1,0:T(8,128)S(1)}, u32[]{:S(2)}, u32[]{:S(2)}) collective-permute-start(f32[8,64,128]{2,1,0:T(8,128)S(1)} %get-tuple-element.24.r0.r_in), channel_id=1, source_target_pairs={{0,1},{1,0},{2,3},{3,2},{4,5},{5,4},{6,7},{7,6},{8,9},{9,8},{10,11... | collective-permute-start | bytes 786440 | tf_op jit(solution)/shard_map/ppermute | solution.py:235
  41.1 1.5 %collective-permute-start.6 = (f32[8,64,128]{2,1,0:T(8,128)S(1)}, f32[8,64,128]{2,1,0:T(8,128)S(1)}, u32[]{:S(2)}, u32[]{:S(2)}) collective-permute-start(f32[8,64,128]{2,1,0:T(8,128)S(1)} %get-tuple-element.24.r0.r_in), channel_id=1, source_target_pairs={{1,2},{2,1},{5,6},{6,5},{9,10},{10,9},{13,14},{14,13},{17,18},{18,... | collective-permute-start | bytes 786440 | tf_op jit(solution)/shard_map/ppermute | solution.py:243
  44.8 0.7 copy-start.2
  45.5 13.8 %all-to-all-start.2 = ((f32[8,64,128]{2,1,0:T(8,128)}), f32[8,64,128]{2,1,0:T(8,128)S(1)}, u32[]{:S(2)}, u32[]{:S(2)}) async-start(f32[8,64,128]{2,1,0:T(8,128)} %copy-done.2), calls=%async_computation.2 | async-start | bytes 524288 | tf_op jit(solution)/shard_map/all_to_all | solution.py:255
  49.0 8.1 %collective-permute-start.7 = (f32[8,128]{1,0:T(8,128)S(1)}, f32[8,128]{1,0:T(8,128)S(1)}, u32[]{:S(2)}, u32[]{:S(2)}) collective-permute-start(f32[8,128]{1,0:T(8,128)S(1)} %get-tuple-element.26.mine), channel_id=1, source_target_pairs={{0,1},{1,0},{2,3},{3,2},{4,5},{5,4},{6,7},{7,6},{8,9},{9,8},{10,11... | collective-permute-start | bytes 12296 | tf_op jit(solution)/shard_map/ppermute | solution.py:250
  55.7 3.6 %collective-permute-start.8 = (f32[8,128]{1,0:T(8,128)S(1)}, f32[8,128]{1,0:T(8,128)S(1)}, u32[]{:S(2)}, u32[]{:S(2)}) collective-permute-start(f32[8,128]{1,0:T(8,128)S(1)} %get-tuple-element.26.mine), channel_id=1, source_target_pairs={{0,2},{1,3},{2,0},{3,1},{4,6},{5,7},{6,4},{7,5},{8,10},{9,11},{10,... | collective-permute-start | bytes 12296 | tf_op jit(solution)/shard_map/ppermute | solution.py:250
  55.9 3.4 %collective-permute-start.9 = (f32[8,128]{1,0:T(8,128)S(1)}, f32[8,128]{1,0:T(8,128)S(1)}, u32[]{:S(2)}, u32[]{:S(2)}) collective-permute-start(f32[8,128]{1,0:T(8,128)S(1)} %get-tuple-element.26.mine), channel_id=1, source_target_pairs={{0,3},{1,2},{2,1},{3,0},{4,7},{5,6},{6,5},{7,4},{8,11},{9,10},{10,... | collective-permute-start | bytes 12296 | tf_op jit(solution)/shard_map/ppermute | solution.py:250
  76.2 3.0 %collective-permute-start.10 = (f32[8,64,128]{2,1,0:T(8,128)S(1)}, f32[8,64,128]{2,1,0:T(8,128)S(1)}, u32[]{:S(2)}, u32[]{:S(2)}) collective-permute-start(f32[8,64,128]{2,1,0:T(8,128)S(1)} %get-tuple-element.28.r0.s0), channel_id=1, source_target_pairs={{0,1},{1,0},{2,3},{3,2},{4,5},{5,4},{6,7},{7,6},{8,9},{9,8},{10,11... | collective-permute-start | bytes 786440 | tf_op jit(solution)/shard_map/ppermute | solution.py:235
  76.3 2.9 %collective-permute-start.11 = (f32[8,64,128]{2,1,0:T(8,128)S(1)}, f32[8,64,128]{2,1,0:T(8,128)S(1)}, u32[]{:S(2)}, u32[]{:S(2)}) collective-permute-start(f32[8,64,128]{2,1,0:T(8,128)S(1)} %get-tuple-element.28.r0.s0), channel_id=1, source_target_pairs={{1,2},{2,1},{5,6},{6,5},{9,10},{10,9},{13,14},{14,13},{17,18},{18,... | collective-permute-start | bytes 786440 | tf_op jit(solution)/shard_map/ppermute | solution.py:243
  77.0 13.7 %collective-permute-start.12 = (f32[2,256,256]{2,1,0:T(8,128)}, f32[2,256,256]{2,1,0:T(8,128)}, u32[]{:S(2)}, u32[]{:S(2)}) collective-permute-start(f32[2,256,256]{2,1,0:T(8,128)} %get-tuple-element.33.mx), channel_id=1, source_target_pairs={{0,1},{1,0},{2,3},{3,2},{4,5},{5,4},{6,7},{7,6},{8,9},{9,8},{10,11... | collective-permute-start | bytes 1572872 | tf_op jit(solution)/shard_map/ppermute | solution.py:235
  79.1 11.6 %collective-permute-start.13 = (f32[2,256,256]{2,1,0:T(8,128)}, f32[2,256,256]{2,1,0:T(8,128)}, u32[]{:S(2)}, u32[]{:S(2)}) collective-permute-start(f32[2,256,256]{2,1,0:T(8,128)} %get-tuple-element.34.mr), channel_id=1, source_target_pairs={{0,1},{1,0},{2,3},{3,2},{4,5},{5,4},{6,7},{7,6},{8,9},{9,8},{10,11... | collective-permute-start | bytes 1572872 | tf_op jit(solution)/shard_map/ppermute | solution.py:235
  81.5 16.7 %collective-permute-start.14 = (f32[2,256,256]{2,1,0:T(8,128)}, f32[2,256,256]{2,1,0:T(8,128)S(1)}, u32[]{:S(2)}, u32[]{:S(2)}) collective-permute-start(f32[2,256,256]{2,1,0:T(8,128)} %get-tuple-element.35.ms), channel_id=1, source_target_pairs={{0,1},{1,0},{2,3},{3,2},{4,5},{5,4},{6,7},{7,6},{8,9},{9,8},{10,11... | collective-permute-start | bytes 1572872 | tf_op jit(solution)/shard_map/ppermute | solution.py:235
  87.5 10.8 %all-to-all-start.4 = ((f32[32,8,128]{2,1,0:T(8,128)}), f32[32,8,128]{2,1,0:T(8,128)S(1)}, u32[]{:S(2)}, u32[]{:S(2)}) async-start(f32[32,8,128]{2,1,0:T(8,128)} %broadcast_in_dim.2), calls=%async_computation.4 | async-start | bytes 262144 | tf_op jit(solution)/shard_map/all_to_all | solution.py:311

commit v4 on v3

--- a/solution.py
+++ b/solution.py
@@ -59,6 +59,12 @@
     return jnp.dot(a, b, preferred_element_type=F32)
 
 
+def three(ah, al, bh, bl):
+    return dot(
+        jnp.concatenate([ah, ah, al], axis=1), jnp.concatenate([bh, bl, bh], axis=0)
+    )
+
+
 def mask(size, side):
     rows = lax.broadcasted_iota(jnp.int32, (side, side), 0)
     cols = lax.broadcasted_iota(jnp.int32, (side, side), 1)
@@ -66,19 +72,21 @@
 
 
 def pick(couple_ref, p, here, ref):
-    source = couple_ref[p, 0]
+    source = couple_ref[p]
     slot = jnp.where(source == here, 0, jnp.where(source == here + 1 - 2 * (here % 2), 1, 2))
     return jnp.where(source >= 0, ref[slot], 0.0)
 
 
-def apply(couple_ref, here, ref, lcat_ref, rcat_ref, m_ref):
+def mix(couple_ref, p, here, ref, lcat_ref):
+    high, low = halves(pick(couple_ref, p, here, ref))
+    return three(lcat_ref[p, 0], lcat_ref[p, 1], high, low)
+
+
+def fold(mixed, rcat_ref):
     total = None
-    for p in range(lcat_ref.shape[0]):
-        high, low = halves(pick(couple_ref, p, here, ref))
-        mixed = dot(lcat_ref[p], jnp.concatenate([high, low, high], axis=0))
-        m_ref[p] = mixed
-        high, low = halves(mixed)
-        term = dot(jnp.concatenate([high, low, high], axis=1), rcat_ref[p])
+    for p, one in enumerate(mixed):
+        high, low = halves(one)
+        term = three(high, low, rcat_ref[p, 0], rcat_ref[p, 1])
         total = term if total is None else total + term
     return total
 
@@ -121,48 +129,90 @@
     pack(x_ref, (), x_ref.shape, jnp.where(live, psi_ref[0].astype(F32), 0.0))
 
 
-def split_body(left_ref, right_ref, diag_ref, lcat_ref, rcat_ref, d_ref):
+def split_body(label_ref, left_ref, right_ref, lcat_ref, rcat_ref, flag_ref):
     for p in range(left_ref.shape[0]):
-        high, low = halves(left_ref[p, 0])
-        lcat_ref[p] = jnp.concatenate([high, high, low], axis=1)
-        high, low = halves(right_ref[p, 0].T)
-        rcat_ref[p] = jnp.concatenate([high, high, low], axis=0)
-    pack(d_ref, (), d_ref.shape, diag_ref[0].astype(F32))
-
-
-def product(size_ref, couple_ref, blocks, lcat_ref, rcat_ref, y_ref, m_ref, v_ref):
+        lcat_ref[p, 0], lcat_ref[p, 1] = halves(left_ref[p, 0])
+        rcat_ref[p, 0], rcat_ref[p, 1] = halves(right_ref[p, 0].T)
+    stay = jnp.where(label_ref[0] == lax.axis_index("sec"), 1.0, 0.0)
+    flag_ref[...] = jnp.full(flag_ref.shape, stay)
+
+
+def mix_all(couple_ref, blocks, lcat_ref, m_ref, v_ref):
     here = lax.axis_index("sec")
     for k, block in enumerate(blocks):
         unpack(v_ref, k, block[...])
-    y = apply(couple_ref, here, v_ref, lcat_ref, rcat_ref, m_ref)
-    y = jnp.where(mask(size_ref[0], v_ref.shape[1]), y, 0.0)
-    pack(y_ref, (), y_ref.shape, y)
+    mixed = [mix(couple_ref, p, here, v_ref, lcat_ref) for p in range(lcat_ref.shape[0])]
+    for p, one in enumerate(mixed):
+        m_ref[p] = one
+    return mixed
+
+
+def fold_all(size_ref, mixed, rcat_ref, y_ref):
+    y = fold(mixed, rcat_ref)
+    pack(y_ref, (), y_ref.shape, jnp.where(mask(size_ref[0], y.shape[0]), y, 0.0))
+    return y_ref[...]
 
 
 def first_body(
     size_ref, couple_ref, x0, x1, x2, lcat_ref, rcat_ref, y_ref, m_ref, part_ref, v_ref
 ):
-    product(size_ref, couple_ref, (x0, x1, x2), lcat_ref, rcat_ref, y_ref, m_ref, v_ref)
+    mixed = mix_all(couple_ref, (x0, x1, x2), lcat_ref, m_ref, v_ref)
+    y = fold_all(size_ref, mixed, rcat_ref, y_ref)
     x = x0[lax.axis_index("ops")]
-    part_ref[...] = tile([rows(x * x), rows(x0[...] * y_ref[...])])
+    part_ref[...] = tile([rows(x * x), rows(x0[...] * y)])
+
+
+def five(x0, r0, h0, y):
+    o = lax.axis_index("ops")
+    x, r, h = x0[o], r0[o], h0[o][: x0.shape[1]]
+    return tile([rows(x * r), rows(r * r), rows(r * h), rows(x0[...] * y), rows(r0[...] * y)])
 
 
 def second_body(
     size_ref, couple_ref, r0, r1, r2, x0, g0, lcat_ref, rcat_ref, y_ref, m_ref, part_ref, v_ref
 ):
-    product(size_ref, couple_ref, (r0, r1, r2), lcat_ref, rcat_ref, y_ref, m_ref, v_ref)
-    o = lax.axis_index("ops")
-    x, r, h = x0[o], r0[o], g0[o][: x0.shape[1]]
-    y = y_ref[...]
-    part_ref[...] = tile(
-        [rows(x * r), rows(r * r), rows(r * h), rows(x0[...] * y), rows(r0[...] * y)]
-    )
-
-
-def sum_body(terms_ref, mine, others, out_ref):
+    mixed = mix_all(couple_ref, (r0, r1, r2), lcat_ref, m_ref, v_ref)
+    part_ref[...] = five(x0, r0, g0, fold_all(size_ref, mixed, rcat_ref, y_ref))
+
+
+def mix_body(couple_ref, r0, r1, r2, lcat_ref, m_ref, v_ref):
+    mix_all(couple_ref, (r0, r1, r2), lcat_ref, m_ref, v_ref)
+
+
+def fold_body(size_ref, m_ref, r0, x0, h0, rcat_ref, part_ref, y_ref):
+    mixed = [m_ref[p] for p in range(m_ref.shape[0])]
+    part_ref[...] = five(x0, r0, h0, fold_all(size_ref, mixed, rcat_ref, y_ref))
+
+
+def blend_body(c_in, a_ref, b_ref, x_ref, out_ref):
+    pairs = a_ref.shape[0]
+    out_ref[:pairs] = c_in[2:3, 0:1] * a_ref[...] + c_in[3:4, 0:1] * b_ref[...]
+    unpack(out_ref, pairs, x_ref[...])
+
+
+def cross_body(flag_ref, b_ref, n_ref, m_ref, w_ref, s0, s1, u_ref, v_ref):
+    stay = flag_ref[0:1, 0:1] > 0.5
+    pairs, side, _ = m_ref.shape
+    unpack(v_ref, 0, jnp.where(stay[None], s0[...], s1[...]))
+    x = jnp.where(stay, b_ref[pairs], n_ref[pairs])
+    left = jnp.concatenate([x.T, v_ref[0].T], axis=0)
+    lh, ll = halves(left)
+    for p in range(pairs):
+        old, new = jnp.where(stay, b_ref[p], n_ref[p]), jnp.where(stay, m_ref[p], w_ref[p])
+        rh, rl = halves(jnp.concatenate([old, new], axis=1))
+        both = three(lh, ll, rh, rl)
+        u_ref[0, p] = both[:side, :side]
+        u_ref[1, p] = both[:side, side:] + both[side:, :side]
+        u_ref[2, p] = both[side:, side:]
+
+
+def sum_body(terms_ref, mine, *refs):
+    others, out_ref = refs[:-1], refs[-1]
     cw = terms_ref.shape[1]
     block = jnp.sum(terms_ref[...], axis=0)
-    scalars = mine[...] + others[...]
+    scalars = mine[...]
+    for one in others:
+        scalars = scalars + one[...]
     for o in range(out_ref.shape[0]):
         out_ref[o, :cw] = block
         out_ref[o, cw:] = scalars
@@ -177,7 +227,8 @@
     out_ref[...] = tile([jnp.broadcast_to(v, (1, LANES)) for v in values])
 
 
-def first_residual_body(g_ref, x_ref, d_ref, r_ref, c_ref):
+def first_residual_body(g_ref, x_ref, diag_ref, r_ref, c_ref, d_ref):
+    pack(d_ref, (), d_ref.shape, diag_ref[0].astype(F32))
     cw = x_ref.shape[1]
     squares, energy = numbers(g_ref[:, cw:], 2)
     factor = lax.rsqrt(squares + 1e-06)
@@ -187,7 +238,10 @@
     store(c_ref, [factor, theta, squares * factor * factor])
 
 
-def second_residual_body(s_ref, g_ref, x_ref, d_ref, r_in, c_in, x_out, h_out, r_ref, c_ref):
+def second_residual_body(
+    s_ref, g_ref, x_ref, diag_ref, r_in, c_in, x_out, h_out, r_ref, c_ref, d_ref
+):
+    pack(d_ref, (), d_ref.shape, diag_ref[0].astype(F32))
     cw = x_ref.shape[1]
     xr, rr, rh, xhr, rhr = numbers(s_ref[:, cw:], 5)
     factor, first, xx = c_in[0:1, 0:1], c_in[1:2, 0:1], c_in[2:3, 0:1]
@@ -203,31 +257,19 @@
     store(c_ref, [theta, xx, on_x, on_r])
 
 
-def last_body(
-    scale, label_ref, parts_ref, c_in, x0, x1, r0, r1, s0, s1, mx, mr, ms, nx, nr, ns,
-    wave_ref, turn_ref, v_ref,
-):
+def last_body(scale, parts_ref, c_in, b_ref, s0, u_ref, wave_ref, turn_ref, v_ref):
     side = v_ref.shape[1]
-    stay = label_ref[0] == lax.axis_index("sec")
+    pairs = u_ref.shape[1]
     xr, rr, rh, xhr, rhr = numbers(parts_ref[...], 5)
-    first, xx, x_part, r_part = [c_in[i : i + 1, 0:1] for i in range(4)]
-    on_x, on_s, _, _ = update(xx, first, xr, rr, rh, xhr, rhr)
-    on_r = on_x * r_part * scale
-    on_x = on_x * x_part * scale
+    on_x, on_s, _, _ = update(c_in[1:2, 0:1], c_in[0:1, 0:1], xr, rr, rh, xhr, rhr)
+    on_x = on_x * scale
     on_s = on_s * scale
-    for k, (x, r, s) in enumerate(((x0, r0, s0), (x1, r1, s1))):
-        unpack(v_ref, k, on_x * x[...] + on_r * r[...] + on_s * s[...])
-    wave_ref[0] = v_ref[0]
-    high, low = halves(jnp.where(stay, v_ref[0], v_ref[1]).T * (1.0 / side**0.5))
-    turning = jnp.concatenate([high, low, high], axis=1)
-    for p in range(turn_ref.shape[0]):
-        inner = (
-            on_x * jnp.where(stay, mx[p], nx[p])
-            + on_r * jnp.where(stay, mr[p], nr[p])
-            + on_s * jnp.where(stay, ms[p], ns[p])
-        )
-        high, low = halves(inner)
-        turn_ref[p, 0] = dot(turning, jnp.concatenate([high, high, low], axis=0))
+    unpack(v_ref, 0, on_s * s0[...])
+    wave_ref[0] = on_x * b_ref[pairs] + v_ref[0]
+    root = 1.0 / side**0.5
+    xx, xs, ss = on_x * on_x * root, on_x * on_s * root, on_s * on_s * root
+    for p in range(pairs):
+        turn_ref[p, 0] = xx * u_ref[0, p] + xs * u_ref[1, p] + ss * u_ref[2, p]
 
 
 def paired(value):
@@ -245,10 +287,10 @@
 
 def over_sectors(value):
     count = lax.axis_size("sec")
-    total = jnp.zeros_like(value)
+    found = []
     for d in range(1, count):
-        total = total + lax.ppermute(value, "sec", [(i, i ^ d) for i in range(count)])
-    return total
+        found.append(lax.ppermute(value, "sec", [(i, i ^ d) for i in range(count)]))
+    return found
 
 
 def exchange(value):
@@ -258,6 +300,7 @@
 def local(sector_states, psi_guess, precond_diag, left_ops, right_ops, couple, new_sector):
     side = psi_guess.shape[1]
     pairs = left_ops.shape[0]
+    couple = couple.reshape(pairs)
     chunks = lax.axis_size("ops")
     sectors = lax.axis_size("sec")
     cw = side // chunks * side // LANES
@@ -271,26 +314,32 @@
 
     def gathered(y, part):
         others = over_sectors(part)
-        (full,) = call(sum_body, (wide,), [VMEM] * 3, [], light, exchange(y), part, others)
+        (full,) = call(
+            sum_body, (wide,), [VMEM] * (2 + len(others)), [], light,
+            exchange(y), part, *others,
+        )
         return exchange(full)
 
     (x0,) = call(start_body, (block,), [SMEM, VMEM], [], light, sector_states, psi_guess)
     x2, x1 = other(x0), paired(x0)
-    lcat, rcat, d = call(
+    lcat, rcat, flag = call(
         split_body,
         (
-            jax.ShapeDtypeStruct((pairs, side, 3 * side), BF16),
-            jax.ShapeDtypeStruct((pairs, 3 * side, side), BF16),
-            block,
+            jax.ShapeDtypeStruct((pairs, 2, side, side), BF16),
+            jax.ShapeDtypeStruct((pairs, 2, side, side), BF16),
+            small,
         ),
-        [VMEM] * 3, [], light * pairs, left_ops, right_ops, precond_diag,
+        [SMEM] + [VMEM] * 2, [], light * pairs, new_sector, left_ops, right_ops,
     )
     y, mx, part = call(
         first_body, (block, inner, small), [SMEM] * 2 + [VMEM] * 5, [scratch], work,
         sector_states, couple, x0, x1, x2, lcat, rcat,
     )
     g = gathered(y, part)
-    r0, c = call(first_residual_body, (block, small), [VMEM] * 3, [], light, g, x0, d)
+    r0, c = call(
+        first_residual_body, (block, small), [VMEM] * 3, [pltpu.VMEM(block.shape, F32)], light,
+        g, x0, precond_diag,
+    )
     r2, r1 = other(r0), paired(r0)
     y, mr, part = call(
         second_body, (block, inner, small), [SMEM] * 2 + [VMEM] * 7, [scratch], work,
@@ -298,25 +347,38 @@
     )
     s = gathered(y, part)
     x, h, s0, c = call(
-        second_residual_body, (block, block, block, small), [VMEM] * 6, [], light,
-        s, g, x0, d, r0, c,
+        second_residual_body, (block, block, block, small), [VMEM] * 6,
+        [pltpu.VMEM(block.shape, F32)], light, s, g, x0, precond_diag, r0, c,
     )
     s2, s1 = other(s0), paired(s0)
-    y, ms, part = call(
-        second_body, (block, inner, small), [SMEM] * 2 + [VMEM] * 7, [scratch], work,
-        sector_states, couple, s0, s1, s2, x, h, lcat, rcat,
-    )
-    nx, nr, ns = paired(mx), paired(mr), paired(ms)
+    (mx,) = call(
+        blend_body, (jax.ShapeDtypeStruct((pairs + 1, side, side), F32),), [VMEM] * 4, [],
+        light, c, mx, mr, x,
+    )
+    nx = paired(mx)
+    (ms,) = call(
+        mix_body, (inner,), [SMEM] + [VMEM] * 4, [scratch], work // 2,
+        couple, s0, s1, s2, lcat,
+    )
+    ns = paired(ms)
+    (part,) = call(
+        fold_body, (small,), [SMEM] + [VMEM] * 5, [pltpu.VMEM(block.shape, F32)], work // 2,
+        sector_states, ms, s0, x, h, rcat,
+    )
     count = chunks * sectors
     parts = lax.all_to_all(jnp.broadcast_to(part[None], (count, 8, LANES)), ("ops", "sec"), 0, 0)
+    single = pltpu.VMEM((1, side, side), F32)
+    (u,) = call(
+        cross_body, (jax.ShapeDtypeStruct((3, pairs, side, side), F32),), [VMEM] * 7,
+        [single], work, flag, mx, nx, ms, ns, s0, s1,
+    )
     return call(
         functools.partial(last_body, float((sectors * side * side) ** 0.5)),
         (
             jax.ShapeDtypeStruct((1, side, side), F32),
             jax.ShapeDtypeStruct((pairs, 1, side, side), F32),
         ),
-        [SMEM] + [VMEM] * 14, [pltpu.VMEM((2, side, side), F32)], work,
-        new_sector, parts, c, x0, x1, r0, r1, s0, s1, mx, mr, ms, nx, nr, ns,
+        [VMEM] * 5, [single], light, parts, c, mx, s0, u,
     )
 
 

time: 102 us -> 99.5 us (0.975)
  starting transfers between devices: 37.3 us -> 32.5 us
  waiting for transfers between devices: 13.6 us -> 16.2 us
  blocking collectives: 32.9 us -> 30.4 us
  local copies, waits for them, and re-layouts: 4.45 us -> 6.93 us
    all_to_all x2, waiting for transfers between devices: 0.01 us -> 6.5 us  [exchange(): return lax.all_to_all(value, 'ops', 0, 0)]
    ppermute x6, starting transfers between devices: 14.2 us -> 8.55 us  [over_sectors(): found.append(lax.ppermute(value, 'sec', [(i, i ^ d) for i in range(count)]))]
    all_to_all x1, waiting for transfers between devices: 7.54 us -> 4.09 us  [local(): lax.all_to_all(jnp.broadcast_to(part[None], (count, 8, LANES)), ('ops', '...]
    all_to_all x2, blocking collectives: 32.9 us -> 30.4 us  [exchange(): return lax.all_to_all(value, 'ops', 0, 0)]
    unnamed x13 -> x20, local copies, waits for them, and re-layouts: 3.78 us -> 6.26 us
    ppermute x6, waiting for transfers between devices: 5.17 us -> 3.17 us  [over_sectors(): found.append(lax.ppermute(value, 'sec', [(i, i ^ d) for i in range(count)]))]
    ppermute x6 -> x5, starting transfers between devices: 8.18 us -> 9.99 us  [paired(): return lax.ppermute(value, 'sec', [(i, i ^ 1) for i in range(count)])]
    ppermute x6 -> x5, waiting for transfers between devices: 0.85 us -> 2.42 us  [paired(): return lax.ppermute(value, 'sec', [(i, i ^ 1) for i in range(count)])]
  transfers between devices with their start and end apart: 18 -> 17, of which waited for: 5 -> 8; matrix products, arithmetic and copies ran while one was open for 1% -> 1% of each run, Pallas kernels for 3% -> 4%
where the time goes in v4:
time: 99.5 us; the launch traced here: 98.8 us
  starting transfers between devices  32.5 us (33%)
  blocking collectives  30.4 us (31%)
  waiting for transfers between devices  16.2 us (16%)
  Pallas kernels  10.7 us (11%)
  local copies, waits for them, and re-layouts  6.93 us (7%)
  between operations  2.11 us (2%)
    all_to_all x2, blocking collectives, exchange(): return lax.all_to_all(value, 'ops', 0, 0)  30.4 us
    pallas_call x13, Pallas kernels, call(): pl.pallas_call(body, out_shape=tuple(outs), in_specs=in_specs, out_specs=...  10.7 us
    ppermute x5, starting transfers between devices, paired(): return lax.ppermute(value, 'sec', [(i, i ^ 1) for i in range(count)])  9.99 us
    all_to_all x2, starting transfers between devices, exchange(): return lax.all_to_all(value, 'ops', 0, 0)  9.31 us
    ppermute x6, starting transfers between devices, over_sectors(): found.append(lax.ppermute(value, 'sec', [(i, i ^ d) for i in range(count)]))  8.55 us
    all_to_all x2, waiting for transfers between devices, exchange(): return lax.all_to_all(value, 'ops', 0, 0)  6.5 us
    unnamed x20, local copies, waits for them, and re-layouts  6.26 us
    all_to_all x1, waiting for transfers between devices, local(): lax.all_to_all(jnp.broadcast_to(part[None], (count, 8, LANES)), ('ops', '...  4.09 us
  transfers between devices with their start and end apart: 17, of which 8 were waited for; matrix products, arithmetic and copies ran while one was open for 1% of the time, Pallas kernels for 4%

profile of v4, /device:TPU:0, one launch (start us, length us, event | category | flops | bytes accessed | tf_op | source)
XLA Modules:
  0.0 98.8 jit_solution(7763648193725834596)
XLA Ops:
  1.3 0.9 copy-done.7
  2.2 0.7 collective-permute-start.1
  2.9 4.4 %collective-permute-start = (f32[8,64,128]{2,1,0:T(8,128)S(1)}, f32[8,64,128]{2,1,0:T(8,128)S(1)}, u32[]{:S(2)}, u32[]{:S(2)}) collective-permute-start(f32[8,64,128]{2,1,0:T(8,128)S(1)} %shard_map.86.x0.x_ref), channel_id=1, source_target_pairs={{0,1},{1,0},{2,3},{3,2},{4,5},{5,4},{6,7},{7,6},{8,9},{9,8},{10,11... | collective-permute-start | bytes 786440 | tf_op jit(solution)/shard_map/ppermute | solution.py:277
  8.0 0.0 copy-start.1
  8.0 1.0 %copy-done.1 = f32[2,1,256,256]{3,2,1,0:T(8,128)S(1)} copy-done((f32[2,1,256,256]{3,2,1,0:T(8,128)S(1)}, f32[2,1,256,256]{3,2,1,0:T(8,128)}, u32[]{:S(2)}) %copy-start.1) | copy-done | bytes 524312
  9.0 1.0 %copy-done.2 = f32[2,1,256,256]{3,2,1,0:T(8,128)S(1)} copy-done((f32[2,1,256,256]{3,2,1,0:T(8,128)S(1)}, f32[2,1,256,256]{3,2,1,0:T(8,128)}, u32[]{:S(2)}) %copy-start.2) | copy-done | bytes 524312
  10.1 0.3 shard_map.87
  10.3 0.0 collective-permute-done.1.x2
  10.3 0.0 collective-permute-done.x1
  10.4 0.0 copy-start.8
  10.4 0.6 copy-done.8
  11.0 2.3 %shard_map.88 = (f32[8,64,128]{2,1,0:T(8,128)}, f32[2,256,256]{2,1,0:T(8,128)S(1)}, f32[8,128]{1,0:T(8,128)S(1)}) custom-call(s32[1]{0:T(128)S(6)} %copy.9.size_ref, s32[2]{0:T(128)S(1)} %bitcast.1, f32[8,64,128]{2,1,0:T(8,128)S(1)} %shard_map.86.x0.x_ref, f32[8,64,128]{2,1,0:T(8,128)S(1)} %collective-permute-done.x1, ...), custom_call_target="tpu_custom_call" | custom-call | flops 402653184 | bytes 2625548 | tf_op jit(solution)/shard_map/pallas_call | solution.py:21
  13.3 5.8 %all-to-all-start = ((f32[8,64,128]{2,1,0:T(8,128)}), f32[8,64,128]{2,1,0:T(8,128)S(1)}, u32[]{:S(2)}, u32[]{:S(2)}) async-start(f32[8,64,128]{2,1,0:T(8,128)} %get-tuple-element.19), calls=%async_computation | async-start | bytes 524288 | tf_op jit(solution)/shard_map/all_to_all | solution.py:297
  19.2 2.6 %collective-permute-start.3 = (f32[8,128]{1,0:T(8,128)S(1)}, f32[8,128]{1,0:T(8,128)S(1)}, u32[]{:S(2)}, u32[]{:S(2)}) collective-permute-start(f32[8,128]{1,0:T(8,128)S(1)} %get-tuple-element.20.mine), channel_id=1, source_target_pairs={{0,2},{1,3},{2,0},{3,1},{4,6},{5,7},{6,4},{7,5},{8,10},{9,11},{10,... | collective-permute-start | bytes 12296 | tf_op jit(solution)/shard_map/ppermute | solution.py:292
  21.8 0.0 collective-permute-start.2
  21.8 0.4 collective-permute-done.4.refs_2_
  22.2 1.2 %collective-permute-done.3.refs_1_ = f32[8,128]{1,0:T(8,128)S(1)} collective-permute-done((f32[8,128]{1,0:T(8,128)S(1)}, f32[8,128]{1,0:T(8,128)S(1)}, u32[]{:S(2)}, u32[]{:S(2)}) %collective-permute-start.3) | collective-permute-done | bytes 4128 | tf_op jit(solution)/shard_map/ppermute | solution.py:292
  23.4 5.8 %all-to-all-done.terms_ref = f32[8,64,128]{2,1,0:T(8,128)S(1)} async-done(((f32[8,64,128]{2,1,0:T(8,128)}), f32[8,64,128]{2,1,0:T(8,128)S(1)}, u32[]{:S(2)}, u32[]{:S(2)}) %all-to-all-start) | async-done | bytes 262176 | tf_op jit(solution)/shard_map/all_to_all | solution.py:297
  29.2 14.0 %all_to_all.25.g_ref.g0 = f32[8,72,128]{2,1,0:T(8,128)S(1)} all-to-all(f32[8,72,128]{2,1,0:T(8,128)S(1)} %shard_map.89), channel_id=1, replica_groups=mesh['ops'=8,'sec'=4] {'ops'}, dimensions={0} | all-to-all | bytes 589824 | tf_op jit(solution)/shard_map/all_to_all | solution.py:297
  43.2 0.2 shard_map.90
  43.4 0.7 collective-permute-start.6
  44.1 0.1 collective-permute-start.5
  44.2 1.5 %collective-permute-done.5.r1 = f32[8,64,128]{2,1,0:T(8,128)S(1)} collective-permute-done((f32[8,64,128]{2,1,0:T(8,128)S(1)}, f32[8,64,128]{2,1,0:T(8,128)S(1)}, u32[]{:S(2)}, u32[]{:S(2)}) %collective-permute-start.5) | collective-permute-done | bytes 262176 | tf_op jit(solution)/shard_map/ppermute | solution.py:277
  45.7 2.3 %shard_map.91 = (f32[8,64,128]{2,1,0:T(8,128)}, f32[2,256,256]{2,1,0:T(8,128)S(1)}, f32[8,128]{1,0:T(8,128)S(1)}) custom-call(s32[1]{0:T(128)S(6)} %copy.9.size_ref, s32[2]{0:T(128)S(1)} %bitcast.2, f32[8,64,128]{2,1,0:T(8,128)S(1)} %get-tuple-element.21.r0.r_in, f32[8,64,128]{2,1,0:T(8,128)S(1)} %collective-permute-done.5.r1, ...), custom_call_target="tpu_custom_call" | custom-call | flops 402653184 | bytes 3182604 | tf_op jit(solution)/shard_map/pallas_call | solution.py:21
  48.0 0.8 copy-done.3
  48.8 3.5 %all-to-all-start.2 = ((f32[8,64,128]{2,1,0:T(8,128)}), f32[8,64,128]{2,1,0:T(8,128)S(1)}, u32[]{:S(2)}, u32[]{:S(2)}) async-start(f32[8,64,128]{2,1,0:T(8,128)} %get-tuple-element.22), calls=%async_computation.2 | async-start | bytes 524288 | tf_op jit(solution)/shard_map/all_to_all | solution.py:297
  52.3 1.5 %collective-permute-start.9 = (f32[8,128]{1,0:T(8,128)S(1)}, f32[8,128]{1,0:T(8,128)S(1)}, u32[]{:S(2)}, u32[]{:S(2)}) collective-permute-start(f32[8,128]{1,0:T(8,128)S(1)} %get-tuple-element.23.mine), channel_id=1, source_target_pairs={{0,3},{1,2},{2,1},{3,0},{4,7},{5,6},{6,5},{7,4},{8,11},{9,10},{10,... | collective-permute-start | bytes 12296 | tf_op jit(solution)/shard_map/ppermute | solution.py:292
  53.8 4.4 %collective-permute-start.8 = (f32[8,128]{1,0:T(8,128)S(1)}, f32[8,128]{1,0:T(8,128)S(1)}, u32[]{:S(2)}, u32[]{:S(2)}) collective-permute-start(f32[8,128]{1,0:T(8,128)S(1)} %get-tuple-element.23.mine), channel_id=1, source_target_pairs={{0,2},{1,3},{2,0},{3,1},{4,6},{5,7},{6,4},{7,5},{8,10},{9,11},{10,... | collective-permute-start | bytes 12296 | tf_op jit(solution)/shard_map/ppermute | solution.py:292
  58.2 1.6 %collective-permute-done.8.refs_1_ = f32[8,128]{1,0:T(8,128)S(1)} collective-permute-done((f32[8,128]{1,0:T(8,128)S(1)}, f32[8,128]{1,0:T(8,128)S(1)}, u32[]{:S(2)}, u32[]{:S(2)}) %collective-permute-start.8) | collective-permute-done | bytes 4128 | tf_op jit(solution)/shard_map/ppermute | solution.py:292
  59.8 0.7 all-to-all-done.2.terms_ref
  60.6 16.4 %all_to_all.26.s_ref = f32[8,72,128]{2,1,0:T(8,128)S(1)} all-to-all(f32[8,72,128]{2,1,0:T(8,128)S(1)} %shard_map.92), channel_id=1, replica_groups=mesh['ops'=8,'sec'=4] {'ops'}, dimensions={0} | all-to-all | bytes 589824 | tf_op jit(solution)/shard_map/all_to_all | solution.py:297
  77.0 0.4 shard_map.93
  77.4 0.7 collective-permute-start.11
  78.1 1.0 %collective-permute-start.10 = (f32[8,64,128]{2,1,0:T(8,128)S(1)}, f32[8,64,128]{2,1,0:T(8,128)S(1)}, u32[]{:S(2)}, u32[]{:S(2)}) collective-permute-start(f32[8,64,128]{2,1,0:T(8,128)S(1)} %get-tuple-element.25.r0.s0), channel_id=1, source_target_pairs={{0,1},{1,0},{2,3},{3,2},{4,5},{5,4},{6,7},{7,6},{8,9},{9,8},{10,11... | collective-permute-start | bytes 786440 | tf_op jit(solution)/shard_map/ppermute | solution.py:277
  79.1 0.2 shard_map.96.b_ref
  79.3 0.1 collective-permute-start.12
  79.4 0.9 collective-permute-done.10.r1.s1
  80.3 1.0 %shard_map.94.m_ref = f32[2,256,256]{2,1,0:T(8,128)S(1)} custom-call(s32[2]{0:T(128)S(1)} %bitcast.3, f32[8,64,128]{2,1,0:T(8,128)S(1)} %get-tuple-element.25.r0.s0, f32[8,64,128]{2,1,0:T(8,128)S(1)} %collective-permute-done.10.r1.s1, f32[8,64,128]{2,1,0:T(8,128)S(1)} %collective-permute-done.11.r2, bf16[2,2,256,256]{3,2,1,0:T(8,128)(2,1)S(1)} %get-tuple-element.17.lcat_ref), custom_call_target="tpu_custom_call" | custom-call | flops 201326592 | bytes 1835016 | tf_op jit(solution)/shard_map/pallas_call | solution.py:21
  81.3 4.4 %collective-permute-start.13 = (f32[2,256,256]{2,1,0:T(8,128)S(1)}, f32[2,256,256]{2,1,0:T(8,128)S(1)}, u32[]{:S(2)}, u32[]{:S(2)}) collective-permute-start(f32[2,256,256]{2,1,0:T(8,128)S(1)} %shard_map.94.m_ref), channel_id=1, source_target_pairs={{0,1},{1,0},{2,3},{3,2},{4,5},{5,4},{6,7},{7,6},{8,9},{9,8},{10,11... | collective-permute-start | bytes 1572872 | tf_op jit(solution)/shard_map/ppermute | solution.py:277
  85.7 0.4 shard_map.95
  86.1 0.7 broadcast_in_dim.2
  86.8 2.6 %all-to-all-start.4 = ((f32[32,8,128]{2,1,0:T(8,128)}), f32[32,8,128]{2,1,0:T(8,128)S(1)}, u32[]{:S(2)}, u32[]{:S(2)}) async-start(f32[32,8,128]{2,1,0:T(8,128)} %broadcast_in_dim.2), calls=%async_computation.4 | async-start | bytes 262144 | tf_op jit(solution)/shard_map/all_to_all | solution.py:369
  89.4 0.0 copy-start.5
  89.4 0.8 copy-done.5
  90.2 1.0 %copy-done.6 = f32[2,256,256]{2,1,0:T(8,128)S(1)} copy-done((f32[2,256,256]{2,1,0:T(8,128)S(1)}, f32[2,256,256]{2,1,0:T(8,128)}, u32[]{:S(2)}) %copy-start.6) | copy-done | bytes 524312
  91.2 2.3 %shard_map.97.u_ref = f32[3,2,256,256]{3,2,1,0:T(8,128)S(1)} custom-call(f32[8,128]{1,0:T(8,128)S(1)} %get-tuple-element.31.flag_ref, f32[3,256,256]{2,1,0:T(8,128)S(1)} %shard_map.96.b_ref, f32[3,256,256]{2,1,0:T(8,128)} %collective-permute-done.12.n_ref, f32[2,256,256]{2,1,0:T(8,128)S(1)} %shard_map.94.m_ref, f32[2,256,256]{2,1,0:T(8,128)S(1)} %copy-done.6, ...), custom_call_target="tpu_custom_call" | custom-call | flops 402653184 | bytes 4722688 | tf_op jit(solution)/shard_map/pallas_call | solution.py:21
  93.5 4.1 %all-to-all-done.4.parts_ref = f32[32,8,128]{2,1,0:T(8,128)S(1)} async-done(((f32[32,8,128]{2,1,0:T(8,128)}), f32[32,8,128]{2,1,0:T(8,128)S(1)}, u32[]{:S(2)}, u32[]{:S(2)}) %all-to-all-start.4) | async-done | bytes 131104 | tf_op jit(solution)/shard_map/all_to_all | solution.py:369
  97.6 1.2 %shard_map.98 = (f32[1,256,256]{2,1,0:T(8,128)}, f32[2,1,256,256]{3,2,1,0:T(8,128)}) custom-call(f32[32,8,128]{2,1,0:T(8,128)S(1)} %all-to-all-done.4.parts_ref, f32[8,128]{1,0:T(8,128)S(1)} %get-tuple-element.28.c_in, f32[3,256,256]{2,1,0:T(8,128)S(1)} %shard_map.96.b_ref, f32[8,64,128]{2,1,0:T(8,128)S(1)} %get-tuple-element.25.r0.s0, ...), custom_call_target="tpu_custom_call" | custom-call | flops 1310720 | bytes 3543040 | tf_op jit(solution)/shard_map/pallas_call | solution.py:21
  (22 shorter events, 0.1 us)
Async XLA Ops:
  1.3 0.9 copy-start.7
  2.2 8.1 %collective-permute-start.1 = (f32[8,64,128]{2,1,0:T(8,128)S(1)}, f32[8,64,128]{2,1,0:T(8,128)S(1)}, u32[]{:S(2)}, u32[]{:S(2)}) collective-permute-start(f32[8,64,128]{2,1,0:T(8,128)S(1)} %shard_map.86.x0.x_ref), channel_id=1, source_target_pairs={{1,2},{2,1},{5,6},{6,5},{9,10},{10,9},{13,14},{14,13},{17,18},{18,... | collective-permute-start | bytes 786440 | tf_op jit(solution)/shard_map/ppermute | solution.py:285
  2.9 7.4 %collective-permute-start = (f32[8,64,128]{2,1,0:T(8,128)S(1)}, f32[8,64,128]{2,1,0:T(8,128)S(1)}, u32[]{:S(2)}, u32[]{:S(2)}) collective-permute-start(f32[8,64,128]{2,1,0:T(8,128)S(1)} %shard_map.86.x0.x_ref), channel_id=1, source_target_pairs={{0,1},{1,0},{2,3},{3,2},{4,5},{5,4},{6,7},{7,6},{8,9},{9,8},{10,11... | collective-permute-start | bytes 786440 | tf_op jit(solution)/shard_map/ppermute | solution.py:277
  8.0 1.0 %copy-start.1 = (f32[2,1,256,256]{3,2,1,0:T(8,128)S(1)}, f32[2,1,256,256]{3,2,1,0:T(8,128)}, u32[]{:S(2)}) copy-start(f32[2,1,256,256]{3,2,1,0:T(8,128)} %left_ref.1) | copy-start | bytes 1572868
  9.0 1.0 %copy-start.2 = (f32[2,1,256,256]{3,2,1,0:T(8,128)S(1)}, f32[2,1,256,256]{3,2,1,0:T(8,128)}, u32[]{:S(2)}) copy-start(f32[2,1,256,256]{3,2,1,0:T(8,128)} %right_ref.1) | copy-start | bytes 1572868
  10.4 0.7 copy-start.8
  11.0 32.2 %copy-start = (bf16[1,256,256]{2,1,0:T(8,128)(2,1)S(1)}, bf16[1,256,256]{2,1,0:T(8,128)(2,1)}, u32[]{:S(2)}) copy-start(bf16[1,256,256]{2,1,0:T(8,128)(2,1)} %diag_ref.3) | copy-start | bytes 393220
  13.3 15.8 %all-to-all-start = ((f32[8,64,128]{2,1,0:T(8,128)}), f32[8,64,128]{2,1,0:T(8,128)S(1)}, u32[]{:S(2)}, u32[]{:S(2)}) async-start(f32[8,64,128]{2,1,0:T(8,128)} %get-tuple-element.19), calls=%async_computation | async-start | bytes 524288 | tf_op jit(solution)/shard_map/all_to_all | solution.py:297
  19.1 3.0 %collective-permute-start.4 = (f32[8,128]{1,0:T(8,128)S(1)}, f32[8,128]{1,0:T(8,128)S(1)}, u32[]{:S(2)}, u32[]{:S(2)}) collective-permute-start(f32[8,128]{1,0:T(8,128)S(1)} %get-tuple-element.20.mine), channel_id=1, source_target_pairs={{0,3},{1,2},{2,1},{3,0},{4,7},{5,6},{6,5},{7,4},{8,11},{9,10},{10,... | collective-permute-start | bytes 12296 | tf_op jit(solution)/shard_map/ppermute | solution.py:292
  19.2 4.2 %collective-permute-start.3 = (f32[8,128]{1,0:T(8,128)S(1)}, f32[8,128]{1,0:T(8,128)S(1)}, u32[]{:S(2)}, u32[]{:S(2)}) collective-permute-start(f32[8,128]{1,0:T(8,128)S(1)} %get-tuple-element.20.mine), channel_id=1, source_target_pairs={{0,2},{1,3},{2,0},{3,1},{4,6},{5,7},{6,4},{7,5},{8,10},{9,11},{10,... | collective-permute-start | bytes 12296 | tf_op jit(solution)/shard_map/ppermute | solution.py:292
  21.8 1.6 %collective-permute-start.2 = (f32[8,128]{1,0:T(8,128)S(1)}, f32[8,128]{1,0:T(8,128)S(1)}, u32[]{:S(2)}, u32[]{:S(2)}) collective-permute-start(f32[8,128]{1,0:T(8,128)S(1)} %get-tuple-element.20.mine), channel_id=1, source_target_pairs={{0,1},{1,0},{2,3},{3,2},{4,5},{5,4},{6,7},{7,6},{8,9},{9,8},{10,11... | collective-permute-start | bytes 12296 | tf_op jit(solution)/shard_map/ppermute | solution.py:292
  43.4 0.8 collective-permute-start.6
  44.1 1.6 %collective-permute-start.5 = (f32[8,64,128]{2,1,0:T(8,128)S(1)}, f32[8,64,128]{2,1,0:T(8,128)S(1)}, u32[]{:S(2)}, u32[]{:S(2)}) collective-permute-start(f32[8,64,128]{2,1,0:T(8,128)S(1)} %get-tuple-element.21.r0.r_in), channel_id=1, source_target_pairs={{0,1},{1,0},{2,3},{3,2},{4,5},{5,4},{6,7},{7,6},{8,9},{9,8},{10,11... | collective-permute-start | bytes 786440 | tf_op jit(solution)/shard_map/ppermute | solution.py:277
  48.0 0.8 copy-start.3
  48.8 11.8 %all-to-all-start.2 = ((f32[8,64,128]{2,1,0:T(8,128)}), f32[8,64,128]{2,1,0:T(8,128)S(1)}, u32[]{:S(2)}, u32[]{:S(2)}) async-start(f32[8,64,128]{2,1,0:T(8,128)} %get-tuple-element.22), calls=%async_computation.2 | async-start | bytes 524288 | tf_op jit(solution)/shard_map/all_to_all | solution.py:297
  52.3 5.9 %collective-permute-start.9 = (f32[8,128]{1,0:T(8,128)S(1)}, f32[8,128]{1,0:T(8,128)S(1)}, u32[]{:S(2)}, u32[]{:S(2)}) collective-permute-start(f32[8,128]{1,0:T(8,128)S(1)} %get-tuple-element.23.mine), channel_id=1, source_target_pairs={{0,3},{1,2},{2,1},{3,0},{4,7},{5,6},{6,5},{7,4},{8,11},{9,10},{10,... | collective-permute-start | bytes 12296 | tf_op jit(solution)/shard_map/ppermute | solution.py:292
  53.8 6.1 %collective-permute-start.8 = (f32[8,128]{1,0:T(8,128)S(1)}, f32[8,128]{1,0:T(8,128)S(1)}, u32[]{:S(2)}, u32[]{:S(2)}) collective-permute-start(f32[8,128]{1,0:T(8,128)S(1)} %get-tuple-element.23.mine), channel_id=1, source_target_pairs={{0,2},{1,3},{2,0},{3,1},{4,6},{5,7},{6,4},{7,5},{8,10},{9,11},{10,... | collective-permute-start | bytes 12296 | tf_op jit(solution)/shard_map/ppermute | solution.py:292
  58.2 1.6 %collective-permute-start.7 = (f32[8,128]{1,0:T(8,128)S(1)}, f32[8,128]{1,0:T(8,128)S(1)}, u32[]{:S(2)}, u32[]{:S(2)}) collective-permute-start(f32[8,128]{1,0:T(8,128)S(1)} %get-tuple-element.23.mine), channel_id=1, source_target_pairs={{0,1},{1,0},{2,3},{3,2},{4,5},{5,4},{6,7},{7,6},{8,9},{9,8},{10,11... | collective-permute-start | bytes 12296 | tf_op jit(solution)/shard_map/ppermute | solution.py:292
  60.6 18.5 %copy-start.4 = (f32[2,256,256]{2,1,0:T(8,128)S(1)}, f32[2,256,256]{2,1,0:T(8,128)}, u32[]{:S(2)}) copy-start(f32[2,256,256]{2,1,0:T(8,128)} %copy-done.3) | copy-start | bytes 1572868
  77.0 3.3 %copy-start.9 = (s32[2,1]{0,1:T(1,128)S(1)}, s32[2,1]{0,1:T(1,128)}, u32[]{:S(2)}) copy-start(s32[2,1]{0,1:T(1,128)} %param.12) | copy-start | bytes 28
  77.4 2.0 %collective-permute-start.11 = (f32[8,64,128]{2,1,0:T(8,128)S(1)}, f32[8,64,128]{2,1,0:T(8,128)S(1)}, u32[]{:S(2)}, u32[]{:S(2)}) collective-permute-start(f32[8,64,128]{2,1,0:T(8,128)S(1)} %get-tuple-element.25.r0.s0), channel_id=1, source_target_pairs={{1,2},{2,1},{5,6},{6,5},{9,10},{10,9},{13,14},{14,13},{17,18},{18,... | collective-permute-start | bytes 786440 | tf_op jit(solution)/shard_map/ppermute | solution.py:285
  78.1 2.2 %collective-permute-start.10 = (f32[8,64,128]{2,1,0:T(8,128)S(1)}, f32[8,64,128]{2,1,0:T(8,128)S(1)}, u32[]{:S(2)}, u32[]{:S(2)}) collective-permute-start(f32[8,64,128]{2,1,0:T(8,128)S(1)} %get-tuple-element.25.r0.s0), channel_id=1, source_target_pairs={{0,1},{1,0},{2,3},{3,2},{4,5},{5,4},{6,7},{7,6},{8,9},{9,8},{10,11... | collective-permute-start | bytes 786440 | tf_op jit(solution)/shard_map/ppermute | solution.py:277
  79.3 10.9 %collective-permute-start.12 = (f32[3,256,256]{2,1,0:T(8,128)S(1)}, f32[3,256,256]{2,1,0:T(8,128)}, u32[]{:S(2)}, u32[]{:S(2)}) collective-permute-start(f32[3,256,256]{2,1,0:T(8,128)S(1)} %shard_map.96.b_ref), channel_id=1, source_target_pairs={{0,1},{1,0},{2,3},{3,2},{4,5},{5,4},{6,7},{7,6},{8,9},{9,8},{10,11... | collective-permute-start | bytes 2359304 | tf_op jit(solution)/shard_map/ppermute | solution.py:277
  81.3 8.0 %collective-permute-start.13 = (f32[2,256,256]{2,1,0:T(8,128)S(1)}, f32[2,256,256]{2,1,0:T(8,128)S(1)}, u32[]{:S(2)}, u32[]{:S(2)}) collective-permute-start(f32[2,256,256]{2,1,0:T(8,128)S(1)} %shard_map.94.m_ref), channel_id=1, source_target_pairs={{0,1},{1,0},{2,3},{3,2},{4,5},{5,4},{6,7},{7,6},{8,9},{9,8},{10,11... | collective-permute-start | bytes 1572872 | tf_op jit(solution)/shard_map/ppermute | solution.py:277
  86.8 10.8 %all-to-all-start.4 = ((f32[32,8,128]{2,1,0:T(8,128)}), f32[32,8,128]{2,1,0:T(8,128)S(1)}, u32[]{:S(2)}, u32[]{:S(2)}) async-start(f32[32,8,128]{2,1,0:T(8,128)} %broadcast_in_dim.2), calls=%async_computation.4 | async-start | bytes 262144 | tf_op jit(solution)/shard_map/all_to_all | solution.py:369
  89.4 0.8 copy-start.5
  90.2 1.0 %copy-start.6 = (f32[2,256,256]{2,1,0:T(8,128)S(1)}, f32[2,256,256]{2,1,0:T(8,128)}, u32[]{:S(2)}) copy-start(f32[2,256,256]{2,1,0:T(8,128)} %copy-done.5) | copy-start | bytes 1572868

commit v5 on v4

--- a/solution.py
+++ b/solution.py
@@ -12,6 +12,7 @@
 F32 = jnp.float32
 BF16 = jnp.bfloat16
 VMEM = pl.BlockSpec(memory_space=pltpu.VMEM)
+HBM = pl.BlockSpec(memory_space=pltpu.HBM)
 SMEM = pl.BlockSpec(memory_space=pltpu.SMEM)
 
 
@@ -22,7 +23,7 @@
         body,
         out_shape=tuple(outs),
         in_specs=in_specs,
-        out_specs=tuple(VMEM for _ in outs),
+        out_specs=tuple(HBM if scratch and i == 1 and len(scratch) == 2 else VMEM for i in range(len(outs))),
         scratch_shapes=scratch,
         compiler_params=pltpu.CompilerParams(vmem_limit_bytes=8 * 1024 * 1024),
         cost_estimate=pl.CostEstimate(flops=flops, bytes_accessed=size, transcendentals=0),
@@ -38,15 +39,17 @@
             ]
 
 
-def unpack(ref, k, value):
-    chunks, _, _ = value.shape
-    side = ref.shape[1]
-    rc = side // chunks
-    for o in range(chunks):
-        for j in range(side // LANES):
-            ref[k, o * rc : (o + 1) * rc, j * LANES : (j + 1) * LANES] = value[
-                o, j * rc : (j + 1) * rc
-            ]
+def unpack(value):
+    chunks, cw, _ = value.shape
+    groups = int((cw * chunks // LANES) ** 0.5)
+    rc = cw // groups
+    return jnp.concatenate(
+        [
+            jnp.concatenate([value[o, j * rc : (j + 1) * rc] for j in range(groups)], axis=1)
+            for o in range(chunks)
+        ],
+        axis=0,
+    )
 
 
 def halves(value):
@@ -71,15 +74,11 @@
     return (rows < size) & (cols < size)
 
 
-def pick(couple_ref, p, here, ref):
-    source = couple_ref[p]
-    slot = jnp.where(source == here, 0, jnp.where(source == here + 1 - 2 * (here % 2), 1, 2))
-    return jnp.where(source >= 0, ref[slot], 0.0)
-
-
-def mix(couple_ref, p, here, ref, lcat_ref):
-    high, low = halves(pick(couple_ref, p, here, ref))
-    return three(lcat_ref[p, 0], lcat_ref[p, 1], high, low)
+def pick(slot, blocks):
+    value = jnp.zeros(blocks[0].shape, F32)
+    for k, block in enumerate(blocks):
+        value = jnp.where(slot == float(k), block[...], value)
+    return unpack(value)
 
 
 def fold(mixed, rcat_ref):
@@ -129,22 +128,35 @@
     pack(x_ref, (), x_ref.shape, jnp.where(live, psi_ref[0].astype(F32), 0.0))
 
 
-def split_body(label_ref, left_ref, right_ref, lcat_ref, rcat_ref, flag_ref):
+def split_body(
+    label_ref, couple_ref, left_ref, right_ref, lcat_ref, rcat_ref, flag_ref, slot_ref
+):
+    here = lax.axis_index("sec")
     for p in range(left_ref.shape[0]):
         lcat_ref[p, 0], lcat_ref[p, 1] = halves(left_ref[p, 0])
         rcat_ref[p, 0], rcat_ref[p, 1] = halves(right_ref[p, 0].T)
-    stay = jnp.where(label_ref[0] == lax.axis_index("sec"), 1.0, 0.0)
-    flag_ref[...] = jnp.full(flag_ref.shape, stay)
-
-
-def mix_all(couple_ref, blocks, lcat_ref, m_ref, v_ref):
-    here = lax.axis_index("sec")
-    for k, block in enumerate(blocks):
-        unpack(v_ref, k, block[...])
-    mixed = [mix(couple_ref, p, here, v_ref, lcat_ref) for p in range(lcat_ref.shape[0])]
+        source = couple_ref[p]
+        near = here + 1 - 2 * (here % 2)
+        slot = jnp.where(source == here, 0.0, jnp.where(source == near, 1.0, 2.0))
+        slot_ref[p] = jnp.full(slot_ref.shape[1:], jnp.where(source >= 0, slot, -1.0))
+    flag_ref[...] = jnp.full(flag_ref.shape, jnp.where(label_ref[0] == here, 1.0, 0.0))
+
+
+def mix_all(slot_ref, blocks, lcat_ref):
+    mixed = []
+    for p in range(lcat_ref.shape[0]):
+        high, low = halves(pick(slot_ref[p, 0:1, 0:1][None], blocks))
+        mixed.append(three(lcat_ref[p, 0], lcat_ref[p, 1], high, low))
+    return mixed
+
+
+def save(mixed, room_ref, m_ref, sem):
+    copies = []
     for p, one in enumerate(mixed):
-        m_ref[p] = one
-    return mixed
+        room_ref[p] = one
+        copies.append(pltpu.make_async_copy(room_ref.at[p], m_ref.at[p], sem.at[p]))
+        copies[-1].start()
+    return copies
 
 
 def fold_all(size_ref, mixed, rcat_ref, y_ref):
@@ -154,12 +166,15 @@
 
 
 def first_body(
-    size_ref, couple_ref, x0, x1, x2, lcat_ref, rcat_ref, y_ref, m_ref, part_ref, v_ref
+    size_ref, slot_ref, x0, x1, x2, lcat_ref, rcat_ref, y_ref, m_ref, part_ref, room_ref, sem
 ):
-    mixed = mix_all(couple_ref, (x0, x1, x2), lcat_ref, m_ref, v_ref)
+    mixed = mix_all(slot_ref, (x0, x1, x2), lcat_ref)
+    copies = save(mixed, room_ref, m_ref, sem)
     y = fold_all(size_ref, mixed, rcat_ref, y_ref)
     x = x0[lax.axis_index("ops")]
     part_ref[...] = tile([rows(x * x), rows(x0[...] * y)])
+    for copy in copies:
+        copy.wait()
 
 
 def five(x0, r0, h0, y):
@@ -169,14 +184,19 @@
 
 
 def second_body(
-    size_ref, couple_ref, r0, r1, r2, x0, g0, lcat_ref, rcat_ref, y_ref, m_ref, part_ref, v_ref
+    size_ref, slot_ref, r0, r1, r2, x0, g0, lcat_ref, rcat_ref,
+    y_ref, m_ref, part_ref, room_ref, sem,
 ):
-    mixed = mix_all(couple_ref, (r0, r1, r2), lcat_ref, m_ref, v_ref)
+    mixed = mix_all(slot_ref, (r0, r1, r2), lcat_ref)
+    copies = save(mixed, room_ref, m_ref, sem)
     part_ref[...] = five(x0, r0, g0, fold_all(size_ref, mixed, rcat_ref, y_ref))
-
-
-def mix_body(couple_ref, r0, r1, r2, lcat_ref, m_ref, v_ref):
-    mix_all(couple_ref, (r0, r1, r2), lcat_ref, m_ref, v_ref)
+    for copy in copies:
+        copy.wait()
+
+
+def mix_body(slot_ref, r0, r1, r2, lcat_ref, m_ref):
+    for p, one in enumerate(mix_all(slot_ref, (r0, r1, r2), lcat_ref)):
+        m_ref[p] = one
 
 
 def fold_body(size_ref, m_ref, r0, x0, h0, rcat_ref, part_ref, y_ref):
@@ -187,15 +207,15 @@
 def blend_body(c_in, a_ref, b_ref, x_ref, out_ref):
     pairs = a_ref.shape[0]
     out_ref[:pairs] = c_in[2:3, 0:1] * a_ref[...] + c_in[3:4, 0:1] * b_ref[...]
-    unpack(out_ref, pairs, x_ref[...])
-
-
-def cross_body(flag_ref, b_ref, n_ref, m_ref, w_ref, s0, s1, u_ref, v_ref):
+    out_ref[pairs] = unpack(x_ref[...])
+
+
+def cross_body(flag_ref, b_ref, n_ref, m_ref, w_ref, s0, s1, u_ref):
     stay = flag_ref[0:1, 0:1] > 0.5
     pairs, side, _ = m_ref.shape
-    unpack(v_ref, 0, jnp.where(stay[None], s0[...], s1[...]))
+    new = unpack(jnp.where(stay[None], s0[...], s1[...]))
     x = jnp.where(stay, b_ref[pairs], n_ref[pairs])
-    left = jnp.concatenate([x.T, v_ref[0].T], axis=0)
+    left = jnp.concatenate([x.T, new.T], axis=0)
     lh, ll = halves(left)
     for p in range(pairs):
         old, new = jnp.where(stay, b_ref[p], n_ref[p]), jnp.where(stay, m_ref[p], w_ref[p])
@@ -257,15 +277,13 @@
     store(c_ref, [theta, xx, on_x, on_r])
 
 
-def last_body(scale, parts_ref, c_in, b_ref, s0, u_ref, wave_ref, turn_ref, v_ref):
-    side = v_ref.shape[1]
-    pairs = u_ref.shape[1]
+def last_body(scale, parts_ref, c_in, b_ref, s0, u_ref, wave_ref, turn_ref):
+    pairs, side = u_ref.shape[1:3]
     xr, rr, rh, xhr, rhr = numbers(parts_ref[...], 5)
     on_x, on_s, _, _ = update(c_in[1:2, 0:1], c_in[0:1, 0:1], xr, rr, rh, xhr, rhr)
     on_x = on_x * scale
     on_s = on_s * scale
-    unpack(v_ref, 0, on_s * s0[...])
-    wave_ref[0] = on_x * b_ref[pairs] + v_ref[0]
+    wave_ref[0] = on_x * b_ref[pairs] + unpack(on_s * s0[...])
     root = 1.0 / side**0.5
     xx, xs, ss = on_x * on_x * root, on_x * on_s * root, on_s * on_s * root
     for p in range(pairs):
@@ -278,11 +296,14 @@
 
 
 def other(value):
-    count = lax.axis_size("sec")
+    count, groups = lax.axis_size("sec"), lax.axis_size("ops")
     route = []
-    for i in range(1, count - 1, 2):
-        route += [(i, i + 1), (i + 1, i)]
-    return lax.ppermute(value, "sec", route)
+    for o in range(groups):
+        for i in range(1, count - 1, 2):
+            route += [(o * count + i, o * count + i + 1), (o * count + i + 1, o * count + i)]
+        if groups % 2 == 0:
+            route += [(o * count + i, (o ^ 1) * count + i) for i in (0, count - 1)]
+    return lax.ppermute(value, ("ops", "sec"), route)
 
 
 def over_sectors(value):
@@ -308,7 +329,7 @@
     wide = jax.ShapeDtypeStruct((chunks, cw + 8, LANES), F32)
     small = jax.ShapeDtypeStruct((8, LANES), F32)
     inner = jax.ShapeDtypeStruct((pairs, side, side), F32)
-    scratch = pltpu.VMEM((3, side, side), F32)
+    kept = [pltpu.VMEM(inner.shape, F32), pltpu.SemaphoreType.DMA((pairs,))]
     work = 12 * pairs * side**3
     light = 20 * side**2
 
@@ -322,18 +343,19 @@
 
     (x0,) = call(start_body, (block,), [SMEM, VMEM], [], light, sector_states, psi_guess)
     x2, x1 = other(x0), paired(x0)
-    lcat, rcat, flag = call(
+    lcat, rcat, flag, slots = call(
         split_body,
         (
             jax.ShapeDtypeStruct((pairs, 2, side, side), BF16),
             jax.ShapeDtypeStruct((pairs, 2, side, side), BF16),
             small,
+            jax.ShapeDtypeStruct((pairs, 8, LANES), F32),
         ),
-        [SMEM] + [VMEM] * 2, [], light * pairs, new_sector, left_ops, right_ops,
+        [SMEM] * 2 + [VMEM] * 2, [], light * pairs, new_sector, couple, left_ops, right_ops,
     )
     y, mx, part = call(
-        first_body, (block, inner, small), [SMEM] * 2 + [VMEM] * 5, [scratch], work,
-        sector_states, couple, x0, x1, x2, lcat, rcat,
+        first_body, (block, inner, small), [SMEM] + [VMEM] * 6, kept, work,
+        sector_states, slots, x0, x1, x2, lcat, rcat,
     )
     g = gathered(y, part)
     r0, c = call(
@@ -342,8 +364,8 @@
     )
     r2, r1 = other(r0), paired(r0)
     y, mr, part = call(
-        second_body, (block, inner, small), [SMEM] * 2 + [VMEM] * 7, [scratch], work,
-        sector_states, couple, r0, r1, r2, x0, g, lcat, rcat,
+        second_body, (block, inner, small), [SMEM] + [VMEM] * 8, kept, work,
+        sector_states, slots, r0, r1, r2, x0, g, lcat, rcat,
     )
     s = gathered(y, part)
     x, h, s0, c = call(
@@ -357,8 +379,8 @@
     )
     nx = paired(mx)
     (ms,) = call(
-        mix_body, (inner,), [SMEM] + [VMEM] * 4, [scratch], work // 2,
-        couple, s0, s1, s2, lcat,
+        mix_body, (inner,), [VMEM] * 5, [], work // 2,
+        slots, s0, s1, s2, lcat,
     )
     ns = paired(ms)
     (part,) = call(
@@ -367,10 +389,9 @@
     )
     count = chunks * sectors
     parts = lax.all_to_all(jnp.broadcast_to(part[None], (count, 8, LANES)), ("ops", "sec"), 0, 0)
-    single = pltpu.VMEM((1, side, side), F32)
     (u,) = call(
         cross_body, (jax.ShapeDtypeStruct((3, pairs, side, side), F32),), [VMEM] * 7,
-        [single], work, flag, mx, nx, ms, ns, s0, s1,
+        [], work, flag, mx, nx, ms, ns, s0, s1,
     )
     return call(
         functools.partial(last_body, float((sectors * side * side) ** 0.5)),
@@ -378,7 +399,7 @@
             jax.ShapeDtypeStruct((1, side, side), F32),
             jax.ShapeDtypeStruct((pairs, 1, side, side), F32),
         ),
-        [VMEM] * 5, [single], light, parts, c, mx, s0, u,
+        [VMEM] * 5, [], light, parts, c, mx, s0, u,
     )
 
 

time: 99.5 us -> 95.8 us (0.963)
  waiting for transfers between devices: 16.2 us -> 27.7 us
  starting transfers between devices: 32.5 us -> 21.7 us
  blocking collectives: 30.4 us -> 26.7 us
    ppermute x3, waiting for transfers between devices: 0.01 us -> 10.3 us  [other(): return lax.ppermute(value, ('ops', 'sec'), route)]
    ppermute x5, starting transfers between devices: 9.99 us -> 1.08 us  [paired(): return lax.ppermute(value, 'sec', [(i, i ^ 1) for i in range(count)])]
    ppermute x6, starting transfers between devices: 8.55 us -> 3.77 us  [over_sectors(): found.append(lax.ppermute(value, 'sec', [(i, i ^ d) for i in range(count)]))]
    all_to_all x2, blocking collectives: 30.4 us -> 26.7 us  [exchange(): return lax.all_to_all(value, 'ops', 0, 0)]
    all_to_all x2, waiting for transfers between devices: 6.5 us -> 9.64 us  [exchange(): return lax.all_to_all(value, 'ops', 0, 0)]
    ppermute x3, starting transfers between devices: 2.03 us -> 4.55 us  [other(): return lax.ppermute(value, ('ops', 'sec'), route)]
    ppermute x5, waiting for transfers between devices: 2.42 us -> 0.01 us  [paired(): return lax.ppermute(value, 'sec', [(i, i ^ 1) for i in range(count)])]
    unnamed x20 -> x18, local copies, waits for them, and re-layouts: 6.26 us -> 6.26 us
  transfers between devices with their start and end apart: 17 -> 17, of which waited for: 8 -> 9; matrix products, arithmetic and copies ran while one was open for 1% -> 1% of each run, Pallas kernels for 4% -> 4%
where the time goes in v5:
time: 95.8 us; the launch traced here: 95.1 us
  waiting for transfers between devices  27.7 us (29%)
  blocking collectives  26.7 us (28%)
  starting transfers between devices  21.7 us (23%)
  Pallas kernels  9.88 us (10%)
  local copies, waits for them, and re-layouts  6.93 us (7%)
  between operations  2.12 us (2%)
    all_to_all x2, blocking collectives, exchange(): return lax.all_to_all(value, 'ops', 0, 0)  26.7 us
    ppermute x3, waiting for transfers between devices, other(): return lax.ppermute(value, ('ops', 'sec'), route)  10.3 us
    pallas_call x13, Pallas kernels, call(): pl.pallas_call(body, out_shape=tuple(outs), in_specs=in_specs, out_specs=...  9.88 us
    all_to_all x2, starting transfers between devices, exchange(): return lax.all_to_all(value, 'ops', 0, 0)  9.72 us
    all_to_all x2, waiting for transfers between devices, exchange(): return lax.all_to_all(value, 'ops', 0, 0)  9.64 us
    unnamed x18, local copies, waits for them, and re-layouts  6.26 us
    ppermute x3, starting transfers between devices, other(): return lax.ppermute(value, ('ops', 'sec'), route)  4.55 us
    all_to_all x1, waiting for transfers between devices, local(): lax.all_to_all(jnp.broadcast_to(part[None], (count, 8, LANES)), ('ops', '...  4.09 us
  transfers between devices with their start and end apart: 17, of which 9 were waited for; matrix products, arithmetic and copies ran while one was open for 1% of the time, Pallas kernels for 4%

profile of v5, /device:TPU:0, one launch (start us, length us, event | category | flops | bytes accessed | tf_op | source)
XLA Modules:
  0.0 95.1 jit_solution(13866776902905281884)
XLA Ops:
  1.3 0.9 copy-done.7
  2.2 3.0 %collective-permute-start.1 = (f32[8,64,128]{2,1,0:T(8,128)S(1)}, f32[8,64,128]{2,1,0:T(8,128)S(1)}, u32[]{:S(2)}, u32[]{:S(2)}) collective-permute-start(f32[8,64,128]{2,1,0:T(8,128)S(1)} %shard_map.87.x0.x_ref), channel_id=1, source_target_pairs={{1,2},{2,1},{0,4},{3,7},{5,6},{6,5},{4,0},{7,3},{9,10},{10,9},{8,1... | collective-permute-start | bytes 786440 | tf_op jit(solution)/shard_map/ppermute | solution.py:306
  5.3 0.1 collective-permute-start
  6.0 0.0 copy-start
  6.1 1.0 %copy-done = f32[2,1,256,256]{3,2,1,0:T(8,128)S(1)} copy-done((f32[2,1,256,256]{3,2,1,0:T(8,128)S(1)}, f32[2,1,256,256]{3,2,1,0:T(8,128)}, u32[]{:S(2)}) %copy-start) | copy-done | bytes 524312
  7.1 1.0 %copy-done.1 = f32[2,1,256,256]{3,2,1,0:T(8,128)S(1)} copy-done((f32[2,1,256,256]{3,2,1,0:T(8,128)S(1)}, f32[2,1,256,256]{3,2,1,0:T(8,128)}, u32[]{:S(2)}) %copy-start.1) | copy-done | bytes 524312
  8.1 0.7 copy-done.8
  8.8 0.8 shard_map.86
  9.6 0.0 copy-start.2
  9.7 1.9 %shard_map.88 = (f32[8,64,128]{2,1,0:T(8,128)}, f32[2,256,256]{2,1,0:T(8,128)S(1)}, f32[8,128]{1,0:T(8,128)S(1)}) custom-call(s32[1]{0:T(128)S(6)} %copy.9.size_ref, f32[2,8,128]{2,1,0:T(8,128)S(1)} %get-tuple-element.18.slot_ref, f32[8,64,128]{2,1,0:T(8,128)S(1)} %shard_map.87.x0.x_ref, f32[8,64,128]{2,1,0:T(8,128)S(1)} %collective-permute-done.x1, ...), custom_call_target="tpu_custom_call" | custom-call | flops 402653184 | bytes 2633732 | tf_op jit(solution)/shard_map/pallas_call | solution.py:22
  11.6 6.3 %all-to-all-start = ((f32[8,64,128]{2,1,0:T(8,128)}), f32[8,64,128]{2,1,0:T(8,128)S(1)}, u32[]{:S(2)}, u32[]{:S(2)}) async-start(f32[8,64,128]{2,1,0:T(8,128)} %get-tuple-element.21), calls=%async_computation | async-start | bytes 524288 | tf_op jit(solution)/shard_map/all_to_all | solution.py:318
  17.9 1.0 %collective-permute-start.3 = (f32[8,128]{1,0:T(8,128)S(1)}, f32[8,128]{1,0:T(8,128)S(1)}, u32[]{:S(2)}, u32[]{:S(2)}) collective-permute-start(f32[8,128]{1,0:T(8,128)S(1)} %get-tuple-element.22.mine), channel_id=1, source_target_pairs={{0,2},{1,3},{2,0},{3,1},{4,6},{5,7},{6,4},{7,5},{8,10},{9,11},{10,... | collective-permute-start | bytes 12296 | tf_op jit(solution)/shard_map/ppermute | solution.py:313
  18.9 0.8 collective-permute-start.2
  19.8 1.2 %collective-permute-done.4.refs_2_ = f32[8,128]{1,0:T(8,128)S(1)} collective-permute-done((f32[8,128]{1,0:T(8,128)S(1)}, f32[8,128]{1,0:T(8,128)S(1)}, u32[]{:S(2)}, u32[]{:S(2)}) %collective-permute-start.4) | collective-permute-done | bytes 4128 | tf_op jit(solution)/shard_map/ppermute | solution.py:313
  20.9 0.7 collective-permute-done.3.refs_1_
  21.6 5.0 %all-to-all-done.terms_ref = f32[8,64,128]{2,1,0:T(8,128)S(1)} async-done(((f32[8,64,128]{2,1,0:T(8,128)}), f32[8,64,128]{2,1,0:T(8,128)S(1)}, u32[]{:S(2)}, u32[]{:S(2)}) %all-to-all-start) | async-done | bytes 262176 | tf_op jit(solution)/shard_map/all_to_all | solution.py:318
  26.6 13.4 %all_to_all.25.g_ref.g0 = f32[8,72,128]{2,1,0:T(8,128)S(1)} all-to-all(f32[8,72,128]{2,1,0:T(8,128)S(1)} %shard_map.89), channel_id=1, replica_groups=mesh['ops'=8,'sec'=4] {'ops'}, dimensions={0} | all-to-all | bytes 589824 | tf_op jit(solution)/shard_map/all_to_all | solution.py:318
  40.1 0.2 shard_map.90
  40.3 0.8 collective-permute-start.6
  41.1 0.3 collective-permute-start.5
  41.4 5.4 %collective-permute-done.6.r2 = f32[8,64,128]{2,1,0:T(8,128)S(1)} collective-permute-done((f32[8,64,128]{2,1,0:T(8,128)S(1)}, f32[8,64,128]{2,1,0:T(8,128)S(1)}, u32[]{:S(2)}, u32[]{:S(2)}) %collective-permute-start.6) | collective-permute-done | bytes 262176 | tf_op jit(solution)/shard_map/ppermute | solution.py:306
  46.7 2.0 %shard_map.91 = (f32[8,64,128]{2,1,0:T(8,128)}, f32[2,256,256]{2,1,0:T(8,128)S(1)}, f32[8,128]{1,0:T(8,128)S(1)}) custom-call(s32[1]{0:T(128)S(6)} %copy.9.size_ref, f32[2,8,128]{2,1,0:T(8,128)S(1)} %get-tuple-element.18.slot_ref, f32[8,64,128]{2,1,0:T(8,128)S(1)} %get-tuple-element.23.r0.r_in, f32[8,64,128]{2,1,0:T(8,128)S(1)} %collective-permute-done.5.r1, ...), custom_call_target="tpu_custom_call" | custom-call | flops 402653184 | bytes 3190788 | tf_op jit(solution)/shard_map/pallas_call | solution.py:22
  48.7 0.0 copy-start.3
  48.7 0.8 copy-done.3
  49.5 3.4 %all-to-all-start.2 = ((f32[8,64,128]{2,1,0:T(8,128)}), f32[8,64,128]{2,1,0:T(8,128)S(1)}, u32[]{:S(2)}, u32[]{:S(2)}) async-start(f32[8,64,128]{2,1,0:T(8,128)} %get-tuple-element.24), calls=%async_computation.2 | async-start | bytes 524288 | tf_op jit(solution)/shard_map/all_to_all | solution.py:318
  52.9 0.1 collective-permute-start.9
  53.0 0.6 collective-permute-start.8
  53.6 1.3 %collective-permute-start.7 = (f32[8,128]{1,0:T(8,128)S(1)}, f32[8,128]{1,0:T(8,128)S(1)}, u32[]{:S(2)}, u32[]{:S(2)}) collective-permute-start(f32[8,128]{1,0:T(8,128)S(1)} %get-tuple-element.25.mine), channel_id=1, source_target_pairs={{0,1},{1,0},{2,3},{3,2},{4,5},{5,4},{6,7},{7,6},{8,9},{9,8},{10,11... | collective-permute-start | bytes 12296 | tf_op jit(solution)/shard_map/ppermute | solution.py:313
  54.9 1.2 %collective-permute-done.9.refs_2_ = f32[8,128]{1,0:T(8,128)S(1)} collective-permute-done((f32[8,128]{1,0:T(8,128)S(1)}, f32[8,128]{1,0:T(8,128)S(1)}, u32[]{:S(2)}, u32[]{:S(2)}) %collective-permute-start.9) | collective-permute-done | bytes 4128 | tf_op jit(solution)/shard_map/ppermute | solution.py:313
  56.0 0.7 collective-permute-done.8.refs_1_
  56.7 4.7 %all-to-all-done.2.terms_ref = f32[8,64,128]{2,1,0:T(8,128)S(1)} async-done(((f32[8,64,128]{2,1,0:T(8,128)}), f32[8,64,128]{2,1,0:T(8,128)S(1)}, u32[]{:S(2)}, u32[]{:S(2)}) %all-to-all-start.2) | async-done | bytes 262176 | tf_op jit(solution)/shard_map/all_to_all | solution.py:318
  61.4 13.3 %all_to_all.26.s_ref = f32[8,72,128]{2,1,0:T(8,128)S(1)} all-to-all(f32[8,72,128]{2,1,0:T(8,128)S(1)} %shard_map.92), channel_id=1, replica_groups=mesh['ops'=8,'sec'=4] {'ops'}, dimensions={0} | all-to-all | bytes 589824 | tf_op jit(solution)/shard_map/all_to_all | solution.py:318
  74.7 0.4 shard_map.93
  75.1 0.8 collective-permute-start.11
  75.8 0.2 shard_map.96.b_ref
  76.0 0.6 collective-permute-start.12
  76.6 4.9 %collective-permute-done.11.r2 = f32[8,64,128]{2,1,0:T(8,128)S(1)} collective-permute-done((f32[8,64,128]{2,1,0:T(8,128)S(1)}, f32[8,64,128]{2,1,0:T(8,128)S(1)}, u32[]{:S(2)}, u32[]{:S(2)}) %collective-permute-start.11) | collective-permute-done | bytes 262176 | tf_op jit(solution)/shard_map/ppermute | solution.py:306
  81.5 0.4 shard_map.94.m_ref
  81.9 0.1 collective-permute-start.13
  82.0 0.4 shard_map.95
  82.4 0.7 broadcast_in_dim.2
  83.1 2.6 %all-to-all-start.4 = ((f32[32,8,128]{2,1,0:T(8,128)}), f32[32,8,128]{2,1,0:T(8,128)S(1)}, u32[]{:S(2)}, u32[]{:S(2)}) async-start(f32[32,8,128]{2,1,0:T(8,128)} %broadcast_in_dim.2), calls=%async_computation.4 | async-start | bytes 262144 | tf_op jit(solution)/shard_map/all_to_all | solution.py:391
  85.7 0.0 copy-start.5
  85.7 0.8 copy-done.5
  86.5 1.0 %copy-done.6 = f32[2,256,256]{2,1,0:T(8,128)S(1)} copy-done((f32[2,256,256]{2,1,0:T(8,128)S(1)}, f32[2,256,256]{2,1,0:T(8,128)}, u32[]{:S(2)}) %copy-start.6) | copy-done | bytes 524312
  87.5 2.3 %shard_map.97.u_ref = f32[3,2,256,256]{3,2,1,0:T(8,128)S(1)} custom-call(f32[8,128]{1,0:T(8,128)S(1)} %get-tuple-element.33.flag_ref, f32[3,256,256]{2,1,0:T(8,128)S(1)} %shard_map.96.b_ref, f32[3,256,256]{2,1,0:T(8,128)} %collective-permute-done.12.n_ref, f32[2,256,256]{2,1,0:T(8,128)S(1)} %shard_map.94.m_ref, f32[2,256,256]{2,1,0:T(8,128)S(1)} %copy-done.6, ...), custom_call_target="tpu_custom_call" | custom-call | flops 402653184 | bytes 4722688 | tf_op jit(solution)/shard_map/pallas_call | solution.py:22
  89.8 4.1 %all-to-all-done.4.parts_ref = f32[32,8,128]{2,1,0:T(8,128)S(1)} async-done(((f32[32,8,128]{2,1,0:T(8,128)}), f32[32,8,128]{2,1,0:T(8,128)S(1)}, u32[]{:S(2)}, u32[]{:S(2)}) %all-to-all-start.4) | async-done | bytes 131104 | tf_op jit(solution)/shard_map/all_to_all | solution.py:391
  93.9 1.2 %shard_map.98 = (f32[1,256,256]{2,1,0:T(8,128)}, f32[2,1,256,256]{3,2,1,0:T(8,128)}) custom-call(f32[32,8,128]{2,1,0:T(8,128)S(1)} %all-to-all-done.4.parts_ref, f32[8,128]{1,0:T(8,128)S(1)} %get-tuple-element.30.c_in, f32[3,256,256]{2,1,0:T(8,128)S(1)} %shard_map.96.b_ref, f32[8,64,128]{2,1,0:T(8,128)S(1)} %get-tuple-element.27.r0.s0, ...), custom_call_target="tpu_custom_call" | custom-call | flops 1310720 | bytes 3543040 | tf_op jit(solution)/shard_map/pallas_call | solution.py:22
  (20 shorter events, 0.1 us)
Async XLA Ops:
  1.3 0.9 copy-start.7
  2.2 7.4 %collective-permute-start.1 = (f32[8,64,128]{2,1,0:T(8,128)S(1)}, f32[8,64,128]{2,1,0:T(8,128)S(1)}, u32[]{:S(2)}, u32[]{:S(2)}) collective-permute-start(f32[8,64,128]{2,1,0:T(8,128)S(1)} %shard_map.87.x0.x_ref), channel_id=1, source_target_pairs={{1,2},{2,1},{0,4},{3,7},{5,6},{6,5},{4,0},{7,3},{9,10},{10,9},{8,1... | collective-permute-start | bytes 786440 | tf_op jit(solution)/shard_map/ppermute | solution.py:306
  5.3 4.4 %collective-permute-start = (f32[8,64,128]{2,1,0:T(8,128)S(1)}, f32[8,64,128]{2,1,0:T(8,128)S(1)}, u32[]{:S(2)}, u32[]{:S(2)}) collective-permute-start(f32[8,64,128]{2,1,0:T(8,128)S(1)} %shard_map.87.x0.x_ref), channel_id=1, source_target_pairs={{0,1},{1,0},{2,3},{3,2},{4,5},{5,4},{6,7},{7,6},{8,9},{9,8},{10,11... | collective-permute-start | bytes 786440 | tf_op jit(solution)/shard_map/ppermute | solution.py:295
  6.0 1.0 %copy-start = (f32[2,1,256,256]{3,2,1,0:T(8,128)S(1)}, f32[2,1,256,256]{3,2,1,0:T(8,128)}, u32[]{:S(2)}) copy-start(f32[2,1,256,256]{3,2,1,0:T(8,128)} %left_ref.1) | copy-start | bytes 1572868
  7.1 1.0 %copy-start.1 = (f32[2,1,256,256]{3,2,1,0:T(8,128)S(1)}, f32[2,1,256,256]{3,2,1,0:T(8,128)}, u32[]{:S(2)}) copy-start(f32[2,1,256,256]{3,2,1,0:T(8,128)} %right_ref.1) | copy-start | bytes 1572868
  8.1 0.7 copy-start.8
  9.6 30.4 %copy-start.2 = (bf16[1,256,256]{2,1,0:T(8,128)(2,1)S(1)}, bf16[1,256,256]{2,1,0:T(8,128)(2,1)}, u32[]{:S(2)}) copy-start(bf16[1,256,256]{2,1,0:T(8,128)(2,1)} %diag_ref.3) | copy-start | bytes 393220
  11.6 15.0 %all-to-all-start = ((f32[8,64,128]{2,1,0:T(8,128)}), f32[8,64,128]{2,1,0:T(8,128)S(1)}, u32[]{:S(2)}, u32[]{:S(2)}) async-start(f32[8,64,128]{2,1,0:T(8,128)} %get-tuple-element.21), calls=%async_computation | async-start | bytes 524288 | tf_op jit(solution)/shard_map/all_to_all | solution.py:318
  17.9 3.0 %collective-permute-start.4 = (f32[8,128]{1,0:T(8,128)S(1)}, f32[8,128]{1,0:T(8,128)S(1)}, u32[]{:S(2)}, u32[]{:S(2)}) collective-permute-start(f32[8,128]{1,0:T(8,128)S(1)} %get-tuple-element.22.mine), channel_id=1, source_target_pairs={{0,3},{1,2},{2,1},{3,0},{4,7},{5,6},{6,5},{7,4},{8,11},{9,10},{10,... | collective-permute-start | bytes 12296 | tf_op jit(solution)/shard_map/ppermute | solution.py:313
  17.9 3.7 %collective-permute-start.3 = (f32[8,128]{1,0:T(8,128)S(1)}, f32[8,128]{1,0:T(8,128)S(1)}, u32[]{:S(2)}, u32[]{:S(2)}) collective-permute-start(f32[8,128]{1,0:T(8,128)S(1)} %get-tuple-element.22.mine), channel_id=1, source_target_pairs={{0,2},{1,3},{2,0},{3,1},{4,6},{5,7},{6,4},{7,5},{8,10},{9,11},{10,... | collective-permute-start | bytes 12296 | tf_op jit(solution)/shard_map/ppermute | solution.py:313
  18.9 2.7 %collective-permute-start.2 = (f32[8,128]{1,0:T(8,128)S(1)}, f32[8,128]{1,0:T(8,128)S(1)}, u32[]{:S(2)}, u32[]{:S(2)}) collective-permute-start(f32[8,128]{1,0:T(8,128)S(1)} %get-tuple-element.22.mine), channel_id=1, source_target_pairs={{0,1},{1,0},{2,3},{3,2},{4,5},{5,4},{6,7},{7,6},{8,9},{9,8},{10,11... | collective-permute-start | bytes 12296 | tf_op jit(solution)/shard_map/ppermute | solution.py:313
  40.3 6.4 %collective-permute-start.6 = (f32[8,64,128]{2,1,0:T(8,128)S(1)}, f32[8,64,128]{2,1,0:T(8,128)S(1)}, u32[]{:S(2)}, u32[]{:S(2)}) collective-permute-start(f32[8,64,128]{2,1,0:T(8,128)S(1)} %get-tuple-element.23.r0.r_in), channel_id=1, source_target_pairs={{1,2},{2,1},{0,4},{3,7},{5,6},{6,5},{4,0},{7,3},{9,10},{10,9},{8,1... | collective-permute-start | bytes 786440 | tf_op jit(solution)/shard_map/ppermute | solution.py:306
  41.1 5.7 %collective-permute-start.5 = (f32[8,64,128]{2,1,0:T(8,128)S(1)}, f32[8,64,128]{2,1,0:T(8,128)S(1)}, u32[]{:S(2)}, u32[]{:S(2)}) collective-permute-start(f32[8,64,128]{2,1,0:T(8,128)S(1)} %get-tuple-element.23.r0.r_in), channel_id=1, source_target_pairs={{0,1},{1,0},{2,3},{3,2},{4,5},{5,4},{6,7},{7,6},{8,9},{9,8},{10,11... | collective-permute-start | bytes 786440 | tf_op jit(solution)/shard_map/ppermute | solution.py:295
  48.7 0.8 copy-start.3
  49.5 11.8 %all-to-all-start.2 = ((f32[8,64,128]{2,1,0:T(8,128)}), f32[8,64,128]{2,1,0:T(8,128)S(1)}, u32[]{:S(2)}, u32[]{:S(2)}) async-start(f32[8,64,128]{2,1,0:T(8,128)} %get-tuple-element.24), calls=%async_computation.2 | async-start | bytes 524288 | tf_op jit(solution)/shard_map/all_to_all | solution.py:318
  52.9 3.1 %collective-permute-start.9 = (f32[8,128]{1,0:T(8,128)S(1)}, f32[8,128]{1,0:T(8,128)S(1)}, u32[]{:S(2)}, u32[]{:S(2)}) collective-permute-start(f32[8,128]{1,0:T(8,128)S(1)} %get-tuple-element.25.mine), channel_id=1, source_target_pairs={{0,3},{1,2},{2,1},{3,0},{4,7},{5,6},{6,5},{7,4},{8,11},{9,10},{10,... | collective-permute-start | bytes 12296 | tf_op jit(solution)/shard_map/ppermute | solution.py:313
  53.0 3.7 %collective-permute-start.8 = (f32[8,128]{1,0:T(8,128)S(1)}, f32[8,128]{1,0:T(8,128)S(1)}, u32[]{:S(2)}, u32[]{:S(2)}) collective-permute-start(f32[8,128]{1,0:T(8,128)S(1)} %get-tuple-element.25.mine), channel_id=1, source_target_pairs={{0,2},{1,3},{2,0},{3,1},{4,6},{5,7},{6,4},{7,5},{8,10},{9,11},{10,... | collective-permute-start | bytes 12296 | tf_op jit(solution)/shard_map/ppermute | solution.py:313
  53.6 3.1 %collective-permute-start.7 = (f32[8,128]{1,0:T(8,128)S(1)}, f32[8,128]{1,0:T(8,128)S(1)}, u32[]{:S(2)}, u32[]{:S(2)}) collective-permute-start(f32[8,128]{1,0:T(8,128)S(1)} %get-tuple-element.25.mine), channel_id=1, source_target_pairs={{0,1},{1,0},{2,3},{3,2},{4,5},{5,4},{6,7},{7,6},{8,9},{9,8},{10,11... | collective-permute-start | bytes 12296 | tf_op jit(solution)/shard_map/ppermute | solution.py:313
  61.3 14.5 %copy-start.4 = (f32[2,256,256]{2,1,0:T(8,128)S(1)}, f32[2,256,256]{2,1,0:T(8,128)}, u32[]{:S(2)}) copy-start(f32[2,256,256]{2,1,0:T(8,128)} %copy-done.3) | copy-start | bytes 1572868
  75.1 6.4 %collective-permute-start.11 = (f32[8,64,128]{2,1,0:T(8,128)S(1)}, f32[8,64,128]{2,1,0:T(8,128)S(1)}, u32[]{:S(2)}, u32[]{:S(2)}) collective-permute-start(f32[8,64,128]{2,1,0:T(8,128)S(1)} %get-tuple-element.27.r0.s0), channel_id=1, source_target_pairs={{1,2},{2,1},{0,4},{3,7},{5,6},{6,5},{4,0},{7,3},{9,10},{10,9},{8,1... | collective-permute-start | bytes 786440 | tf_op jit(solution)/shard_map/ppermute | solution.py:306
  75.8 5.7 %collective-permute-start.10 = (f32[8,64,128]{2,1,0:T(8,128)S(1)}, f32[8,64,128]{2,1,0:T(8,128)S(1)}, u32[]{:S(2)}, u32[]{:S(2)}) collective-permute-start(f32[8,64,128]{2,1,0:T(8,128)S(1)} %get-tuple-element.27.r0.s0), channel_id=1, source_target_pairs={{0,1},{1,0},{2,3},{3,2},{4,5},{5,4},{6,7},{7,6},{8,9},{9,8},{10,11... | collective-permute-start | bytes 786440 | tf_op jit(solution)/shard_map/ppermute | solution.py:295
  76.0 10.5 %collective-permute-start.12 = (f32[3,256,256]{2,1,0:T(8,128)S(1)}, f32[3,256,256]{2,1,0:T(8,128)}, u32[]{:S(2)}, u32[]{:S(2)}) collective-permute-start(f32[3,256,256]{2,1,0:T(8,128)S(1)} %shard_map.96.b_ref), channel_id=1, source_target_pairs={{0,1},{1,0},{2,3},{3,2},{4,5},{5,4},{6,7},{7,6},{8,9},{9,8},{10,11... | collective-permute-start | bytes 2359304 | tf_op jit(solution)/shard_map/ppermute | solution.py:295
  81.9 3.7 %collective-permute-start.13 = (f32[2,256,256]{2,1,0:T(8,128)S(1)}, f32[2,256,256]{2,1,0:T(8,128)S(1)}, u32[]{:S(2)}, u32[]{:S(2)}) collective-permute-start(f32[2,256,256]{2,1,0:T(8,128)S(1)} %shard_map.94.m_ref), channel_id=1, source_target_pairs={{0,1},{1,0},{2,3},{3,2},{4,5},{5,4},{6,7},{7,6},{8,9},{9,8},{10,11... | collective-permute-start | bytes 1572872 | tf_op jit(solution)/shard_map/ppermute | solution.py:295
  83.1 10.8 %all-to-all-start.4 = ((f32[32,8,128]{2,1,0:T(8,128)}), f32[32,8,128]{2,1,0:T(8,128)S(1)}, u32[]{:S(2)}, u32[]{:S(2)}) async-start(f32[32,8,128]{2,1,0:T(8,128)} %broadcast_in_dim.2), calls=%async_computation.4 | async-start | bytes 262144 | tf_op jit(solution)/shard_map/all_to_all | solution.py:391
  85.7 0.8 copy-start.5
  86.5 1.0 %copy-start.6 = (f32[2,256,256]{2,1,0:T(8,128)S(1)}, f32[2,256,256]{2,1,0:T(8,128)}, u32[]{:S(2)}) copy-start(f32[2,256,256]{2,1,0:T(8,128)} %copy-done.5) | copy-start | bytes 1572868

commit v6 on v5

--- a/solution.py
+++ b/solution.py
@@ -12,20 +12,20 @@
 F32 = jnp.float32
 BF16 = jnp.bfloat16
 VMEM = pl.BlockSpec(memory_space=pltpu.VMEM)
-HBM = pl.BlockSpec(memory_space=pltpu.HBM)
+ANY = pl.BlockSpec(memory_space=pl.ANY)
 SMEM = pl.BlockSpec(memory_space=pltpu.SMEM)
 
 
-def call(body, outs, in_specs, scratch, flops, *args):
+def call(body, outs, in_specs, scratch, flops, *args, limit=8):
     size = sum(a.size * a.dtype.itemsize for a in args)
     size += sum(o.size * o.dtype.itemsize for o in outs)
     return pl.pallas_call(
         body,
         out_shape=tuple(outs),
         in_specs=in_specs,
-        out_specs=tuple(HBM if scratch and i == 1 and len(scratch) == 2 else VMEM for i in range(len(outs))),
+        out_specs=tuple(VMEM for _ in outs),
         scratch_shapes=scratch,
-        compiler_params=pltpu.CompilerParams(vmem_limit_bytes=8 * 1024 * 1024),
+        compiler_params=pltpu.CompilerParams(vmem_limit_bytes=int(limit * 1024 * 1024)),
         cost_estimate=pl.CostEstimate(flops=flops, bytes_accessed=size, transcendentals=0),
     )(*args)
 
@@ -128,13 +128,31 @@
     pack(x_ref, (), x_ref.shape, jnp.where(live, psi_ref[0].astype(F32), 0.0))
 
 
+def split_pairs(left_ref, right_ref, lcat_ref, rcat_ref, left, right, sem):
+    pairs = lcat_ref.shape[0]
+    copies = []
+    for p in range(pairs):
+        copies.append(pltpu.make_async_copy(left_ref.at[p, 0], left.at[p], sem.at[2 * p]))
+        copies.append(pltpu.make_async_copy(right_ref.at[p, 0], right.at[p], sem.at[2 * p + 1]))
+    for copy in copies:
+        copy.start()
+    for p in range(pairs):
+        copies[2 * p].wait()
+        lcat_ref[p, 0], lcat_ref[p, 1] = halves(left[p])
+        copies[2 * p + 1].wait()
+        rcat_ref[p, 0], rcat_ref[p, 1] = halves(right[p].T)
+
+
 def split_body(
-    label_ref, couple_ref, left_ref, right_ref, lcat_ref, rcat_ref, flag_ref, slot_ref
+    label_ref, couple_hbm, left_ref, right_ref, lcat_ref, rcat_ref, flag_ref, slot_ref,
+    left, right, sem, couple_ref, mark,
 ):
     here = lax.axis_index("sec")
-    for p in range(left_ref.shape[0]):
-        lcat_ref[p, 0], lcat_ref[p, 1] = halves(left_ref[p, 0])
-        rcat_ref[p, 0], rcat_ref[p, 1] = halves(right_ref[p, 0].T)
+    copy = pltpu.make_async_copy(couple_hbm, couple_ref, mark)
+    copy.start()
+    split_pairs(left_ref, right_ref, lcat_ref, rcat_ref, left, right, sem)
+    copy.wait()
+    for p in range(lcat_ref.shape[0]):
         source = couple_ref[p]
         near = here + 1 - 2 * (here % 2)
         slot = jnp.where(source == here, 0.0, jnp.where(source == near, 1.0, 2.0))
@@ -142,21 +160,13 @@
     flag_ref[...] = jnp.full(flag_ref.shape, jnp.where(label_ref[0] == here, 1.0, 0.0))
 
 
-def mix_all(slot_ref, blocks, lcat_ref):
+def mix_all(slot_ref, blocks, lcat_ref, m_ref):
     mixed = []
     for p in range(lcat_ref.shape[0]):
         high, low = halves(pick(slot_ref[p, 0:1, 0:1][None], blocks))
         mixed.append(three(lcat_ref[p, 0], lcat_ref[p, 1], high, low))
+        m_ref[p] = mixed[p]
     return mixed
-
-
-def save(mixed, room_ref, m_ref, sem):
-    copies = []
-    for p, one in enumerate(mixed):
-        room_ref[p] = one
-        copies.append(pltpu.make_async_copy(room_ref.at[p], m_ref.at[p], sem.at[p]))
-        copies[-1].start()
-    return copies
 
 
 def fold_all(size_ref, mixed, rcat_ref, y_ref):
@@ -165,16 +175,11 @@
     return y_ref[...]
 
 
-def first_body(
-    size_ref, slot_ref, x0, x1, x2, lcat_ref, rcat_ref, y_ref, m_ref, part_ref, room_ref, sem
-):
-    mixed = mix_all(slot_ref, (x0, x1, x2), lcat_ref)
-    copies = save(mixed, room_ref, m_ref, sem)
+def first_body(size_ref, slot_ref, x0, x1, x2, lcat_ref, rcat_ref, y_ref, m_ref, part_ref):
+    mixed = mix_all(slot_ref, (x0, x1, x2), lcat_ref, m_ref)
     y = fold_all(size_ref, mixed, rcat_ref, y_ref)
     x = x0[lax.axis_index("ops")]
     part_ref[...] = tile([rows(x * x), rows(x0[...] * y)])
-    for copy in copies:
-        copy.wait()
 
 
 def five(x0, r0, h0, y):
@@ -184,24 +189,20 @@
 
 
 def second_body(
-    size_ref, slot_ref, r0, r1, r2, x0, g0, lcat_ref, rcat_ref,
-    y_ref, m_ref, part_ref, room_ref, sem,
+    size_ref, slot_ref, r0, r1, r2, x0, g0, lcat_ref, rcat_ref, y_ref, m_ref, part_ref
 ):
-    mixed = mix_all(slot_ref, (r0, r1, r2), lcat_ref)
-    copies = save(mixed, room_ref, m_ref, sem)
+    mixed = mix_all(slot_ref, (r0, r1, r2), lcat_ref, m_ref)
     part_ref[...] = five(x0, r0, g0, fold_all(size_ref, mixed, rcat_ref, y_ref))
-    for copy in copies:
-        copy.wait()
 
 
 def mix_body(slot_ref, r0, r1, r2, lcat_ref, m_ref):
-    for p, one in enumerate(mix_all(slot_ref, (r0, r1, r2), lcat_ref)):
-        m_ref[p] = one
+    mix_all(slot_ref, (r0, r1, r2), lcat_ref, m_ref)
 
 
 def fold_body(size_ref, m_ref, r0, x0, h0, rcat_ref, part_ref, y_ref):
     mixed = [m_ref[p] for p in range(m_ref.shape[0])]
-    part_ref[...] = five(x0, r0, h0, fold_all(size_ref, mixed, rcat_ref, y_ref))
+    part = five(x0, r0, h0, fold_all(size_ref, mixed, rcat_ref, y_ref))
+    part_ref[...] = jnp.broadcast_to(part[None], part_ref.shape)
 
 
 def blend_body(c_in, a_ref, b_ref, x_ref, out_ref):
@@ -329,7 +330,8 @@
     wide = jax.ShapeDtypeStruct((chunks, cw + 8, LANES), F32)
     small = jax.ShapeDtypeStruct((8, LANES), F32)
     inner = jax.ShapeDtypeStruct((pairs, side, side), F32)
-    kept = [pltpu.VMEM(inner.shape, F32), pltpu.SemaphoreType.DMA((pairs,))]
+    pieces = jax.ShapeDtypeStruct((pairs, 2, side, side), BF16)
+    loads = [pltpu.VMEM((pairs, side, side), F32)] * 2 + [pltpu.SemaphoreType.DMA((2 * pairs,))]
     work = 12 * pairs * side**3
     light = 20 * side**2
 
@@ -344,17 +346,13 @@
     (x0,) = call(start_body, (block,), [SMEM, VMEM], [], light, sector_states, psi_guess)
     x2, x1 = other(x0), paired(x0)
     lcat, rcat, flag, slots = call(
-        split_body,
-        (
-            jax.ShapeDtypeStruct((pairs, 2, side, side), BF16),
-            jax.ShapeDtypeStruct((pairs, 2, side, side), BF16),
-            small,
-            jax.ShapeDtypeStruct((pairs, 8, LANES), F32),
-        ),
-        [SMEM] * 2 + [VMEM] * 2, [], light * pairs, new_sector, couple, left_ops, right_ops,
+        split_body, (pieces, pieces, small, jax.ShapeDtypeStruct((pairs, 8, LANES), F32)),
+        [SMEM] + [ANY] * 3,
+        loads + [pltpu.SMEM((pairs,), jnp.int32), pltpu.SemaphoreType.DMA(())],
+        light * pairs, new_sector, couple, left_ops, right_ops, limit=52.5,
     )
     y, mx, part = call(
-        first_body, (block, inner, small), [SMEM] + [VMEM] * 6, kept, work,
+        first_body, (block, inner, small), [SMEM] + [VMEM] * 6, [], work,
         sector_states, slots, x0, x1, x2, lcat, rcat,
     )
     g = gathered(y, part)
@@ -364,7 +362,7 @@
     )
     r2, r1 = other(r0), paired(r0)
     y, mr, part = call(
-        second_body, (block, inner, small), [SMEM] + [VMEM] * 8, kept, work,
+        second_body, (block, inner, small), [SMEM] + [VMEM] * 8, [], work,
         sector_states, slots, r0, r1, r2, x0, g, lcat, rcat,
     )
     s = gathered(y, part)
@@ -383,12 +381,12 @@
         slots, s0, s1, s2, lcat,
     )
     ns = paired(ms)
+    many = jax.ShapeDtypeStruct((chunks * sectors, 8, LANES), F32)
     (part,) = call(
-        fold_body, (small,), [SMEM] + [VMEM] * 5, [pltpu.VMEM(block.shape, F32)], work // 2,
+        fold_body, (many,), [SMEM] + [VMEM] * 5, [pltpu.VMEM(block.shape, F32)], work // 2,
         sector_states, ms, s0, x, h, rcat,
     )
-    count = chunks * sectors
-    parts = lax.all_to_all(jnp.broadcast_to(part[None], (count, 8, LANES)), ("ops", "sec"), 0, 0)
+    parts = lax.all_to_all(part, ("ops", "sec"), 0, 0)
     (u,) = call(
         cross_body, (jax.ShapeDtypeStruct((3, pairs, side, side), F32),), [VMEM] * 7,
         [], work, flag, mx, nx, ms, ns, s0, s1,

time: 95.8 us -> 95.3 us (level)
  local copies, waits for them, and re-layouts: 6.93 us -> 4.18 us
  waiting for transfers between devices: 27.7 us -> 29.2 us
    unnamed x18 -> x14, local copies, waits for them, and re-layouts: 6.26 us -> 4.18 us
    ppermute x3, waiting for transfers between devices: 10.3 us -> 11.8 us  [other(): return lax.ppermute(value, ('ops', 'sec'), route)]
  transfers between devices with their start and end apart: 17 -> 17, of which waited for: 9 -> 10; matrix products, arithmetic and copies ran while one was open for 1% -> 0% of each run, Pallas kernels for 4% -> 6%
where the time goes in v6:
time: 95.3 us; the launch traced here: 94.7 us
  waiting for transfers between devices  29.2 us (31%)
  blocking collectives  26.7 us (28%)
  starting transfers between devices  21.7 us (23%)
  Pallas kernels  10.8 us (11%)
  local copies, waits for them, and re-layouts  4.18 us (4%)
  between operations  2.07 us (2%)
    all_to_all x2, blocking collectives, exchange(): return lax.all_to_all(value, 'ops', 0, 0)  26.7 us
    ppermute x3, waiting for transfers between devices, other(): return lax.ppermute(value, ('ops', 'sec'), route)  11.8 us
    pallas_call x13, Pallas kernels, call(): pl.pallas_call(body, out_shape=tuple(outs), in_specs=in_specs, out_specs=...  10.8 us
    all_to_all x2, starting transfers between devices, exchange(): return lax.all_to_all(value, 'ops', 0, 0)  9.75 us
    all_to_all x2, waiting for transfers between devices, exchange(): return lax.all_to_all(value, 'ops', 0, 0)  9.64 us
    ppermute x3, starting transfers between devices, other(): return lax.ppermute(value, ('ops', 'sec'), route)  4.55 us
    unnamed x14, local copies, waits for them, and re-layouts  4.18 us
    all_to_all x1, waiting for transfers between devices, local(): parts = lax.all_to_all(part, ('ops', 'sec'), 0, 0)  4.09 us
  transfers between devices with their start and end apart: 17, of which 10 were waited for; matrix products, arithmetic and copies ran while one was open for 0% of the time, Pallas kernels for 6%

profile of v6, /device:TPU:0, one launch (start us, length us, event | category | flops | bytes accessed | tf_op | source)
XLA Modules:
  0.0 94.7 jit_solution(18381285788679900249)
XLA Ops:
  1.3 0.9 copy-done.5
  2.2 3.0 %collective-permute-start.1 = (f32[8,64,128]{2,1,0:T(8,128)S(1)}, f32[8,64,128]{2,1,0:T(8,128)S(1)}, u32[]{:S(2)}, u32[]{:S(2)}) collective-permute-start(f32[8,64,128]{2,1,0:T(8,128)S(1)} %shard_map.87.x0.x_ref), channel_id=1, source_target_pairs={{1,2},{2,1},{0,4},{3,7},{5,6},{6,5},{4,0},{7,3},{9,10},{10,9},{8,1... | collective-permute-start | bytes 786440 | tf_op jit(solution)/shard_map/ppermute | solution.py:307
  5.3 0.1 collective-permute-start
  6.0 0.0 copy-start.6
  6.1 0.6 copy-done.6
  6.7 1.4 %shard_map.86 = (bf16[2,2,256,256]{3,2,1,0:T(8,128)(2,1)S(1)}, bf16[2,2,256,256]{3,2,1,0:T(8,128)(2,1)S(1)}, f32[8,128]{1,0:T(8,128)S(1)}, f32[2,8,128]{2,1,0:T(8,128)S(1)}) custom-call(s32[1]{0:T(128)S(6)} %copy.10.label_ref, s32[2]{0:T(128)S(1)} %bitcast.1, f32[2,1,256,256]{3,2,1,0:T(8,128)} %left_ref.1, f32[2,1,256,256]{3,2,1,0:T(8,128)} %right_ref.1), custom_call_target="tpu_custom_call" | custom-call | flops 2621440 | bytes 2109452 | tf_op jit(solution)/shard_map/pallas_call | solution.py:22
  8.1 1.5 %collective-permute-done.1.x2 = f32[8,64,128]{2,1,0:T(8,128)S(1)} collective-permute-done((f32[8,64,128]{2,1,0:T(8,128)S(1)}, f32[8,64,128]{2,1,0:T(8,128)S(1)}, u32[]{:S(2)}, u32[]{:S(2)}) %collective-permute-start.1) | collective-permute-done | bytes 262176 | tf_op jit(solution)/shard_map/ppermute | solution.py:307
  9.6 0.0 collective-permute-done.x1
  9.6 1.8 %shard_map.88 = (f32[8,64,128]{2,1,0:T(8,128)}, f32[2,256,256]{2,1,0:T(8,128)S(1)}, f32[8,128]{1,0:T(8,128)S(1)}) custom-call(s32[1]{0:T(128)S(6)} %copy.9.size_ref, f32[2,8,128]{2,1,0:T(8,128)S(1)} %get-tuple-element.18.slot_ref, f32[8,64,128]{2,1,0:T(8,128)S(1)} %shard_map.87.x0.x_ref, f32[8,64,128]{2,1,0:T(8,128)S(1)} %collective-permute-done.x1, ...), custom_call_target="tpu_custom_call" | custom-call | flops 402653184 | bytes 2633732 | tf_op jit(solution)/shard_map/pallas_call | solution.py:22
  11.4 6.3 %all-to-all-start = ((f32[8,64,128]{2,1,0:T(8,128)}), f32[8,64,128]{2,1,0:T(8,128)S(1)}, u32[]{:S(2)}, u32[]{:S(2)}) async-start(f32[8,64,128]{2,1,0:T(8,128)} %get-tuple-element.21), calls=%async_computation | async-start | bytes 524288 | tf_op jit(solution)/shard_map/all_to_all | solution.py:319
  17.7 0.0 collective-permute-start.4
  17.7 1.0 %collective-permute-start.3 = (f32[8,128]{1,0:T(8,128)S(1)}, f32[8,128]{1,0:T(8,128)S(1)}, u32[]{:S(2)}, u32[]{:S(2)}) collective-permute-start(f32[8,128]{1,0:T(8,128)S(1)} %get-tuple-element.22.mine), channel_id=1, source_target_pairs={{0,2},{1,3},{2,0},{3,1},{4,6},{5,7},{6,4},{7,5},{8,10},{9,11},{10,... | collective-permute-start | bytes 12296 | tf_op jit(solution)/shard_map/ppermute | solution.py:314
  18.7 0.8 collective-permute-start.2
  19.6 1.2 %collective-permute-done.4.refs_2_ = f32[8,128]{1,0:T(8,128)S(1)} collective-permute-done((f32[8,128]{1,0:T(8,128)S(1)}, f32[8,128]{1,0:T(8,128)S(1)}, u32[]{:S(2)}, u32[]{:S(2)}) %collective-permute-start.4) | collective-permute-done | bytes 4128 | tf_op jit(solution)/shard_map/ppermute | solution.py:314
  20.7 0.7 collective-permute-done.3.refs_1_
  21.4 0.0 collective-permute-done.2.refs_0_
  21.4 5.0 %all-to-all-done.terms_ref = f32[8,64,128]{2,1,0:T(8,128)S(1)} async-done(((f32[8,64,128]{2,1,0:T(8,128)}), f32[8,64,128]{2,1,0:T(8,128)S(1)}, u32[]{:S(2)}, u32[]{:S(2)}) %all-to-all-start) | async-done | bytes 262176 | tf_op jit(solution)/shard_map/all_to_all | solution.py:319
  26.4 13.4 %all_to_all.25.g_ref.g0 = f32[8,72,128]{2,1,0:T(8,128)S(1)} all-to-all(f32[8,72,128]{2,1,0:T(8,128)S(1)} %shard_map.89), channel_id=1, replica_groups=mesh['ops'=8,'sec'=4] {'ops'}, dimensions={0} | all-to-all | bytes 589824 | tf_op jit(solution)/shard_map/all_to_all | solution.py:319
  39.9 0.2 shard_map.90
  40.1 0.8 collective-permute-start.6
  40.9 0.3 collective-permute-start.5
  41.2 5.4 %collective-permute-done.6.r2 = f32[8,64,128]{2,1,0:T(8,128)S(1)} collective-permute-done((f32[8,64,128]{2,1,0:T(8,128)S(1)}, f32[8,64,128]{2,1,0:T(8,128)S(1)}, u32[]{:S(2)}, u32[]{:S(2)}) %collective-permute-start.6) | collective-permute-done | bytes 262176 | tf_op jit(solution)/shard_map/ppermute | solution.py:307
  46.5 0.0 collective-permute-done.5.r1
  46.5 1.8 %shard_map.91 = (f32[8,64,128]{2,1,0:T(8,128)}, f32[2,256,256]{2,1,0:T(8,128)S(1)}, f32[8,128]{1,0:T(8,128)S(1)}) custom-call(s32[1]{0:T(128)S(6)} %copy.9.size_ref, f32[2,8,128]{2,1,0:T(8,128)S(1)} %get-tuple-element.18.slot_ref, f32[8,64,128]{2,1,0:T(8,128)S(1)} %get-tuple-element.23.r0.r_in, f32[8,64,128]{2,1,0:T(8,128)S(1)} %collective-permute-done.5.r1, ...), custom_call_target="tpu_custom_call" | custom-call | flops 402653184 | bytes 3190788 | tf_op jit(solution)/shard_map/pallas_call | solution.py:22
  48.3 0.8 copy-done.1
  49.1 3.4 %all-to-all-start.2 = ((f32[8,64,128]{2,1,0:T(8,128)}), f32[8,64,128]{2,1,0:T(8,128)S(1)}, u32[]{:S(2)}, u32[]{:S(2)}) async-start(f32[8,64,128]{2,1,0:T(8,128)} %get-tuple-element.24), calls=%async_computation.2 | async-start | bytes 524288 | tf_op jit(solution)/shard_map/all_to_all | solution.py:319
  52.5 0.1 collective-permute-start.9
  52.6 0.6 collective-permute-start.8
  53.2 1.3 %collective-permute-start.7 = (f32[8,128]{1,0:T(8,128)S(1)}, f32[8,128]{1,0:T(8,128)S(1)}, u32[]{:S(2)}, u32[]{:S(2)}) collective-permute-start(f32[8,128]{1,0:T(8,128)S(1)} %get-tuple-element.25.mine), channel_id=1, source_target_pairs={{0,1},{1,0},{2,3},{3,2},{4,5},{5,4},{6,7},{7,6},{8,9},{9,8},{10,11... | collective-permute-start | bytes 12296 | tf_op jit(solution)/shard_map/ppermute | solution.py:314
  54.5 1.2 %collective-permute-done.9.refs_2_ = f32[8,128]{1,0:T(8,128)S(1)} collective-permute-done((f32[8,128]{1,0:T(8,128)S(1)}, f32[8,128]{1,0:T(8,128)S(1)}, u32[]{:S(2)}, u32[]{:S(2)}) %collective-permute-start.9) | collective-permute-done | bytes 4128 | tf_op jit(solution)/shard_map/ppermute | solution.py:314
  55.6 0.7 collective-permute-done.8.refs_1_
  56.3 4.6 %all-to-all-done.2.terms_ref = f32[8,64,128]{2,1,0:T(8,128)S(1)} async-done(((f32[8,64,128]{2,1,0:T(8,128)}), f32[8,64,128]{2,1,0:T(8,128)S(1)}, u32[]{:S(2)}, u32[]{:S(2)}) %all-to-all-start.2) | async-done | bytes 262176 | tf_op jit(solution)/shard_map/all_to_all | solution.py:319
  61.0 13.3 %all_to_all.26.s_ref = f32[8,72,128]{2,1,0:T(8,128)S(1)} all-to-all(f32[8,72,128]{2,1,0:T(8,128)S(1)} %shard_map.92), channel_id=1, replica_groups=mesh['ops'=8,'sec'=4] {'ops'}, dimensions={0} | all-to-all | bytes 589824 | tf_op jit(solution)/shard_map/all_to_all | solution.py:319
  74.3 0.4 shard_map.93
  74.7 0.8 collective-permute-start.11
  75.4 0.2 shard_map.96.b_ref
  75.6 0.6 collective-permute-start.12
  76.2 4.9 %collective-permute-done.11.r2 = f32[8,64,128]{2,1,0:T(8,128)S(1)} collective-permute-done((f32[8,64,128]{2,1,0:T(8,128)S(1)}, f32[8,64,128]{2,1,0:T(8,128)S(1)}, u32[]{:S(2)}, u32[]{:S(2)}) %collective-permute-start.11) | collective-permute-done | bytes 262176 | tf_op jit(solution)/shard_map/ppermute | solution.py:307
  81.1 0.4 shard_map.94.m_ref
  81.6 0.1 collective-permute-start.13
  81.6 1.1 %shard_map.95 = f32[32,8,128]{2,1,0:T(8,128)} custom-call(s32[1]{0:T(128)S(6)} %copy.9.size_ref, f32[2,256,256]{2,1,0:T(8,128)S(1)} %shard_map.94.m_ref, f32[8,64,128]{2,1,0:T(8,128)S(1)} %get-tuple-element.27.r0.s0, f32[8,64,128]{2,1,0:T(8,128)S(1)} %get-tuple-element.28.x0.x_ref, f32[8,64,128]{2,1,0:T(8,128)S(1)} %get-tuple-element.29.h0, ...), custom_call_target="tpu_custom_call" | custom-call | flops 201326592 | bytes 1966084 | tf_op jit(solution)/shard_map/pallas_call | solution.py:22
  82.7 2.6 %all-to-all-start.4 = ((f32[32,8,128]{2,1,0:T(8,128)}), f32[32,8,128]{2,1,0:T(8,128)S(1)}, u32[]{:S(2)}, u32[]{:S(2)}) async-start(f32[32,8,128]{2,1,0:T(8,128)} %shard_map.95), calls=%async_computation.4 | async-start | bytes 262144 | tf_op jit(solution)/shard_map/all_to_all | solution.py:389
  85.3 0.0 copy-start.3
  85.3 0.8 copy-done.3
  86.1 1.0 %copy-done.4 = f32[2,256,256]{2,1,0:T(8,128)S(1)} copy-done((f32[2,256,256]{2,1,0:T(8,128)S(1)}, f32[2,256,256]{2,1,0:T(8,128)}, u32[]{:S(2)}) %copy-start.4) | copy-done | bytes 524312
  87.1 2.3 %shard_map.97.u_ref = f32[3,2,256,256]{3,2,1,0:T(8,128)S(1)} custom-call(f32[8,128]{1,0:T(8,128)S(1)} %get-tuple-element.33.flag_ref, f32[3,256,256]{2,1,0:T(8,128)S(1)} %shard_map.96.b_ref, f32[3,256,256]{2,1,0:T(8,128)} %collective-permute-done.12.n_ref, f32[2,256,256]{2,1,0:T(8,128)S(1)} %shard_map.94.m_ref, f32[2,256,256]{2,1,0:T(8,128)S(1)} %copy-done.4, ...), custom_call_target="tpu_custom_call" | custom-call | flops 402653184 | bytes 4722688 | tf_op jit(solution)/shard_map/pallas_call | solution.py:22
  89.4 4.1 %all-to-all-done.4.parts_ref = f32[32,8,128]{2,1,0:T(8,128)S(1)} async-done(((f32[32,8,128]{2,1,0:T(8,128)}), f32[32,8,128]{2,1,0:T(8,128)S(1)}, u32[]{:S(2)}, u32[]{:S(2)}) %all-to-all-start.4) | async-done | bytes 131104 | tf_op jit(solution)/shard_map/all_to_all | solution.py:389
  93.5 1.2 %shard_map.98 = (f32[1,256,256]{2,1,0:T(8,128)}, f32[2,1,256,256]{3,2,1,0:T(8,128)}) custom-call(f32[32,8,128]{2,1,0:T(8,128)S(1)} %all-to-all-done.4.parts_ref, f32[8,128]{1,0:T(8,128)S(1)} %get-tuple-element.30.c_in, f32[3,256,256]{2,1,0:T(8,128)S(1)} %shard_map.96.b_ref, f32[8,64,128]{2,1,0:T(8,128)S(1)} %get-tuple-element.27.r0.s0, ...), custom_call_target="tpu_custom_call" | custom-call | flops 1310720 | bytes 3543040 | tf_op jit(solution)/shard_map/pallas_call | solution.py:22
  (15 shorter events, 0.1 us)
Async XLA Ops:
  1.3 0.9 copy-start.5
  2.2 7.4 %collective-permute-start.1 = (f32[8,64,128]{2,1,0:T(8,128)S(1)}, f32[8,64,128]{2,1,0:T(8,128)S(1)}, u32[]{:S(2)}, u32[]{:S(2)}) collective-permute-start(f32[8,64,128]{2,1,0:T(8,128)S(1)} %shard_map.87.x0.x_ref), channel_id=1, source_target_pairs={{1,2},{2,1},{0,4},{3,7},{5,6},{6,5},{4,0},{7,3},{9,10},{10,9},{8,1... | collective-permute-start | bytes 786440 | tf_op jit(solution)/shard_map/ppermute | solution.py:307
  5.3 4.4 %collective-permute-start = (f32[8,64,128]{2,1,0:T(8,128)S(1)}, f32[8,64,128]{2,1,0:T(8,128)S(1)}, u32[]{:S(2)}, u32[]{:S(2)}) collective-permute-start(f32[8,64,128]{2,1,0:T(8,128)S(1)} %shard_map.87.x0.x_ref), channel_id=1, source_target_pairs={{0,1},{1,0},{2,3},{3,2},{4,5},{5,4},{6,7},{7,6},{8,9},{9,8},{10,11... | collective-permute-start | bytes 786440 | tf_op jit(solution)/shard_map/ppermute | solution.py:296
  6.0 0.7 copy-start.6
  9.6 30.3 %copy-start = (bf16[1,256,256]{2,1,0:T(8,128)(2,1)S(1)}, bf16[1,256,256]{2,1,0:T(8,128)(2,1)}, u32[]{:S(2)}) copy-start(bf16[1,256,256]{2,1,0:T(8,128)(2,1)} %diag_ref.3) | copy-start | bytes 393220
  11.4 15.0 %all-to-all-start = ((f32[8,64,128]{2,1,0:T(8,128)}), f32[8,64,128]{2,1,0:T(8,128)S(1)}, u32[]{:S(2)}, u32[]{:S(2)}) async-start(f32[8,64,128]{2,1,0:T(8,128)} %get-tuple-element.21), calls=%async_computation | async-start | bytes 524288 | tf_op jit(solution)/shard_map/all_to_all | solution.py:319
  17.7 3.0 %collective-permute-start.4 = (f32[8,128]{1,0:T(8,128)S(1)}, f32[8,128]{1,0:T(8,128)S(1)}, u32[]{:S(2)}, u32[]{:S(2)}) collective-permute-start(f32[8,128]{1,0:T(8,128)S(1)} %get-tuple-element.22.mine), channel_id=1, source_target_pairs={{0,3},{1,2},{2,1},{3,0},{4,7},{5,6},{6,5},{7,4},{8,11},{9,10},{10,... | collective-permute-start | bytes 12296 | tf_op jit(solution)/shard_map/ppermute | solution.py:314
  17.7 3.7 %collective-permute-start.3 = (f32[8,128]{1,0:T(8,128)S(1)}, f32[8,128]{1,0:T(8,128)S(1)}, u32[]{:S(2)}, u32[]{:S(2)}) collective-permute-start(f32[8,128]{1,0:T(8,128)S(1)} %get-tuple-element.22.mine), channel_id=1, source_target_pairs={{0,2},{1,3},{2,0},{3,1},{4,6},{5,7},{6,4},{7,5},{8,10},{9,11},{10,... | collective-permute-start | bytes 12296 | tf_op jit(solution)/shard_map/ppermute | solution.py:314
  18.7 2.7 %collective-permute-start.2 = (f32[8,128]{1,0:T(8,128)S(1)}, f32[8,128]{1,0:T(8,128)S(1)}, u32[]{:S(2)}, u32[]{:S(2)}) collective-permute-start(f32[8,128]{1,0:T(8,128)S(1)} %get-tuple-element.22.mine), channel_id=1, source_target_pairs={{0,1},{1,0},{2,3},{3,2},{4,5},{5,4},{6,7},{7,6},{8,9},{9,8},{10,11... | collective-permute-start | bytes 12296 | tf_op jit(solution)/shard_map/ppermute | solution.py:314
  40.1 6.4 %collective-permute-start.6 = (f32[8,64,128]{2,1,0:T(8,128)S(1)}, f32[8,64,128]{2,1,0:T(8,128)S(1)}, u32[]{:S(2)}, u32[]{:S(2)}) collective-permute-start(f32[8,64,128]{2,1,0:T(8,128)S(1)} %get-tuple-element.23.r0.r_in), channel_id=1, source_target_pairs={{1,2},{2,1},{0,4},{3,7},{5,6},{6,5},{4,0},{7,3},{9,10},{10,9},{8,1... | collective-permute-start | bytes 786440 | tf_op jit(solution)/shard_map/ppermute | solution.py:307
  40.9 5.7 %collective-permute-start.5 = (f32[8,64,128]{2,1,0:T(8,128)S(1)}, f32[8,64,128]{2,1,0:T(8,128)S(1)}, u32[]{:S(2)}, u32[]{:S(2)}) collective-permute-start(f32[8,64,128]{2,1,0:T(8,128)S(1)} %get-tuple-element.23.r0.r_in), channel_id=1, source_target_pairs={{0,1},{1,0},{2,3},{3,2},{4,5},{5,4},{6,7},{7,6},{8,9},{9,8},{10,11... | collective-permute-start | bytes 786440 | tf_op jit(solution)/shard_map/ppermute | solution.py:296
  48.3 0.8 copy-start.1
  49.1 11.8 %all-to-all-start.2 = ((f32[8,64,128]{2,1,0:T(8,128)}), f32[8,64,128]{2,1,0:T(8,128)S(1)}, u32[]{:S(2)}, u32[]{:S(2)}) async-start(f32[8,64,128]{2,1,0:T(8,128)} %get-tuple-element.24), calls=%async_computation.2 | async-start | bytes 524288 | tf_op jit(solution)/shard_map/all_to_all | solution.py:319
  52.5 3.1 %collective-permute-start.9 = (f32[8,128]{1,0:T(8,128)S(1)}, f32[8,128]{1,0:T(8,128)S(1)}, u32[]{:S(2)}, u32[]{:S(2)}) collective-permute-start(f32[8,128]{1,0:T(8,128)S(1)} %get-tuple-element.25.mine), channel_id=1, source_target_pairs={{0,3},{1,2},{2,1},{3,0},{4,7},{5,6},{6,5},{7,4},{8,11},{9,10},{10,... | collective-permute-start | bytes 12296 | tf_op jit(solution)/shard_map/ppermute | solution.py:314
  52.6 3.7 %collective-permute-start.8 = (f32[8,128]{1,0:T(8,128)S(1)}, f32[8,128]{1,0:T(8,128)S(1)}, u32[]{:S(2)}, u32[]{:S(2)}) collective-permute-start(f32[8,128]{1,0:T(8,128)S(1)} %get-tuple-element.25.mine), channel_id=1, source_target_pairs={{0,2},{1,3},{2,0},{3,1},{4,6},{5,7},{6,4},{7,5},{8,10},{9,11},{10,... | collective-permute-start | bytes 12296 | tf_op jit(solution)/shard_map/ppermute | solution.py:314
  53.2 3.1 %collective-permute-start.7 = (f32[8,128]{1,0:T(8,128)S(1)}, f32[8,128]{1,0:T(8,128)S(1)}, u32[]{:S(2)}, u32[]{:S(2)}) collective-permute-start(f32[8,128]{1,0:T(8,128)S(1)} %get-tuple-element.25.mine), channel_id=1, source_target_pairs={{0,1},{1,0},{2,3},{3,2},{4,5},{5,4},{6,7},{7,6},{8,9},{9,8},{10,11... | collective-permute-start | bytes 12296 | tf_op jit(solution)/shard_map/ppermute | solution.py:314
  61.0 14.5 %copy-start.2 = (f32[2,256,256]{2,1,0:T(8,128)S(1)}, f32[2,256,256]{2,1,0:T(8,128)}, u32[]{:S(2)}) copy-start(f32[2,256,256]{2,1,0:T(8,128)} %copy-done.1) | copy-start | bytes 1572868
  74.7 6.4 %collective-permute-start.11 = (f32[8,64,128]{2,1,0:T(8,128)S(1)}, f32[8,64,128]{2,1,0:T(8,128)S(1)}, u32[]{:S(2)}, u32[]{:S(2)}) collective-permute-start(f32[8,64,128]{2,1,0:T(8,128)S(1)} %get-tuple-element.27.r0.s0), channel_id=1, source_target_pairs={{1,2},{2,1},{0,4},{3,7},{5,6},{6,5},{4,0},{7,3},{9,10},{10,9},{8,1... | collective-permute-start | bytes 786440 | tf_op jit(solution)/shard_map/ppermute | solution.py:307
  75.4 5.7 %collective-permute-start.10 = (f32[8,64,128]{2,1,0:T(8,128)S(1)}, f32[8,64,128]{2,1,0:T(8,128)S(1)}, u32[]{:S(2)}, u32[]{:S(2)}) collective-permute-start(f32[8,64,128]{2,1,0:T(8,128)S(1)} %get-tuple-element.27.r0.s0), channel_id=1, source_target_pairs={{0,1},{1,0},{2,3},{3,2},{4,5},{5,4},{6,7},{7,6},{8,9},{9,8},{10,11... | collective-permute-start | bytes 786440 | tf_op jit(solution)/shard_map/ppermute | solution.py:296
  75.6 10.5 %collective-permute-start.12 = (f32[3,256,256]{2,1,0:T(8,128)S(1)}, f32[3,256,256]{2,1,0:T(8,128)}, u32[]{:S(2)}, u32[]{:S(2)}) collective-permute-start(f32[3,256,256]{2,1,0:T(8,128)S(1)} %shard_map.96.b_ref), channel_id=1, source_target_pairs={{0,1},{1,0},{2,3},{3,2},{4,5},{5,4},{6,7},{7,6},{8,9},{9,8},{10,11... | collective-permute-start | bytes 2359304 | tf_op jit(solution)/shard_map/ppermute | solution.py:296
  81.6 3.7 %collective-permute-start.13 = (f32[2,256,256]{2,1,0:T(8,128)S(1)}, f32[2,256,256]{2,1,0:T(8,128)S(1)}, u32[]{:S(2)}, u32[]{:S(2)}) collective-permute-start(f32[2,256,256]{2,1,0:T(8,128)S(1)} %shard_map.94.m_ref), channel_id=1, source_target_pairs={{0,1},{1,0},{2,3},{3,2},{4,5},{5,4},{6,7},{7,6},{8,9},{9,8},{10,11... | collective-permute-start | bytes 1572872 | tf_op jit(solution)/shard_map/ppermute | solution.py:296
  82.7 10.8 %all-to-all-start.4 = ((f32[32,8,128]{2,1,0:T(8,128)}), f32[32,8,128]{2,1,0:T(8,128)S(1)}, u32[]{:S(2)}, u32[]{:S(2)}) async-start(f32[32,8,128]{2,1,0:T(8,128)} %shard_map.95), calls=%async_computation.4 | async-start | bytes 262144 | tf_op jit(solution)/shard_map/all_to_all | solution.py:389
  85.3 0.8 copy-start.3
  86.1 1.0 %copy-start.4 = (f32[2,256,256]{2,1,0:T(8,128)S(1)}, f32[2,256,256]{2,1,0:T(8,128)}, u32[]{:S(2)}) copy-start(f32[2,256,256]{2,1,0:T(8,128)} %copy-done.3) | copy-start | bytes 1572868

commit v7 on v6

--- a/solution.py
+++ b/solution.py
@@ -227,10 +227,14 @@
         u_ref[2, p] = both[side:, side:]
 
 
-def sum_body(terms_ref, mine, *refs):
+def chunk_body(terms_ref, out_ref):
+    out_ref[...] = jnp.sum(terms_ref[...], axis=0)
+
+
+def fan_body(block_ref, mine, *refs):
     others, out_ref = refs[:-1], refs[-1]
-    cw = terms_ref.shape[1]
-    block = jnp.sum(terms_ref[...], axis=0)
+    cw = block_ref.shape[0]
+    block = block_ref[...]
     scalars = mine[...]
     for one in others:
         scalars = scalars + one[...]
@@ -307,12 +311,27 @@
     return lax.ppermute(value, ("ops", "sec"), route)
 
 
+def last_step(count):
+    step = 1
+    while step * 4 < count:
+        step *= 4
+    return step
+
+
 def over_sectors(value):
     count = lax.axis_size("sec")
-    found = []
-    for d in range(1, count):
-        found.append(lax.ppermute(value, "sec", [(i, i ^ d) for i in range(count)]))
-    return found
+    step = 1
+    while True:
+        last = step == last_step(count)
+        found = []
+        for d in range(1, min(4, count // step)):
+            route = [(i, i ^ (d * step)) for i in range(count)]
+            found.append(lax.ppermute(value, "sec", route))
+        if last:
+            return value, found
+        for one in found:
+            value = value + one
+        step *= 4
 
 
 def exchange(value):
@@ -336,10 +355,13 @@
     light = 20 * side**2
 
     def gathered(y, part):
-        others = over_sectors(part)
+        part, others = over_sectors(part)
+        terms = exchange(y)
+        (one,) = call(
+            chunk_body, (jax.ShapeDtypeStruct((cw, LANES), F32),), [VMEM], [], light, terms
+        )
         (full,) = call(
-            sum_body, (wide,), [VMEM] * (2 + len(others)), [], light,
-            exchange(y), part, *others,
+            fan_body, (wide,), [VMEM] * (2 + len(others)), [], light, one, part, *others
         )
         return exchange(full)
 

time: 95.3 us -> 95.4 us (level)
    all_to_all x2, waiting for transfers between devices: 9.64 us -> 13.3 us  [exchange(): return lax.all_to_all(value, 'ops', 0, 0)]
    ppermute x6, waiting for transfers between devices: 3.67 us -> 0.02 us  [over_sectors(): found.append(lax.ppermute(value, 'sec', route))]
    pallas_call x13 -> x15, Pallas kernels: 10.8 us -> 10.8 us  [call(): pl.pallas_call(body, out_shape=tuple(outs), in_specs=in_specs, out_specs=...]
  transfers between devices with their start and end apart: 17 -> 17, of which waited for: 10 -> 6; matrix products, arithmetic and copies ran while one was open for 0% -> 0% of each run, Pallas kernels for 6% -> 6%
where the time goes in v7:
time: 95.4 us; the launch traced here: 94.8 us
  waiting for transfers between devices  29.2 us (31%)
  blocking collectives  26.7 us (28%)
  starting transfers between devices  21.7 us (23%)
  Pallas kernels  10.8 us (11%)
  local copies, waits for them, and re-layouts  4.18 us (4%)
  between operations  2.13 us (2%)
    all_to_all x2, blocking collectives, exchange(): return lax.all_to_all(value, 'ops', 0, 0)  26.7 us
    all_to_all x2, waiting for transfers between devices, exchange(): return lax.all_to_all(value, 'ops', 0, 0)  13.3 us
    ppermute x3, waiting for transfers between devices, other(): return lax.ppermute(value, ('ops', 'sec'), route)  11.8 us
    pallas_call x15, Pallas kernels, call(): pl.pallas_call(body, out_shape=tuple(outs), in_specs=in_specs, out_specs=...  10.8 us
    all_to_all x2, starting transfers between devices, exchange(): return lax.all_to_all(value, 'ops', 0, 0)  9.75 us
    ppermute x3, starting transfers between devices, other(): return lax.ppermute(value, ('ops', 'sec'), route)  4.55 us
    unnamed x14, local copies, waits for them, and re-layouts  4.18 us
    all_to_all x1, waiting for transfers between devices, local(): parts = lax.all_to_all(part, ('ops', 'sec'), 0, 0)  4.09 us
  transfers between devices with their start and end apart: 17, of which 6 were waited for; matrix products, arithmetic and copies ran while one was open for 0% of the time, Pallas kernels for 6%

profile of v7, /device:TPU:0, one launch (start us, length us, event | category | flops | bytes accessed | tf_op | source)
XLA Modules:
  0.0 94.8 jit_solution(4457353098109562169)
XLA Ops:
  1.3 0.9 copy-done.5
  2.2 3.0 %collective-permute-start.1 = (f32[8,64,128]{2,1,0:T(8,128)S(1)}, f32[8,64,128]{2,1,0:T(8,128)S(1)}, u32[]{:S(2)}, u32[]{:S(2)}) collective-permute-start(f32[8,64,128]{2,1,0:T(8,128)S(1)} %shard_map.87.x0.x_ref), channel_id=1, source_target_pairs={{1,2},{2,1},{0,4},{3,7},{5,6},{6,5},{4,0},{7,3},{9,10},{10,9},{8,1... | collective-permute-start | bytes 786440 | tf_op jit(solution)/shard_map/ppermute | solution.py:311
  5.3 0.1 collective-permute-start
  6.0 0.0 copy-start.6
  6.1 0.6 copy-done.6
  6.7 1.4 %shard_map.86 = (bf16[2,2,256,256]{3,2,1,0:T(8,128)(2,1)S(1)}, bf16[2,2,256,256]{3,2,1,0:T(8,128)(2,1)S(1)}, f32[8,128]{1,0:T(8,128)S(1)}, f32[2,8,128]{2,1,0:T(8,128)S(1)}) custom-call(s32[1]{0:T(128)S(6)} %copy.10.label_ref, s32[2]{0:T(128)S(1)} %bitcast.1, f32[2,1,256,256]{3,2,1,0:T(8,128)} %left_ref.1, f32[2,1,256,256]{3,2,1,0:T(8,128)} %right_ref.1), custom_call_target="tpu_custom_call" | custom-call | flops 2621440 | bytes 2109452 | tf_op jit(solution)/shard_map/pallas_call | solution.py:22
  8.1 1.5 %collective-permute-done.1.x2 = f32[8,64,128]{2,1,0:T(8,128)S(1)} collective-permute-done((f32[8,64,128]{2,1,0:T(8,128)S(1)}, f32[8,64,128]{2,1,0:T(8,128)S(1)}, u32[]{:S(2)}, u32[]{:S(2)}) %collective-permute-start.1) | collective-permute-done | bytes 262176 | tf_op jit(solution)/shard_map/ppermute | solution.py:311
  9.6 0.0 collective-permute-done.x1
  9.6 1.8 %shard_map.88 = (f32[8,64,128]{2,1,0:T(8,128)}, f32[2,256,256]{2,1,0:T(8,128)S(1)}, f32[8,128]{1,0:T(8,128)S(1)}) custom-call(s32[1]{0:T(128)S(6)} %copy.9.size_ref, f32[2,8,128]{2,1,0:T(8,128)S(1)} %get-tuple-element.18.slot_ref, f32[8,64,128]{2,1,0:T(8,128)S(1)} %shard_map.87.x0.x_ref, f32[8,64,128]{2,1,0:T(8,128)S(1)} %collective-permute-done.x1, ...), custom_call_target="tpu_custom_call" | custom-call | flops 402653184 | bytes 2633732 | tf_op jit(solution)/shard_map/pallas_call | solution.py:22
  11.4 6.3 %all-to-all-start = ((f32[8,64,128]{2,1,0:T(8,128)}), f32[8,64,128]{2,1,0:T(8,128)S(1)}, u32[]{:S(2)}, u32[]{:S(2)}) async-start(f32[8,64,128]{2,1,0:T(8,128)} %get-tuple-element.21), calls=%async_computation | async-start | bytes 524288 | tf_op jit(solution)/shard_map/all_to_all | solution.py:338
  17.7 0.0 collective-permute-start.4
  17.7 1.0 %collective-permute-start.3 = (f32[8,128]{1,0:T(8,128)S(1)}, f32[8,128]{1,0:T(8,128)S(1)}, u32[]{:S(2)}, u32[]{:S(2)}) collective-permute-start(f32[8,128]{1,0:T(8,128)S(1)} %get-tuple-element.22.mine), channel_id=1, source_target_pairs={{0,2},{1,3},{2,0},{3,1},{4,6},{5,7},{6,4},{7,5},{8,10},{9,11},{10,... | collective-permute-start | bytes 12296 | tf_op jit(solution)/shard_map/ppermute | solution.py:329
  18.7 0.8 collective-permute-start.2
  19.6 6.8 %all-to-all-done.terms_ref = f32[8,64,128]{2,1,0:T(8,128)S(1)} async-done(((f32[8,64,128]{2,1,0:T(8,128)}), f32[8,64,128]{2,1,0:T(8,128)S(1)}, u32[]{:S(2)}, u32[]{:S(2)}) %all-to-all-start) | async-done | bytes 262176 | tf_op jit(solution)/shard_map/all_to_all | solution.py:338
  26.4 0.0 collective-permute-done.4.refs_2_
  26.5 0.0 collective-permute-done.2.refs_0_
  26.5 13.4 %all_to_all.25.g_ref.g0 = f32[8,72,128]{2,1,0:T(8,128)S(1)} all-to-all(f32[8,72,128]{2,1,0:T(8,128)S(1)} %shard_map.90), channel_id=1, replica_groups=mesh['ops'=8,'sec'=4] {'ops'}, dimensions={0} | all-to-all | bytes 589824 | tf_op jit(solution)/shard_map/all_to_all | solution.py:338
  39.9 0.2 shard_map.91
  40.2 0.8 collective-permute-start.6
  40.9 0.3 collective-permute-start.5
  41.2 5.4 %collective-permute-done.6.r2 = f32[8,64,128]{2,1,0:T(8,128)S(1)} collective-permute-done((f32[8,64,128]{2,1,0:T(8,128)S(1)}, f32[8,64,128]{2,1,0:T(8,128)S(1)}, u32[]{:S(2)}, u32[]{:S(2)}) %collective-permute-start.6) | collective-permute-done | bytes 262176 | tf_op jit(solution)/shard_map/ppermute | solution.py:311
  46.6 1.8 %shard_map.92 = (f32[8,64,128]{2,1,0:T(8,128)}, f32[2,256,256]{2,1,0:T(8,128)S(1)}, f32[8,128]{1,0:T(8,128)S(1)}) custom-call(s32[1]{0:T(128)S(6)} %copy.9.size_ref, f32[2,8,128]{2,1,0:T(8,128)S(1)} %get-tuple-element.18.slot_ref, f32[8,64,128]{2,1,0:T(8,128)S(1)} %get-tuple-element.23.r0.r_in, f32[8,64,128]{2,1,0:T(8,128)S(1)} %collective-permute-done.5.r1, ...), custom_call_target="tpu_custom_call" | custom-call | flops 402653184 | bytes 3190788 | tf_op jit(solution)/shard_map/pallas_call | solution.py:22
  48.4 0.8 copy-done.1
  49.2 3.4 %all-to-all-start.2 = ((f32[8,64,128]{2,1,0:T(8,128)}), f32[8,64,128]{2,1,0:T(8,128)S(1)}, u32[]{:S(2)}, u32[]{:S(2)}) async-start(f32[8,64,128]{2,1,0:T(8,128)} %get-tuple-element.24), calls=%async_computation.2 | async-start | bytes 524288 | tf_op jit(solution)/shard_map/all_to_all | solution.py:338
  52.6 0.1 collective-permute-start.9
  52.7 0.6 collective-permute-start.8
  53.3 1.3 %collective-permute-start.7 = (f32[8,128]{1,0:T(8,128)S(1)}, f32[8,128]{1,0:T(8,128)S(1)}, u32[]{:S(2)}, u32[]{:S(2)}) collective-permute-start(f32[8,128]{1,0:T(8,128)S(1)} %get-tuple-element.25.mine), channel_id=1, source_target_pairs={{0,1},{1,0},{2,3},{3,2},{4,5},{5,4},{6,7},{7,6},{8,9},{9,8},{10,11... | collective-permute-start | bytes 12296 | tf_op jit(solution)/shard_map/ppermute | solution.py:329
  54.5 6.5 %all-to-all-done.2.terms_ref = f32[8,64,128]{2,1,0:T(8,128)S(1)} async-done(((f32[8,64,128]{2,1,0:T(8,128)}), f32[8,64,128]{2,1,0:T(8,128)S(1)}, u32[]{:S(2)}, u32[]{:S(2)}) %all-to-all-start.2) | async-done | bytes 262176 | tf_op jit(solution)/shard_map/all_to_all | solution.py:338
  61.0 0.0 collective-permute-done.8.refs_1_
  61.0 0.0 collective-permute-done.7.refs_0_
  61.1 13.3 %all_to_all.26.s_ref = f32[8,72,128]{2,1,0:T(8,128)S(1)} all-to-all(f32[8,72,128]{2,1,0:T(8,128)S(1)} %shard_map.94), channel_id=1, replica_groups=mesh['ops'=8,'sec'=4] {'ops'}, dimensions={0} | all-to-all | bytes 589824 | tf_op jit(solution)/shard_map/all_to_all | solution.py:338
  74.4 0.4 shard_map.95
  74.8 0.8 collective-permute-start.11
  75.5 0.0 collective-permute-start.10
  75.5 0.2 shard_map.98.b_ref
  75.7 0.6 collective-permute-start.12
  76.3 4.9 %collective-permute-done.11.r2 = f32[8,64,128]{2,1,0:T(8,128)S(1)} collective-permute-done((f32[8,64,128]{2,1,0:T(8,128)S(1)}, f32[8,64,128]{2,1,0:T(8,128)S(1)}, u32[]{:S(2)}, u32[]{:S(2)}) %collective-permute-start.11) | collective-permute-done | bytes 262176 | tf_op jit(solution)/shard_map/ppermute | solution.py:311
  81.2 0.4 shard_map.96.m_ref
  81.7 0.1 collective-permute-start.13
  81.7 1.1 %shard_map.97 = f32[32,8,128]{2,1,0:T(8,128)} custom-call(s32[1]{0:T(128)S(6)} %copy.9.size_ref, f32[2,256,256]{2,1,0:T(8,128)S(1)} %shard_map.96.m_ref, f32[8,64,128]{2,1,0:T(8,128)S(1)} %get-tuple-element.27.r0.s0, f32[8,64,128]{2,1,0:T(8,128)S(1)} %get-tuple-element.28.x0.x_ref, f32[8,64,128]{2,1,0:T(8,128)S(1)} %get-tuple-element.29.h0, ...), custom_call_target="tpu_custom_call" | custom-call | flops 201326592 | bytes 1966084 | tf_op jit(solution)/shard_map/pallas_call | solution.py:22
  82.8 2.6 %all-to-all-start.4 = ((f32[32,8,128]{2,1,0:T(8,128)}), f32[32,8,128]{2,1,0:T(8,128)S(1)}, u32[]{:S(2)}, u32[]{:S(2)}) async-start(f32[32,8,128]{2,1,0:T(8,128)} %shard_map.97), calls=%async_computation.4 | async-start | bytes 262144 | tf_op jit(solution)/shard_map/all_to_all | solution.py:411
  85.4 0.0 collective-permute-done.13.w_ref
  85.4 0.0 copy-start.3
  85.4 0.8 copy-done.3
  86.2 1.0 %copy-done.4 = f32[2,256,256]{2,1,0:T(8,128)S(1)} copy-done((f32[2,256,256]{2,1,0:T(8,128)S(1)}, f32[2,256,256]{2,1,0:T(8,128)}, u32[]{:S(2)}) %copy-start.4) | copy-done | bytes 524312
  87.2 2.3 %shard_map.99.u_ref = f32[3,2,256,256]{3,2,1,0:T(8,128)S(1)} custom-call(f32[8,128]{1,0:T(8,128)S(1)} %get-tuple-element.33.flag_ref, f32[3,256,256]{2,1,0:T(8,128)S(1)} %shard_map.98.b_ref, f32[3,256,256]{2,1,0:T(8,128)} %collective-permute-done.12.n_ref, f32[2,256,256]{2,1,0:T(8,128)S(1)} %shard_map.96.m_ref, f32[2,256,256]{2,1,0:T(8,128)S(1)} %copy-done.4, ...), custom_call_target="tpu_custom_call" | custom-call | flops 402653184 | bytes 4722688 | tf_op jit(solution)/shard_map/pallas_call | solution.py:22
  89.5 4.1 %all-to-all-done.4.parts_ref = f32[32,8,128]{2,1,0:T(8,128)S(1)} async-done(((f32[32,8,128]{2,1,0:T(8,128)}), f32[32,8,128]{2,1,0:T(8,128)S(1)}, u32[]{:S(2)}, u32[]{:S(2)}) %all-to-all-start.4) | async-done | bytes 131104 | tf_op jit(solution)/shard_map/all_to_all | solution.py:411
  93.6 1.2 %shard_map.100 = (f32[1,256,256]{2,1,0:T(8,128)}, f32[2,1,256,256]{3,2,1,0:T(8,128)}) custom-call(f32[32,8,128]{2,1,0:T(8,128)S(1)} %all-to-all-done.4.parts_ref, f32[8,128]{1,0:T(8,128)S(1)} %get-tuple-element.30.c_in, f32[3,256,256]{2,1,0:T(8,128)S(1)} %shard_map.98.b_ref, f32[8,64,128]{2,1,0:T(8,128)S(1)} %get-tuple-element.27.r0.s0, ...), custom_call_target="tpu_custom_call" | custom-call | flops 1310720 | bytes 3543040 | tf_op jit(solution)/shard_map/pallas_call | solution.py:22
  (17 shorter events, 0.1 us)
Async XLA Ops:
  1.3 0.9 copy-start.5
  2.2 7.4 %collective-permute-start.1 = (f32[8,64,128]{2,1,0:T(8,128)S(1)}, f32[8,64,128]{2,1,0:T(8,128)S(1)}, u32[]{:S(2)}, u32[]{:S(2)}) collective-permute-start(f32[8,64,128]{2,1,0:T(8,128)S(1)} %shard_map.87.x0.x_ref), channel_id=1, source_target_pairs={{1,2},{2,1},{0,4},{3,7},{5,6},{6,5},{4,0},{7,3},{9,10},{10,9},{8,1... | collective-permute-start | bytes 786440 | tf_op jit(solution)/shard_map/ppermute | solution.py:311
  5.3 4.4 %collective-permute-start = (f32[8,64,128]{2,1,0:T(8,128)S(1)}, f32[8,64,128]{2,1,0:T(8,128)S(1)}, u32[]{:S(2)}, u32[]{:S(2)}) collective-permute-start(f32[8,64,128]{2,1,0:T(8,128)S(1)} %shard_map.87.x0.x_ref), channel_id=1, source_target_pairs={{0,1},{1,0},{2,3},{3,2},{4,5},{5,4},{6,7},{7,6},{8,9},{9,8},{10,11... | collective-permute-start | bytes 786440 | tf_op jit(solution)/shard_map/ppermute | solution.py:300
  6.0 0.7 copy-start.6
  9.6 30.3 %copy-start = (bf16[1,256,256]{2,1,0:T(8,128)(2,1)S(1)}, bf16[1,256,256]{2,1,0:T(8,128)(2,1)}, u32[]{:S(2)}) copy-start(bf16[1,256,256]{2,1,0:T(8,128)(2,1)} %diag_ref.3) | copy-start | bytes 393220
  11.4 15.0 %all-to-all-start = ((f32[8,64,128]{2,1,0:T(8,128)}), f32[8,64,128]{2,1,0:T(8,128)S(1)}, u32[]{:S(2)}, u32[]{:S(2)}) async-start(f32[8,64,128]{2,1,0:T(8,128)} %get-tuple-element.21), calls=%async_computation | async-start | bytes 524288 | tf_op jit(solution)/shard_map/all_to_all | solution.py:338
  17.7 8.7 %collective-permute-start.4 = (f32[8,128]{1,0:T(8,128)S(1)}, f32[8,128]{1,0:T(8,128)S(1)}, u32[]{:S(2)}, u32[]{:S(2)}) collective-permute-start(f32[8,128]{1,0:T(8,128)S(1)} %get-tuple-element.22.mine), channel_id=1, source_target_pairs={{0,3},{1,2},{2,1},{3,0},{4,7},{5,6},{6,5},{7,4},{8,11},{9,10},{10,... | collective-permute-start | bytes 12296 | tf_op jit(solution)/shard_map/ppermute | solution.py:329
  17.7 8.7 %collective-permute-start.3 = (f32[8,128]{1,0:T(8,128)S(1)}, f32[8,128]{1,0:T(8,128)S(1)}, u32[]{:S(2)}, u32[]{:S(2)}) collective-permute-start(f32[8,128]{1,0:T(8,128)S(1)} %get-tuple-element.22.mine), channel_id=1, source_target_pairs={{0,2},{1,3},{2,0},{3,1},{4,6},{5,7},{6,4},{7,5},{8,10},{9,11},{10,... | collective-permute-start | bytes 12296 | tf_op jit(solution)/shard_map/ppermute | solution.py:329
  18.7 7.7 %collective-permute-start.2 = (f32[8,128]{1,0:T(8,128)S(1)}, f32[8,128]{1,0:T(8,128)S(1)}, u32[]{:S(2)}, u32[]{:S(2)}) collective-permute-start(f32[8,128]{1,0:T(8,128)S(1)} %get-tuple-element.22.mine), channel_id=1, source_target_pairs={{0,1},{1,0},{2,3},{3,2},{4,5},{5,4},{6,7},{7,6},{8,9},{9,8},{10,11... | collective-permute-start | bytes 12296 | tf_op jit(solution)/shard_map/ppermute | solution.py:329
  40.2 6.4 %collective-permute-start.6 = (f32[8,64,128]{2,1,0:T(8,128)S(1)}, f32[8,64,128]{2,1,0:T(8,128)S(1)}, u32[]{:S(2)}, u32[]{:S(2)}) collective-permute-start(f32[8,64,128]{2,1,0:T(8,128)S(1)} %get-tuple-element.23.r0.r_in), channel_id=1, source_target_pairs={{1,2},{2,1},{0,4},{3,7},{5,6},{6,5},{4,0},{7,3},{9,10},{10,9},{8,1... | collective-permute-start | bytes 786440 | tf_op jit(solution)/shard_map/ppermute | solution.py:311
  40.9 5.7 %collective-permute-start.5 = (f32[8,64,128]{2,1,0:T(8,128)S(1)}, f32[8,64,128]{2,1,0:T(8,128)S(1)}, u32[]{:S(2)}, u32[]{:S(2)}) collective-permute-start(f32[8,64,128]{2,1,0:T(8,128)S(1)} %get-tuple-element.23.r0.r_in), channel_id=1, source_target_pairs={{0,1},{1,0},{2,3},{3,2},{4,5},{5,4},{6,7},{7,6},{8,9},{9,8},{10,11... | collective-permute-start | bytes 786440 | tf_op jit(solution)/shard_map/ppermute | solution.py:300
  48.4 0.8 copy-start.1
  49.2 11.8 %all-to-all-start.2 = ((f32[8,64,128]{2,1,0:T(8,128)}), f32[8,64,128]{2,1,0:T(8,128)S(1)}, u32[]{:S(2)}, u32[]{:S(2)}) async-start(f32[8,64,128]{2,1,0:T(8,128)} %get-tuple-element.24), calls=%async_computation.2 | async-start | bytes 524288 | tf_op jit(solution)/shard_map/all_to_all | solution.py:338
  52.6 8.4 %collective-permute-start.9 = (f32[8,128]{1,0:T(8,128)S(1)}, f32[8,128]{1,0:T(8,128)S(1)}, u32[]{:S(2)}, u32[]{:S(2)}) collective-permute-start(f32[8,128]{1,0:T(8,128)S(1)} %get-tuple-element.25.mine), channel_id=1, source_target_pairs={{0,3},{1,2},{2,1},{3,0},{4,7},{5,6},{6,5},{7,4},{8,11},{9,10},{10,... | collective-permute-start | bytes 12296 | tf_op jit(solution)/shard_map/ppermute | solution.py:329
  52.7 8.4 %collective-permute-start.8 = (f32[8,128]{1,0:T(8,128)S(1)}, f32[8,128]{1,0:T(8,128)S(1)}, u32[]{:S(2)}, u32[]{:S(2)}) collective-permute-start(f32[8,128]{1,0:T(8,128)S(1)} %get-tuple-element.25.mine), channel_id=1, source_target_pairs={{0,2},{1,3},{2,0},{3,1},{4,6},{5,7},{6,4},{7,5},{8,10},{9,11},{10,... | collective-permute-start | bytes 12296 | tf_op jit(solution)/shard_map/ppermute | solution.py:329
  53.3 7.8 %collective-permute-start.7 = (f32[8,128]{1,0:T(8,128)S(1)}, f32[8,128]{1,0:T(8,128)S(1)}, u32[]{:S(2)}, u32[]{:S(2)}) collective-permute-start(f32[8,128]{1,0:T(8,128)S(1)} %get-tuple-element.25.mine), channel_id=1, source_target_pairs={{0,1},{1,0},{2,3},{3,2},{4,5},{5,4},{6,7},{7,6},{8,9},{9,8},{10,11... | collective-permute-start | bytes 12296 | tf_op jit(solution)/shard_map/ppermute | solution.py:329
  61.0 14.5 %copy-start.2 = (f32[2,256,256]{2,1,0:T(8,128)S(1)}, f32[2,256,256]{2,1,0:T(8,128)}, u32[]{:S(2)}) copy-start(f32[2,256,256]{2,1,0:T(8,128)} %copy-done.1) | copy-start | bytes 1572868
  74.8 6.4 %collective-permute-start.11 = (f32[8,64,128]{2,1,0:T(8,128)S(1)}, f32[8,64,128]{2,1,0:T(8,128)S(1)}, u32[]{:S(2)}, u32[]{:S(2)}) collective-permute-start(f32[8,64,128]{2,1,0:T(8,128)S(1)} %get-tuple-element.27.r0.s0), channel_id=1, source_target_pairs={{1,2},{2,1},{0,4},{3,7},{5,6},{6,5},{4,0},{7,3},{9,10},{10,9},{8,1... | collective-permute-start | bytes 786440 | tf_op jit(solution)/shard_map/ppermute | solution.py:311
  75.5 5.7 %collective-permute-start.10 = (f32[8,64,128]{2,1,0:T(8,128)S(1)}, f32[8,64,128]{2,1,0:T(8,128)S(1)}, u32[]{:S(2)}, u32[]{:S(2)}) collective-permute-start(f32[8,64,128]{2,1,0:T(8,128)S(1)} %get-tuple-element.27.r0.s0), channel_id=1, source_target_pairs={{0,1},{1,0},{2,3},{3,2},{4,5},{5,4},{6,7},{7,6},{8,9},{9,8},{10,11... | collective-permute-start | bytes 786440 | tf_op jit(solution)/shard_map/ppermute | solution.py:300
  75.7 10.5 %collective-permute-start.12 = (f32[3,256,256]{2,1,0:T(8,128)S(1)}, f32[3,256,256]{2,1,0:T(8,128)}, u32[]{:S(2)}, u32[]{:S(2)}) collective-permute-start(f32[3,256,256]{2,1,0:T(8,128)S(1)} %shard_map.98.b_ref), channel_id=1, source_target_pairs={{0,1},{1,0},{2,3},{3,2},{4,5},{5,4},{6,7},{7,6},{8,9},{9,8},{10,11... | collective-permute-start | bytes 2359304 | tf_op jit(solution)/shard_map/ppermute | solution.py:300
  81.7 3.7 %collective-permute-start.13 = (f32[2,256,256]{2,1,0:T(8,128)S(1)}, f32[2,256,256]{2,1,0:T(8,128)S(1)}, u32[]{:S(2)}, u32[]{:S(2)}) collective-permute-start(f32[2,256,256]{2,1,0:T(8,128)S(1)} %shard_map.96.m_ref), channel_id=1, source_target_pairs={{0,1},{1,0},{2,3},{3,2},{4,5},{5,4},{6,7},{7,6},{8,9},{9,8},{10,11... | collective-permute-start | bytes 1572872 | tf_op jit(solution)/shard_map/ppermute | solution.py:300
  82.8 10.8 %all-to-all-start.4 = ((f32[32,8,128]{2,1,0:T(8,128)}), f32[32,8,128]{2,1,0:T(8,128)S(1)}, u32[]{:S(2)}, u32[]{:S(2)}) async-start(f32[32,8,128]{2,1,0:T(8,128)} %shard_map.97), calls=%async_computation.4 | async-start | bytes 262144 | tf_op jit(solution)/shard_map/all_to_all | solution.py:411
  85.4 0.8 copy-start.3
  86.2 1.0 %copy-start.4 = (f32[2,256,256]{2,1,0:T(8,128)S(1)}, f32[2,256,256]{2,1,0:T(8,128)}, u32[]{:S(2)}) copy-start(f32[2,256,256]{2,1,0:T(8,128)} %copy-done.3) | copy-start | bytes 1572868

commit v8 on v7

--- a/solution.py
+++ b/solution.py
@@ -97,6 +97,15 @@
 def tile(parts):
     parts = parts + [jnp.zeros((8 - len(parts), LANES), F32)]
     return jnp.concatenate(parts, axis=0)
+
+
+def lanes(value, out_ref):
+    place = lax.broadcasted_iota(jnp.int32, (1, LANES), 1)
+    sums = jnp.sum(value, axis=1, keepdims=True)
+    row = jnp.zeros((1, LANES), F32)
+    for k in range(value.shape[0]):
+        row = jnp.where(place == k, sums[k : k + 1], row)
+    out_ref[...] = jnp.broadcast_to(row, out_ref.shape)
 
 
 def half_angle(middle, first, last):
@@ -201,8 +210,7 @@
 
 def fold_body(size_ref, m_ref, r0, x0, h0, rcat_ref, part_ref, y_ref):
     mixed = [m_ref[p] for p in range(m_ref.shape[0])]
-    part = five(x0, r0, h0, fold_all(size_ref, mixed, rcat_ref, y_ref))
-    part_ref[...] = jnp.broadcast_to(part[None], part_ref.shape)
+    lanes(five(x0, r0, h0, fold_all(size_ref, mixed, rcat_ref, y_ref)), part_ref)
 
 
 def blend_body(c_in, a_ref, b_ref, x_ref, out_ref):
@@ -227,14 +235,10 @@
         u_ref[2, p] = both[side:, side:]
 
 
-def chunk_body(terms_ref, out_ref):
-    out_ref[...] = jnp.sum(terms_ref[...], axis=0)
-
-
-def fan_body(block_ref, mine, *refs):
+def sum_body(terms_ref, mine, *refs):
     others, out_ref = refs[:-1], refs[-1]
-    cw = block_ref.shape[0]
-    block = block_ref[...]
+    cw = terms_ref.shape[1]
+    block = jnp.sum(terms_ref[...], axis=0)
     scalars = mine[...]
     for one in others:
         scalars = scalars + one[...]
@@ -284,7 +288,8 @@
 
 def last_body(scale, parts_ref, c_in, b_ref, s0, u_ref, wave_ref, turn_ref):
     pairs, side = u_ref.shape[1:3]
-    xr, rr, rh, xhr, rhr = numbers(parts_ref[...], 5)
+    total = jnp.sum(parts_ref[...], axis=0, keepdims=True)
+    xr, rr, rh, xhr, rhr = [total[:, k : k + 1] for k in range(5)]
     on_x, on_s, _, _ = update(c_in[1:2, 0:1], c_in[0:1, 0:1], xr, rr, rh, xhr, rhr)
     on_x = on_x * scale
     on_s = on_s * scale
@@ -356,12 +361,9 @@
 
     def gathered(y, part):
         part, others = over_sectors(part)
-        terms = exchange(y)
-        (one,) = call(
-            chunk_body, (jax.ShapeDtypeStruct((cw, LANES), F32),), [VMEM], [], light, terms
-        )
         (full,) = call(
-            fan_body, (wide,), [VMEM] * (2 + len(others)), [], light, one, part, *others
+            sum_body, (wide,), [VMEM] * (2 + len(others)), [], light,
+            exchange(y), part, *others,
         )
         return exchange(full)
 
@@ -375,7 +377,7 @@
     )
     y, mx, part = call(
         first_body, (block, inner, small), [SMEM] + [VMEM] * 6, [], work,
-        sector_states, slots, x0, x1, x2, lcat, rcat,
+        sector_states, slots, x0, x1, x2, lcat, rcat, limit=52,
     )
     g = gathered(y, part)
     r0, c = call(
@@ -385,7 +387,7 @@
     r2, r1 = other(r0), paired(r0)
     y, mr, part = call(
         second_body, (block, inner, small), [SMEM] + [VMEM] * 8, [], work,
-        sector_states, slots, r0, r1, r2, x0, g, lcat, rcat,
+        sector_states, slots, r0, r1, r2, x0, g, lcat, rcat, limit=51.5,
     )
     s = gathered(y, part)
     x, h, s0, c = call(
@@ -403,7 +405,7 @@
         slots, s0, s1, s2, lcat,
     )
     ns = paired(ms)
-    many = jax.ShapeDtypeStruct((chunks * sectors, 8, LANES), F32)
+    many = jax.ShapeDtypeStruct((chunks * sectors, LANES), F32)
     (part,) = call(
         fold_body, (many,), [SMEM] + [VMEM] * 5, [pltpu.VMEM(block.shape, F32)], work // 2,
         sector_states, ms, s0, x, h, rcat,

time: 95.4 us -> 95.9 us (level)
  waiting for transfers between devices: 29.2 us -> 26.5 us
  Pallas kernels: 10.8 us -> 13.3 us
  local copies, waits for them, and re-layouts: 4.18 us -> 5.17 us
    all_to_all x2, waiting for transfers between devices: 13.3 us -> 9.64 us  [exchange(): return lax.all_to_all(value, 'ops', 0, 0)]
    ppermute x6, waiting for transfers between devices: 0.02 us -> 3.67 us  [over_sectors(): found.append(lax.ppermute(value, 'sec', route))]
    pallas_call x15 -> x13, Pallas kernels: 10.8 us -> 13.3 us  [call(): pl.pallas_call(body, out_shape=tuple(outs), in_specs=in_specs, out_specs=...]
    ppermute x3, waiting for transfers between devices: 11.8 us -> 10.3 us  [other(): return lax.ppermute(value, ('ops', 'sec'), route)]
    all_to_all x1, waiting for transfers between devices: 4.09 us -> 2.87 us  [local(): parts = lax.all_to_all(part, ('ops', 'sec'), 0, 0)]
    unnamed x14 -> x18, local copies, waits for them, and re-layouts: 4.18 us -> 5.17 us
  transfers between devices with their start and end apart: 17 -> 17, of which waited for: 6 -> 9; matrix products, arithmetic and copies ran while one was open for 0% -> 0% of each run, Pallas kernels for 6% -> 6%
where the time goes in v8:
time: 95.9 us; the launch traced here: 95.3 us
  blocking collectives  26.6 us (28%)
  waiting for transfers between devices  26.5 us (28%)
  starting transfers between devices  21.6 us (23%)
  Pallas kernels  13.3 us (14%)
  local copies, waits for them, and re-layouts  5.17 us (5%)
  between operations  2.1 us (2%)
    all_to_all x2, blocking collectives, exchange(): return lax.all_to_all(value, 'ops', 0, 0)  26.6 us
    pallas_call x13, Pallas kernels, call(): pl.pallas_call(body, out_shape=tuple(outs), in_specs=in_specs, out_specs=...  13.3 us
    ppermute x3, waiting for transfers between devices, other(): return lax.ppermute(value, ('ops', 'sec'), route)  10.3 us
    all_to_all x2, waiting for transfers between devices, exchange(): return lax.all_to_all(value, 'ops', 0, 0)  9.64 us
    all_to_all x2, starting transfers between devices, exchange(): return lax.all_to_all(value, 'ops', 0, 0)  9.64 us
    unnamed x18, local copies, waits for them, and re-layouts  5.17 us
    ppermute x3, starting transfers between devices, other(): return lax.ppermute(value, ('ops', 'sec'), route)  4.55 us
    ppermute x6, starting transfers between devices, over_sectors(): found.append(lax.ppermute(value, 'sec', route))  3.77 us
  transfers between devices with their start and end apart: 17, of which 9 were waited for; matrix products, arithmetic and copies ran while one was open for 0% of the time, Pallas kernels for 6%

profile of v8, /device:TPU:0, one launch (start us, length us, event | category | flops | bytes accessed | tf_op | source)
XLA Modules:
  0.0 95.3 jit_solution(5944896831618813085)
XLA Ops:
  1.3 0.9 copy-done.7
  2.2 3.0 %collective-permute-start.1 = (f32[8,64,128]{2,1,0:T(8,128)S(1)}, f32[8,64,128]{2,1,0:T(8,128)S(1)}, u32[]{:S(2)}, u32[]{:S(2)}) collective-permute-start(f32[8,64,128]{2,1,0:T(8,128)S(1)} %shard_map.87.x0.x_ref), channel_id=1, source_target_pairs={{1,2},{2,1},{0,4},{3,7},{5,6},{6,5},{4,0},{7,3},{9,10},{10,9},{8,1... | collective-permute-start | bytes 786440 | tf_op jit(solution)/shard_map/ppermute | solution.py:316
  5.3 0.1 collective-permute-start
  6.0 0.0 copy-start.8
  6.1 0.6 copy-done.8
  6.7 1.4 %shard_map.86 = (bf16[2,2,256,256]{3,2,1,0:T(8,128)(2,1)S(1)}, bf16[2,2,256,256]{3,2,1,0:T(8,128)(2,1)S(1)}, f32[8,128]{1,0:T(8,128)S(1)}, f32[2,8,128]{2,1,0:T(8,128)S(1)}) custom-call(s32[1]{0:T(128)S(6)} %copy.11.label_ref, s32[2]{0:T(128)S(1)} %bitcast.6, f32[2,1,256,256]{3,2,1,0:T(8,128)} %left_ref.1, f32[2,1,256,256]{3,2,1,0:T(8,128)} %right_ref.1), custom_call_target="tpu_custom_call" | custom-call | flops 2621440 | bytes 2109452 | tf_op jit(solution)/shard_map/pallas_call | solution.py:22
  8.1 0.0 copy-start
  8.1 0.8 copy-done
  8.9 0.8 copy-done.2
  9.7 0.0 collective-permute-done.x1
  9.7 3.0 %shard_map.88 = (f32[8,64,128]{2,1,0:T(8,128)}, f32[2,256,256]{2,1,0:T(8,128)S(1)}, f32[8,128]{1,0:T(8,128)S(1)}) custom-call(s32[1]{0:T(128)S(6)} %copy.10.size_ref, f32[2,8,128]{2,1,0:T(8,128)S(1)} %get-tuple-element.18.slot_ref, f32[8,64,128]{2,1,0:T(8,128)S(1)} %shard_map.87.x0.x_ref, f32[8,64,128]{2,1,0:T(8,128)S(1)} %collective-permute-done.x1, ...), custom_call_target="tpu_custom_call" | custom-call | flops 402653184 | bytes 2633732 | tf_op jit(solution)/shard_map/pallas_call | solution.py:22
  12.7 6.2 %all-to-all-start = ((f32[8,64,128]{2,1,0:T(8,128)}), f32[8,64,128]{2,1,0:T(8,128)S(1)}, u32[]{:S(2)}, u32[]{:S(2)}) async-start(f32[8,64,128]{2,1,0:T(8,128)} %get-tuple-element.21), calls=%async_computation | async-start | bytes 524288 | tf_op jit(solution)/shard_map/all_to_all | solution.py:343
  19.0 1.0 %collective-permute-start.3 = (f32[8,128]{1,0:T(8,128)S(1)}, f32[8,128]{1,0:T(8,128)S(1)}, u32[]{:S(2)}, u32[]{:S(2)}) collective-permute-start(f32[8,128]{1,0:T(8,128)S(1)} %get-tuple-element.22.mine), channel_id=1, source_target_pairs={{0,2},{1,3},{2,0},{3,1},{4,6},{5,7},{6,4},{7,5},{8,10},{9,11},{10,... | collective-permute-start | bytes 12296 | tf_op jit(solution)/shard_map/ppermute | solution.py:334
  20.0 0.8 collective-permute-start.2
  20.8 1.2 %collective-permute-done.4.refs_2_ = f32[8,128]{1,0:T(8,128)S(1)} collective-permute-done((f32[8,128]{1,0:T(8,128)S(1)}, f32[8,128]{1,0:T(8,128)S(1)}, u32[]{:S(2)}, u32[]{:S(2)}) %collective-permute-start.4) | collective-permute-done | bytes 4128 | tf_op jit(solution)/shard_map/ppermute | solution.py:334
  22.0 0.7 collective-permute-done.3.refs_1_
  22.7 0.0 collective-permute-done.2.refs_0_
  22.7 5.0 %all-to-all-done.terms_ref = f32[8,64,128]{2,1,0:T(8,128)S(1)} async-done(((f32[8,64,128]{2,1,0:T(8,128)}), f32[8,64,128]{2,1,0:T(8,128)S(1)}, u32[]{:S(2)}, u32[]{:S(2)}) %all-to-all-start) | async-done | bytes 262176 | tf_op jit(solution)/shard_map/all_to_all | solution.py:343
  27.7 13.4 %all_to_all.31.g_ref.g0 = f32[8,72,128]{2,1,0:T(8,128)S(1)} all-to-all(f32[8,72,128]{2,1,0:T(8,128)S(1)} %shard_map.89), channel_id=1, replica_groups=mesh['ops'=8,'sec'=4] {'ops'}, dimensions={0} | all-to-all | bytes 589824 | tf_op jit(solution)/shard_map/all_to_all | solution.py:343
  41.1 0.2 shard_map.90
  41.3 0.8 collective-permute-start.6
  42.1 0.3 collective-permute-start.5
  42.4 5.4 %collective-permute-done.6.r2 = f32[8,64,128]{2,1,0:T(8,128)S(1)} collective-permute-done((f32[8,64,128]{2,1,0:T(8,128)S(1)}, f32[8,64,128]{2,1,0:T(8,128)S(1)}, u32[]{:S(2)}, u32[]{:S(2)}) %collective-permute-start.6) | collective-permute-done | bytes 262176 | tf_op jit(solution)/shard_map/ppermute | solution.py:316
  47.8 0.0 collective-permute-done.5.r1
  47.8 3.0 %shard_map.91 = (f32[8,64,128]{2,1,0:T(8,128)}, f32[2,256,256]{2,1,0:T(8,128)S(1)}, f32[8,128]{1,0:T(8,128)S(1)}) custom-call(s32[1]{0:T(128)S(6)} %copy.10.size_ref, f32[2,8,128]{2,1,0:T(8,128)S(1)} %get-tuple-element.18.slot_ref, f32[8,64,128]{2,1,0:T(8,128)S(1)} %get-tuple-element.23.r0.r_in, f32[8,64,128]{2,1,0:T(8,128)S(1)} %collective-permute-done.5.r1, ...), custom_call_target="tpu_custom_call" | custom-call | flops 402653184 | bytes 3190788 | tf_op jit(solution)/shard_map/pallas_call | solution.py:22
  50.8 3.4 %all-to-all-start.2 = ((f32[8,64,128]{2,1,0:T(8,128)}), f32[8,64,128]{2,1,0:T(8,128)S(1)}, u32[]{:S(2)}, u32[]{:S(2)}) async-start(f32[8,64,128]{2,1,0:T(8,128)} %get-tuple-element.24), calls=%async_computation.2 | async-start | bytes 524288 | tf_op jit(solution)/shard_map/all_to_all | solution.py:343
  54.2 0.1 collective-permute-start.9
  54.3 0.6 collective-permute-start.8
  54.9 1.3 %collective-permute-start.7 = (f32[8,128]{1,0:T(8,128)S(1)}, f32[8,128]{1,0:T(8,128)S(1)}, u32[]{:S(2)}, u32[]{:S(2)}) collective-permute-start(f32[8,128]{1,0:T(8,128)S(1)} %get-tuple-element.25.mine), channel_id=1, source_target_pairs={{0,1},{1,0},{2,3},{3,2},{4,5},{5,4},{6,7},{7,6},{8,9},{9,8},{10,11... | collective-permute-start | bytes 12296 | tf_op jit(solution)/shard_map/ppermute | solution.py:334
  56.1 1.2 %collective-permute-done.9.refs_2_ = f32[8,128]{1,0:T(8,128)S(1)} collective-permute-done((f32[8,128]{1,0:T(8,128)S(1)}, f32[8,128]{1,0:T(8,128)S(1)}, u32[]{:S(2)}, u32[]{:S(2)}) %collective-permute-start.9) | collective-permute-done | bytes 4128 | tf_op jit(solution)/shard_map/ppermute | solution.py:334
  57.3 0.7 collective-permute-done.8.refs_1_
  57.9 0.0 collective-permute-done.7.refs_0_
  57.9 4.7 %all-to-all-done.2.terms_ref = f32[8,64,128]{2,1,0:T(8,128)S(1)} async-done(((f32[8,64,128]{2,1,0:T(8,128)}), f32[8,64,128]{2,1,0:T(8,128)S(1)}, u32[]{:S(2)}, u32[]{:S(2)}) %all-to-all-start.2) | async-done | bytes 262176 | tf_op jit(solution)/shard_map/all_to_all | solution.py:343
  62.6 13.2 %all_to_all.32.s_ref = f32[8,72,128]{2,1,0:T(8,128)S(1)} all-to-all(f32[8,72,128]{2,1,0:T(8,128)S(1)} %shard_map.92), channel_id=1, replica_groups=mesh['ops'=8,'sec'=4] {'ops'}, dimensions={0} | all-to-all | bytes 589824 | tf_op jit(solution)/shard_map/all_to_all | solution.py:343
  75.8 0.4 shard_map.93
  76.2 0.8 collective-permute-start.11
  77.0 0.2 shard_map.96.b_ref
  77.1 0.6 collective-permute-start.12
  77.7 4.9 %collective-permute-done.11.r2 = f32[8,64,128]{2,1,0:T(8,128)S(1)} collective-permute-done((f32[8,64,128]{2,1,0:T(8,128)S(1)}, f32[8,64,128]{2,1,0:T(8,128)S(1)}, u32[]{:S(2)}, u32[]{:S(2)}) %collective-permute-start.11) | collective-permute-done | bytes 262176 | tf_op jit(solution)/shard_map/ppermute | solution.py:316
  82.6 0.4 shard_map.94.m_ref
  83.1 0.1 collective-permute-start.13
  83.2 1.1 %shard_map.95 = f32[32,128]{1,0:T(8,128)} custom-call(s32[1]{0:T(128)S(6)} %copy.10.size_ref, f32[2,256,256]{2,1,0:T(8,128)S(1)} %shard_map.94.m_ref, f32[8,64,128]{2,1,0:T(8,128)S(1)} %get-tuple-element.27.r0.s0, f32[8,64,128]{2,1,0:T(8,128)S(1)} %get-tuple-element.28.x0.x_ref, f32[8,64,128]{2,1,0:T(8,128)S(1)} %get-tuple-element.29.h0, ...), custom_call_target="tpu_custom_call" | custom-call | flops 201326592 | bytes 1851396 | tf_op jit(solution)/shard_map/pallas_call | solution.py:22
  84.3 2.5 %all-to-all-start.4 = ((f32[32,1,128]{2,1,0:T(1,128)}), f32[32,1,128]{2,1,0:T(1,128)S(1)}, u32[]{:S(2)}, u32[]{:S(2)}) async-start(f32[32,1,128]{2,1,0:T(1,128)} %bitcast.2), calls=%async_computation.4 | async-start | bytes 32768 | tf_op jit(solution)/shard_map/all_to_all | solution.py:413
  86.9 0.9 copy-done.4
  87.8 1.1 %copy-done.5 = f32[3,256,256]{2,1,0:T(8,128)S(1)} copy-done((f32[3,256,256]{2,1,0:T(8,128)S(1)}, f32[3,256,256]{2,1,0:T(8,128)}, u32[]{:S(2)}) %copy-start.5) | copy-done | bytes 786456
  88.9 2.2 %shard_map.97.u_ref = f32[3,2,256,256]{3,2,1,0:T(8,128)S(1)} custom-call(f32[8,128]{1,0:T(8,128)S(1)} %get-tuple-element.33.flag_ref, f32[3,256,256]{2,1,0:T(8,128)S(1)} %shard_map.96.b_ref, f32[3,256,256]{2,1,0:T(8,128)S(1)} %copy-done.5, f32[2,256,256]{2,1,0:T(8,128)S(1)} %shard_map.94.m_ref, f32[2,256,256]{2,1,0:T(8,128)} %collective-permute-done.13.w_ref, ...), custom_call_target="tpu_custom_call" | custom-call | flops 402653184 | bytes 4722688 | tf_op jit(solution)/shard_map/pallas_call | solution.py:22
  91.1 2.9 %all-to-all-done.4 = f32[32,1,128]{2,1,0:T(1,128)S(1)} async-done(((f32[32,1,128]{2,1,0:T(1,128)}), f32[32,1,128]{2,1,0:T(1,128)S(1)}, u32[]{:S(2)}, u32[]{:S(2)}) %all-to-all-start.4) | async-done | bytes 16416 | tf_op jit(solution)/shard_map/all_to_all | solution.py:413
  93.9 1.4 %shard_map.98 = (f32[1,256,256]{2,1,0:T(8,128)}, f32[2,1,256,256]{3,2,1,0:T(8,128)}) custom-call(f32[32,128]{1,0:T(8,128)S(1)} %bitcast.5, f32[8,128]{1,0:T(8,128)S(1)} %get-tuple-element.30.c_in, f32[3,256,256]{2,1,0:T(8,128)S(1)} %shard_map.96.b_ref, f32[8,64,128]{2,1,0:T(8,128)S(1)} %get-tuple-element.27.r0.s0, f32[3,2,256,256]{3,2,1,0:T(8,128)S(1)} %shard_map.97.u_ref), custom_call_target="tpu_custom_call" | custom-call | flops 1310720 | bytes 3428352 | tf_op jit(solution)/shard_map/pallas_call | solution.py:22
  (19 shorter events, 0.1 us)
Async XLA Ops:
  1.3 0.9 copy-start.7
  2.2 7.5 %collective-permute-start.1 = (f32[8,64,128]{2,1,0:T(8,128)S(1)}, f32[8,64,128]{2,1,0:T(8,128)S(1)}, u32[]{:S(2)}, u32[]{:S(2)}) collective-permute-start(f32[8,64,128]{2,1,0:T(8,128)S(1)} %shard_map.87.x0.x_ref), channel_id=1, source_target_pairs={{1,2},{2,1},{0,4},{3,7},{5,6},{6,5},{4,0},{7,3},{9,10},{10,9},{8,1... | collective-permute-start | bytes 786440 | tf_op jit(solution)/shard_map/ppermute | solution.py:316
  5.3 4.5 %collective-permute-start = (f32[8,64,128]{2,1,0:T(8,128)S(1)}, f32[8,64,128]{2,1,0:T(8,128)S(1)}, u32[]{:S(2)}, u32[]{:S(2)}) collective-permute-start(f32[8,64,128]{2,1,0:T(8,128)S(1)} %shard_map.87.x0.x_ref), channel_id=1, source_target_pairs={{0,1},{1,0},{2,3},{3,2},{4,5},{5,4},{6,7},{7,6},{8,9},{9,8},{10,11... | collective-permute-start | bytes 786440 | tf_op jit(solution)/shard_map/ppermute | solution.py:305
  6.0 0.7 copy-start.8
  8.1 0.8 copy-start
  8.9 0.8 copy-start.2
  9.7 31.4 %copy-start.6 = (bf16[1,256,256]{2,1,0:T(8,128)(2,1)S(1)}, bf16[1,256,256]{2,1,0:T(8,128)(2,1)}, u32[]{:S(2)}) copy-start(bf16[1,256,256]{2,1,0:T(8,128)(2,1)} %diag_ref.3) | copy-start | bytes 393220
  12.7 14.9 %all-to-all-start = ((f32[8,64,128]{2,1,0:T(8,128)}), f32[8,64,128]{2,1,0:T(8,128)S(1)}, u32[]{:S(2)}, u32[]{:S(2)}) async-start(f32[8,64,128]{2,1,0:T(8,128)} %get-tuple-element.21), calls=%async_computation | async-start | bytes 524288 | tf_op jit(solution)/shard_map/all_to_all | solution.py:343
  19.0 3.0 %collective-permute-start.4 = (f32[8,128]{1,0:T(8,128)S(1)}, f32[8,128]{1,0:T(8,128)S(1)}, u32[]{:S(2)}, u32[]{:S(2)}) collective-permute-start(f32[8,128]{1,0:T(8,128)S(1)} %get-tuple-element.22.mine), channel_id=1, source_target_pairs={{0,3},{1,2},{2,1},{3,0},{4,7},{5,6},{6,5},{7,4},{8,11},{9,10},{10,... | collective-permute-start | bytes 12296 | tf_op jit(solution)/shard_map/ppermute | solution.py:334
  19.0 3.7 %collective-permute-start.3 = (f32[8,128]{1,0:T(8,128)S(1)}, f32[8,128]{1,0:T(8,128)S(1)}, u32[]{:S(2)}, u32[]{:S(2)}) collective-permute-start(f32[8,128]{1,0:T(8,128)S(1)} %get-tuple-element.22.mine), channel_id=1, source_target_pairs={{0,2},{1,3},{2,0},{3,1},{4,6},{5,7},{6,4},{7,5},{8,10},{9,11},{10,... | collective-permute-start | bytes 12296 | tf_op jit(solution)/shard_map/ppermute | solution.py:334
  20.0 2.7 %collective-permute-start.2 = (f32[8,128]{1,0:T(8,128)S(1)}, f32[8,128]{1,0:T(8,128)S(1)}, u32[]{:S(2)}, u32[]{:S(2)}) collective-permute-start(f32[8,128]{1,0:T(8,128)S(1)} %get-tuple-element.22.mine), channel_id=1, source_target_pairs={{0,1},{1,0},{2,3},{3,2},{4,5},{5,4},{6,7},{7,6},{8,9},{9,8},{10,11... | collective-permute-start | bytes 12296 | tf_op jit(solution)/shard_map/ppermute | solution.py:334
  41.3 6.4 %collective-permute-start.6 = (f32[8,64,128]{2,1,0:T(8,128)S(1)}, f32[8,64,128]{2,1,0:T(8,128)S(1)}, u32[]{:S(2)}, u32[]{:S(2)}) collective-permute-start(f32[8,64,128]{2,1,0:T(8,128)S(1)} %get-tuple-element.23.r0.r_in), channel_id=1, source_target_pairs={{1,2},{2,1},{0,4},{3,7},{5,6},{6,5},{4,0},{7,3},{9,10},{10,9},{8,1... | collective-permute-start | bytes 786440 | tf_op jit(solution)/shard_map/ppermute | solution.py:316
  42.1 5.7 %collective-permute-start.5 = (f32[8,64,128]{2,1,0:T(8,128)S(1)}, f32[8,64,128]{2,1,0:T(8,128)S(1)}, u32[]{:S(2)}, u32[]{:S(2)}) collective-permute-start(f32[8,64,128]{2,1,0:T(8,128)S(1)} %get-tuple-element.23.r0.r_in), channel_id=1, source_target_pairs={{0,1},{1,0},{2,3},{3,2},{4,5},{5,4},{6,7},{7,6},{8,9},{9,8},{10,11... | collective-permute-start | bytes 786440 | tf_op jit(solution)/shard_map/ppermute | solution.py:305
  50.8 11.8 %all-to-all-start.2 = ((f32[8,64,128]{2,1,0:T(8,128)}), f32[8,64,128]{2,1,0:T(8,128)S(1)}, u32[]{:S(2)}, u32[]{:S(2)}) async-start(f32[8,64,128]{2,1,0:T(8,128)} %get-tuple-element.24), calls=%async_computation.2 | async-start | bytes 524288 | tf_op jit(solution)/shard_map/all_to_all | solution.py:343
  54.2 3.1 %collective-permute-start.9 = (f32[8,128]{1,0:T(8,128)S(1)}, f32[8,128]{1,0:T(8,128)S(1)}, u32[]{:S(2)}, u32[]{:S(2)}) collective-permute-start(f32[8,128]{1,0:T(8,128)S(1)} %get-tuple-element.25.mine), channel_id=1, source_target_pairs={{0,3},{1,2},{2,1},{3,0},{4,7},{5,6},{6,5},{7,4},{8,11},{9,10},{10,... | collective-permute-start | bytes 12296 | tf_op jit(solution)/shard_map/ppermute | solution.py:334
  54.3 3.7 %collective-permute-start.8 = (f32[8,128]{1,0:T(8,128)S(1)}, f32[8,128]{1,0:T(8,128)S(1)}, u32[]{:S(2)}, u32[]{:S(2)}) collective-permute-start(f32[8,128]{1,0:T(8,128)S(1)} %get-tuple-element.25.mine), channel_id=1, source_target_pairs={{0,2},{1,3},{2,0},{3,1},{4,6},{5,7},{6,4},{7,5},{8,10},{9,11},{10,... | collective-permute-start | bytes 12296 | tf_op jit(solution)/shard_map/ppermute | solution.py:334
  54.9 3.1 %collective-permute-start.7 = (f32[8,128]{1,0:T(8,128)S(1)}, f32[8,128]{1,0:T(8,128)S(1)}, u32[]{:S(2)}, u32[]{:S(2)}) collective-permute-start(f32[8,128]{1,0:T(8,128)S(1)} %get-tuple-element.25.mine), channel_id=1, source_target_pairs={{0,1},{1,0},{2,3},{3,2},{4,5},{5,4},{6,7},{7,6},{8,9},{9,8},{10,11... | collective-permute-start | bytes 12296 | tf_op jit(solution)/shard_map/ppermute | solution.py:334
  75.8 6.8 %copy-start.1 = (bf16[2,2,256,256]{3,2,1,0:T(8,128)(2,1)S(1)}, bf16[2,2,256,256]{3,2,1,0:T(8,128)(2,1)}, u32[]{:S(2)}) copy-start(bf16[2,2,256,256]{3,2,1,0:T(8,128)(2,1)} %copy-done) | copy-start | bytes 1572868
  76.2 6.4 %collective-permute-start.11 = (f32[8,64,128]{2,1,0:T(8,128)S(1)}, f32[8,64,128]{2,1,0:T(8,128)S(1)}, u32[]{:S(2)}, u32[]{:S(2)}) collective-permute-start(f32[8,64,128]{2,1,0:T(8,128)S(1)} %get-tuple-element.27.r0.s0), channel_id=1, source_target_pairs={{1,2},{2,1},{0,4},{3,7},{5,6},{6,5},{4,0},{7,3},{9,10},{10,9},{8,1... | collective-permute-start | bytes 786440 | tf_op jit(solution)/shard_map/ppermute | solution.py:316
  76.9 5.7 %collective-permute-start.10 = (f32[8,64,128]{2,1,0:T(8,128)S(1)}, f32[8,64,128]{2,1,0:T(8,128)S(1)}, u32[]{:S(2)}, u32[]{:S(2)}) collective-permute-start(f32[8,64,128]{2,1,0:T(8,128)S(1)} %get-tuple-element.27.r0.s0), channel_id=1, source_target_pairs={{0,1},{1,0},{2,3},{3,2},{4,5},{5,4},{6,7},{7,6},{8,9},{9,8},{10,11... | collective-permute-start | bytes 786440 | tf_op jit(solution)/shard_map/ppermute | solution.py:305
  77.0 6.2 %copy-start.3 = (bf16[2,2,256,256]{3,2,1,0:T(8,128)(2,1)S(1)}, bf16[2,2,256,256]{3,2,1,0:T(8,128)(2,1)}, u32[]{:S(2)}) copy-start(bf16[2,2,256,256]{3,2,1,0:T(8,128)(2,1)} %copy-done.2) | copy-start | bytes 1572868
  77.1 9.7 %collective-permute-start.12 = (f32[3,256,256]{2,1,0:T(8,128)S(1)}, f32[3,256,256]{2,1,0:T(8,128)S(1)}, u32[]{:S(2)}, u32[]{:S(2)}) collective-permute-start(f32[3,256,256]{2,1,0:T(8,128)S(1)} %shard_map.96.b_ref), channel_id=1, source_target_pairs={{0,1},{1,0},{2,3},{3,2},{4,5},{5,4},{6,7},{7,6},{8,9},{9,8},{10,11... | collective-permute-start | bytes 2359304 | tf_op jit(solution)/shard_map/ppermute | solution.py:305
  83.1 3.7 %collective-permute-start.13 = (f32[2,256,256]{2,1,0:T(8,128)S(1)}, f32[2,256,256]{2,1,0:T(8,128)}, u32[]{:S(2)}, u32[]{:S(2)}) collective-permute-start(f32[2,256,256]{2,1,0:T(8,128)S(1)} %shard_map.94.m_ref), channel_id=1, source_target_pairs={{0,1},{1,0},{2,3},{3,2},{4,5},{5,4},{6,7},{7,6},{8,9},{9,8},{10,11... | collective-permute-start | bytes 1572872 | tf_op jit(solution)/shard_map/ppermute | solution.py:305
  84.3 9.7 %all-to-all-start.4 = ((f32[32,1,128]{2,1,0:T(1,128)}), f32[32,1,128]{2,1,0:T(1,128)S(1)}, u32[]{:S(2)}, u32[]{:S(2)}) async-start(f32[32,1,128]{2,1,0:T(1,128)} %bitcast.2), calls=%async_computation.4 | async-start | bytes 32768 | tf_op jit(solution)/shard_map/all_to_all | solution.py:413
  86.8 0.9 copy-start.4
  87.8 1.1 %copy-start.5 = (f32[3,256,256]{2,1,0:T(8,128)S(1)}, f32[3,256,256]{2,1,0:T(8,128)}, u32[]{:S(2)}) copy-start(f32[3,256,256]{2,1,0:T(8,128)} %copy-done.4) | copy-start | bytes 2359300

commit v9 on v8

--- a/solution.py
+++ b/solution.py
@@ -16,14 +16,14 @@
 SMEM = pl.BlockSpec(memory_space=pltpu.SMEM)
 
 
-def call(body, outs, in_specs, scratch, flops, *args, limit=8):
+def call(body, outs, in_specs, scratch, flops, *args, limit=8, away=()):
     size = sum(a.size * a.dtype.itemsize for a in args)
     size += sum(o.size * o.dtype.itemsize for o in outs)
     return pl.pallas_call(
         body,
         out_shape=tuple(outs),
         in_specs=in_specs,
-        out_specs=tuple(VMEM for _ in outs),
+        out_specs=tuple(ANY if k in away else VMEM for k in range(len(outs))),
         scratch_shapes=scratch,
         compiler_params=pltpu.CompilerParams(vmem_limit_bytes=int(limit * 1024 * 1024)),
         cost_estimate=pl.CostEstimate(flops=flops, bytes_accessed=size, transcendentals=0),
@@ -181,14 +181,17 @@
 def fold_all(size_ref, mixed, rcat_ref, y_ref):
     y = fold(mixed, rcat_ref)
     pack(y_ref, (), y_ref.shape, jnp.where(mask(size_ref[0], y.shape[0]), y, 0.0))
-    return y_ref[...]
-
-
-def first_body(size_ref, slot_ref, x0, x1, x2, lcat_ref, rcat_ref, y_ref, m_ref, part_ref):
-    mixed = mix_all(slot_ref, (x0, x1, x2), lcat_ref, m_ref)
-    y = fold_all(size_ref, mixed, rcat_ref, y_ref)
+
+
+def first_body(
+    size_ref, slot_ref, x0, x1, x2, lcat_ref, rcat_ref, y_out, m_ref, part_ref, y_ref, sem
+):
+    fold_all(size_ref, mix_all(slot_ref, (x0, x1, x2), lcat_ref, m_ref), rcat_ref, y_ref)
+    copy = pltpu.make_async_copy(y_ref, y_out, sem)
+    copy.start()
     x = x0[lax.axis_index("ops")]
-    part_ref[...] = tile([rows(x * x), rows(x0[...] * y)])
+    part_ref[...] = tile([rows(x * x), rows(x0[...] * y_ref[...])])
+    copy.wait()
 
 
 def five(x0, r0, h0, y):
@@ -198,10 +201,14 @@
 
 
 def second_body(
-    size_ref, slot_ref, r0, r1, r2, x0, g0, lcat_ref, rcat_ref, y_ref, m_ref, part_ref
+    size_ref, slot_ref, r0, r1, r2, x0, g0, lcat_ref, rcat_ref, y_out, m_ref, part_ref,
+    y_ref, sem,
 ):
-    mixed = mix_all(slot_ref, (r0, r1, r2), lcat_ref, m_ref)
-    part_ref[...] = five(x0, r0, g0, fold_all(size_ref, mixed, rcat_ref, y_ref))
+    fold_all(size_ref, mix_all(slot_ref, (r0, r1, r2), lcat_ref, m_ref), rcat_ref, y_ref)
+    copy = pltpu.make_async_copy(y_ref, y_out, sem)
+    copy.start()
+    part_ref[...] = five(x0, r0, g0, y_ref[...])
+    copy.wait()
 
 
 def mix_body(slot_ref, r0, r1, r2, lcat_ref, m_ref):
@@ -210,7 +217,8 @@
 
 def fold_body(size_ref, m_ref, r0, x0, h0, rcat_ref, part_ref, y_ref):
     mixed = [m_ref[p] for p in range(m_ref.shape[0])]
-    lanes(five(x0, r0, h0, fold_all(size_ref, mixed, rcat_ref, y_ref)), part_ref)
+    fold_all(size_ref, mixed, rcat_ref, y_ref)
+    lanes(five(x0, r0, h0, y_ref[...]), part_ref)
 
 
 def blend_body(c_in, a_ref, b_ref, x_ref, out_ref):
@@ -286,18 +294,27 @@
     store(c_ref, [theta, xx, on_x, on_r])
 
 
-def last_body(scale, parts_ref, c_in, b_ref, s0, u_ref, wave_ref, turn_ref):
+def last_body(
+    scale, parts_ref, c_in, b_ref, s0, u_ref, wave_out, turn_out, wave_ref, turn_ref, sem
+):
     pairs, side = u_ref.shape[1:3]
     total = jnp.sum(parts_ref[...], axis=0, keepdims=True)
     xr, rr, rh, xhr, rhr = [total[:, k : k + 1] for k in range(5)]
     on_x, on_s, _, _ = update(c_in[1:2, 0:1], c_in[0:1, 0:1], xr, rr, rh, xhr, rhr)
     on_x = on_x * scale
     on_s = on_s * scale
-    wave_ref[0] = on_x * b_ref[pairs] + unpack(on_s * s0[...])
     root = 1.0 / side**0.5
     xx, xs, ss = on_x * on_x * root, on_x * on_s * root, on_s * on_s * root
+    copies = []
     for p in range(pairs):
-        turn_ref[p, 0] = xx * u_ref[0, p] + xs * u_ref[1, p] + ss * u_ref[2, p]
+        turn_ref[p] = xx * u_ref[0, p] + xs * u_ref[1, p] + ss * u_ref[2, p]
+        copies.append(pltpu.make_async_copy(turn_ref.at[p], turn_out.at[p, 0], sem.at[p]))
+        copies[p].start()
+    wave_ref[...] = on_x * b_ref[pairs] + unpack(on_s * s0[...])
+    copies.append(pltpu.make_async_copy(wave_ref, wave_out.at[0], sem.at[pairs]))
+    copies[pairs].start()
+    for copy in copies:
+        copy.wait()
 
 
 def paired(value):
@@ -354,6 +371,7 @@
     wide = jax.ShapeDtypeStruct((chunks, cw + 8, LANES), F32)
     small = jax.ShapeDtypeStruct((8, LANES), F32)
     inner = jax.ShapeDtypeStruct((pairs, side, side), F32)
+    room = [pltpu.VMEM(block.shape, F32), pltpu.SemaphoreType.DMA(())]
     pieces = jax.ShapeDtypeStruct((pairs, 2, side, side), BF16)
     loads = [pltpu.VMEM((pairs, side, side), F32)] * 2 + [pltpu.SemaphoreType.DMA((2 * pairs,))]
     work = 12 * pairs * side**3
@@ -376,8 +394,8 @@
         light * pairs, new_sector, couple, left_ops, right_ops, limit=52.5,
     )
     y, mx, part = call(
-        first_body, (block, inner, small), [SMEM] + [VMEM] * 6, [], work,
-        sector_states, slots, x0, x1, x2, lcat, rcat, limit=52,
+        first_body, (block, inner, small), [SMEM] + [VMEM] * 6, room, work,
+        sector_states, slots, x0, x1, x2, lcat, rcat, away=(0,),
     )
     g = gathered(y, part)
     r0, c = call(
@@ -386,8 +404,8 @@
     )
     r2, r1 = other(r0), paired(r0)
     y, mr, part = call(
-        second_body, (block, inner, small), [SMEM] + [VMEM] * 8, [], work,
-        sector_states, slots, r0, r1, r2, x0, g, lcat, rcat, limit=51.5,
+        second_body, (block, inner, small), [SMEM] + [VMEM] * 8, room, work,
+        sector_states, slots, r0, r1, r2, x0, g, lcat, rcat, away=(0,),
     )
     s = gathered(y, part)
     x, h, s0, c = call(
@@ -421,7 +439,13 @@
             jax.ShapeDtypeStruct((1, side, side), F32),
             jax.ShapeDtypeStruct((pairs, 1, side, side), F32),
         ),
-        [VMEM] * 5, [], light, parts, c, mx, s0, u,
+        [VMEM] * 5,
+        [
+            pltpu.VMEM((side, side), F32),
+            pltpu.VMEM((pairs, side, side), F32),
+            pltpu.SemaphoreType.DMA((pairs + 1,)),
+        ],
+        light, parts, c, mx, s0, u, away=(0, 1),
     )
 
 

time: 95.9 us -> 94.4 us (0.984)
  Pallas kernels: 13.3 us -> 11 us
  waiting for transfers between devices: 26.5 us -> 28.1 us
  local copies, waits for them, and re-layouts: 5.17 us -> 4.17 us
    pallas_call x13, Pallas kernels: 13.3 us -> 11 us  [call(): pl.pallas_call(body, out_shape=tuple(outs), in_specs=in_specs, out_specs=...]
    ppermute x3, waiting for transfers between devices: 10.3 us -> 11.8 us  [other(): return lax.ppermute(value, ('ops', 'sec'), route)]
    unnamed x18 -> x14, local copies, waits for them, and re-layouts: 5.17 us -> 4.17 us
  transfers between devices with their start and end apart: 17 -> 17, of which waited for: 9 -> 10; matrix products, arithmetic and copies ran while one was open for 0% -> 0% of each run, Pallas kernels for 6% -> 6%
where the time goes in v9:
time: 94.4 us; the launch traced here: 93.8 us
  waiting for transfers between devices  28.1 us (30%)
  blocking collectives  26.7 us (28%)
  starting transfers between devices  21.7 us (23%)
  Pallas kernels  11 us (12%)
  local copies, waits for them, and re-layouts  4.17 us (4%)
  between operations  2.09 us (2%)
    all_to_all x2, blocking collectives, exchange(): return lax.all_to_all(value, 'ops', 0, 0)  26.7 us
    ppermute x3, waiting for transfers between devices, other(): return lax.ppermute(value, ('ops', 'sec'), route)  11.8 us
    pallas_call x13, Pallas kernels, call(): pl.pallas_call(body, out_shape=tuple(outs), in_specs=in_specs, out_specs=...  11 us
    all_to_all x2, starting transfers between devices, exchange(): return lax.all_to_all(value, 'ops', 0, 0)  9.76 us
    all_to_all x2, waiting for transfers between devices, exchange(): return lax.all_to_all(value, 'ops', 0, 0)  9.64 us
    ppermute x3, starting transfers between devices, other(): return lax.ppermute(value, ('ops', 'sec'), route)  4.55 us
    unnamed x14, local copies, waits for them, and re-layouts  4.17 us
    ppermute x6, starting transfers between devices, over_sectors(): found.append(lax.ppermute(value, 'sec', route))  3.77 us
  transfers between devices with their start and end apart: 17, of which 10 were waited for; matrix products, arithmetic and copies ran while one was open for 0% of the time, Pallas kernels for 6%

profile of v9, /device:TPU:0, one launch (start us, length us, event | category | flops | bytes accessed | tf_op | source)
XLA Modules:
  0.0 93.8 jit_solution(13779511156952158124)
XLA Ops:
  1.3 0.9 copy-done.5
  2.2 3.0 %collective-permute-start.1 = (f32[8,64,128]{2,1,0:T(8,128)S(1)}, f32[8,64,128]{2,1,0:T(8,128)S(1)}, u32[]{:S(2)}, u32[]{:S(2)}) collective-permute-start(f32[8,64,128]{2,1,0:T(8,128)S(1)} %shard_map.87.x0.x_ref), channel_id=1, source_target_pairs={{1,2},{2,1},{0,4},{3,7},{5,6},{6,5},{4,0},{7,3},{9,10},{10,9},{8,1... | collective-permute-start | bytes 786440 | tf_op jit(solution)/shard_map/ppermute | solution.py:333
  5.3 0.1 collective-permute-start
  6.0 0.0 copy-start.6
  6.1 0.6 copy-done.6
  6.7 1.4 %shard_map.86 = (bf16[2,2,256,256]{3,2,1,0:T(8,128)(2,1)S(1)}, bf16[2,2,256,256]{3,2,1,0:T(8,128)(2,1)S(1)}, f32[8,128]{1,0:T(8,128)S(1)}, f32[2,8,128]{2,1,0:T(8,128)S(1)}) custom-call(s32[1]{0:T(128)S(6)} %copy.11.label_ref, s32[2]{0:T(128)S(1)} %bitcast.6, f32[2,1,256,256]{3,2,1,0:T(8,128)} %left_ref.1, f32[2,1,256,256]{3,2,1,0:T(8,128)} %right_ref.1), custom_call_target="tpu_custom_call" | custom-call | flops 2621440 | bytes 2109452 | tf_op jit(solution)/shard_map/pallas_call | solution.py:22
  8.1 1.5 %collective-permute-done.1.x2 = f32[8,64,128]{2,1,0:T(8,128)S(1)} collective-permute-done((f32[8,64,128]{2,1,0:T(8,128)S(1)}, f32[8,64,128]{2,1,0:T(8,128)S(1)}, u32[]{:S(2)}, u32[]{:S(2)}) %collective-permute-start.1) | collective-permute-done | bytes 262176 | tf_op jit(solution)/shard_map/ppermute | solution.py:333
  9.6 0.0 collective-permute-done.x1
  9.6 1.8 %shard_map.88 = (f32[8,64,128]{2,1,0:T(8,128)}, f32[2,256,256]{2,1,0:T(8,128)S(1)}, f32[8,128]{1,0:T(8,128)S(1)}) custom-call(s32[1]{0:T(128)S(6)} %copy.10.size_ref, f32[2,8,128]{2,1,0:T(8,128)S(1)} %get-tuple-element.18.slot_ref, f32[8,64,128]{2,1,0:T(8,128)S(1)} %shard_map.87.x0.x_ref, f32[8,64,128]{2,1,0:T(8,128)S(1)} %collective-permute-done.x1, ...), custom_call_target="tpu_custom_call" | custom-call | flops 402653184 | bytes 2633732 | tf_op jit(solution)/shard_map/pallas_call | solution.py:22
  11.4 6.3 %all-to-all-start = ((f32[8,64,128]{2,1,0:T(8,128)}), f32[8,64,128]{2,1,0:T(8,128)S(1)}, u32[]{:S(2)}, u32[]{:S(2)}) async-start(f32[8,64,128]{2,1,0:T(8,128)} %get-tuple-element.21), calls=%async_computation | async-start | bytes 524288 | tf_op jit(solution)/shard_map/all_to_all | solution.py:360
  17.7 0.0 collective-permute-start.4
  17.8 1.0 %collective-permute-start.3 = (f32[8,128]{1,0:T(8,128)S(1)}, f32[8,128]{1,0:T(8,128)S(1)}, u32[]{:S(2)}, u32[]{:S(2)}) collective-permute-start(f32[8,128]{1,0:T(8,128)S(1)} %get-tuple-element.22.mine), channel_id=1, source_target_pairs={{0,2},{1,3},{2,0},{3,1},{4,6},{5,7},{6,4},{7,5},{8,10},{9,11},{10,... | collective-permute-start | bytes 12296 | tf_op jit(solution)/shard_map/ppermute | solution.py:351
  18.8 0.8 collective-permute-start.2
  19.6 1.2 %collective-permute-done.4.refs_2_ = f32[8,128]{1,0:T(8,128)S(1)} collective-permute-done((f32[8,128]{1,0:T(8,128)S(1)}, f32[8,128]{1,0:T(8,128)S(1)}, u32[]{:S(2)}, u32[]{:S(2)}) %collective-permute-start.4) | collective-permute-done | bytes 4128 | tf_op jit(solution)/shard_map/ppermute | solution.py:351
  20.8 0.7 collective-permute-done.3.refs_1_
  21.5 5.0 %all-to-all-done.terms_ref = f32[8,64,128]{2,1,0:T(8,128)S(1)} async-done(((f32[8,64,128]{2,1,0:T(8,128)}), f32[8,64,128]{2,1,0:T(8,128)S(1)}, u32[]{:S(2)}, u32[]{:S(2)}) %all-to-all-start) | async-done | bytes 262176 | tf_op jit(solution)/shard_map/all_to_all | solution.py:360
  26.5 13.4 %all_to_all.31.g_ref.g0 = f32[8,72,128]{2,1,0:T(8,128)S(1)} all-to-all(f32[8,72,128]{2,1,0:T(8,128)S(1)} %shard_map.89), channel_id=1, replica_groups=mesh['ops'=8,'sec'=4] {'ops'}, dimensions={0} | all-to-all | bytes 589824 | tf_op jit(solution)/shard_map/all_to_all | solution.py:360
  39.9 0.2 shard_map.90
  40.1 0.8 collective-permute-start.6
  40.9 0.3 collective-permute-start.5
  41.2 5.4 %collective-permute-done.6.r2 = f32[8,64,128]{2,1,0:T(8,128)S(1)} collective-permute-done((f32[8,64,128]{2,1,0:T(8,128)S(1)}, f32[8,64,128]{2,1,0:T(8,128)S(1)}, u32[]{:S(2)}, u32[]{:S(2)}) %collective-permute-start.6) | collective-permute-done | bytes 262176 | tf_op jit(solution)/shard_map/ppermute | solution.py:333
  46.6 1.8 %shard_map.91 = (f32[8,64,128]{2,1,0:T(8,128)}, f32[2,256,256]{2,1,0:T(8,128)S(1)}, f32[8,128]{1,0:T(8,128)S(1)}) custom-call(s32[1]{0:T(128)S(6)} %copy.10.size_ref, f32[2,8,128]{2,1,0:T(8,128)S(1)} %get-tuple-element.18.slot_ref, f32[8,64,128]{2,1,0:T(8,128)S(1)} %get-tuple-element.23.r0.r_in, f32[8,64,128]{2,1,0:T(8,128)S(1)} %collective-permute-done.5.r1, ...), custom_call_target="tpu_custom_call" | custom-call | flops 402653184 | bytes 3190788 | tf_op jit(solution)/shard_map/pallas_call | solution.py:22
  48.4 0.0 copy-start.1
  48.4 0.8 copy-done.1
  49.2 3.4 %all-to-all-start.2 = ((f32[8,64,128]{2,1,0:T(8,128)}), f32[8,64,128]{2,1,0:T(8,128)S(1)}, u32[]{:S(2)}, u32[]{:S(2)}) async-start(f32[8,64,128]{2,1,0:T(8,128)} %get-tuple-element.24), calls=%async_computation.2 | async-start | bytes 524288 | tf_op jit(solution)/shard_map/all_to_all | solution.py:360
  52.6 0.1 collective-permute-start.9
  52.7 0.6 collective-permute-start.8
  53.2 1.3 %collective-permute-start.7 = (f32[8,128]{1,0:T(8,128)S(1)}, f32[8,128]{1,0:T(8,128)S(1)}, u32[]{:S(2)}, u32[]{:S(2)}) collective-permute-start(f32[8,128]{1,0:T(8,128)S(1)} %get-tuple-element.25.mine), channel_id=1, source_target_pairs={{0,1},{1,0},{2,3},{3,2},{4,5},{5,4},{6,7},{7,6},{8,9},{9,8},{10,11... | collective-permute-start | bytes 12296 | tf_op jit(solution)/shard_map/ppermute | solution.py:351
  54.5 1.2 %collective-permute-done.9.refs_2_ = f32[8,128]{1,0:T(8,128)S(1)} collective-permute-done((f32[8,128]{1,0:T(8,128)S(1)}, f32[8,128]{1,0:T(8,128)S(1)}, u32[]{:S(2)}, u32[]{:S(2)}) %collective-permute-start.9) | collective-permute-done | bytes 4128 | tf_op jit(solution)/shard_map/ppermute | solution.py:351
  55.7 0.7 collective-permute-done.8.refs_1_
  56.3 0.0 collective-permute-done.7.refs_0_
  56.3 4.7 %all-to-all-done.2.terms_ref = f32[8,64,128]{2,1,0:T(8,128)S(1)} async-done(((f32[8,64,128]{2,1,0:T(8,128)}), f32[8,64,128]{2,1,0:T(8,128)S(1)}, u32[]{:S(2)}, u32[]{:S(2)}) %all-to-all-start.2) | async-done | bytes 262176 | tf_op jit(solution)/shard_map/all_to_all | solution.py:360
  61.0 13.3 %all_to_all.32.s_ref = f32[8,72,128]{2,1,0:T(8,128)S(1)} all-to-all(f32[8,72,128]{2,1,0:T(8,128)S(1)} %shard_map.92), channel_id=1, replica_groups=mesh['ops'=8,'sec'=4] {'ops'}, dimensions={0} | all-to-all | bytes 589824 | tf_op jit(solution)/shard_map/all_to_all | solution.py:360
  74.3 0.4 shard_map.93
  74.7 0.8 collective-permute-start.11
  75.5 0.2 shard_map.96.b_ref
  75.6 0.6 collective-permute-start.12
  76.2 4.9 %collective-permute-done.11.r2 = f32[8,64,128]{2,1,0:T(8,128)S(1)} collective-permute-done((f32[8,64,128]{2,1,0:T(8,128)S(1)}, f32[8,64,128]{2,1,0:T(8,128)S(1)}, u32[]{:S(2)}, u32[]{:S(2)}) %collective-permute-start.11) | collective-permute-done | bytes 262176 | tf_op jit(solution)/shard_map/ppermute | solution.py:333
  81.2 0.4 shard_map.94.m_ref
  81.6 0.1 collective-permute-start.13
  81.7 1.1 %shard_map.95 = f32[32,128]{1,0:T(8,128)} custom-call(s32[1]{0:T(128)S(6)} %copy.10.size_ref, f32[2,256,256]{2,1,0:T(8,128)S(1)} %shard_map.94.m_ref, f32[8,64,128]{2,1,0:T(8,128)S(1)} %get-tuple-element.27.r0.s0, f32[8,64,128]{2,1,0:T(8,128)S(1)} %get-tuple-element.28.x0.x_ref, f32[8,64,128]{2,1,0:T(8,128)S(1)} %get-tuple-element.29.h0, ...), custom_call_target="tpu_custom_call" | custom-call | flops 201326592 | bytes 1851396 | tf_op jit(solution)/shard_map/pallas_call | solution.py:22
  82.8 2.5 %all-to-all-start.4 = ((f32[32,1,128]{2,1,0:T(1,128)}), f32[32,1,128]{2,1,0:T(1,128)S(1)}, u32[]{:S(2)}, u32[]{:S(2)}) async-start(f32[32,1,128]{2,1,0:T(1,128)} %bitcast.2), calls=%async_computation.4 | async-start | bytes 32768 | tf_op jit(solution)/shard_map/all_to_all | solution.py:431
  85.3 0.0 copy-start.3
  85.3 0.8 copy-done.3
  86.1 1.0 %copy-done.4 = f32[2,256,256]{2,1,0:T(8,128)S(1)} copy-done((f32[2,256,256]{2,1,0:T(8,128)S(1)}, f32[2,256,256]{2,1,0:T(8,128)}, u32[]{:S(2)}) %copy-start.4) | copy-done | bytes 524312
  87.2 2.3 %shard_map.97.u_ref = f32[3,2,256,256]{3,2,1,0:T(8,128)S(1)} custom-call(f32[8,128]{1,0:T(8,128)S(1)} %get-tuple-element.33.flag_ref, f32[3,256,256]{2,1,0:T(8,128)S(1)} %shard_map.96.b_ref, f32[3,256,256]{2,1,0:T(8,128)} %collective-permute-done.12.n_ref, f32[2,256,256]{2,1,0:T(8,128)S(1)} %shard_map.94.m_ref, f32[2,256,256]{2,1,0:T(8,128)S(1)} %copy-done.4, ...), custom_call_target="tpu_custom_call" | custom-call | flops 402653184 | bytes 4722688 | tf_op jit(solution)/shard_map/pallas_call | solution.py:22
  89.4 3.0 %all-to-all-done.4 = f32[32,1,128]{2,1,0:T(1,128)S(1)} async-done(((f32[32,1,128]{2,1,0:T(1,128)}), f32[32,1,128]{2,1,0:T(1,128)S(1)}, u32[]{:S(2)}, u32[]{:S(2)}) %all-to-all-start.4) | async-done | bytes 16416 | tf_op jit(solution)/shard_map/all_to_all | solution.py:431
  92.4 1.3 %shard_map.98 = (f32[1,256,256]{2,1,0:T(8,128)}, f32[2,1,256,256]{3,2,1,0:T(8,128)}) custom-call(f32[32,128]{1,0:T(8,128)S(1)} %bitcast.5, f32[8,128]{1,0:T(8,128)S(1)} %get-tuple-element.30.c_in, f32[3,256,256]{2,1,0:T(8,128)S(1)} %shard_map.96.b_ref, f32[8,64,128]{2,1,0:T(8,128)S(1)} %get-tuple-element.27.r0.s0, f32[3,2,256,256]{3,2,1,0:T(8,128)S(1)} %shard_map.97.u_ref), custom_call_target="tpu_custom_call" | custom-call | flops 1310720 | bytes 3428352 | tf_op jit(solution)/shard_map/pallas_call | solution.py:22
  (15 shorter events, 0.1 us)
Async XLA Ops:
  1.3 0.9 copy-start.5
  2.2 7.4 %collective-permute-start.1 = (f32[8,64,128]{2,1,0:T(8,128)S(1)}, f32[8,64,128]{2,1,0:T(8,128)S(1)}, u32[]{:S(2)}, u32[]{:S(2)}) collective-permute-start(f32[8,64,128]{2,1,0:T(8,128)S(1)} %shard_map.87.x0.x_ref), channel_id=1, source_target_pairs={{1,2},{2,1},{0,4},{3,7},{5,6},{6,5},{4,0},{7,3},{9,10},{10,9},{8,1... | collective-permute-start | bytes 786440 | tf_op jit(solution)/shard_map/ppermute | solution.py:333
  5.3 4.4 %collective-permute-start = (f32[8,64,128]{2,1,0:T(8,128)S(1)}, f32[8,64,128]{2,1,0:T(8,128)S(1)}, u32[]{:S(2)}, u32[]{:S(2)}) collective-permute-start(f32[8,64,128]{2,1,0:T(8,128)S(1)} %shard_map.87.x0.x_ref), channel_id=1, source_target_pairs={{0,1},{1,0},{2,3},{3,2},{4,5},{5,4},{6,7},{7,6},{8,9},{9,8},{10,11... | collective-permute-start | bytes 786440 | tf_op jit(solution)/shard_map/ppermute | solution.py:322
  6.0 0.7 copy-start.6
  9.6 30.3 %copy-start = (bf16[1,256,256]{2,1,0:T(8,128)(2,1)S(1)}, bf16[1,256,256]{2,1,0:T(8,128)(2,1)}, u32[]{:S(2)}) copy-start(bf16[1,256,256]{2,1,0:T(8,128)(2,1)} %diag_ref.3) | copy-start | bytes 393220
  11.4 15.0 %all-to-all-start = ((f32[8,64,128]{2,1,0:T(8,128)}), f32[8,64,128]{2,1,0:T(8,128)S(1)}, u32[]{:S(2)}, u32[]{:S(2)}) async-start(f32[8,64,128]{2,1,0:T(8,128)} %get-tuple-element.21), calls=%async_computation | async-start | bytes 524288 | tf_op jit(solution)/shard_map/all_to_all | solution.py:360
  17.7 3.0 %collective-permute-start.4 = (f32[8,128]{1,0:T(8,128)S(1)}, f32[8,128]{1,0:T(8,128)S(1)}, u32[]{:S(2)}, u32[]{:S(2)}) collective-permute-start(f32[8,128]{1,0:T(8,128)S(1)} %get-tuple-element.22.mine), channel_id=1, source_target_pairs={{0,3},{1,2},{2,1},{3,0},{4,7},{5,6},{6,5},{7,4},{8,11},{9,10},{10,... | collective-permute-start | bytes 12296 | tf_op jit(solution)/shard_map/ppermute | solution.py:351
  17.8 3.7 %collective-permute-start.3 = (f32[8,128]{1,0:T(8,128)S(1)}, f32[8,128]{1,0:T(8,128)S(1)}, u32[]{:S(2)}, u32[]{:S(2)}) collective-permute-start(f32[8,128]{1,0:T(8,128)S(1)} %get-tuple-element.22.mine), channel_id=1, source_target_pairs={{0,2},{1,3},{2,0},{3,1},{4,6},{5,7},{6,4},{7,5},{8,10},{9,11},{10,... | collective-permute-start | bytes 12296 | tf_op jit(solution)/shard_map/ppermute | solution.py:351
  18.8 2.7 %collective-permute-start.2 = (f32[8,128]{1,0:T(8,128)S(1)}, f32[8,128]{1,0:T(8,128)S(1)}, u32[]{:S(2)}, u32[]{:S(2)}) collective-permute-start(f32[8,128]{1,0:T(8,128)S(1)} %get-tuple-element.22.mine), channel_id=1, source_target_pairs={{0,1},{1,0},{2,3},{3,2},{4,5},{5,4},{6,7},{7,6},{8,9},{9,8},{10,11... | collective-permute-start | bytes 12296 | tf_op jit(solution)/shard_map/ppermute | solution.py:351
  40.1 6.4 %collective-permute-start.6 = (f32[8,64,128]{2,1,0:T(8,128)S(1)}, f32[8,64,128]{2,1,0:T(8,128)S(1)}, u32[]{:S(2)}, u32[]{:S(2)}) collective-permute-start(f32[8,64,128]{2,1,0:T(8,128)S(1)} %get-tuple-element.23.r0.r_in), channel_id=1, source_target_pairs={{1,2},{2,1},{0,4},{3,7},{5,6},{6,5},{4,0},{7,3},{9,10},{10,9},{8,1... | collective-permute-start | bytes 786440 | tf_op jit(solution)/shard_map/ppermute | solution.py:333
  40.9 5.7 %collective-permute-start.5 = (f32[8,64,128]{2,1,0:T(8,128)S(1)}, f32[8,64,128]{2,1,0:T(8,128)S(1)}, u32[]{:S(2)}, u32[]{:S(2)}) collective-permute-start(f32[8,64,128]{2,1,0:T(8,128)S(1)} %get-tuple-element.23.r0.r_in), channel_id=1, source_target_pairs={{0,1},{1,0},{2,3},{3,2},{4,5},{5,4},{6,7},{7,6},{8,9},{9,8},{10,11... | collective-permute-start | bytes 786440 | tf_op jit(solution)/shard_map/ppermute | solution.py:322
  48.4 0.8 copy-start.1
  49.2 11.8 %all-to-all-start.2 = ((f32[8,64,128]{2,1,0:T(8,128)}), f32[8,64,128]{2,1,0:T(8,128)S(1)}, u32[]{:S(2)}, u32[]{:S(2)}) async-start(f32[8,64,128]{2,1,0:T(8,128)} %get-tuple-element.24), calls=%async_computation.2 | async-start | bytes 524288 | tf_op jit(solution)/shard_map/all_to_all | solution.py:360
  52.6 3.1 %collective-permute-start.9 = (f32[8,128]{1,0:T(8,128)S(1)}, f32[8,128]{1,0:T(8,128)S(1)}, u32[]{:S(2)}, u32[]{:S(2)}) collective-permute-start(f32[8,128]{1,0:T(8,128)S(1)} %get-tuple-element.25.mine), channel_id=1, source_target_pairs={{0,3},{1,2},{2,1},{3,0},{4,7},{5,6},{6,5},{7,4},{8,11},{9,10},{10,... | collective-permute-start | bytes 12296 | tf_op jit(solution)/shard_map/ppermute | solution.py:351
  52.7 3.7 %collective-permute-start.8 = (f32[8,128]{1,0:T(8,128)S(1)}, f32[8,128]{1,0:T(8,128)S(1)}, u32[]{:S(2)}, u32[]{:S(2)}) collective-permute-start(f32[8,128]{1,0:T(8,128)S(1)} %get-tuple-element.25.mine), channel_id=1, source_target_pairs={{0,2},{1,3},{2,0},{3,1},{4,6},{5,7},{6,4},{7,5},{8,10},{9,11},{10,... | collective-permute-start | bytes 12296 | tf_op jit(solution)/shard_map/ppermute | solution.py:351
  53.2 3.1 %collective-permute-start.7 = (f32[8,128]{1,0:T(8,128)S(1)}, f32[8,128]{1,0:T(8,128)S(1)}, u32[]{:S(2)}, u32[]{:S(2)}) collective-permute-start(f32[8,128]{1,0:T(8,128)S(1)} %get-tuple-element.25.mine), channel_id=1, source_target_pairs={{0,1},{1,0},{2,3},{3,2},{4,5},{5,4},{6,7},{7,6},{8,9},{9,8},{10,11... | collective-permute-start | bytes 12296 | tf_op jit(solution)/shard_map/ppermute | solution.py:351
  61.0 14.5 %copy-start.2 = (f32[2,256,256]{2,1,0:T(8,128)S(1)}, f32[2,256,256]{2,1,0:T(8,128)}, u32[]{:S(2)}) copy-start(f32[2,256,256]{2,1,0:T(8,128)} %copy-done.1) | copy-start | bytes 1572868
  74.7 6.4 %collective-permute-start.11 = (f32[8,64,128]{2,1,0:T(8,128)S(1)}, f32[8,64,128]{2,1,0:T(8,128)S(1)}, u32[]{:S(2)}, u32[]{:S(2)}) collective-permute-start(f32[8,64,128]{2,1,0:T(8,128)S(1)} %get-tuple-element.27.r0.s0), channel_id=1, source_target_pairs={{1,2},{2,1},{0,4},{3,7},{5,6},{6,5},{4,0},{7,3},{9,10},{10,9},{8,1... | collective-permute-start | bytes 786440 | tf_op jit(solution)/shard_map/ppermute | solution.py:333
  75.5 5.7 %collective-permute-start.10 = (f32[8,64,128]{2,1,0:T(8,128)S(1)}, f32[8,64,128]{2,1,0:T(8,128)S(1)}, u32[]{:S(2)}, u32[]{:S(2)}) collective-permute-start(f32[8,64,128]{2,1,0:T(8,128)S(1)} %get-tuple-element.27.r0.s0), channel_id=1, source_target_pairs={{0,1},{1,0},{2,3},{3,2},{4,5},{5,4},{6,7},{7,6},{8,9},{9,8},{10,11... | collective-permute-start | bytes 786440 | tf_op jit(solution)/shard_map/ppermute | solution.py:322
  75.6 10.5 %collective-permute-start.12 = (f32[3,256,256]{2,1,0:T(8,128)S(1)}, f32[3,256,256]{2,1,0:T(8,128)}, u32[]{:S(2)}, u32[]{:S(2)}) collective-permute-start(f32[3,256,256]{2,1,0:T(8,128)S(1)} %shard_map.96.b_ref), channel_id=1, source_target_pairs={{0,1},{1,0},{2,3},{3,2},{4,5},{5,4},{6,7},{7,6},{8,9},{9,8},{10,11... | collective-permute-start | bytes 2359304 | tf_op jit(solution)/shard_map/ppermute | solution.py:322
  81.6 3.7 %collective-permute-start.13 = (f32[2,256,256]{2,1,0:T(8,128)S(1)}, f32[2,256,256]{2,1,0:T(8,128)S(1)}, u32[]{:S(2)}, u32[]{:S(2)}) collective-permute-start(f32[2,256,256]{2,1,0:T(8,128)S(1)} %shard_map.94.m_ref), channel_id=1, source_target_pairs={{0,1},{1,0},{2,3},{3,2},{4,5},{5,4},{6,7},{7,6},{8,9},{9,8},{10,11... | collective-permute-start | bytes 1572872 | tf_op jit(solution)/shard_map/ppermute | solution.py:322
  82.8 9.7 %all-to-all-start.4 = ((f32[32,1,128]{2,1,0:T(1,128)}), f32[32,1,128]{2,1,0:T(1,128)S(1)}, u32[]{:S(2)}, u32[]{:S(2)}) async-start(f32[32,1,128]{2,1,0:T(1,128)} %bitcast.2), calls=%async_computation.4 | async-start | bytes 32768 | tf_op jit(solution)/shard_map/all_to_all | solution.py:431
  85.3 0.8 copy-start.3
  86.1 1.0 %copy-start.4 = (f32[2,256,256]{2,1,0:T(8,128)S(1)}, f32[2,256,256]{2,1,0:T(8,128)}, u32[]{:S(2)}) copy-start(f32[2,256,256]{2,1,0:T(8,128)} %copy-done.3) | copy-start | bytes 1572868

commit v10 on v8

--- a/solution.py
+++ b/solution.py
@@ -16,14 +16,14 @@
 SMEM = pl.BlockSpec(memory_space=pltpu.SMEM)
 
 
-def call(body, outs, in_specs, scratch, flops, *args, limit=8):
+def call(body, outs, in_specs, scratch, flops, *args, limit=8, away=()):
     size = sum(a.size * a.dtype.itemsize for a in args)
     size += sum(o.size * o.dtype.itemsize for o in outs)
     return pl.pallas_call(
         body,
-        out_shape=tuple(outs),
+        out_shape=tuple(pltpu.HBM(o.shape, o.dtype) if k in away else o for k, o in enumerate(outs)),
         in_specs=in_specs,
-        out_specs=tuple(VMEM for _ in outs),
+        out_specs=tuple(pl.BlockSpec(memory_space=pltpu.HBM) if k in away else VMEM for k in range(len(outs))),
         scratch_shapes=scratch,
         compiler_params=pltpu.CompilerParams(vmem_limit_bytes=int(limit * 1024 * 1024)),
         cost_estimate=pl.CostEstimate(flops=flops, bytes_accessed=size, transcendentals=0),
@@ -198,10 +198,14 @@
 
 
 def second_body(
-    size_ref, slot_ref, r0, r1, r2, x0, g0, lcat_ref, rcat_ref, y_ref, m_ref, part_ref
+    size_ref, slot_ref, r0, r1, r2, x0, g0, lcat_ref, rcat_ref, y_ref, m_out, part_ref,
+    m_ref, sem,
 ):
     mixed = mix_all(slot_ref, (r0, r1, r2), lcat_ref, m_ref)
+    copy = pltpu.make_async_copy(m_ref, m_out, sem)
+    copy.start()
     part_ref[...] = five(x0, r0, g0, fold_all(size_ref, mixed, rcat_ref, y_ref))
+    copy.wait()
 
 
 def mix_body(slot_ref, r0, r1, r2, lcat_ref, m_ref):
@@ -354,6 +358,7 @@
     wide = jax.ShapeDtypeStruct((chunks, cw + 8, LANES), F32)
     small = jax.ShapeDtypeStruct((8, LANES), F32)
     inner = jax.ShapeDtypeStruct((pairs, side, side), F32)
+    room = [pltpu.VMEM(inner.shape, F32), pltpu.SemaphoreType.DMA(())]
     pieces = jax.ShapeDtypeStruct((pairs, 2, side, side), BF16)
     loads = [pltpu.VMEM((pairs, side, side), F32)] * 2 + [pltpu.SemaphoreType.DMA((2 * pairs,))]
     work = 12 * pairs * side**3
@@ -377,7 +382,7 @@
     )
     y, mx, part = call(
         first_body, (block, inner, small), [SMEM] + [VMEM] * 6, [], work,
-        sector_states, slots, x0, x1, x2, lcat, rcat, limit=52,
+        sector_states, slots, x0, x1, x2, lcat, rcat,
     )
     g = gathered(y, part)
     r0, c = call(
@@ -386,8 +391,8 @@
     )
     r2, r1 = other(r0), paired(r0)
     y, mr, part = call(
-        second_body, (block, inner, small), [SMEM] + [VMEM] * 8, [], work,
-        sector_states, slots, r0, r1, r2, x0, g, lcat, rcat, limit=51.5,
+        second_body, (block, inner, small), [SMEM] + [VMEM] * 8, room, work,
+        sector_states, slots, r0, r1, r2, x0, g, lcat, rcat, away=(1,),
     )
     s = gathered(y, part)
     x, h, s0, c = call(

time: 95.9 us -> 93.9 us (0.979)
  Pallas kernels: 13.3 us -> 11.3 us
  local copies, waits for them, and re-layouts: 5.17 us -> 3.39 us
  waiting for transfers between devices: 26.5 us -> 28.1 us
    pallas_call x13, Pallas kernels: 13.3 us -> 11.3 us  [call(): pl.pallas_call(body, out_shape=tuple((pltpu.HBM(o.shape, o.dtype) if k in...]
    unnamed x18 -> x12, local copies, waits for them, and re-layouts: 5.17 us -> 3.39 us
    ppermute x3, waiting for transfers between devices: 10.3 us -> 11.8 us  [other(): return lax.ppermute(value, ('ops', 'sec'), route)]
  transfers between devices with their start and end apart: 17 -> 17, of which waited for: 9 -> 10; matrix products, arithmetic and copies ran while one was open for 0% -> 0% of each run, Pallas kernels for 6% -> 6%
where the time goes in v10:
time: 93.9 us; the launch traced here: 93.3 us
  waiting for transfers between devices  28.1 us (30%)
  blocking collectives  26.7 us (28%)
  starting transfers between devices  21.7 us (23%)
  Pallas kernels  11.3 us (12%)
  local copies, waits for them, and re-layouts  3.39 us (4%)
  between operations  2.07 us (2%)
    all_to_all x2, blocking collectives, exchange(): return lax.all_to_all(value, 'ops', 0, 0)  26.7 us
    ppermute x3, waiting for transfers between devices, other(): return lax.ppermute(value, ('ops', 'sec'), route)  11.8 us
    pallas_call x13, Pallas kernels, call(): pl.pallas_call(body, out_shape=tuple((pltpu.HBM(o.shape, o.dtype) if k in...  11.3 us
    all_to_all x2, starting transfers between devices, exchange(): return lax.all_to_all(value, 'ops', 0, 0)  9.76 us
    all_to_all x2, waiting for transfers between devices, exchange(): return lax.all_to_all(value, 'ops', 0, 0)  9.64 us
    ppermute x3, starting transfers between devices, other(): return lax.ppermute(value, ('ops', 'sec'), route)  4.55 us
    ppermute x6, starting transfers between devices, over_sectors(): found.append(lax.ppermute(value, 'sec', route))  3.77 us
    ppermute x6, waiting for transfers between devices, over_sectors(): found.append(lax.ppermute(value, 'sec', route))  3.67 us
  transfers between devices with their start and end apart: 17, of which 10 were waited for; matrix products, arithmetic and copies ran while one was open for 0% of the time, Pallas kernels for 6%

profile of v10, /device:TPU:0, one launch (start us, length us, event | category | flops | bytes accessed | tf_op | source)
XLA Modules:
  0.0 93.3 jit_solution(7996278947955631146)
XLA Ops:
  1.3 0.9 copy-done.4
  2.2 3.0 %collective-permute-start.1 = (f32[8,64,128]{2,1,0:T(8,128)S(1)}, f32[8,64,128]{2,1,0:T(8,128)S(1)}, u32[]{:S(2)}, u32[]{:S(2)}) collective-permute-start(f32[8,64,128]{2,1,0:T(8,128)S(1)} %shard_map.87.x0.x_ref), channel_id=1, source_target_pairs={{1,2},{2,1},{0,4},{3,7},{5,6},{6,5},{4,0},{7,3},{9,10},{10,9},{8,1... | collective-permute-start | bytes 786440 | tf_op jit(solution)/shard_map/ppermute | solution.py:320
  5.3 0.1 collective-permute-start
  6.0 0.0 copy-start.5
  6.1 0.6 copy-done.5
  6.7 1.4 %shard_map.86 = (bf16[2,2,256,256]{3,2,1,0:T(8,128)(2,1)S(1)}, bf16[2,2,256,256]{3,2,1,0:T(8,128)(2,1)S(1)}, f32[8,128]{1,0:T(8,128)S(1)}, f32[2,8,128]{2,1,0:T(8,128)S(1)}) custom-call(s32[1]{0:T(128)S(6)} %copy.11.label_ref, s32[2]{0:T(128)S(1)} %bitcast.6, f32[2,1,256,256]{3,2,1,0:T(8,128)} %left_ref.1, f32[2,1,256,256]{3,2,1,0:T(8,128)} %right_ref.1), custom_call_target="tpu_custom_call" | custom-call | flops 2621440 | bytes 2109452 | tf_op jit(solution)/shard_map/pallas_call | solution.py:22
  8.1 1.5 %collective-permute-done.1.x2 = f32[8,64,128]{2,1,0:T(8,128)S(1)} collective-permute-done((f32[8,64,128]{2,1,0:T(8,128)S(1)}, f32[8,64,128]{2,1,0:T(8,128)S(1)}, u32[]{:S(2)}, u32[]{:S(2)}) %collective-permute-start.1) | collective-permute-done | bytes 262176 | tf_op jit(solution)/shard_map/ppermute | solution.py:320
  9.6 0.0 collective-permute-done.x1
  9.6 1.8 %shard_map.88 = (f32[8,64,128]{2,1,0:T(8,128)}, f32[2,256,256]{2,1,0:T(8,128)S(1)}, f32[8,128]{1,0:T(8,128)S(1)}) custom-call(s32[1]{0:T(128)S(6)} %copy.10.size_ref, f32[2,8,128]{2,1,0:T(8,128)S(1)} %get-tuple-element.18.slot_ref, f32[8,64,128]{2,1,0:T(8,128)S(1)} %shard_map.87.x0.x_ref, f32[8,64,128]{2,1,0:T(8,128)S(1)} %collective-permute-done.x1, ...), custom_call_target="tpu_custom_call" | custom-call | flops 402653184 | bytes 2633732 | tf_op jit(solution)/shard_map/pallas_call | solution.py:22
  11.4 6.3 %all-to-all-start = ((f32[8,64,128]{2,1,0:T(8,128)}), f32[8,64,128]{2,1,0:T(8,128)S(1)}, u32[]{:S(2)}, u32[]{:S(2)}) async-start(f32[8,64,128]{2,1,0:T(8,128)} %get-tuple-element.21), calls=%async_computation | async-start | bytes 524288 | tf_op jit(solution)/shard_map/all_to_all | solution.py:347
  17.7 0.0 collective-permute-start.4
  17.7 1.0 %collective-permute-start.3 = (f32[8,128]{1,0:T(8,128)S(1)}, f32[8,128]{1,0:T(8,128)S(1)}, u32[]{:S(2)}, u32[]{:S(2)}) collective-permute-start(f32[8,128]{1,0:T(8,128)S(1)} %get-tuple-element.22.mine), channel_id=1, source_target_pairs={{0,2},{1,3},{2,0},{3,1},{4,6},{5,7},{6,4},{7,5},{8,10},{9,11},{10,... | collective-permute-start | bytes 12296 | tf_op jit(solution)/shard_map/ppermute | solution.py:338
  18.7 0.8 collective-permute-start.2
  19.6 1.2 %collective-permute-done.4.refs_2_ = f32[8,128]{1,0:T(8,128)S(1)} collective-permute-done((f32[8,128]{1,0:T(8,128)S(1)}, f32[8,128]{1,0:T(8,128)S(1)}, u32[]{:S(2)}, u32[]{:S(2)}) %collective-permute-start.4) | collective-permute-done | bytes 4128 | tf_op jit(solution)/shard_map/ppermute | solution.py:338
  20.7 0.7 collective-permute-done.3.refs_1_
  21.4 0.0 collective-permute-done.2.refs_0_
  21.4 5.0 %all-to-all-done.terms_ref = f32[8,64,128]{2,1,0:T(8,128)S(1)} async-done(((f32[8,64,128]{2,1,0:T(8,128)}), f32[8,64,128]{2,1,0:T(8,128)S(1)}, u32[]{:S(2)}, u32[]{:S(2)}) %all-to-all-start) | async-done | bytes 262176 | tf_op jit(solution)/shard_map/all_to_all | solution.py:347
  26.4 13.4 %all_to_all.31.g_ref.g0 = f32[8,72,128]{2,1,0:T(8,128)S(1)} all-to-all(f32[8,72,128]{2,1,0:T(8,128)S(1)} %shard_map.89), channel_id=1, replica_groups=mesh['ops'=8,'sec'=4] {'ops'}, dimensions={0} | all-to-all | bytes 589824 | tf_op jit(solution)/shard_map/all_to_all | solution.py:347
  39.9 0.2 shard_map.90
  40.1 0.8 collective-permute-start.6
  40.9 0.3 collective-permute-start.5
  41.2 5.4 %collective-permute-done.6.r2 = f32[8,64,128]{2,1,0:T(8,128)S(1)} collective-permute-done((f32[8,64,128]{2,1,0:T(8,128)S(1)}, f32[8,64,128]{2,1,0:T(8,128)S(1)}, u32[]{:S(2)}, u32[]{:S(2)}) %collective-permute-start.6) | collective-permute-done | bytes 262176 | tf_op jit(solution)/shard_map/ppermute | solution.py:320
  46.5 0.0 collective-permute-done.5.r1
  46.5 2.1 %shard_map.91 = (f32[8,64,128]{2,1,0:T(8,128)}, f32[2,256,256]{2,1,0:T(8,128)}, f32[8,128]{1,0:T(8,128)S(1)}) custom-call(s32[1]{0:T(128)S(6)} %copy.10.size_ref, f32[2,8,128]{2,1,0:T(8,128)S(1)} %get-tuple-element.18.slot_ref, f32[8,64,128]{2,1,0:T(8,128)S(1)} %get-tuple-element.23.r0.r_in, f32[8,64,128]{2,1,0:T(8,128)S(1)} %collective-permute-done.5.r1, ...), custom_call_target="tpu_custom_call" | custom-call | flops 402653184 | bytes 3190788 | tf_op jit(solution)/shard_map/pallas_call | solution.py:22
  48.7 3.4 %all-to-all-start.2 = ((f32[8,64,128]{2,1,0:T(8,128)}), f32[8,64,128]{2,1,0:T(8,128)S(1)}, u32[]{:S(2)}, u32[]{:S(2)}) async-start(f32[8,64,128]{2,1,0:T(8,128)} %get-tuple-element.24), calls=%async_computation.2 | async-start | bytes 524288 | tf_op jit(solution)/shard_map/all_to_all | solution.py:347
  52.1 0.1 collective-permute-start.9
  52.2 0.6 collective-permute-start.8
  52.8 1.3 %collective-permute-start.7 = (f32[8,128]{1,0:T(8,128)S(1)}, f32[8,128]{1,0:T(8,128)S(1)}, u32[]{:S(2)}, u32[]{:S(2)}) collective-permute-start(f32[8,128]{1,0:T(8,128)S(1)} %get-tuple-element.25.mine), channel_id=1, source_target_pairs={{0,1},{1,0},{2,3},{3,2},{4,5},{5,4},{6,7},{7,6},{8,9},{9,8},{10,11... | collective-permute-start | bytes 12296 | tf_op jit(solution)/shard_map/ppermute | solution.py:338
  54.0 1.2 %collective-permute-done.9.refs_2_ = f32[8,128]{1,0:T(8,128)S(1)} collective-permute-done((f32[8,128]{1,0:T(8,128)S(1)}, f32[8,128]{1,0:T(8,128)S(1)}, u32[]{:S(2)}, u32[]{:S(2)}) %collective-permute-start.9) | collective-permute-done | bytes 4128 | tf_op jit(solution)/shard_map/ppermute | solution.py:338
  55.2 0.7 collective-permute-done.8.refs_1_
  55.9 4.6 %all-to-all-done.2.terms_ref = f32[8,64,128]{2,1,0:T(8,128)S(1)} async-done(((f32[8,64,128]{2,1,0:T(8,128)}), f32[8,64,128]{2,1,0:T(8,128)S(1)}, u32[]{:S(2)}, u32[]{:S(2)}) %all-to-all-start.2) | async-done | bytes 262176 | tf_op jit(solution)/shard_map/all_to_all | solution.py:347
  60.6 13.3 %all_to_all.32.s_ref = f32[8,72,128]{2,1,0:T(8,128)S(1)} all-to-all(f32[8,72,128]{2,1,0:T(8,128)S(1)} %shard_map.92), channel_id=1, replica_groups=mesh['ops'=8,'sec'=4] {'ops'}, dimensions={0} | all-to-all | bytes 589824 | tf_op jit(solution)/shard_map/all_to_all | solution.py:347
  73.9 0.4 shard_map.93
  74.2 0.8 collective-permute-start.11
  75.0 0.2 shard_map.96.b_ref
  75.2 0.6 collective-permute-start.12
  75.7 4.9 %collective-permute-done.11.r2 = f32[8,64,128]{2,1,0:T(8,128)S(1)} collective-permute-done((f32[8,64,128]{2,1,0:T(8,128)S(1)}, f32[8,64,128]{2,1,0:T(8,128)S(1)}, u32[]{:S(2)}, u32[]{:S(2)}) %collective-permute-start.11) | collective-permute-done | bytes 262176 | tf_op jit(solution)/shard_map/ppermute | solution.py:320
  80.7 0.0 collective-permute-done.10.r1.s1
  80.7 0.4 shard_map.94.m_ref
  81.1 0.1 collective-permute-start.13
  81.2 1.1 %shard_map.95 = f32[32,128]{1,0:T(8,128)} custom-call(s32[1]{0:T(128)S(6)} %copy.10.size_ref, f32[2,256,256]{2,1,0:T(8,128)S(1)} %shard_map.94.m_ref, f32[8,64,128]{2,1,0:T(8,128)S(1)} %get-tuple-element.27.r0.s0, f32[8,64,128]{2,1,0:T(8,128)S(1)} %get-tuple-element.28.x0.x_ref, f32[8,64,128]{2,1,0:T(8,128)S(1)} %get-tuple-element.29.h0, ...), custom_call_target="tpu_custom_call" | custom-call | flops 201326592 | bytes 1851396 | tf_op jit(solution)/shard_map/pallas_call | solution.py:22
  82.3 2.5 %all-to-all-start.4 = ((f32[32,1,128]{2,1,0:T(1,128)}), f32[32,1,128]{2,1,0:T(1,128)S(1)}, u32[]{:S(2)}, u32[]{:S(2)}) async-start(f32[32,1,128]{2,1,0:T(1,128)} %bitcast.2), calls=%async_computation.4 | async-start | bytes 32768 | tf_op jit(solution)/shard_map/all_to_all | solution.py:418
  84.9 0.0 copy-start.2
  84.9 0.8 copy-done.2
  85.7 1.0 %copy-done.3 = f32[2,256,256]{2,1,0:T(8,128)S(1)} copy-done((f32[2,256,256]{2,1,0:T(8,128)S(1)}, f32[2,256,256]{2,1,0:T(8,128)}, u32[]{:S(2)}) %copy-start.3) | copy-done | bytes 524312
  86.7 2.3 %shard_map.97.u_ref = f32[3,2,256,256]{3,2,1,0:T(8,128)S(1)} custom-call(f32[8,128]{1,0:T(8,128)S(1)} %get-tuple-element.33.flag_ref, f32[3,256,256]{2,1,0:T(8,128)S(1)} %shard_map.96.b_ref, f32[3,256,256]{2,1,0:T(8,128)} %collective-permute-done.12.n_ref, f32[2,256,256]{2,1,0:T(8,128)S(1)} %shard_map.94.m_ref, f32[2,256,256]{2,1,0:T(8,128)S(1)} %copy-done.3, ...), custom_call_target="tpu_custom_call" | custom-call | flops 402653184 | bytes 4722688 | tf_op jit(solution)/shard_map/pallas_call | solution.py:22
  89.0 3.0 %all-to-all-done.4 = f32[32,1,128]{2,1,0:T(1,128)S(1)} async-done(((f32[32,1,128]{2,1,0:T(1,128)}), f32[32,1,128]{2,1,0:T(1,128)S(1)}, u32[]{:S(2)}, u32[]{:S(2)}) %all-to-all-start.4) | async-done | bytes 16416 | tf_op jit(solution)/shard_map/all_to_all | solution.py:418
  92.0 1.4 %shard_map.98 = (f32[1,256,256]{2,1,0:T(8,128)}, f32[2,1,256,256]{3,2,1,0:T(8,128)}) custom-call(f32[32,128]{1,0:T(8,128)S(1)} %bitcast.5, f32[8,128]{1,0:T(8,128)S(1)} %get-tuple-element.30.c_in, f32[3,256,256]{2,1,0:T(8,128)S(1)} %shard_map.96.b_ref, f32[8,64,128]{2,1,0:T(8,128)S(1)} %get-tuple-element.27.r0.s0, f32[3,2,256,256]{3,2,1,0:T(8,128)S(1)} %shard_map.97.u_ref), custom_call_target="tpu_custom_call" | custom-call | flops 1310720 | bytes 3428352 | tf_op jit(solution)/shard_map/pallas_call | solution.py:22
  (13 shorter events, 0.1 us)
Async XLA Ops:
  1.3 0.9 copy-start.4
  2.2 7.4 %collective-permute-start.1 = (f32[8,64,128]{2,1,0:T(8,128)S(1)}, f32[8,64,128]{2,1,0:T(8,128)S(1)}, u32[]{:S(2)}, u32[]{:S(2)}) collective-permute-start(f32[8,64,128]{2,1,0:T(8,128)S(1)} %shard_map.87.x0.x_ref), channel_id=1, source_target_pairs={{1,2},{2,1},{0,4},{3,7},{5,6},{6,5},{4,0},{7,3},{9,10},{10,9},{8,1... | collective-permute-start | bytes 786440 | tf_op jit(solution)/shard_map/ppermute | solution.py:320
  5.3 4.4 %collective-permute-start = (f32[8,64,128]{2,1,0:T(8,128)S(1)}, f32[8,64,128]{2,1,0:T(8,128)S(1)}, u32[]{:S(2)}, u32[]{:S(2)}) collective-permute-start(f32[8,64,128]{2,1,0:T(8,128)S(1)} %shard_map.87.x0.x_ref), channel_id=1, source_target_pairs={{0,1},{1,0},{2,3},{3,2},{4,5},{5,4},{6,7},{7,6},{8,9},{9,8},{10,11... | collective-permute-start | bytes 786440 | tf_op jit(solution)/shard_map/ppermute | solution.py:309
  6.0 0.7 copy-start.5
  9.6 30.3 %copy-start = (bf16[1,256,256]{2,1,0:T(8,128)(2,1)S(1)}, bf16[1,256,256]{2,1,0:T(8,128)(2,1)}, u32[]{:S(2)}) copy-start(bf16[1,256,256]{2,1,0:T(8,128)(2,1)} %diag_ref.3) | copy-start | bytes 393220
  11.4 15.0 %all-to-all-start = ((f32[8,64,128]{2,1,0:T(8,128)}), f32[8,64,128]{2,1,0:T(8,128)S(1)}, u32[]{:S(2)}, u32[]{:S(2)}) async-start(f32[8,64,128]{2,1,0:T(8,128)} %get-tuple-element.21), calls=%async_computation | async-start | bytes 524288 | tf_op jit(solution)/shard_map/all_to_all | solution.py:347
  17.7 3.0 %collective-permute-start.4 = (f32[8,128]{1,0:T(8,128)S(1)}, f32[8,128]{1,0:T(8,128)S(1)}, u32[]{:S(2)}, u32[]{:S(2)}) collective-permute-start(f32[8,128]{1,0:T(8,128)S(1)} %get-tuple-element.22.mine), channel_id=1, source_target_pairs={{0,3},{1,2},{2,1},{3,0},{4,7},{5,6},{6,5},{7,4},{8,11},{9,10},{10,... | collective-permute-start | bytes 12296 | tf_op jit(solution)/shard_map/ppermute | solution.py:338
  17.7 3.7 %collective-permute-start.3 = (f32[8,128]{1,0:T(8,128)S(1)}, f32[8,128]{1,0:T(8,128)S(1)}, u32[]{:S(2)}, u32[]{:S(2)}) collective-permute-start(f32[8,128]{1,0:T(8,128)S(1)} %get-tuple-element.22.mine), channel_id=1, source_target_pairs={{0,2},{1,3},{2,0},{3,1},{4,6},{5,7},{6,4},{7,5},{8,10},{9,11},{10,... | collective-permute-start | bytes 12296 | tf_op jit(solution)/shard_map/ppermute | solution.py:338
  18.7 2.7 %collective-permute-start.2 = (f32[8,128]{1,0:T(8,128)S(1)}, f32[8,128]{1,0:T(8,128)S(1)}, u32[]{:S(2)}, u32[]{:S(2)}) collective-permute-start(f32[8,128]{1,0:T(8,128)S(1)} %get-tuple-element.22.mine), channel_id=1, source_target_pairs={{0,1},{1,0},{2,3},{3,2},{4,5},{5,4},{6,7},{7,6},{8,9},{9,8},{10,11... | collective-permute-start | bytes 12296 | tf_op jit(solution)/shard_map/ppermute | solution.py:338
  40.1 6.4 %collective-permute-start.6 = (f32[8,64,128]{2,1,0:T(8,128)S(1)}, f32[8,64,128]{2,1,0:T(8,128)S(1)}, u32[]{:S(2)}, u32[]{:S(2)}) collective-permute-start(f32[8,64,128]{2,1,0:T(8,128)S(1)} %get-tuple-element.23.r0.r_in), channel_id=1, source_target_pairs={{1,2},{2,1},{0,4},{3,7},{5,6},{6,5},{4,0},{7,3},{9,10},{10,9},{8,1... | collective-permute-start | bytes 786440 | tf_op jit(solution)/shard_map/ppermute | solution.py:320
  40.9 5.7 %collective-permute-start.5 = (f32[8,64,128]{2,1,0:T(8,128)S(1)}, f32[8,64,128]{2,1,0:T(8,128)S(1)}, u32[]{:S(2)}, u32[]{:S(2)}) collective-permute-start(f32[8,64,128]{2,1,0:T(8,128)S(1)} %get-tuple-element.23.r0.r_in), channel_id=1, source_target_pairs={{0,1},{1,0},{2,3},{3,2},{4,5},{5,4},{6,7},{7,6},{8,9},{9,8},{10,11... | collective-permute-start | bytes 786440 | tf_op jit(solution)/shard_map/ppermute | solution.py:309
  48.7 11.8 %all-to-all-start.2 = ((f32[8,64,128]{2,1,0:T(8,128)}), f32[8,64,128]{2,1,0:T(8,128)S(1)}, u32[]{:S(2)}, u32[]{:S(2)}) async-start(f32[8,64,128]{2,1,0:T(8,128)} %get-tuple-element.24), calls=%async_computation.2 | async-start | bytes 524288 | tf_op jit(solution)/shard_map/all_to_all | solution.py:347
  52.1 3.1 %collective-permute-start.9 = (f32[8,128]{1,0:T(8,128)S(1)}, f32[8,128]{1,0:T(8,128)S(1)}, u32[]{:S(2)}, u32[]{:S(2)}) collective-permute-start(f32[8,128]{1,0:T(8,128)S(1)} %get-tuple-element.25.mine), channel_id=1, source_target_pairs={{0,3},{1,2},{2,1},{3,0},{4,7},{5,6},{6,5},{7,4},{8,11},{9,10},{10,... | collective-permute-start | bytes 12296 | tf_op jit(solution)/shard_map/ppermute | solution.py:338
  52.2 3.7 %collective-permute-start.8 = (f32[8,128]{1,0:T(8,128)S(1)}, f32[8,128]{1,0:T(8,128)S(1)}, u32[]{:S(2)}, u32[]{:S(2)}) collective-permute-start(f32[8,128]{1,0:T(8,128)S(1)} %get-tuple-element.25.mine), channel_id=1, source_target_pairs={{0,2},{1,3},{2,0},{3,1},{4,6},{5,7},{6,4},{7,5},{8,10},{9,11},{10,... | collective-permute-start | bytes 12296 | tf_op jit(solution)/shard_map/ppermute | solution.py:338
  52.8 3.1 %collective-permute-start.7 = (f32[8,128]{1,0:T(8,128)S(1)}, f32[8,128]{1,0:T(8,128)S(1)}, u32[]{:S(2)}, u32[]{:S(2)}) collective-permute-start(f32[8,128]{1,0:T(8,128)S(1)} %get-tuple-element.25.mine), channel_id=1, source_target_pairs={{0,1},{1,0},{2,3},{3,2},{4,5},{5,4},{6,7},{7,6},{8,9},{9,8},{10,11... | collective-permute-start | bytes 12296 | tf_op jit(solution)/shard_map/ppermute | solution.py:338
  60.5 14.5 %copy-start.1 = (f32[2,256,256]{2,1,0:T(8,128)S(1)}, f32[2,256,256]{2,1,0:T(8,128)}, u32[]{:S(2)}) copy-start(f32[2,256,256]{2,1,0:T(8,128)} %get-tuple-element.32.b_ref) | copy-start | bytes 1572868
  74.2 6.4 %collective-permute-start.11 = (f32[8,64,128]{2,1,0:T(8,128)S(1)}, f32[8,64,128]{2,1,0:T(8,128)S(1)}, u32[]{:S(2)}, u32[]{:S(2)}) collective-permute-start(f32[8,64,128]{2,1,0:T(8,128)S(1)} %get-tuple-element.27.r0.s0), channel_id=1, source_target_pairs={{1,2},{2,1},{0,4},{3,7},{5,6},{6,5},{4,0},{7,3},{9,10},{10,9},{8,1... | collective-permute-start | bytes 786440 | tf_op jit(solution)/shard_map/ppermute | solution.py:320
  75.0 5.7 %collective-permute-start.10 = (f32[8,64,128]{2,1,0:T(8,128)S(1)}, f32[8,64,128]{2,1,0:T(8,128)S(1)}, u32[]{:S(2)}, u32[]{:S(2)}) collective-permute-start(f32[8,64,128]{2,1,0:T(8,128)S(1)} %get-tuple-element.27.r0.s0), channel_id=1, source_target_pairs={{0,1},{1,0},{2,3},{3,2},{4,5},{5,4},{6,7},{7,6},{8,9},{9,8},{10,11... | collective-permute-start | bytes 786440 | tf_op jit(solution)/shard_map/ppermute | solution.py:309
  75.2 10.5 %collective-permute-start.12 = (f32[3,256,256]{2,1,0:T(8,128)S(1)}, f32[3,256,256]{2,1,0:T(8,128)}, u32[]{:S(2)}, u32[]{:S(2)}) collective-permute-start(f32[3,256,256]{2,1,0:T(8,128)S(1)} %shard_map.96.b_ref), channel_id=1, source_target_pairs={{0,1},{1,0},{2,3},{3,2},{4,5},{5,4},{6,7},{7,6},{8,9},{9,8},{10,11... | collective-permute-start | bytes 2359304 | tf_op jit(solution)/shard_map/ppermute | solution.py:309
  81.1 3.7 %collective-permute-start.13 = (f32[2,256,256]{2,1,0:T(8,128)S(1)}, f32[2,256,256]{2,1,0:T(8,128)S(1)}, u32[]{:S(2)}, u32[]{:S(2)}) collective-permute-start(f32[2,256,256]{2,1,0:T(8,128)S(1)} %shard_map.94.m_ref), channel_id=1, source_target_pairs={{0,1},{1,0},{2,3},{3,2},{4,5},{5,4},{6,7},{7,6},{8,9},{9,8},{10,11... | collective-permute-start | bytes 1572872 | tf_op jit(solution)/shard_map/ppermute | solution.py:309
  82.3 9.7 %all-to-all-start.4 = ((f32[32,1,128]{2,1,0:T(1,128)}), f32[32,1,128]{2,1,0:T(1,128)S(1)}, u32[]{:S(2)}, u32[]{:S(2)}) async-start(f32[32,1,128]{2,1,0:T(1,128)} %bitcast.2), calls=%async_computation.4 | async-start | bytes 32768 | tf_op jit(solution)/shard_map/all_to_all | solution.py:418
  84.9 0.8 copy-start.2
  85.7 1.0 %copy-start.3 = (f32[2,256,256]{2,1,0:T(8,128)S(1)}, f32[2,256,256]{2,1,0:T(8,128)}, u32[]{:S(2)}) copy-start(f32[2,256,256]{2,1,0:T(8,128)} %copy-done.2) | copy-start | bytes 1572868

commit v11 on v10

--- a/solution.py
+++ b/solution.py
@@ -132,9 +132,11 @@
     return on_x, on_r, theta, xx
 
 
-def start_body(size_ref, psi_ref, x_ref):
+def start_body(size_ref, psi_ref, x_ref, q_ref):
     live = mask(size_ref[0], psi_ref.shape[1])
     pack(x_ref, (), x_ref.shape, jnp.where(live, psi_ref[0].astype(F32), 0.0))
+    x = x_ref[lax.axis_index("ops")]
+    q_ref[...] = tile([rows(x * x)])
 
 
 def split_pairs(left_ref, right_ref, lcat_ref, rcat_ref, left, right, sem):
@@ -184,11 +186,13 @@
     return y_ref[...]
 
 
-def first_body(size_ref, slot_ref, x0, x1, x2, lcat_ref, rcat_ref, y_ref, m_ref, part_ref):
+def first_body(
+    size_ref, slot_ref, x0, x1, x2, q_ref, p_ref, lcat_ref, rcat_ref, y_ref, m_ref, part_ref
+):
     mixed = mix_all(slot_ref, (x0, x1, x2), lcat_ref, m_ref)
     y = fold_all(size_ref, mixed, rcat_ref, y_ref)
-    x = x0[lax.axis_index("ops")]
-    part_ref[...] = tile([rows(x * x), rows(x0[...] * y)])
+    squares = 0.5 * (q_ref[0:1] + p_ref[0:1])
+    part_ref[...] = tile([squares, rows(x0[...] * y)])
 
 
 def five(x0, r0, h0, y):
@@ -318,6 +322,11 @@
         if groups % 2 == 0:
             route += [(o * count + i, (o ^ 1) * count + i) for i in (0, count - 1)]
     return lax.ppermute(value, ("ops", "sec"), route)
+
+
+def across(value):
+    count = lax.axis_size("ops")
+    return lax.ppermute(value, "ops", [(i, (i + count // 2) % count) for i in range(count)])
 
 
 def last_step(count):
@@ -372,8 +381,9 @@
         )
         return exchange(full)
 
-    (x0,) = call(start_body, (block,), [SMEM, VMEM], [], light, sector_states, psi_guess)
+    x0, q = call(start_body, (block, small), [SMEM, VMEM], [], light, sector_states, psi_guess)
     x2, x1 = other(x0), paired(x0)
+    p = across(q)
     lcat, rcat, flag, slots = call(
         split_body, (pieces, pieces, small, jax.ShapeDtypeStruct((pairs, 8, LANES), F32)),
         [SMEM] + [ANY] * 3,
@@ -381,8 +391,8 @@
         light * pairs, new_sector, couple, left_ops, right_ops, limit=52.5,
     )
     y, mx, part = call(
-        first_body, (block, inner, small), [SMEM] + [VMEM] * 6, [], work,
-        sector_states, slots, x0, x1, x2, lcat, rcat,
+        first_body, (block, inner, small), [SMEM] + [VMEM] * 8, [], work,
+        sector_states, slots, x0, x1, x2, q, p, lcat, rcat,
     )
     g = gathered(y, part)
     r0, c = call(

time: 93.9 us -> 93.9 us (level)
  starting transfers between devices: 21.7 us -> 23.2 us
  waiting for transfers between devices: 28.1 us -> 26.6 us
    ppermute x0 -> x1, starting transfers between devices: none -> 2.59 us  [across(): lax.ppermute(value, 'ops', [(i, (i + count // 2) % count) for i in range(...]
    ppermute x3, waiting for transfers between devices: 11.8 us -> 10.3 us  [other(): return lax.ppermute(value, ('ops', 'sec'), route)]
    all_to_all x2, starting transfers between devices: 9.76 us -> 8.61 us  [exchange(): return lax.all_to_all(value, 'ops', 0, 0)]
  transfers between devices with their start and end apart: 17 -> 18, of which waited for: 10 -> 9; matrix products, arithmetic and copies ran while one was open for 0% -> 0% of each run, Pallas kernels for 6% -> 6%
where the time goes in v11:
time: 93.9 us; the launch traced here: 93.3 us
  blocking collectives  26.7 us (28%)
  waiting for transfers between devices  26.6 us (28%)
  starting transfers between devices  23.2 us (25%)
  Pallas kernels  11.3 us (12%)
  local copies, waits for them, and re-layouts  3.39 us (4%)
  between operations  2.1 us (2%)
    all_to_all x2, blocking collectives, exchange(): return lax.all_to_all(value, 'ops', 0, 0)  26.7 us
    pallas_call x13, Pallas kernels, call(): pl.pallas_call(body, out_shape=tuple((pltpu.HBM(o.shape, o.dtype) if k in...  11.3 us
    ppermute x3, waiting for transfers between devices, other(): return lax.ppermute(value, ('ops', 'sec'), route)  10.3 us
    all_to_all x2, waiting for transfers between devices, exchange(): return lax.all_to_all(value, 'ops', 0, 0)  9.64 us
    all_to_all x2, starting transfers between devices, exchange(): return lax.all_to_all(value, 'ops', 0, 0)  8.61 us
    ppermute x3, starting transfers between devices, other(): return lax.ppermute(value, ('ops', 'sec'), route)  4.55 us
    ppermute x6, starting transfers between devices, over_sectors(): found.append(lax.ppermute(value, 'sec', route))  3.77 us
    ppermute x6, waiting for transfers between devices, over_sectors(): found.append(lax.ppermute(value, 'sec', route))  3.67 us
  transfers between devices with their start and end apart: 18, of which 9 were waited for; matrix products, arithmetic and copies ran while one was open for 0% of the time, Pallas kernels for 6%

profile of v11, /device:TPU:0, one launch (start us, length us, event | category | flops | bytes accessed | tf_op | source)
XLA Modules:
  0.0 93.3 jit_solution(614540847921762599)
XLA Ops:
  1.3 0.9 copy-done.4
  2.2 0.1 shard_map.87
  2.2 3.0 %collective-permute-start.1 = (f32[8,64,128]{2,1,0:T(8,128)S(1)}, f32[8,64,128]{2,1,0:T(8,128)S(1)}, u32[]{:S(2)}, u32[]{:S(2)}) collective-permute-start(f32[8,64,128]{2,1,0:T(8,128)S(1)} %get-tuple-element.21.x0.x_ref), channel_id=1, source_target_pairs={{1,2},{2,1},{0,4},{3,7},{5,6},{6,5},{4,0},{7,3},{9,10},{10,9},{8,1... | collective-permute-start | bytes 786440 | tf_op jit(solution)/shard_map/ppermute | solution.py:324
  5.3 0.1 collective-permute-start
  5.4 2.6 %collective-permute-start.2 = (f32[8,128]{1,0:T(8,128)S(1)}, f32[8,128]{1,0:T(8,128)S(1)}, u32[]{:S(2)}, u32[]{:S(2)}) collective-permute-start(f32[8,128]{1,0:T(8,128)S(1)} %get-tuple-element.22.q_ref), channel_id=1, source_target_pairs={{0,16},{4,20},{8,24},{12,28},{16,0},{20,4},{24,8},{28,12},{1,17},{... | collective-permute-start | bytes 12296 | tf_op jit(solution)/shard_map/ppermute | solution.py:329
  8.6 0.0 copy-start.5
  8.7 0.6 copy-done.5
  9.3 1.4 %shard_map.86 = (bf16[2,2,256,256]{3,2,1,0:T(8,128)(2,1)S(1)}, bf16[2,2,256,256]{3,2,1,0:T(8,128)(2,1)S(1)}, f32[8,128]{1,0:T(8,128)S(1)}, f32[2,8,128]{2,1,0:T(8,128)S(1)}) custom-call(s32[1]{0:T(128)S(6)} %copy.11.label_ref, s32[2]{0:T(128)S(1)} %bitcast.6, f32[2,1,256,256]{3,2,1,0:T(8,128)} %left_ref.1, f32[2,1,256,256]{3,2,1,0:T(8,128)} %right_ref.1), custom_call_target="tpu_custom_call" | custom-call | flops 2621440 | bytes 2109452 | tf_op jit(solution)/shard_map/pallas_call | solution.py:22
  10.7 0.0 collective-permute-done.2.p_ref
  10.7 0.0 collective-permute-done.x1
  10.8 0.0 copy-start
  10.8 1.8 %shard_map.88 = (f32[8,64,128]{2,1,0:T(8,128)}, f32[2,256,256]{2,1,0:T(8,128)S(1)}, f32[8,128]{1,0:T(8,128)S(1)}) custom-call(s32[1]{0:T(128)S(6)} %copy.10.size_ref, f32[2,8,128]{2,1,0:T(8,128)S(1)} %get-tuple-element.20.slot_ref, f32[8,64,128]{2,1,0:T(8,128)S(1)} %get-tuple-element.21.x0.x_ref, f32[8,64,128]{2,1,0:T(8,128)S(1)} %collective-permute-done.x1, ...), custom_call_target="tpu_custom_call" | custom-call | flops 402653184 | bytes 2641924 | tf_op jit(solution)/shard_map/pallas_call | solution.py:22
  12.5 5.2 %all-to-all-start = ((f32[8,64,128]{2,1,0:T(8,128)}), f32[8,64,128]{2,1,0:T(8,128)S(1)}, u32[]{:S(2)}, u32[]{:S(2)}) async-start(f32[8,64,128]{2,1,0:T(8,128)} %get-tuple-element.25), calls=%async_computation | async-start | bytes 524288 | tf_op jit(solution)/shard_map/all_to_all | solution.py:356
  17.7 0.0 collective-permute-start.5
  17.7 1.0 %collective-permute-start.4 = (f32[8,128]{1,0:T(8,128)S(1)}, f32[8,128]{1,0:T(8,128)S(1)}, u32[]{:S(2)}, u32[]{:S(2)}) collective-permute-start(f32[8,128]{1,0:T(8,128)S(1)} %get-tuple-element.26.mine), channel_id=1, source_target_pairs={{0,2},{1,3},{2,0},{3,1},{4,6},{5,7},{6,4},{7,5},{8,10},{9,11},{10,... | collective-permute-start | bytes 12296 | tf_op jit(solution)/shard_map/ppermute | solution.py:347
  18.7 0.8 collective-permute-start.3
  19.6 1.2 %collective-permute-done.5.refs_2_ = f32[8,128]{1,0:T(8,128)S(1)} collective-permute-done((f32[8,128]{1,0:T(8,128)S(1)}, f32[8,128]{1,0:T(8,128)S(1)}, u32[]{:S(2)}, u32[]{:S(2)}) %collective-permute-start.5) | collective-permute-done | bytes 4128 | tf_op jit(solution)/shard_map/ppermute | solution.py:347
  20.8 0.7 collective-permute-done.4.refs_1_
  21.4 5.0 %all-to-all-done.terms_ref = f32[8,64,128]{2,1,0:T(8,128)S(1)} async-done(((f32[8,64,128]{2,1,0:T(8,128)}), f32[8,64,128]{2,1,0:T(8,128)S(1)}, u32[]{:S(2)}, u32[]{:S(2)}) %all-to-all-start) | async-done | bytes 262176 | tf_op jit(solution)/shard_map/all_to_all | solution.py:356
  26.5 13.4 %all_to_all.31.g_ref.g0 = f32[8,72,128]{2,1,0:T(8,128)S(1)} all-to-all(f32[8,72,128]{2,1,0:T(8,128)S(1)} %shard_map.89), channel_id=1, replica_groups=mesh['ops'=8,'sec'=4] {'ops'}, dimensions={0} | all-to-all | bytes 589824 | tf_op jit(solution)/shard_map/all_to_all | solution.py:356
  39.9 0.2 shard_map.90
  40.1 0.8 collective-permute-start.7
  40.9 0.3 collective-permute-start.6
  41.2 5.4 %collective-permute-done.7.r2 = f32[8,64,128]{2,1,0:T(8,128)S(1)} collective-permute-done((f32[8,64,128]{2,1,0:T(8,128)S(1)}, f32[8,64,128]{2,1,0:T(8,128)S(1)}, u32[]{:S(2)}, u32[]{:S(2)}) %collective-permute-start.7) | collective-permute-done | bytes 262176 | tf_op jit(solution)/shard_map/ppermute | solution.py:324
  46.6 2.1 %shard_map.91 = (f32[8,64,128]{2,1,0:T(8,128)}, f32[2,256,256]{2,1,0:T(8,128)}, f32[8,128]{1,0:T(8,128)S(1)}) custom-call(s32[1]{0:T(128)S(6)} %copy.10.size_ref, f32[2,8,128]{2,1,0:T(8,128)S(1)} %get-tuple-element.20.slot_ref, f32[8,64,128]{2,1,0:T(8,128)S(1)} %get-tuple-element.27.r0.r_in, f32[8,64,128]{2,1,0:T(8,128)S(1)} %collective-permute-done.6.r1, ...), custom_call_target="tpu_custom_call" | custom-call | flops 402653184 | bytes 3190788 | tf_op jit(solution)/shard_map/pallas_call | solution.py:22
  48.7 3.4 %all-to-all-start.2 = ((f32[8,64,128]{2,1,0:T(8,128)}), f32[8,64,128]{2,1,0:T(8,128)S(1)}, u32[]{:S(2)}, u32[]{:S(2)}) async-start(f32[8,64,128]{2,1,0:T(8,128)} %get-tuple-element.28), calls=%async_computation.2 | async-start | bytes 524288 | tf_op jit(solution)/shard_map/all_to_all | solution.py:356
  52.1 0.1 collective-permute-start.10
  52.2 0.6 collective-permute-start.9
  52.8 1.3 %collective-permute-start.8 = (f32[8,128]{1,0:T(8,128)S(1)}, f32[8,128]{1,0:T(8,128)S(1)}, u32[]{:S(2)}, u32[]{:S(2)}) collective-permute-start(f32[8,128]{1,0:T(8,128)S(1)} %get-tuple-element.29.mine), channel_id=1, source_target_pairs={{0,1},{1,0},{2,3},{3,2},{4,5},{5,4},{6,7},{7,6},{8,9},{9,8},{10,11... | collective-permute-start | bytes 12296 | tf_op jit(solution)/shard_map/ppermute | solution.py:347
  54.1 1.2 %collective-permute-done.10.refs_2_ = f32[8,128]{1,0:T(8,128)S(1)} collective-permute-done((f32[8,128]{1,0:T(8,128)S(1)}, f32[8,128]{1,0:T(8,128)S(1)}, u32[]{:S(2)}, u32[]{:S(2)}) %collective-permute-start.10) | collective-permute-done | bytes 4128 | tf_op jit(solution)/shard_map/ppermute | solution.py:347
  55.2 0.7 collective-permute-done.9.refs_1_
  55.9 4.7 %all-to-all-done.2.terms_ref = f32[8,64,128]{2,1,0:T(8,128)S(1)} async-done(((f32[8,64,128]{2,1,0:T(8,128)}), f32[8,64,128]{2,1,0:T(8,128)S(1)}, u32[]{:S(2)}, u32[]{:S(2)}) %all-to-all-start.2) | async-done | bytes 262176 | tf_op jit(solution)/shard_map/all_to_all | solution.py:356
  60.6 13.3 %all_to_all.32.s_ref = f32[8,72,128]{2,1,0:T(8,128)S(1)} all-to-all(f32[8,72,128]{2,1,0:T(8,128)S(1)} %shard_map.92), channel_id=1, replica_groups=mesh['ops'=8,'sec'=4] {'ops'}, dimensions={0} | all-to-all | bytes 589824 | tf_op jit(solution)/shard_map/all_to_all | solution.py:356
  73.9 0.4 shard_map.93
  74.3 0.8 collective-permute-start.12
  75.0 0.2 shard_map.96.b_ref
  75.2 0.6 collective-permute-start.13
  75.8 4.9 %collective-permute-done.12.r2 = f32[8,64,128]{2,1,0:T(8,128)S(1)} collective-permute-done((f32[8,64,128]{2,1,0:T(8,128)S(1)}, f32[8,64,128]{2,1,0:T(8,128)S(1)}, u32[]{:S(2)}, u32[]{:S(2)}) %collective-permute-start.12) | collective-permute-done | bytes 262176 | tf_op jit(solution)/shard_map/ppermute | solution.py:324
  80.7 0.4 shard_map.94.m_ref
  81.2 0.1 collective-permute-start.14
  81.2 1.1 %shard_map.95 = f32[32,128]{1,0:T(8,128)} custom-call(s32[1]{0:T(128)S(6)} %copy.10.size_ref, f32[2,256,256]{2,1,0:T(8,128)S(1)} %shard_map.94.m_ref, f32[8,64,128]{2,1,0:T(8,128)S(1)} %get-tuple-element.31.r0.s0, f32[8,64,128]{2,1,0:T(8,128)S(1)} %get-tuple-element.32.x0.x_ref, f32[8,64,128]{2,1,0:T(8,128)S(1)} %get-tuple-element.33.h0, ...), custom_call_target="tpu_custom_call" | custom-call | flops 201326592 | bytes 1851396 | tf_op jit(solution)/shard_map/pallas_call | solution.py:22
  82.3 2.5 %all-to-all-start.4 = ((f32[32,1,128]{2,1,0:T(1,128)}), f32[32,1,128]{2,1,0:T(1,128)S(1)}, u32[]{:S(2)}, u32[]{:S(2)}) async-start(f32[32,1,128]{2,1,0:T(1,128)} %bitcast.2), calls=%async_computation.4 | async-start | bytes 32768 | tf_op jit(solution)/shard_map/all_to_all | solution.py:428
  84.9 0.0 copy-start.2
  84.9 0.8 copy-done.2
  85.7 1.0 %copy-done.3 = f32[2,256,256]{2,1,0:T(8,128)S(1)} copy-done((f32[2,256,256]{2,1,0:T(8,128)S(1)}, f32[2,256,256]{2,1,0:T(8,128)}, u32[]{:S(2)}) %copy-start.3) | copy-done | bytes 524312
  86.7 2.3 %shard_map.97.u_ref = f32[3,2,256,256]{3,2,1,0:T(8,128)S(1)} custom-call(f32[8,128]{1,0:T(8,128)S(1)} %get-tuple-element.37.flag_ref, f32[3,256,256]{2,1,0:T(8,128)S(1)} %shard_map.96.b_ref, f32[3,256,256]{2,1,0:T(8,128)} %collective-permute-done.13.n_ref, f32[2,256,256]{2,1,0:T(8,128)S(1)} %shard_map.94.m_ref, f32[2,256,256]{2,1,0:T(8,128)S(1)} %copy-done.3, ...), custom_call_target="tpu_custom_call" | custom-call | flops 402653184 | bytes 4722688 | tf_op jit(solution)/shard_map/pallas_call | solution.py:22
  89.0 3.0 %all-to-all-done.4 = f32[32,1,128]{2,1,0:T(1,128)S(1)} async-done(((f32[32,1,128]{2,1,0:T(1,128)}), f32[32,1,128]{2,1,0:T(1,128)S(1)}, u32[]{:S(2)}, u32[]{:S(2)}) %all-to-all-start.4) | async-done | bytes 16416 | tf_op jit(solution)/shard_map/all_to_all | solution.py:428
  92.0 1.4 %shard_map.98 = (f32[1,256,256]{2,1,0:T(8,128)}, f32[2,1,256,256]{3,2,1,0:T(8,128)}) custom-call(f32[32,128]{1,0:T(8,128)S(1)} %bitcast.5, f32[8,128]{1,0:T(8,128)S(1)} %get-tuple-element.34.c_in, f32[3,256,256]{2,1,0:T(8,128)S(1)} %shard_map.96.b_ref, f32[8,64,128]{2,1,0:T(8,128)S(1)} %get-tuple-element.31.r0.s0, f32[3,2,256,256]{3,2,1,0:T(8,128)S(1)} %shard_map.97.u_ref), custom_call_target="tpu_custom_call" | custom-call | flops 1310720 | bytes 3428352 | tf_op jit(solution)/shard_map/pallas_call | solution.py:22
  (15 shorter events, 0.1 us)
Async XLA Ops:
  1.3 0.9 copy-start.4
  2.2 8.5 %collective-permute-start.1 = (f32[8,64,128]{2,1,0:T(8,128)S(1)}, f32[8,64,128]{2,1,0:T(8,128)S(1)}, u32[]{:S(2)}, u32[]{:S(2)}) collective-permute-start(f32[8,64,128]{2,1,0:T(8,128)S(1)} %get-tuple-element.21.x0.x_ref), channel_id=1, source_target_pairs={{1,2},{2,1},{0,4},{3,7},{5,6},{6,5},{4,0},{7,3},{9,10},{10,9},{8,1... | collective-permute-start | bytes 786440 | tf_op jit(solution)/shard_map/ppermute | solution.py:324
  5.3 5.5 %collective-permute-start = (f32[8,64,128]{2,1,0:T(8,128)S(1)}, f32[8,64,128]{2,1,0:T(8,128)S(1)}, u32[]{:S(2)}, u32[]{:S(2)}) collective-permute-start(f32[8,64,128]{2,1,0:T(8,128)S(1)} %get-tuple-element.21.x0.x_ref), channel_id=1, source_target_pairs={{0,1},{1,0},{2,3},{3,2},{4,5},{5,4},{6,7},{7,6},{8,9},{9,8},{10,11... | collective-permute-start | bytes 786440 | tf_op jit(solution)/shard_map/ppermute | solution.py:313
  5.4 5.3 %collective-permute-start.2 = (f32[8,128]{1,0:T(8,128)S(1)}, f32[8,128]{1,0:T(8,128)S(1)}, u32[]{:S(2)}, u32[]{:S(2)}) collective-permute-start(f32[8,128]{1,0:T(8,128)S(1)} %get-tuple-element.22.q_ref), channel_id=1, source_target_pairs={{0,16},{4,20},{8,24},{12,28},{16,0},{20,4},{24,8},{28,12},{1,17},{... | collective-permute-start | bytes 12296 | tf_op jit(solution)/shard_map/ppermute | solution.py:329
  8.6 0.7 copy-start.5
  10.8 29.1 %copy-start = (bf16[1,256,256]{2,1,0:T(8,128)(2,1)S(1)}, bf16[1,256,256]{2,1,0:T(8,128)(2,1)}, u32[]{:S(2)}) copy-start(bf16[1,256,256]{2,1,0:T(8,128)(2,1)} %diag_ref.3) | copy-start | bytes 393220
  12.5 13.9 %all-to-all-start = ((f32[8,64,128]{2,1,0:T(8,128)}), f32[8,64,128]{2,1,0:T(8,128)S(1)}, u32[]{:S(2)}, u32[]{:S(2)}) async-start(f32[8,64,128]{2,1,0:T(8,128)} %get-tuple-element.25), calls=%async_computation | async-start | bytes 524288 | tf_op jit(solution)/shard_map/all_to_all | solution.py:356
  17.7 3.0 %collective-permute-start.5 = (f32[8,128]{1,0:T(8,128)S(1)}, f32[8,128]{1,0:T(8,128)S(1)}, u32[]{:S(2)}, u32[]{:S(2)}) collective-permute-start(f32[8,128]{1,0:T(8,128)S(1)} %get-tuple-element.26.mine), channel_id=1, source_target_pairs={{0,3},{1,2},{2,1},{3,0},{4,7},{5,6},{6,5},{7,4},{8,11},{9,10},{10,... | collective-permute-start | bytes 12296 | tf_op jit(solution)/shard_map/ppermute | solution.py:347
  17.7 3.7 %collective-permute-start.4 = (f32[8,128]{1,0:T(8,128)S(1)}, f32[8,128]{1,0:T(8,128)S(1)}, u32[]{:S(2)}, u32[]{:S(2)}) collective-permute-start(f32[8,128]{1,0:T(8,128)S(1)} %get-tuple-element.26.mine), channel_id=1, source_target_pairs={{0,2},{1,3},{2,0},{3,1},{4,6},{5,7},{6,4},{7,5},{8,10},{9,11},{10,... | collective-permute-start | bytes 12296 | tf_op jit(solution)/shard_map/ppermute | solution.py:347
  18.7 2.7 %collective-permute-start.3 = (f32[8,128]{1,0:T(8,128)S(1)}, f32[8,128]{1,0:T(8,128)S(1)}, u32[]{:S(2)}, u32[]{:S(2)}) collective-permute-start(f32[8,128]{1,0:T(8,128)S(1)} %get-tuple-element.26.mine), channel_id=1, source_target_pairs={{0,1},{1,0},{2,3},{3,2},{4,5},{5,4},{6,7},{7,6},{8,9},{9,8},{10,11... | collective-permute-start | bytes 12296 | tf_op jit(solution)/shard_map/ppermute | solution.py:347
  40.1 6.4 %collective-permute-start.7 = (f32[8,64,128]{2,1,0:T(8,128)S(1)}, f32[8,64,128]{2,1,0:T(8,128)S(1)}, u32[]{:S(2)}, u32[]{:S(2)}) collective-permute-start(f32[8,64,128]{2,1,0:T(8,128)S(1)} %get-tuple-element.27.r0.r_in), channel_id=1, source_target_pairs={{1,2},{2,1},{0,4},{3,7},{5,6},{6,5},{4,0},{7,3},{9,10},{10,9},{8,1... | collective-permute-start | bytes 786440 | tf_op jit(solution)/shard_map/ppermute | solution.py:324
  40.9 5.7 %collective-permute-start.6 = (f32[8,64,128]{2,1,0:T(8,128)S(1)}, f32[8,64,128]{2,1,0:T(8,128)S(1)}, u32[]{:S(2)}, u32[]{:S(2)}) collective-permute-start(f32[8,64,128]{2,1,0:T(8,128)S(1)} %get-tuple-element.27.r0.r_in), channel_id=1, source_target_pairs={{0,1},{1,0},{2,3},{3,2},{4,5},{5,4},{6,7},{7,6},{8,9},{9,8},{10,11... | collective-permute-start | bytes 786440 | tf_op jit(solution)/shard_map/ppermute | solution.py:313
  48.7 11.8 %all-to-all-start.2 = ((f32[8,64,128]{2,1,0:T(8,128)}), f32[8,64,128]{2,1,0:T(8,128)S(1)}, u32[]{:S(2)}, u32[]{:S(2)}) async-start(f32[8,64,128]{2,1,0:T(8,128)} %get-tuple-element.28), calls=%async_computation.2 | async-start | bytes 524288 | tf_op jit(solution)/shard_map/all_to_all | solution.py:356
  52.1 3.1 %collective-permute-start.10 = (f32[8,128]{1,0:T(8,128)S(1)}, f32[8,128]{1,0:T(8,128)S(1)}, u32[]{:S(2)}, u32[]{:S(2)}) collective-permute-start(f32[8,128]{1,0:T(8,128)S(1)} %get-tuple-element.29.mine), channel_id=1, source_target_pairs={{0,3},{1,2},{2,1},{3,0},{4,7},{5,6},{6,5},{7,4},{8,11},{9,10},{10,... | collective-permute-start | bytes 12296 | tf_op jit(solution)/shard_map/ppermute | solution.py:347
  52.2 3.7 %collective-permute-start.9 = (f32[8,128]{1,0:T(8,128)S(1)}, f32[8,128]{1,0:T(8,128)S(1)}, u32[]{:S(2)}, u32[]{:S(2)}) collective-permute-start(f32[8,128]{1,0:T(8,128)S(1)} %get-tuple-element.29.mine), channel_id=1, source_target_pairs={{0,2},{1,3},{2,0},{3,1},{4,6},{5,7},{6,4},{7,5},{8,10},{9,11},{10,... | collective-permute-start | bytes 12296 | tf_op jit(solution)/shard_map/ppermute | solution.py:347
  52.8 3.1 %collective-permute-start.8 = (f32[8,128]{1,0:T(8,128)S(1)}, f32[8,128]{1,0:T(8,128)S(1)}, u32[]{:S(2)}, u32[]{:S(2)}) collective-permute-start(f32[8,128]{1,0:T(8,128)S(1)} %get-tuple-element.29.mine), channel_id=1, source_target_pairs={{0,1},{1,0},{2,3},{3,2},{4,5},{5,4},{6,7},{7,6},{8,9},{9,8},{10,11... | collective-permute-start | bytes 12296 | tf_op jit(solution)/shard_map/ppermute | solution.py:347
  60.5 14.5 %copy-start.1 = (f32[2,256,256]{2,1,0:T(8,128)S(1)}, f32[2,256,256]{2,1,0:T(8,128)}, u32[]{:S(2)}) copy-start(f32[2,256,256]{2,1,0:T(8,128)} %get-tuple-element.36.b_ref) | copy-start | bytes 1572868
  74.3 6.4 %collective-permute-start.12 = (f32[8,64,128]{2,1,0:T(8,128)S(1)}, f32[8,64,128]{2,1,0:T(8,128)S(1)}, u32[]{:S(2)}, u32[]{:S(2)}) collective-permute-start(f32[8,64,128]{2,1,0:T(8,128)S(1)} %get-tuple-element.31.r0.s0), channel_id=1, source_target_pairs={{1,2},{2,1},{0,4},{3,7},{5,6},{6,5},{4,0},{7,3},{9,10},{10,9},{8,1... | collective-permute-start | bytes 786440 | tf_op jit(solution)/shard_map/ppermute | solution.py:324
  75.0 5.7 %collective-permute-start.11 = (f32[8,64,128]{2,1,0:T(8,128)S(1)}, f32[8,64,128]{2,1,0:T(8,128)S(1)}, u32[]{:S(2)}, u32[]{:S(2)}) collective-permute-start(f32[8,64,128]{2,1,0:T(8,128)S(1)} %get-tuple-element.31.r0.s0), channel_id=1, source_target_pairs={{0,1},{1,0},{2,3},{3,2},{4,5},{5,4},{6,7},{7,6},{8,9},{9,8},{10,11... | collective-permute-start | bytes 786440 | tf_op jit(solution)/shard_map/ppermute | solution.py:313
  75.2 10.5 %collective-permute-start.13 = (f32[3,256,256]{2,1,0:T(8,128)S(1)}, f32[3,256,256]{2,1,0:T(8,128)}, u32[]{:S(2)}, u32[]{:S(2)}) collective-permute-start(f32[3,256,256]{2,1,0:T(8,128)S(1)} %shard_map.96.b_ref), channel_id=1, source_target_pairs={{0,1},{1,0},{2,3},{3,2},{4,5},{5,4},{6,7},{7,6},{8,9},{9,8},{10,11... | collective-permute-start | bytes 2359304 | tf_op jit(solution)/shard_map/ppermute | solution.py:313
  81.2 3.7 %collective-permute-start.14 = (f32[2,256,256]{2,1,0:T(8,128)S(1)}, f32[2,256,256]{2,1,0:T(8,128)S(1)}, u32[]{:S(2)}, u32[]{:S(2)}) collective-permute-start(f32[2,256,256]{2,1,0:T(8,128)S(1)} %shard_map.94.m_ref), channel_id=1, source_target_pairs={{0,1},{1,0},{2,3},{3,2},{4,5},{5,4},{6,7},{7,6},{8,9},{9,8},{10,11... | collective-permute-start | bytes 1572872 | tf_op jit(solution)/shard_map/ppermute | solution.py:313
  82.3 9.7 %all-to-all-start.4 = ((f32[32,1,128]{2,1,0:T(1,128)}), f32[32,1,128]{2,1,0:T(1,128)S(1)}, u32[]{:S(2)}, u32[]{:S(2)}) async-start(f32[32,1,128]{2,1,0:T(1,128)} %bitcast.2), calls=%async_computation.4 | async-start | bytes 32768 | tf_op jit(solution)/shard_map/all_to_all | solution.py:428
  84.9 0.8 copy-start.2
  85.7 1.0 %copy-start.3 = (f32[2,256,256]{2,1,0:T(8,128)S(1)}, f32[2,256,256]{2,1,0:T(8,128)}, u32[]{:S(2)}) copy-start(f32[2,256,256]{2,1,0:T(8,128)} %copy-done.2) | copy-start | bytes 1572868

commit v12 on v10

--- a/solution.py
+++ b/solution.py
@@ -309,13 +309,13 @@
     return lax.ppermute(value, "sec", [(i, i ^ 1) for i in range(count)])
 
 
-def other(value):
+def other(value, stage):
     count, groups = lax.axis_size("sec"), lax.axis_size("ops")
     route = []
     for o in range(groups):
         for i in range(1, count - 1, 2):
             route += [(o * count + i, o * count + i + 1), (o * count + i + 1, o * count + i)]
-        if groups % 2 == 0:
+        if groups % 2 == 0 and stage < 2:
             route += [(o * count + i, (o ^ 1) * count + i) for i in (0, count - 1)]
     return lax.ppermute(value, ("ops", "sec"), route)
 
@@ -373,7 +373,7 @@
         return exchange(full)
 
     (x0,) = call(start_body, (block,), [SMEM, VMEM], [], light, sector_states, psi_guess)
-    x2, x1 = other(x0), paired(x0)
+    x2, x1 = other(x0, 0), paired(x0)
     lcat, rcat, flag, slots = call(
         split_body, (pieces, pieces, small, jax.ShapeDtypeStruct((pairs, 8, LANES), F32)),
         [SMEM] + [ANY] * 3,
@@ -389,7 +389,7 @@
         first_residual_body, (block, small), [VMEM] * 3, [pltpu.VMEM(block.shape, F32)], light,
         g, x0, precond_diag,
     )
-    r2, r1 = other(r0), paired(r0)
+    r2, r1 = other(r0, 1), paired(r0)
     y, mr, part = call(
         second_body, (block, inner, small), [SMEM] + [VMEM] * 8, room, work,
         sector_states, slots, r0, r1, r2, x0, g, lcat, rcat, away=(1,),
@@ -399,7 +399,7 @@
         second_residual_body, (block, block, block, small), [VMEM] * 6,
         [pltpu.VMEM(block.shape, F32)], light, s, g, x0, precond_diag, r0, c,
     )
-    s2, s1 = other(s0), paired(s0)
+    s2, s1 = other(s0, 2), paired(s0)
     (mx,) = call(
         blend_body, (jax.ShapeDtypeStruct((pairs + 1, side, side), F32),), [VMEM] * 4, [],
         light, c, mx, mr, x,

time: 93.9 us -> 93.9 us (level)
  starting transfers between devices: 21.7 us -> 25.8 us
  waiting for transfers between devices: 28.1 us -> 24.1 us
    ppermute x3, waiting for transfers between devices: 11.8 us -> 6.87 us  [other(): return lax.ppermute(value, ('ops', 'sec'), route)]
    ppermute x5, starting transfers between devices: 1.08 us -> 4.43 us  [paired(): return lax.ppermute(value, 'sec', [(i, i ^ 1) for i in range(count)])]
where the time goes in v12:
time: 93.9 us; the launch traced here: 93.3 us
  blocking collectives  26.7 us (28%)
  starting transfers between devices  25.8 us (27%)
  waiting for transfers between devices  24.1 us (26%)
  Pallas kernels  11.3 us (12%)
  local copies, waits for them, and re-layouts  3.39 us (4%)
  between operations  2.07 us (2%)
    all_to_all x2, blocking collectives, exchange(): return lax.all_to_all(value, 'ops', 0, 0)  26.7 us
    pallas_call x13, Pallas kernels, call(): pl.pallas_call(body, out_shape=tuple((pltpu.HBM(o.shape, o.dtype) if k in...  11.3 us
    all_to_all x2, starting transfers between devices, exchange(): return lax.all_to_all(value, 'ops', 0, 0)  9.76 us
    all_to_all x2, waiting for transfers between devices, exchange(): return lax.all_to_all(value, 'ops', 0, 0)  9.64 us
    ppermute x3, waiting for transfers between devices, other(): return lax.ppermute(value, ('ops', 'sec'), route)  6.87 us
    ppermute x3, starting transfers between devices, other(): return lax.ppermute(value, ('ops', 'sec'), route)  4.47 us
    ppermute x5, starting transfers between devices, paired(): return lax.ppermute(value, 'sec', [(i, i ^ 1) for i in range(count)])  4.43 us
    ppermute x6, starting transfers between devices, over_sectors(): found.append(lax.ppermute(value, 'sec', route))  3.77 us
  transfers between devices with their start and end apart: 17, of which 10 were waited for; matrix products, arithmetic and copies ran while one was open for 0% of the time, Pallas kernels for 6%

profile of v12, /device:TPU:0, one launch (start us, length us, event | category | flops | bytes accessed | tf_op | source)
XLA Modules:
  0.0 93.3 jit_solution(18220894132943560466)
XLA Ops:
  1.3 0.9 copy-done.4
  2.2 3.0 %collective-permute-start.1 = (f32[8,64,128]{2,1,0:T(8,128)S(1)}, f32[8,64,128]{2,1,0:T(8,128)S(1)}, u32[]{:S(2)}, u32[]{:S(2)}) collective-permute-start(f32[8,64,128]{2,1,0:T(8,128)S(1)} %shard_map.87.x0.x_ref), channel_id=1, source_target_pairs={{1,2},{2,1},{0,4},{3,7},{5,6},{6,5},{4,0},{7,3},{9,10},{10,9},{8,1... | collective-permute-start | bytes 786440 | tf_op jit(solution)/shard_map/ppermute | solution.py:320
  5.3 0.1 collective-permute-start
  6.0 0.0 copy-start.5
  6.1 0.6 copy-done.5
  6.7 1.4 %shard_map.86 = (bf16[2,2,256,256]{3,2,1,0:T(8,128)(2,1)S(1)}, bf16[2,2,256,256]{3,2,1,0:T(8,128)(2,1)S(1)}, f32[8,128]{1,0:T(8,128)S(1)}, f32[2,8,128]{2,1,0:T(8,128)S(1)}) custom-call(s32[1]{0:T(128)S(6)} %copy.11.label_ref, s32[2]{0:T(128)S(1)} %bitcast.6, f32[2,1,256,256]{3,2,1,0:T(8,128)} %left_ref.1, f32[2,1,256,256]{3,2,1,0:T(8,128)} %right_ref.1), custom_call_target="tpu_custom_call" | custom-call | flops 2621440 | bytes 2109452 | tf_op jit(solution)/shard_map/pallas_call | solution.py:22
  8.1 1.5 %collective-permute-done.1.x2 = f32[8,64,128]{2,1,0:T(8,128)S(1)} collective-permute-done((f32[8,64,128]{2,1,0:T(8,128)S(1)}, f32[8,64,128]{2,1,0:T(8,128)S(1)}, u32[]{:S(2)}, u32[]{:S(2)}) %collective-permute-start.1) | collective-permute-done | bytes 262176 | tf_op jit(solution)/shard_map/ppermute | solution.py:320
  9.6 0.0 collective-permute-done.x1
  9.6 1.8 %shard_map.88 = (f32[8,64,128]{2,1,0:T(8,128)}, f32[2,256,256]{2,1,0:T(8,128)S(1)}, f32[8,128]{1,0:T(8,128)S(1)}) custom-call(s32[1]{0:T(128)S(6)} %copy.10.size_ref, f32[2,8,128]{2,1,0:T(8,128)S(1)} %get-tuple-element.18.slot_ref, f32[8,64,128]{2,1,0:T(8,128)S(1)} %shard_map.87.x0.x_ref, f32[8,64,128]{2,1,0:T(8,128)S(1)} %collective-permute-done.x1, ...), custom_call_target="tpu_custom_call" | custom-call | flops 402653184 | bytes 2633732 | tf_op jit(solution)/shard_map/pallas_call | solution.py:22
  11.4 6.3 %all-to-all-start = ((f32[8,64,128]{2,1,0:T(8,128)}), f32[8,64,128]{2,1,0:T(8,128)S(1)}, u32[]{:S(2)}, u32[]{:S(2)}) async-start(f32[8,64,128]{2,1,0:T(8,128)} %get-tuple-element.21), calls=%async_computation | async-start | bytes 524288 | tf_op jit(solution)/shard_map/all_to_all | solution.py:347
  17.7 0.0 collective-permute-start.4
  17.7 1.0 %collective-permute-start.3 = (f32[8,128]{1,0:T(8,128)S(1)}, f32[8,128]{1,0:T(8,128)S(1)}, u32[]{:S(2)}, u32[]{:S(2)}) collective-permute-start(f32[8,128]{1,0:T(8,128)S(1)} %get-tuple-element.22.mine), channel_id=1, source_target_pairs={{0,2},{1,3},{2,0},{3,1},{4,6},{5,7},{6,4},{7,5},{8,10},{9,11},{10,... | collective-permute-start | bytes 12296 | tf_op jit(solution)/shard_map/ppermute | solution.py:338
  18.7 0.8 collective-permute-start.2
  19.6 1.2 %collective-permute-done.4.refs_2_ = f32[8,128]{1,0:T(8,128)S(1)} collective-permute-done((f32[8,128]{1,0:T(8,128)S(1)}, f32[8,128]{1,0:T(8,128)S(1)}, u32[]{:S(2)}, u32[]{:S(2)}) %collective-permute-start.4) | collective-permute-done | bytes 4128 | tf_op jit(solution)/shard_map/ppermute | solution.py:338
  20.7 0.7 collective-permute-done.3.refs_1_
  21.4 0.0 collective-permute-done.2.refs_0_
  21.4 5.0 %all-to-all-done.terms_ref = f32[8,64,128]{2,1,0:T(8,128)S(1)} async-done(((f32[8,64,128]{2,1,0:T(8,128)}), f32[8,64,128]{2,1,0:T(8,128)S(1)}, u32[]{:S(2)}, u32[]{:S(2)}) %all-to-all-start) | async-done | bytes 262176 | tf_op jit(solution)/shard_map/all_to_all | solution.py:347
  26.4 13.4 %all_to_all.31.g_ref.g0 = f32[8,72,128]{2,1,0:T(8,128)S(1)} all-to-all(f32[8,72,128]{2,1,0:T(8,128)S(1)} %shard_map.89), channel_id=1, replica_groups=mesh['ops'=8,'sec'=4] {'ops'}, dimensions={0} | all-to-all | bytes 589824 | tf_op jit(solution)/shard_map/all_to_all | solution.py:347
  39.9 0.2 shard_map.90
  40.1 0.8 collective-permute-start.6
  40.9 0.3 collective-permute-start.5
  41.2 5.4 %collective-permute-done.6.r2 = f32[8,64,128]{2,1,0:T(8,128)S(1)} collective-permute-done((f32[8,64,128]{2,1,0:T(8,128)S(1)}, f32[8,64,128]{2,1,0:T(8,128)S(1)}, u32[]{:S(2)}, u32[]{:S(2)}) %collective-permute-start.6) | collective-permute-done | bytes 262176 | tf_op jit(solution)/shard_map/ppermute | solution.py:320
  46.5 0.0 collective-permute-done.5.r1
  46.5 2.1 %shard_map.91 = (f32[8,64,128]{2,1,0:T(8,128)}, f32[2,256,256]{2,1,0:T(8,128)}, f32[8,128]{1,0:T(8,128)S(1)}) custom-call(s32[1]{0:T(128)S(6)} %copy.10.size_ref, f32[2,8,128]{2,1,0:T(8,128)S(1)} %get-tuple-element.18.slot_ref, f32[8,64,128]{2,1,0:T(8,128)S(1)} %get-tuple-element.23.r0.r_in, f32[8,64,128]{2,1,0:T(8,128)S(1)} %collective-permute-done.5.r1, ...), custom_call_target="tpu_custom_call" | custom-call | flops 402653184 | bytes 3190788 | tf_op jit(solution)/shard_map/pallas_call | solution.py:22
  48.7 3.4 %all-to-all-start.2 = ((f32[8,64,128]{2,1,0:T(8,128)}), f32[8,64,128]{2,1,0:T(8,128)S(1)}, u32[]{:S(2)}, u32[]{:S(2)}) async-start(f32[8,64,128]{2,1,0:T(8,128)} %get-tuple-element.24), calls=%async_computation.2 | async-start | bytes 524288 | tf_op jit(solution)/shard_map/all_to_all | solution.py:347
  52.1 0.1 collective-permute-start.9
  52.2 0.6 collective-permute-start.8
  52.8 1.3 %collective-permute-start.7 = (f32[8,128]{1,0:T(8,128)S(1)}, f32[8,128]{1,0:T(8,128)S(1)}, u32[]{:S(2)}, u32[]{:S(2)}) collective-permute-start(f32[8,128]{1,0:T(8,128)S(1)} %get-tuple-element.25.mine), channel_id=1, source_target_pairs={{0,1},{1,0},{2,3},{3,2},{4,5},{5,4},{6,7},{7,6},{8,9},{9,8},{10,11... | collective-permute-start | bytes 12296 | tf_op jit(solution)/shard_map/ppermute | solution.py:338
  54.0 1.2 %collective-permute-done.9.refs_2_ = f32[8,128]{1,0:T(8,128)S(1)} collective-permute-done((f32[8,128]{1,0:T(8,128)S(1)}, f32[8,128]{1,0:T(8,128)S(1)}, u32[]{:S(2)}, u32[]{:S(2)}) %collective-permute-start.9) | collective-permute-done | bytes 4128 | tf_op jit(solution)/shard_map/ppermute | solution.py:338
  55.2 0.7 collective-permute-done.8.refs_1_
  55.9 4.6 %all-to-all-done.2.terms_ref = f32[8,64,128]{2,1,0:T(8,128)S(1)} async-done(((f32[8,64,128]{2,1,0:T(8,128)}), f32[8,64,128]{2,1,0:T(8,128)S(1)}, u32[]{:S(2)}, u32[]{:S(2)}) %all-to-all-start.2) | async-done | bytes 262176 | tf_op jit(solution)/shard_map/all_to_all | solution.py:347
  60.6 13.3 %all_to_all.32.s_ref = f32[8,72,128]{2,1,0:T(8,128)S(1)} all-to-all(f32[8,72,128]{2,1,0:T(8,128)S(1)} %shard_map.92), channel_id=1, replica_groups=mesh['ops'=8,'sec'=4] {'ops'}, dimensions={0} | all-to-all | bytes 589824 | tf_op jit(solution)/shard_map/all_to_all | solution.py:347
  73.9 0.4 shard_map.93
  74.2 0.7 collective-permute-start.11
  74.9 1.0 %collective-permute-start.10 = (f32[8,64,128]{2,1,0:T(8,128)S(1)}, f32[8,64,128]{2,1,0:T(8,128)S(1)}, u32[]{:S(2)}, u32[]{:S(2)}) collective-permute-start(f32[8,64,128]{2,1,0:T(8,128)S(1)} %get-tuple-element.27.r0.s0), channel_id=1, source_target_pairs={{0,1},{1,0},{2,3},{3,2},{4,5},{5,4},{6,7},{7,6},{8,9},{9,8},{10,11... | collective-permute-start | bytes 786440 | tf_op jit(solution)/shard_map/ppermute | solution.py:309
  76.0 0.2 shard_map.96.b_ref
  76.1 0.1 collective-permute-start.12
  76.2 0.9 collective-permute-done.10.r1.s1
  77.1 0.4 shard_map.94.m_ref
  77.6 2.9 %collective-permute-start.13 = (f32[2,256,256]{2,1,0:T(8,128)S(1)}, f32[2,256,256]{2,1,0:T(8,128)S(1)}, u32[]{:S(2)}, u32[]{:S(2)}) collective-permute-start(f32[2,256,256]{2,1,0:T(8,128)S(1)} %shard_map.94.m_ref), channel_id=1, source_target_pairs={{0,1},{1,0},{2,3},{3,2},{4,5},{5,4},{6,7},{7,6},{8,9},{9,8},{10,11... | collective-permute-start | bytes 1572872 | tf_op jit(solution)/shard_map/ppermute | solution.py:309
  80.4 1.1 %shard_map.95 = f32[32,128]{1,0:T(8,128)} custom-call(s32[1]{0:T(128)S(6)} %copy.10.size_ref, f32[2,256,256]{2,1,0:T(8,128)S(1)} %shard_map.94.m_ref, f32[8,64,128]{2,1,0:T(8,128)S(1)} %get-tuple-element.27.r0.s0, f32[8,64,128]{2,1,0:T(8,128)S(1)} %get-tuple-element.28.x0.x_ref, f32[8,64,128]{2,1,0:T(8,128)S(1)} %get-tuple-element.29.h0, ...), custom_call_target="tpu_custom_call" | custom-call | flops 201326592 | bytes 1851396 | tf_op jit(solution)/shard_map/pallas_call | solution.py:22
  81.5 3.3 %all-to-all-start.4 = ((f32[32,1,128]{2,1,0:T(1,128)}), f32[32,1,128]{2,1,0:T(1,128)S(1)}, u32[]{:S(2)}, u32[]{:S(2)}) async-start(f32[32,1,128]{2,1,0:T(1,128)} %bitcast.2), calls=%async_computation.4 | async-start | bytes 32768 | tf_op jit(solution)/shard_map/all_to_all | solution.py:418
  84.9 0.0 copy-start.2
  84.9 0.8 copy-done.2
  85.7 1.0 %copy-done.3 = f32[2,256,256]{2,1,0:T(8,128)S(1)} copy-done((f32[2,256,256]{2,1,0:T(8,128)S(1)}, f32[2,256,256]{2,1,0:T(8,128)}, u32[]{:S(2)}) %copy-start.3) | copy-done | bytes 524312
  86.7 2.3 %shard_map.97.u_ref = f32[3,2,256,256]{3,2,1,0:T(8,128)S(1)} custom-call(f32[8,128]{1,0:T(8,128)S(1)} %get-tuple-element.33.flag_ref, f32[3,256,256]{2,1,0:T(8,128)S(1)} %shard_map.96.b_ref, f32[3,256,256]{2,1,0:T(8,128)} %collective-permute-done.12.n_ref, f32[2,256,256]{2,1,0:T(8,128)S(1)} %shard_map.94.m_ref, f32[2,256,256]{2,1,0:T(8,128)S(1)} %copy-done.3, ...), custom_call_target="tpu_custom_call" | custom-call | flops 402653184 | bytes 4722688 | tf_op jit(solution)/shard_map/pallas_call | solution.py:22
  89.0 3.0 %all-to-all-done.4 = f32[32,1,128]{2,1,0:T(1,128)S(1)} async-done(((f32[32,1,128]{2,1,0:T(1,128)}), f32[32,1,128]{2,1,0:T(1,128)S(1)}, u32[]{:S(2)}, u32[]{:S(2)}) %all-to-all-start.4) | async-done | bytes 16416 | tf_op jit(solution)/shard_map/all_to_all | solution.py:418
  92.0 1.4 %shard_map.98 = (f32[1,256,256]{2,1,0:T(8,128)}, f32[2,1,256,256]{3,2,1,0:T(8,128)}) custom-call(f32[32,128]{1,0:T(8,128)S(1)} %bitcast.5, f32[8,128]{1,0:T(8,128)S(1)} %get-tuple-element.30.c_in, f32[3,256,256]{2,1,0:T(8,128)S(1)} %shard_map.96.b_ref, f32[8,64,128]{2,1,0:T(8,128)S(1)} %get-tuple-element.27.r0.s0, f32[3,2,256,256]{3,2,1,0:T(8,128)S(1)} %shard_map.97.u_ref), custom_call_target="tpu_custom_call" | custom-call | flops 1310720 | bytes 3428352 | tf_op jit(solution)/shard_map/pallas_call | solution.py:22
  (13 shorter events, 0.1 us)
Async XLA Ops:
  1.3 0.9 copy-start.4
  2.2 7.4 %collective-permute-start.1 = (f32[8,64,128]{2,1,0:T(8,128)S(1)}, f32[8,64,128]{2,1,0:T(8,128)S(1)}, u32[]{:S(2)}, u32[]{:S(2)}) collective-permute-start(f32[8,64,128]{2,1,0:T(8,128)S(1)} %shard_map.87.x0.x_ref), channel_id=1, source_target_pairs={{1,2},{2,1},{0,4},{3,7},{5,6},{6,5},{4,0},{7,3},{9,10},{10,9},{8,1... | collective-permute-start | bytes 786440 | tf_op jit(solution)/shard_map/ppermute | solution.py:320
  5.3 4.4 %collective-permute-start = (f32[8,64,128]{2,1,0:T(8,128)S(1)}, f32[8,64,128]{2,1,0:T(8,128)S(1)}, u32[]{:S(2)}, u32[]{:S(2)}) collective-permute-start(f32[8,64,128]{2,1,0:T(8,128)S(1)} %shard_map.87.x0.x_ref), channel_id=1, source_target_pairs={{0,1},{1,0},{2,3},{3,2},{4,5},{5,4},{6,7},{7,6},{8,9},{9,8},{10,11... | collective-permute-start | bytes 786440 | tf_op jit(solution)/shard_map/ppermute | solution.py:309
  6.0 0.7 copy-start.5
  9.6 30.3 %copy-start = (bf16[1,256,256]{2,1,0:T(8,128)(2,1)S(1)}, bf16[1,256,256]{2,1,0:T(8,128)(2,1)}, u32[]{:S(2)}) copy-start(bf16[1,256,256]{2,1,0:T(8,128)(2,1)} %diag_ref.3) | copy-start | bytes 393220
  11.4 15.0 %all-to-all-start = ((f32[8,64,128]{2,1,0:T(8,128)}), f32[8,64,128]{2,1,0:T(8,128)S(1)}, u32[]{:S(2)}, u32[]{:S(2)}) async-start(f32[8,64,128]{2,1,0:T(8,128)} %get-tuple-element.21), calls=%async_computation | async-start | bytes 524288 | tf_op jit(solution)/shard_map/all_to_all | solution.py:347
  17.7 3.0 %collective-permute-start.4 = (f32[8,128]{1,0:T(8,128)S(1)}, f32[8,128]{1,0:T(8,128)S(1)}, u32[]{:S(2)}, u32[]{:S(2)}) collective-permute-start(f32[8,128]{1,0:T(8,128)S(1)} %get-tuple-element.22.mine), channel_id=1, source_target_pairs={{0,3},{1,2},{2,1},{3,0},{4,7},{5,6},{6,5},{7,4},{8,11},{9,10},{10,... | collective-permute-start | bytes 12296 | tf_op jit(solution)/shard_map/ppermute | solution.py:338
  17.7 3.7 %collective-permute-start.3 = (f32[8,128]{1,0:T(8,128)S(1)}, f32[8,128]{1,0:T(8,128)S(1)}, u32[]{:S(2)}, u32[]{:S(2)}) collective-permute-start(f32[8,128]{1,0:T(8,128)S(1)} %get-tuple-element.22.mine), channel_id=1, source_target_pairs={{0,2},{1,3},{2,0},{3,1},{4,6},{5,7},{6,4},{7,5},{8,10},{9,11},{10,... | collective-permute-start | bytes 12296 | tf_op jit(solution)/shard_map/ppermute | solution.py:338
  18.7 2.7 %collective-permute-start.2 = (f32[8,128]{1,0:T(8,128)S(1)}, f32[8,128]{1,0:T(8,128)S(1)}, u32[]{:S(2)}, u32[]{:S(2)}) collective-permute-start(f32[8,128]{1,0:T(8,128)S(1)} %get-tuple-element.22.mine), channel_id=1, source_target_pairs={{0,1},{1,0},{2,3},{3,2},{4,5},{5,4},{6,7},{7,6},{8,9},{9,8},{10,11... | collective-permute-start | bytes 12296 | tf_op jit(solution)/shard_map/ppermute | solution.py:338
  40.1 6.4 %collective-permute-start.6 = (f32[8,64,128]{2,1,0:T(8,128)S(1)}, f32[8,64,128]{2,1,0:T(8,128)S(1)}, u32[]{:S(2)}, u32[]{:S(2)}) collective-permute-start(f32[8,64,128]{2,1,0:T(8,128)S(1)} %get-tuple-element.23.r0.r_in), channel_id=1, source_target_pairs={{1,2},{2,1},{0,4},{3,7},{5,6},{6,5},{4,0},{7,3},{9,10},{10,9},{8,1... | collective-permute-start | bytes 786440 | tf_op jit(solution)/shard_map/ppermute | solution.py:320
  40.9 5.7 %collective-permute-start.5 = (f32[8,64,128]{2,1,0:T(8,128)S(1)}, f32[8,64,128]{2,1,0:T(8,128)S(1)}, u32[]{:S(2)}, u32[]{:S(2)}) collective-permute-start(f32[8,64,128]{2,1,0:T(8,128)S(1)} %get-tuple-element.23.r0.r_in), channel_id=1, source_target_pairs={{0,1},{1,0},{2,3},{3,2},{4,5},{5,4},{6,7},{7,6},{8,9},{9,8},{10,11... | collective-permute-start | bytes 786440 | tf_op jit(solution)/shard_map/ppermute | solution.py:309
  48.7 11.8 %all-to-all-start.2 = ((f32[8,64,128]{2,1,0:T(8,128)}), f32[8,64,128]{2,1,0:T(8,128)S(1)}, u32[]{:S(2)}, u32[]{:S(2)}) async-start(f32[8,64,128]{2,1,0:T(8,128)} %get-tuple-element.24), calls=%async_computation.2 | async-start | bytes 524288 | tf_op jit(solution)/shard_map/all_to_all | solution.py:347
  52.1 3.1 %collective-permute-start.9 = (f32[8,128]{1,0:T(8,128)S(1)}, f32[8,128]{1,0:T(8,128)S(1)}, u32[]{:S(2)}, u32[]{:S(2)}) collective-permute-start(f32[8,128]{1,0:T(8,128)S(1)} %get-tuple-element.25.mine), channel_id=1, source_target_pairs={{0,3},{1,2},{2,1},{3,0},{4,7},{5,6},{6,5},{7,4},{8,11},{9,10},{10,... | collective-permute-start | bytes 12296 | tf_op jit(solution)/shard_map/ppermute | solution.py:338
  52.2 3.7 %collective-permute-start.8 = (f32[8,128]{1,0:T(8,128)S(1)}, f32[8,128]{1,0:T(8,128)S(1)}, u32[]{:S(2)}, u32[]{:S(2)}) collective-permute-start(f32[8,128]{1,0:T(8,128)S(1)} %get-tuple-element.25.mine), channel_id=1, source_target_pairs={{0,2},{1,3},{2,0},{3,1},{4,6},{5,7},{6,4},{7,5},{8,10},{9,11},{10,... | collective-permute-start | bytes 12296 | tf_op jit(solution)/shard_map/ppermute | solution.py:338
  52.8 3.1 %collective-permute-start.7 = (f32[8,128]{1,0:T(8,128)S(1)}, f32[8,128]{1,0:T(8,128)S(1)}, u32[]{:S(2)}, u32[]{:S(2)}) collective-permute-start(f32[8,128]{1,0:T(8,128)S(1)} %get-tuple-element.25.mine), channel_id=1, source_target_pairs={{0,1},{1,0},{2,3},{3,2},{4,5},{5,4},{6,7},{7,6},{8,9},{9,8},{10,11... | collective-permute-start | bytes 12296 | tf_op jit(solution)/shard_map/ppermute | solution.py:338
  60.5 15.4 %copy-start.1 = (f32[2,256,256]{2,1,0:T(8,128)S(1)}, f32[2,256,256]{2,1,0:T(8,128)}, u32[]{:S(2)}) copy-start(f32[2,256,256]{2,1,0:T(8,128)} %get-tuple-element.32.b_ref) | copy-start | bytes 1572868
  74.2 2.0 %collective-permute-start.11 = (f32[8,64,128]{2,1,0:T(8,128)S(1)}, f32[8,64,128]{2,1,0:T(8,128)S(1)}, u32[]{:S(2)}, u32[]{:S(2)}) collective-permute-start(f32[8,64,128]{2,1,0:T(8,128)S(1)} %get-tuple-element.27.r0.s0), channel_id=1, source_target_pairs={{1,2},{2,1},{5,6},{6,5},{9,10},{10,9},{13,14},{14,13},{17,18},{18,... | collective-permute-start | bytes 786440 | tf_op jit(solution)/shard_map/ppermute | solution.py:320
  74.9 2.2 %collective-permute-start.10 = (f32[8,64,128]{2,1,0:T(8,128)S(1)}, f32[8,64,128]{2,1,0:T(8,128)S(1)}, u32[]{:S(2)}, u32[]{:S(2)}) collective-permute-start(f32[8,64,128]{2,1,0:T(8,128)S(1)} %get-tuple-element.27.r0.s0), channel_id=1, source_target_pairs={{0,1},{1,0},{2,3},{3,2},{4,5},{5,4},{6,7},{7,6},{8,9},{9,8},{10,11... | collective-permute-start | bytes 786440 | tf_op jit(solution)/shard_map/ppermute | solution.py:309
  76.1 9.6 %collective-permute-start.12 = (f32[3,256,256]{2,1,0:T(8,128)S(1)}, f32[3,256,256]{2,1,0:T(8,128)}, u32[]{:S(2)}, u32[]{:S(2)}) collective-permute-start(f32[3,256,256]{2,1,0:T(8,128)S(1)} %shard_map.96.b_ref), channel_id=1, source_target_pairs={{0,1},{1,0},{2,3},{3,2},{4,5},{5,4},{6,7},{7,6},{8,9},{9,8},{10,11... | collective-permute-start | bytes 2359304 | tf_op jit(solution)/shard_map/ppermute | solution.py:309
  77.6 7.3 %collective-permute-start.13 = (f32[2,256,256]{2,1,0:T(8,128)S(1)}, f32[2,256,256]{2,1,0:T(8,128)S(1)}, u32[]{:S(2)}, u32[]{:S(2)}) collective-permute-start(f32[2,256,256]{2,1,0:T(8,128)S(1)} %shard_map.94.m_ref), channel_id=1, source_target_pairs={{0,1},{1,0},{2,3},{3,2},{4,5},{5,4},{6,7},{7,6},{8,9},{9,8},{10,11... | collective-permute-start | bytes 1572872 | tf_op jit(solution)/shard_map/ppermute | solution.py:309
  81.5 10.4 %all-to-all-start.4 = ((f32[32,1,128]{2,1,0:T(1,128)}), f32[32,1,128]{2,1,0:T(1,128)S(1)}, u32[]{:S(2)}, u32[]{:S(2)}) async-start(f32[32,1,128]{2,1,0:T(1,128)} %bitcast.2), calls=%async_computation.4 | async-start | bytes 32768 | tf_op jit(solution)/shard_map/all_to_all | solution.py:418
  84.9 0.8 copy-start.2
  85.7 1.0 %copy-start.3 = (f32[2,256,256]{2,1,0:T(8,128)S(1)}, f32[2,256,256]{2,1,0:T(8,128)}, u32[]{:S(2)}) copy-start(f32[2,256,256]{2,1,0:T(8,128)} %copy-done.2) | copy-start | bytes 1572868

commit v13 on v12

--- a/solution.py
+++ b/solution.py
@@ -132,9 +132,12 @@
     return on_x, on_r, theta, xx
 
 
-def start_body(size_ref, psi_ref, x_ref):
-    live = mask(size_ref[0], psi_ref.shape[1])
-    pack(x_ref, (), x_ref.shape, jnp.where(live, psi_ref[0].astype(F32), 0.0))
+def start_body(size_ref, psi_hbm, x_ref, psi_ref, sem):
+    copy = pltpu.make_async_copy(psi_hbm.at[0], psi_ref, sem)
+    copy.start()
+    live = mask(size_ref[0], psi_ref.shape[0])
+    copy.wait()
+    pack(x_ref, (), x_ref.shape, jnp.where(live, psi_ref[...].astype(F32), 0.0))
 
 
 def split_pairs(left_ref, right_ref, lcat_ref, rcat_ref, left, right, sem):
@@ -372,7 +375,11 @@
         )
         return exchange(full)
 
-    (x0,) = call(start_body, (block,), [SMEM, VMEM], [], light, sector_states, psi_guess)
+    (x0,) = call(
+        start_body, (block,), [SMEM, pl.BlockSpec(memory_space=pltpu.HBM)],
+        [pltpu.VMEM((side, side), BF16), pltpu.SemaphoreType.DMA(())], light,
+        sector_states, pltpu.with_memory_space_constraint(psi_guess, pltpu.HBM),
+    )
     x2, x1 = other(x0, 0), paired(x0)
     lcat, rcat, flag, slots = call(
         split_body, (pieces, pieces, small, jax.ShapeDtypeStruct((pairs, 8, LANES), F32)),

time: 93.9 us -> 93.9 us (level)
    unnamed x12 -> x10, local copies, waits for them, and re-layouts: 3.39 us -> 2.49 us
where the time goes in v13:
time: 93.9 us; the launch traced here: 93.3 us
  blocking collectives  26.7 us (28%)
  starting transfers between devices  25.8 us (27%)
  waiting for transfers between devices  24.1 us (26%)
  Pallas kernels  12.2 us (13%)
  local copies, waits for them, and re-layouts  2.49 us (3%)
  between operations  2.07 us (2%)
    all_to_all x2, blocking collectives, exchange(): return lax.all_to_all(value, 'ops', 0, 0)  26.7 us
    pallas_call x13, Pallas kernels, call(): pl.pallas_call(body, out_shape=tuple((pltpu.HBM(o.shape, o.dtype) if k in...  12.2 us
    all_to_all x2, starting transfers between devices, exchange(): return lax.all_to_all(value, 'ops', 0, 0)  9.76 us
    all_to_all x2, waiting for transfers between devices, exchange(): return lax.all_to_all(value, 'ops', 0, 0)  9.64 us
    ppermute x3, waiting for transfers between devices, other(): return lax.ppermute(value, ('ops', 'sec'), route)  6.87 us
    ppermute x3, starting transfers between devices, other(): return lax.ppermute(value, ('ops', 'sec'), route)  4.47 us
    ppermute x5, starting transfers between devices, paired(): return lax.ppermute(value, 'sec', [(i, i ^ 1) for i in range(count)])  4.43 us
    ppermute x6, starting transfers between devices, over_sectors(): found.append(lax.ppermute(value, 'sec', route))  3.77 us
  transfers between devices with their start and end apart: 17, of which 10 were waited for; matrix products, arithmetic and copies ran while one was open for 0% of the time, Pallas kernels for 6%

profile of v13, /device:TPU:0, one launch (start us, length us, event | category | flops | bytes accessed | tf_op | source)
XLA Modules:
  0.0 93.3 jit_solution(18019757998040350464)
XLA Ops:
  1.3 0.9 %shard_map.87.x0.x_ref = f32[8,64,128]{2,1,0:T(8,128)S(1)} custom-call(s32[1]{0:T(128)S(6)} %copy.10.size_ref, bf16[1,256,256]{2,1,0:T(8,128)(2,1)} %psi_hbm.1), custom_call_target="tpu_custom_call" | custom-call | flops 1310720 | bytes 393220 | tf_op jit(solution)/shard_map/pallas_call | solution.py:22
  2.2 3.0 %collective-permute-start.1 = (f32[8,64,128]{2,1,0:T(8,128)S(1)}, f32[8,64,128]{2,1,0:T(8,128)S(1)}, u32[]{:S(2)}, u32[]{:S(2)}) collective-permute-start(f32[8,64,128]{2,1,0:T(8,128)S(1)} %shard_map.87.x0.x_ref), channel_id=1, source_target_pairs={{1,2},{2,1},{0,4},{3,7},{5,6},{6,5},{4,0},{7,3},{9,10},{10,9},{8,1... | collective-permute-start | bytes 786440 | tf_op jit(solution)/shard_map/ppermute | solution.py:323
  5.3 0.1 collective-permute-start
  6.1 0.0 copy-start.4
  6.1 0.6 copy-done.4
  6.7 1.4 %shard_map.86 = (bf16[2,2,256,256]{3,2,1,0:T(8,128)(2,1)S(1)}, bf16[2,2,256,256]{3,2,1,0:T(8,128)(2,1)S(1)}, f32[8,128]{1,0:T(8,128)S(1)}, f32[2,8,128]{2,1,0:T(8,128)S(1)}) custom-call(s32[1]{0:T(128)S(6)} %copy.11.label_ref, s32[2]{0:T(128)S(1)} %bitcast.6, f32[2,1,256,256]{3,2,1,0:T(8,128)} %left_ref.1, f32[2,1,256,256]{3,2,1,0:T(8,128)} %right_ref.1), custom_call_target="tpu_custom_call" | custom-call | flops 2621440 | bytes 2109452 | tf_op jit(solution)/shard_map/pallas_call | solution.py:22
  8.1 1.5 %collective-permute-done.1.x2 = f32[8,64,128]{2,1,0:T(8,128)S(1)} collective-permute-done((f32[8,64,128]{2,1,0:T(8,128)S(1)}, f32[8,64,128]{2,1,0:T(8,128)S(1)}, u32[]{:S(2)}, u32[]{:S(2)}) %collective-permute-start.1) | collective-permute-done | bytes 262176 | tf_op jit(solution)/shard_map/ppermute | solution.py:323
  9.6 1.8 %shard_map.88 = (f32[8,64,128]{2,1,0:T(8,128)}, f32[2,256,256]{2,1,0:T(8,128)S(1)}, f32[8,128]{1,0:T(8,128)S(1)}) custom-call(s32[1]{0:T(128)S(6)} %copy.10.size_ref, f32[2,8,128]{2,1,0:T(8,128)S(1)} %get-tuple-element.18.slot_ref, f32[8,64,128]{2,1,0:T(8,128)S(1)} %shard_map.87.x0.x_ref, f32[8,64,128]{2,1,0:T(8,128)S(1)} %collective-permute-done.x1, ...), custom_call_target="tpu_custom_call" | custom-call | flops 402653184 | bytes 2633732 | tf_op jit(solution)/shard_map/pallas_call | solution.py:22
  11.4 6.3 %all-to-all-start = ((f32[8,64,128]{2,1,0:T(8,128)}), f32[8,64,128]{2,1,0:T(8,128)S(1)}, u32[]{:S(2)}, u32[]{:S(2)}) async-start(f32[8,64,128]{2,1,0:T(8,128)} %get-tuple-element.21), calls=%async_computation | async-start | bytes 524288 | tf_op jit(solution)/shard_map/all_to_all | solution.py:350
  17.7 0.0 collective-permute-start.4
  17.7 1.0 %collective-permute-start.3 = (f32[8,128]{1,0:T(8,128)S(1)}, f32[8,128]{1,0:T(8,128)S(1)}, u32[]{:S(2)}, u32[]{:S(2)}) collective-permute-start(f32[8,128]{1,0:T(8,128)S(1)} %get-tuple-element.22.mine), channel_id=1, source_target_pairs={{0,2},{1,3},{2,0},{3,1},{4,6},{5,7},{6,4},{7,5},{8,10},{9,11},{10,... | collective-permute-start | bytes 12296 | tf_op jit(solution)/shard_map/ppermute | solution.py:341
  18.7 0.8 collective-permute-start.2
  19.6 1.2 %collective-permute-done.4.refs_2_ = f32[8,128]{1,0:T(8,128)S(1)} collective-permute-done((f32[8,128]{1,0:T(8,128)S(1)}, f32[8,128]{1,0:T(8,128)S(1)}, u32[]{:S(2)}, u32[]{:S(2)}) %collective-permute-start.4) | collective-permute-done | bytes 4128 | tf_op jit(solution)/shard_map/ppermute | solution.py:341
  20.8 0.7 collective-permute-done.3.refs_1_
  21.4 5.0 %all-to-all-done.terms_ref = f32[8,64,128]{2,1,0:T(8,128)S(1)} async-done(((f32[8,64,128]{2,1,0:T(8,128)}), f32[8,64,128]{2,1,0:T(8,128)S(1)}, u32[]{:S(2)}, u32[]{:S(2)}) %all-to-all-start) | async-done | bytes 262176 | tf_op jit(solution)/shard_map/all_to_all | solution.py:350
  26.5 13.4 %all_to_all.31.g_ref.g0 = f32[8,72,128]{2,1,0:T(8,128)S(1)} all-to-all(f32[8,72,128]{2,1,0:T(8,128)S(1)} %shard_map.89), channel_id=1, replica_groups=mesh['ops'=8,'sec'=4] {'ops'}, dimensions={0} | all-to-all | bytes 589824 | tf_op jit(solution)/shard_map/all_to_all | solution.py:350
  39.9 0.2 shard_map.90
  40.1 0.8 collective-permute-start.6
  40.9 0.3 collective-permute-start.5
  41.2 5.4 %collective-permute-done.6.r2 = f32[8,64,128]{2,1,0:T(8,128)S(1)} collective-permute-done((f32[8,64,128]{2,1,0:T(8,128)S(1)}, f32[8,64,128]{2,1,0:T(8,128)S(1)}, u32[]{:S(2)}, u32[]{:S(2)}) %collective-permute-start.6) | collective-permute-done | bytes 262176 | tf_op jit(solution)/shard_map/ppermute | solution.py:323
  46.6 0.0 collective-permute-done.5.r1
  46.6 2.1 %shard_map.91 = (f32[8,64,128]{2,1,0:T(8,128)}, f32[2,256,256]{2,1,0:T(8,128)}, f32[8,128]{1,0:T(8,128)S(1)}) custom-call(s32[1]{0:T(128)S(6)} %copy.10.size_ref, f32[2,8,128]{2,1,0:T(8,128)S(1)} %get-tuple-element.18.slot_ref, f32[8,64,128]{2,1,0:T(8,128)S(1)} %get-tuple-element.23.r0.r_in, f32[8,64,128]{2,1,0:T(8,128)S(1)} %collective-permute-done.5.r1, ...), custom_call_target="tpu_custom_call" | custom-call | flops 402653184 | bytes 3190788 | tf_op jit(solution)/shard_map/pallas_call | solution.py:22
  48.7 3.4 %all-to-all-start.2 = ((f32[8,64,128]{2,1,0:T(8,128)}), f32[8,64,128]{2,1,0:T(8,128)S(1)}, u32[]{:S(2)}, u32[]{:S(2)}) async-start(f32[8,64,128]{2,1,0:T(8,128)} %get-tuple-element.24), calls=%async_computation.2 | async-start | bytes 524288 | tf_op jit(solution)/shard_map/all_to_all | solution.py:350
  52.1 0.1 collective-permute-start.9
  52.2 0.6 collective-permute-start.8
  52.8 1.3 %collective-permute-start.7 = (f32[8,128]{1,0:T(8,128)S(1)}, f32[8,128]{1,0:T(8,128)S(1)}, u32[]{:S(2)}, u32[]{:S(2)}) collective-permute-start(f32[8,128]{1,0:T(8,128)S(1)} %get-tuple-element.25.mine), channel_id=1, source_target_pairs={{0,1},{1,0},{2,3},{3,2},{4,5},{5,4},{6,7},{7,6},{8,9},{9,8},{10,11... | collective-permute-start | bytes 12296 | tf_op jit(solution)/shard_map/ppermute | solution.py:341
  54.0 1.2 %collective-permute-done.9.refs_2_ = f32[8,128]{1,0:T(8,128)S(1)} collective-permute-done((f32[8,128]{1,0:T(8,128)S(1)}, f32[8,128]{1,0:T(8,128)S(1)}, u32[]{:S(2)}, u32[]{:S(2)}) %collective-permute-start.9) | collective-permute-done | bytes 4128 | tf_op jit(solution)/shard_map/ppermute | solution.py:341
  55.2 0.7 collective-permute-done.8.refs_1_
  55.9 0.0 collective-permute-done.7.refs_0_
  55.9 4.7 %all-to-all-done.2.terms_ref = f32[8,64,128]{2,1,0:T(8,128)S(1)} async-done(((f32[8,64,128]{2,1,0:T(8,128)}), f32[8,64,128]{2,1,0:T(8,128)S(1)}, u32[]{:S(2)}, u32[]{:S(2)}) %all-to-all-start.2) | async-done | bytes 262176 | tf_op jit(solution)/shard_map/all_to_all | solution.py:350
  60.6 13.3 %all_to_all.32.s_ref = f32[8,72,128]{2,1,0:T(8,128)S(1)} all-to-all(f32[8,72,128]{2,1,0:T(8,128)S(1)} %shard_map.92), channel_id=1, replica_groups=mesh['ops'=8,'sec'=4] {'ops'}, dimensions={0} | all-to-all | bytes 589824 | tf_op jit(solution)/shard_map/all_to_all | solution.py:350
  73.9 0.4 shard_map.93
  74.2 0.7 collective-permute-start.11
  74.9 1.0 %collective-permute-start.10 = (f32[8,64,128]{2,1,0:T(8,128)S(1)}, f32[8,64,128]{2,1,0:T(8,128)S(1)}, u32[]{:S(2)}, u32[]{:S(2)}) collective-permute-start(f32[8,64,128]{2,1,0:T(8,128)S(1)} %get-tuple-element.27.r0.s0), channel_id=1, source_target_pairs={{0,1},{1,0},{2,3},{3,2},{4,5},{5,4},{6,7},{7,6},{8,9},{9,8},{10,11... | collective-permute-start | bytes 786440 | tf_op jit(solution)/shard_map/ppermute | solution.py:312
  76.0 0.2 shard_map.96.b_ref
  76.1 0.1 collective-permute-start.12
  76.2 0.9 collective-permute-done.10.r1.s1
  77.1 0.4 shard_map.94.m_ref
  77.6 2.9 %collective-permute-start.13 = (f32[2,256,256]{2,1,0:T(8,128)S(1)}, f32[2,256,256]{2,1,0:T(8,128)S(1)}, u32[]{:S(2)}, u32[]{:S(2)}) collective-permute-start(f32[2,256,256]{2,1,0:T(8,128)S(1)} %shard_map.94.m_ref), channel_id=1, source_target_pairs={{0,1},{1,0},{2,3},{3,2},{4,5},{5,4},{6,7},{7,6},{8,9},{9,8},{10,11... | collective-permute-start | bytes 1572872 | tf_op jit(solution)/shard_map/ppermute | solution.py:312
  80.5 1.1 %shard_map.95 = f32[32,128]{1,0:T(8,128)} custom-call(s32[1]{0:T(128)S(6)} %copy.10.size_ref, f32[2,256,256]{2,1,0:T(8,128)S(1)} %shard_map.94.m_ref, f32[8,64,128]{2,1,0:T(8,128)S(1)} %get-tuple-element.27.r0.s0, f32[8,64,128]{2,1,0:T(8,128)S(1)} %get-tuple-element.28.x0.x_ref, f32[8,64,128]{2,1,0:T(8,128)S(1)} %get-tuple-element.29.h0, ...), custom_call_target="tpu_custom_call" | custom-call | flops 201326592 | bytes 1851396 | tf_op jit(solution)/shard_map/pallas_call | solution.py:22
  81.5 3.3 %all-to-all-start.4 = ((f32[32,1,128]{2,1,0:T(1,128)}), f32[32,1,128]{2,1,0:T(1,128)S(1)}, u32[]{:S(2)}, u32[]{:S(2)}) async-start(f32[32,1,128]{2,1,0:T(1,128)} %bitcast.2), calls=%async_computation.4 | async-start | bytes 32768 | tf_op jit(solution)/shard_map/all_to_all | solution.py:425
  84.9 0.0 collective-permute-done.13.w_ref
  84.9 0.0 copy-start.2
  84.9 0.8 copy-done.2
  85.7 1.0 %copy-done.3 = f32[2,256,256]{2,1,0:T(8,128)S(1)} copy-done((f32[2,256,256]{2,1,0:T(8,128)S(1)}, f32[2,256,256]{2,1,0:T(8,128)}, u32[]{:S(2)}) %copy-start.3) | copy-done | bytes 524312
  86.7 2.3 %shard_map.97.u_ref = f32[3,2,256,256]{3,2,1,0:T(8,128)S(1)} custom-call(f32[8,128]{1,0:T(8,128)S(1)} %get-tuple-element.33.flag_ref, f32[3,256,256]{2,1,0:T(8,128)S(1)} %shard_map.96.b_ref, f32[3,256,256]{2,1,0:T(8,128)} %collective-permute-done.12.n_ref, f32[2,256,256]{2,1,0:T(8,128)S(1)} %shard_map.94.m_ref, f32[2,256,256]{2,1,0:T(8,128)S(1)} %copy-done.3, ...), custom_call_target="tpu_custom_call" | custom-call | flops 402653184 | bytes 4722688 | tf_op jit(solution)/shard_map/pallas_call | solution.py:22
  89.0 3.0 %all-to-all-done.4 = f32[32,1,128]{2,1,0:T(1,128)S(1)} async-done(((f32[32,1,128]{2,1,0:T(1,128)}), f32[32,1,128]{2,1,0:T(1,128)S(1)}, u32[]{:S(2)}, u32[]{:S(2)}) %all-to-all-start.4) | async-done | bytes 16416 | tf_op jit(solution)/shard_map/all_to_all | solution.py:425
  92.0 1.4 %shard_map.98 = (f32[1,256,256]{2,1,0:T(8,128)}, f32[2,1,256,256]{3,2,1,0:T(8,128)}) custom-call(f32[32,128]{1,0:T(8,128)S(1)} %bitcast.5, f32[8,128]{1,0:T(8,128)S(1)} %get-tuple-element.30.c_in, f32[3,256,256]{2,1,0:T(8,128)S(1)} %shard_map.96.b_ref, f32[8,64,128]{2,1,0:T(8,128)S(1)} %get-tuple-element.27.r0.s0, f32[3,2,256,256]{3,2,1,0:T(8,128)S(1)} %shard_map.97.u_ref), custom_call_target="tpu_custom_call" | custom-call | flops 1310720 | bytes 3428352 | tf_op jit(solution)/shard_map/pallas_call | solution.py:22
  (11 shorter events, 0.1 us)
Async XLA Ops:
  2.2 7.4 %collective-permute-start.1 = (f32[8,64,128]{2,1,0:T(8,128)S(1)}, f32[8,64,128]{2,1,0:T(8,128)S(1)}, u32[]{:S(2)}, u32[]{:S(2)}) collective-permute-start(f32[8,64,128]{2,1,0:T(8,128)S(1)} %shard_map.87.x0.x_ref), channel_id=1, source_target_pairs={{1,2},{2,1},{0,4},{3,7},{5,6},{6,5},{4,0},{7,3},{9,10},{10,9},{8,1... | collective-permute-start | bytes 786440 | tf_op jit(solution)/shard_map/ppermute | solution.py:323
  5.3 4.4 %collective-permute-start = (f32[8,64,128]{2,1,0:T(8,128)S(1)}, f32[8,64,128]{2,1,0:T(8,128)S(1)}, u32[]{:S(2)}, u32[]{:S(2)}) collective-permute-start(f32[8,64,128]{2,1,0:T(8,128)S(1)} %shard_map.87.x0.x_ref), channel_id=1, source_target_pairs={{0,1},{1,0},{2,3},{3,2},{4,5},{5,4},{6,7},{7,6},{8,9},{9,8},{10,11... | collective-permute-start | bytes 786440 | tf_op jit(solution)/shard_map/ppermute | solution.py:312
  6.1 0.7 copy-start.4
  9.6 30.3 %copy-start = (bf16[1,256,256]{2,1,0:T(8,128)(2,1)S(1)}, bf16[1,256,256]{2,1,0:T(8,128)(2,1)}, u32[]{:S(2)}) copy-start(bf16[1,256,256]{2,1,0:T(8,128)(2,1)} %diag_ref.3) | copy-start | bytes 393220
  11.4 15.0 %all-to-all-start = ((f32[8,64,128]{2,1,0:T(8,128)}), f32[8,64,128]{2,1,0:T(8,128)S(1)}, u32[]{:S(2)}, u32[]{:S(2)}) async-start(f32[8,64,128]{2,1,0:T(8,128)} %get-tuple-element.21), calls=%async_computation | async-start | bytes 524288 | tf_op jit(solution)/shard_map/all_to_all | solution.py:350
  17.7 3.0 %collective-permute-start.4 = (f32[8,128]{1,0:T(8,128)S(1)}, f32[8,128]{1,0:T(8,128)S(1)}, u32[]{:S(2)}, u32[]{:S(2)}) collective-permute-start(f32[8,128]{1,0:T(8,128)S(1)} %get-tuple-element.22.mine), channel_id=1, source_target_pairs={{0,3},{1,2},{2,1},{3,0},{4,7},{5,6},{6,5},{7,4},{8,11},{9,10},{10,... | collective-permute-start | bytes 12296 | tf_op jit(solution)/shard_map/ppermute | solution.py:341
  17.7 3.7 %collective-permute-start.3 = (f32[8,128]{1,0:T(8,128)S(1)}, f32[8,128]{1,0:T(8,128)S(1)}, u32[]{:S(2)}, u32[]{:S(2)}) collective-permute-start(f32[8,128]{1,0:T(8,128)S(1)} %get-tuple-element.22.mine), channel_id=1, source_target_pairs={{0,2},{1,3},{2,0},{3,1},{4,6},{5,7},{6,4},{7,5},{8,10},{9,11},{10,... | collective-permute-start | bytes 12296 | tf_op jit(solution)/shard_map/ppermute | solution.py:341
  18.7 2.7 %collective-permute-start.2 = (f32[8,128]{1,0:T(8,128)S(1)}, f32[8,128]{1,0:T(8,128)S(1)}, u32[]{:S(2)}, u32[]{:S(2)}) collective-permute-start(f32[8,128]{1,0:T(8,128)S(1)} %get-tuple-element.22.mine), channel_id=1, source_target_pairs={{0,1},{1,0},{2,3},{3,2},{4,5},{5,4},{6,7},{7,6},{8,9},{9,8},{10,11... | collective-permute-start | bytes 12296 | tf_op jit(solution)/shard_map/ppermute | solution.py:341
  40.1 6.4 %collective-permute-start.6 = (f32[8,64,128]{2,1,0:T(8,128)S(1)}, f32[8,64,128]{2,1,0:T(8,128)S(1)}, u32[]{:S(2)}, u32[]{:S(2)}) collective-permute-start(f32[8,64,128]{2,1,0:T(8,128)S(1)} %get-tuple-element.23.r0.r_in), channel_id=1, source_target_pairs={{1,2},{2,1},{0,4},{3,7},{5,6},{6,5},{4,0},{7,3},{9,10},{10,9},{8,1... | collective-permute-start | bytes 786440 | tf_op jit(solution)/shard_map/ppermute | solution.py:323
  40.9 5.7 %collective-permute-start.5 = (f32[8,64,128]{2,1,0:T(8,128)S(1)}, f32[8,64,128]{2,1,0:T(8,128)S(1)}, u32[]{:S(2)}, u32[]{:S(2)}) collective-permute-start(f32[8,64,128]{2,1,0:T(8,128)S(1)} %get-tuple-element.23.r0.r_in), channel_id=1, source_target_pairs={{0,1},{1,0},{2,3},{3,2},{4,5},{5,4},{6,7},{7,6},{8,9},{9,8},{10,11... | collective-permute-start | bytes 786440 | tf_op jit(solution)/shard_map/ppermute | solution.py:312
  48.7 11.8 %all-to-all-start.2 = ((f32[8,64,128]{2,1,0:T(8,128)}), f32[8,64,128]{2,1,0:T(8,128)S(1)}, u32[]{:S(2)}, u32[]{:S(2)}) async-start(f32[8,64,128]{2,1,0:T(8,128)} %get-tuple-element.24), calls=%async_computation.2 | async-start | bytes 524288 | tf_op jit(solution)/shard_map/all_to_all | solution.py:350
  52.1 3.1 %collective-permute-start.9 = (f32[8,128]{1,0:T(8,128)S(1)}, f32[8,128]{1,0:T(8,128)S(1)}, u32[]{:S(2)}, u32[]{:S(2)}) collective-permute-start(f32[8,128]{1,0:T(8,128)S(1)} %get-tuple-element.25.mine), channel_id=1, source_target_pairs={{0,3},{1,2},{2,1},{3,0},{4,7},{5,6},{6,5},{7,4},{8,11},{9,10},{10,... | collective-permute-start | bytes 12296 | tf_op jit(solution)/shard_map/ppermute | solution.py:341
  52.2 3.7 %collective-permute-start.8 = (f32[8,128]{1,0:T(8,128)S(1)}, f32[8,128]{1,0:T(8,128)S(1)}, u32[]{:S(2)}, u32[]{:S(2)}) collective-permute-start(f32[8,128]{1,0:T(8,128)S(1)} %get-tuple-element.25.mine), channel_id=1, source_target_pairs={{0,2},{1,3},{2,0},{3,1},{4,6},{5,7},{6,4},{7,5},{8,10},{9,11},{10,... | collective-permute-start | bytes 12296 | tf_op jit(solution)/shard_map/ppermute | solution.py:341
  52.8 3.1 %collective-permute-start.7 = (f32[8,128]{1,0:T(8,128)S(1)}, f32[8,128]{1,0:T(8,128)S(1)}, u32[]{:S(2)}, u32[]{:S(2)}) collective-permute-start(f32[8,128]{1,0:T(8,128)S(1)} %get-tuple-element.25.mine), channel_id=1, source_target_pairs={{0,1},{1,0},{2,3},{3,2},{4,5},{5,4},{6,7},{7,6},{8,9},{9,8},{10,11... | collective-permute-start | bytes 12296 | tf_op jit(solution)/shard_map/ppermute | solution.py:341
  60.5 15.4 %copy-start.1 = (f32[2,256,256]{2,1,0:T(8,128)S(1)}, f32[2,256,256]{2,1,0:T(8,128)}, u32[]{:S(2)}) copy-start(f32[2,256,256]{2,1,0:T(8,128)} %get-tuple-element.32.b_ref) | copy-start | bytes 1572868
  74.2 2.0 %collective-permute-start.11 = (f32[8,64,128]{2,1,0:T(8,128)S(1)}, f32[8,64,128]{2,1,0:T(8,128)S(1)}, u32[]{:S(2)}, u32[]{:S(2)}) collective-permute-start(f32[8,64,128]{2,1,0:T(8,128)S(1)} %get-tuple-element.27.r0.s0), channel_id=1, source_target_pairs={{1,2},{2,1},{5,6},{6,5},{9,10},{10,9},{13,14},{14,13},{17,18},{18,... | collective-permute-start | bytes 786440 | tf_op jit(solution)/shard_map/ppermute | solution.py:323
  74.9 2.2 %collective-permute-start.10 = (f32[8,64,128]{2,1,0:T(8,128)S(1)}, f32[8,64,128]{2,1,0:T(8,128)S(1)}, u32[]{:S(2)}, u32[]{:S(2)}) collective-permute-start(f32[8,64,128]{2,1,0:T(8,128)S(1)} %get-tuple-element.27.r0.s0), channel_id=1, source_target_pairs={{0,1},{1,0},{2,3},{3,2},{4,5},{5,4},{6,7},{7,6},{8,9},{9,8},{10,11... | collective-permute-start | bytes 786440 | tf_op jit(solution)/shard_map/ppermute | solution.py:312
  76.1 9.6 %collective-permute-start.12 = (f32[3,256,256]{2,1,0:T(8,128)S(1)}, f32[3,256,256]{2,1,0:T(8,128)}, u32[]{:S(2)}, u32[]{:S(2)}) collective-permute-start(f32[3,256,256]{2,1,0:T(8,128)S(1)} %shard_map.96.b_ref), channel_id=1, source_target_pairs={{0,1},{1,0},{2,3},{3,2},{4,5},{5,4},{6,7},{7,6},{8,9},{9,8},{10,11... | collective-permute-start | bytes 2359304 | tf_op jit(solution)/shard_map/ppermute | solution.py:312
  77.6 7.3 %collective-permute-start.13 = (f32[2,256,256]{2,1,0:T(8,128)S(1)}, f32[2,256,256]{2,1,0:T(8,128)S(1)}, u32[]{:S(2)}, u32[]{:S(2)}) collective-permute-start(f32[2,256,256]{2,1,0:T(8,128)S(1)} %shard_map.94.m_ref), channel_id=1, source_target_pairs={{0,1},{1,0},{2,3},{3,2},{4,5},{5,4},{6,7},{7,6},{8,9},{9,8},{10,11... | collective-permute-start | bytes 1572872 | tf_op jit(solution)/shard_map/ppermute | solution.py:312
  81.5 10.4 %all-to-all-start.4 = ((f32[32,1,128]{2,1,0:T(1,128)}), f32[32,1,128]{2,1,0:T(1,128)S(1)}, u32[]{:S(2)}, u32[]{:S(2)}) async-start(f32[32,1,128]{2,1,0:T(1,128)} %bitcast.2), calls=%async_computation.4 | async-start | bytes 32768 | tf_op jit(solution)/shard_map/all_to_all | solution.py:425
  84.9 0.8 copy-start.2
  85.7 1.0 %copy-start.3 = (f32[2,256,256]{2,1,0:T(8,128)S(1)}, f32[2,256,256]{2,1,0:T(8,128)}, u32[]{:S(2)}) copy-start(f32[2,256,256]{2,1,0:T(8,128)} %copy-done.2) | copy-start | bytes 1572868

commit v14 on v12

--- a/solution.py
+++ b/solution.py
@@ -184,11 +184,16 @@
     return y_ref[...]
 
 
-def first_body(size_ref, slot_ref, x0, x1, x2, lcat_ref, rcat_ref, y_ref, m_ref, part_ref):
+def first_body(
+    size_ref, slot_ref, x0, x1, x2, lcat_ref, rcat_ref, y_ref, m_out, part_ref, m_ref, sem
+):
     mixed = mix_all(slot_ref, (x0, x1, x2), lcat_ref, m_ref)
+    copy = pltpu.make_async_copy(m_ref, m_out, sem)
+    copy.start()
     y = fold_all(size_ref, mixed, rcat_ref, y_ref)
     x = x0[lax.axis_index("ops")]
     part_ref[...] = tile([rows(x * x), rows(x0[...] * y)])
+    copy.wait()
 
 
 def five(x0, r0, h0, y):
@@ -212,9 +217,32 @@
     mix_all(slot_ref, (r0, r1, r2), lcat_ref, m_ref)
 
 
-def fold_body(size_ref, m_ref, r0, x0, h0, rcat_ref, part_ref, y_ref):
-    mixed = [m_ref[p] for p in range(m_ref.shape[0])]
-    lanes(five(x0, r0, h0, fold_all(size_ref, mixed, rcat_ref, y_ref)), part_ref)
+def probe_body(x_ref, s_ref, rcat_ref, probe_ref):
+    high, low = halves(jnp.concatenate([unpack(x_ref[...]), unpack(s_ref[...])], axis=0))
+    side = rcat_ref.shape[2]
+    for p in range(rcat_ref.shape[0]):
+        both = lax.dot_general(
+            jnp.concatenate([high, high, low], axis=1),
+            jnp.concatenate([rcat_ref[p, 0], rcat_ref[p, 1], rcat_ref[p, 0]], axis=1),
+            (((1,), (1,)), ((), ())),
+            preferred_element_type=F32,
+        )
+        probe_ref[0, p] = both[:side]
+        probe_ref[1, p] = both[side:]
+
+
+def spread(value):
+    total = jnp.sum(value, axis=0, keepdims=True)
+    return sum(total[:, j : j + LANES] for j in range(0, total.shape[1], LANES))
+
+
+def meet_body(m_ref, probe_ref, s0, x0, h0, part_ref):
+    o = lax.axis_index("ops")
+    x, r, h = x0[o], s0[o], h0[o]
+    on_x, on_s = [
+        sum(probe_ref[k, p] * m_ref[p] for p in range(m_ref.shape[0])) for k in range(2)
+    ]
+    lanes(tile([rows(x * r), rows(r * r), rows(r * h), spread(on_x), spread(on_s)]), part_ref)
 
 
 def blend_body(c_in, a_ref, b_ref, x_ref, out_ref):
@@ -381,8 +409,8 @@
         light * pairs, new_sector, couple, left_ops, right_ops, limit=52.5,
     )
     y, mx, part = call(
-        first_body, (block, inner, small), [SMEM] + [VMEM] * 6, [], work,
-        sector_states, slots, x0, x1, x2, lcat, rcat,
+        first_body, (block, inner, small), [SMEM] + [VMEM] * 6, room, work,
+        sector_states, slots, x0, x1, x2, lcat, rcat, away=(1,),
     )
     g = gathered(y, part)
     r0, c = call(
@@ -405,6 +433,10 @@
         light, c, mx, mr, x,
     )
     nx = paired(mx)
+    (probe,) = call(
+        probe_body, (jax.ShapeDtypeStruct((2, pairs, side, side), F32),), [VMEM] * 3, [],
+        work, x, s0, rcat,
+    )
     (ms,) = call(
         mix_body, (inner,), [VMEM] * 5, [], work // 2,
         slots, s0, s1, s2, lcat,
@@ -412,8 +444,7 @@
     ns = paired(ms)
     many = jax.ShapeDtypeStruct((chunks * sectors, LANES), F32)
     (part,) = call(
-        fold_body, (many,), [SMEM] + [VMEM] * 5, [pltpu.VMEM(block.shape, F32)], work // 2,
-        sector_states, ms, s0, x, h, rcat,
+        meet_body, (many,), [VMEM] * 5, [], light * pairs, ms, probe, s0, x, h
     )
     parts = lax.all_to_all(part, ("ops", "sec"), 0, 0)
     (u,) = call(

time: 93.9 us -> 94.7 us (level)
  local copies, waits for them, and re-layouts: 3.39 us -> 4.43 us
    unnamed x12 -> x14, local copies, waits for them, and re-layouts: 3.39 us -> 4.43 us
    pallas_call x13 -> x14, Pallas kernels: 11.3 us -> 12 us  [call(): pl.pallas_call(body, out_shape=tuple((pltpu.HBM(o.shape, o.dtype) if k in...]
  transfers between devices with their start and end apart: 17 -> 17, of which waited for: 10 -> 9; matrix products, arithmetic and copies ran while one was open for 0% -> 0% of each run, Pallas kernels for 6% -> 6%
where the time goes in v14:
time: 94.7 us; the launch traced here: 94.1 us
  blocking collectives  26.7 us (28%)
  starting transfers between devices  25.6 us (27%)
  waiting for transfers between devices  23.2 us (24%)
  Pallas kernels  12 us (13%)
  local copies, waits for them, and re-layouts  4.43 us (5%)
  between operations  2.1 us (2%)
    all_to_all x2, blocking collectives, exchange(): return lax.all_to_all(value, 'ops', 0, 0)  26.7 us
    pallas_call x14, Pallas kernels, call(): pl.pallas_call(body, out_shape=tuple((pltpu.HBM(o.shape, o.dtype) if k in...  12 us
    all_to_all x2, starting transfers between devices, exchange(): return lax.all_to_all(value, 'ops', 0, 0)  9.77 us
    all_to_all x2, waiting for transfers between devices, exchange(): return lax.all_to_all(value, 'ops', 0, 0)  9.64 us
    ppermute x3, waiting for transfers between devices, other(): return lax.ppermute(value, ('ops', 'sec'), route)  6.87 us
    ppermute x3, starting transfers between devices, other(): return lax.ppermute(value, ('ops', 'sec'), route)  4.47 us
    unnamed x14, local copies, waits for them, and re-layouts  4.43 us
    ppermute x5, starting transfers between devices, paired(): return lax.ppermute(value, 'sec', [(i, i ^ 1) for i in range(count)])  4.29 us
  transfers between devices with their start and end apart: 17, of which 9 were waited for; matrix products, arithmetic and copies ran while one was open for 0% of the time, Pallas kernels for 6%

profile of v14, /device:TPU:0, one launch (start us, length us, event | category | flops | bytes accessed | tf_op | source)
XLA Modules:
  0.0 94.1 jit_solution(9852667168921745243)
XLA Ops:
  1.3 0.9 copy-done.5
  2.2 3.0 %collective-permute-start.1 = (f32[8,64,128]{2,1,0:T(8,128)S(1)}, f32[8,64,128]{2,1,0:T(8,128)S(1)}, u32[]{:S(2)}, u32[]{:S(2)}) collective-permute-start(f32[8,64,128]{2,1,0:T(8,128)S(1)} %shard_map.87.x0.x_ref), channel_id=1, source_target_pairs={{1,2},{2,1},{0,4},{3,7},{5,6},{6,5},{4,0},{7,3},{9,10},{10,9},{8,1... | collective-permute-start | bytes 786440 | tf_op jit(solution)/shard_map/ppermute | solution.py:348
  5.3 0.1 collective-permute-start
  6.0 0.0 copy-start.6
  6.1 0.6 copy-done.6
  6.7 1.4 %shard_map.86 = (bf16[2,2,256,256]{3,2,1,0:T(8,128)(2,1)S(1)}, bf16[2,2,256,256]{3,2,1,0:T(8,128)(2,1)S(1)}, f32[8,128]{1,0:T(8,128)S(1)}, f32[2,8,128]{2,1,0:T(8,128)S(1)}) custom-call(s32[1]{0:T(128)S(6)} %copy.11.label_ref, s32[2]{0:T(128)S(1)} %bitcast.6, f32[2,1,256,256]{3,2,1,0:T(8,128)} %left_ref.1, f32[2,1,256,256]{3,2,1,0:T(8,128)} %right_ref.1), custom_call_target="tpu_custom_call" | custom-call | flops 2621440 | bytes 2109452 | tf_op jit(solution)/shard_map/pallas_call | solution.py:22
  8.1 1.5 %collective-permute-done.1.x2 = f32[8,64,128]{2,1,0:T(8,128)S(1)} collective-permute-done((f32[8,64,128]{2,1,0:T(8,128)S(1)}, f32[8,64,128]{2,1,0:T(8,128)S(1)}, u32[]{:S(2)}, u32[]{:S(2)}) %collective-permute-start.1) | collective-permute-done | bytes 262176 | tf_op jit(solution)/shard_map/ppermute | solution.py:348
  9.6 0.0 collective-permute-done.x1
  9.6 2.1 %shard_map.88 = (f32[8,64,128]{2,1,0:T(8,128)}, f32[2,256,256]{2,1,0:T(8,128)}, f32[8,128]{1,0:T(8,128)S(1)}) custom-call(s32[1]{0:T(128)S(6)} %copy.10.size_ref, f32[2,8,128]{2,1,0:T(8,128)S(1)} %get-tuple-element.18.slot_ref, f32[8,64,128]{2,1,0:T(8,128)S(1)} %shard_map.87.x0.x_ref, f32[8,64,128]{2,1,0:T(8,128)S(1)} %collective-permute-done.x1, ...), custom_call_target="tpu_custom_call" | custom-call | flops 402653184 | bytes 2633732 | tf_op jit(solution)/shard_map/pallas_call | solution.py:22
  11.7 6.3 %all-to-all-start = ((f32[8,64,128]{2,1,0:T(8,128)}), f32[8,64,128]{2,1,0:T(8,128)S(1)}, u32[]{:S(2)}, u32[]{:S(2)}) async-start(f32[8,64,128]{2,1,0:T(8,128)} %get-tuple-element.21), calls=%async_computation | async-start | bytes 524288 | tf_op jit(solution)/shard_map/all_to_all | solution.py:375
  18.1 1.0 %collective-permute-start.3 = (f32[8,128]{1,0:T(8,128)S(1)}, f32[8,128]{1,0:T(8,128)S(1)}, u32[]{:S(2)}, u32[]{:S(2)}) collective-permute-start(f32[8,128]{1,0:T(8,128)S(1)} %get-tuple-element.22.mine), channel_id=1, source_target_pairs={{0,2},{1,3},{2,0},{3,1},{4,6},{5,7},{6,4},{7,5},{8,10},{9,11},{10,... | collective-permute-start | bytes 12296 | tf_op jit(solution)/shard_map/ppermute | solution.py:366
  19.1 0.8 collective-permute-start.2
  19.9 1.2 %collective-permute-done.4.refs_2_ = f32[8,128]{1,0:T(8,128)S(1)} collective-permute-done((f32[8,128]{1,0:T(8,128)S(1)}, f32[8,128]{1,0:T(8,128)S(1)}, u32[]{:S(2)}, u32[]{:S(2)}) %collective-permute-start.4) | collective-permute-done | bytes 4128 | tf_op jit(solution)/shard_map/ppermute | solution.py:366
  21.1 0.7 collective-permute-done.3.refs_1_
  21.8 0.0 collective-permute-done.2.refs_0_
  21.8 5.0 %all-to-all-done.terms_ref = f32[8,64,128]{2,1,0:T(8,128)S(1)} async-done(((f32[8,64,128]{2,1,0:T(8,128)}), f32[8,64,128]{2,1,0:T(8,128)S(1)}, u32[]{:S(2)}, u32[]{:S(2)}) %all-to-all-start) | async-done | bytes 262176 | tf_op jit(solution)/shard_map/all_to_all | solution.py:375
  26.8 13.4 %all_to_all.31.g_ref.g0 = f32[8,72,128]{2,1,0:T(8,128)S(1)} all-to-all(f32[8,72,128]{2,1,0:T(8,128)S(1)} %shard_map.89), channel_id=1, replica_groups=mesh['ops'=8,'sec'=4] {'ops'}, dimensions={0} | all-to-all | bytes 589824 | tf_op jit(solution)/shard_map/all_to_all | solution.py:375
  40.2 0.2 shard_map.90
  40.5 0.8 collective-permute-start.6
  41.2 0.3 collective-permute-start.5
  41.5 5.4 %collective-permute-done.6.r2 = f32[8,64,128]{2,1,0:T(8,128)S(1)} collective-permute-done((f32[8,64,128]{2,1,0:T(8,128)S(1)}, f32[8,64,128]{2,1,0:T(8,128)S(1)}, u32[]{:S(2)}, u32[]{:S(2)}) %collective-permute-start.6) | collective-permute-done | bytes 262176 | tf_op jit(solution)/shard_map/ppermute | solution.py:348
  46.9 2.1 %shard_map.91 = (f32[8,64,128]{2,1,0:T(8,128)}, f32[2,256,256]{2,1,0:T(8,128)}, f32[8,128]{1,0:T(8,128)S(1)}) custom-call(s32[1]{0:T(128)S(6)} %copy.10.size_ref, f32[2,8,128]{2,1,0:T(8,128)S(1)} %get-tuple-element.18.slot_ref, f32[8,64,128]{2,1,0:T(8,128)S(1)} %get-tuple-element.23.r0.r_in, f32[8,64,128]{2,1,0:T(8,128)S(1)} %collective-permute-done.5.r1, ...), custom_call_target="tpu_custom_call" | custom-call | flops 402653184 | bytes 3190788 | tf_op jit(solution)/shard_map/pallas_call | solution.py:22
  49.1 3.4 %all-to-all-start.2 = ((f32[8,64,128]{2,1,0:T(8,128)}), f32[8,64,128]{2,1,0:T(8,128)S(1)}, u32[]{:S(2)}, u32[]{:S(2)}) async-start(f32[8,64,128]{2,1,0:T(8,128)} %get-tuple-element.24), calls=%async_computation.2 | async-start | bytes 524288 | tf_op jit(solution)/shard_map/all_to_all | solution.py:375
  52.5 0.1 collective-permute-start.9
  52.6 0.6 collective-permute-start.8
  53.2 1.3 %collective-permute-start.7 = (f32[8,128]{1,0:T(8,128)S(1)}, f32[8,128]{1,0:T(8,128)S(1)}, u32[]{:S(2)}, u32[]{:S(2)}) collective-permute-start(f32[8,128]{1,0:T(8,128)S(1)} %get-tuple-element.25.mine), channel_id=1, source_target_pairs={{0,1},{1,0},{2,3},{3,2},{4,5},{5,4},{6,7},{7,6},{8,9},{9,8},{10,11... | collective-permute-start | bytes 12296 | tf_op jit(solution)/shard_map/ppermute | solution.py:366
  54.4 1.2 %collective-permute-done.9.refs_2_ = f32[8,128]{1,0:T(8,128)S(1)} collective-permute-done((f32[8,128]{1,0:T(8,128)S(1)}, f32[8,128]{1,0:T(8,128)S(1)}, u32[]{:S(2)}, u32[]{:S(2)}) %collective-permute-start.9) | collective-permute-done | bytes 4128 | tf_op jit(solution)/shard_map/ppermute | solution.py:366
  55.6 0.7 collective-permute-done.8.refs_1_
  56.3 0.0 collective-permute-done.7.refs_0_
  56.3 4.6 %all-to-all-done.2.terms_ref = f32[8,64,128]{2,1,0:T(8,128)S(1)} async-done(((f32[8,64,128]{2,1,0:T(8,128)}), f32[8,64,128]{2,1,0:T(8,128)S(1)}, u32[]{:S(2)}, u32[]{:S(2)}) %all-to-all-start.2) | async-done | bytes 262176 | tf_op jit(solution)/shard_map/all_to_all | solution.py:375
  60.9 13.3 %all_to_all.32.s_ref = f32[8,72,128]{2,1,0:T(8,128)S(1)} all-to-all(f32[8,72,128]{2,1,0:T(8,128)S(1)} %shard_map.92), channel_id=1, replica_groups=mesh['ops'=8,'sec'=4] {'ops'}, dimensions={0} | all-to-all | bytes 589824 | tf_op jit(solution)/shard_map/all_to_all | solution.py:375
  74.2 0.4 shard_map.93
  74.6 0.7 collective-permute-start.11
  75.3 1.0 %collective-permute-start.10 = (f32[8,64,128]{2,1,0:T(8,128)S(1)}, f32[8,64,128]{2,1,0:T(8,128)S(1)}, u32[]{:S(2)}, u32[]{:S(2)}) collective-permute-start(f32[8,64,128]{2,1,0:T(8,128)S(1)} %get-tuple-element.27.r0.s_ref.s0), channel_id=1, source_target_pairs={{0,1},{1,0},{2,3},{3,2},{4,5},{5,4},{6,7},{7,6},{8,9},{9,8},{10,11... | collective-permute-start | bytes 786440 | tf_op jit(solution)/shard_map/ppermute | solution.py:337
  76.3 1.0 %copy-done.1 = f32[2,256,256]{2,1,0:T(8,128)S(1)} copy-done((f32[2,256,256]{2,1,0:T(8,128)S(1)}, f32[2,256,256]{2,1,0:T(8,128)}, u32[]{:S(2)}) %copy-start.1) | copy-done | bytes 524312
  77.4 0.2 shard_map.97.b_ref
  77.5 0.1 collective-permute-start.12
  77.6 0.4 shard_map.94.m_ref
  78.1 2.7 %collective-permute-start.13 = (f32[2,256,256]{2,1,0:T(8,128)S(1)}, f32[2,256,256]{2,1,0:T(8,128)S(1)}, u32[]{:S(2)}, u32[]{:S(2)}) collective-permute-start(f32[2,256,256]{2,1,0:T(8,128)S(1)} %shard_map.94.m_ref), channel_id=1, source_target_pairs={{0,1},{1,0},{2,3},{3,2},{4,5},{5,4},{6,7},{7,6},{8,9},{9,8},{10,11... | collective-permute-start | bytes 1572872 | tf_op jit(solution)/shard_map/ppermute | solution.py:337
  80.8 0.6 shard_map.95.probe_ref
  81.4 0.9 shard_map.96
  82.3 3.3 %all-to-all-start.4 = ((f32[32,1,128]{2,1,0:T(1,128)}), f32[32,1,128]{2,1,0:T(1,128)S(1)}, u32[]{:S(2)}, u32[]{:S(2)}) async-start(f32[32,1,128]{2,1,0:T(1,128)} %bitcast.2), calls=%async_computation.4 | async-start | bytes 32768 | tf_op jit(solution)/shard_map/all_to_all | solution.py:449
  85.6 0.0 copy-start.3
  85.6 0.8 copy-done.3
  86.4 1.0 %copy-done.4 = f32[2,256,256]{2,1,0:T(8,128)S(1)} copy-done((f32[2,256,256]{2,1,0:T(8,128)S(1)}, f32[2,256,256]{2,1,0:T(8,128)}, u32[]{:S(2)}) %copy-start.4) | copy-done | bytes 524312
  87.5 2.3 %shard_map.98.u_ref = f32[3,2,256,256]{3,2,1,0:T(8,128)S(1)} custom-call(f32[8,128]{1,0:T(8,128)S(1)} %get-tuple-element.33.flag_ref, f32[3,256,256]{2,1,0:T(8,128)S(1)} %shard_map.97.b_ref, f32[3,256,256]{2,1,0:T(8,128)} %collective-permute-done.12.n_ref, f32[2,256,256]{2,1,0:T(8,128)S(1)} %shard_map.94.m_ref, f32[2,256,256]{2,1,0:T(8,128)S(1)} %copy-done.4, ...), custom_call_target="tpu_custom_call" | custom-call | flops 402653184 | bytes 4722688 | tf_op jit(solution)/shard_map/pallas_call | solution.py:22
  89.7 3.0 %all-to-all-done.4 = f32[32,1,128]{2,1,0:T(1,128)S(1)} async-done(((f32[32,1,128]{2,1,0:T(1,128)}), f32[32,1,128]{2,1,0:T(1,128)S(1)}, u32[]{:S(2)}, u32[]{:S(2)}) %all-to-all-start.4) | async-done | bytes 16416 | tf_op jit(solution)/shard_map/all_to_all | solution.py:449
  92.7 1.4 %shard_map.99 = (f32[1,256,256]{2,1,0:T(8,128)}, f32[2,1,256,256]{3,2,1,0:T(8,128)}) custom-call(f32[32,128]{1,0:T(8,128)S(1)} %bitcast.5, f32[8,128]{1,0:T(8,128)S(1)} %get-tuple-element.30.c_in, f32[3,256,256]{2,1,0:T(8,128)S(1)} %shard_map.97.b_ref, f32[8,64,128]{2,1,0:T(8,128)S(1)} %get-tuple-element.27.r0.s_ref.s0, f32[3,2,256,256]{3,2,1,0:T(8,128)S(1)} %shard_map.98.u_ref), custom_call_target="tpu_custom_call" | custom-call | flops 1310720 | bytes 3428352 | tf_op jit(solution)/shard_map/pallas_call | solution.py:22
  (16 shorter events, 0.1 us)
Async XLA Ops:
  1.3 0.9 copy-start.5
  2.2 7.4 %collective-permute-start.1 = (f32[8,64,128]{2,1,0:T(8,128)S(1)}, f32[8,64,128]{2,1,0:T(8,128)S(1)}, u32[]{:S(2)}, u32[]{:S(2)}) collective-permute-start(f32[8,64,128]{2,1,0:T(8,128)S(1)} %shard_map.87.x0.x_ref), channel_id=1, source_target_pairs={{1,2},{2,1},{0,4},{3,7},{5,6},{6,5},{4,0},{7,3},{9,10},{10,9},{8,1... | collective-permute-start | bytes 786440 | tf_op jit(solution)/shard_map/ppermute | solution.py:348
  5.3 4.4 %collective-permute-start = (f32[8,64,128]{2,1,0:T(8,128)S(1)}, f32[8,64,128]{2,1,0:T(8,128)S(1)}, u32[]{:S(2)}, u32[]{:S(2)}) collective-permute-start(f32[8,64,128]{2,1,0:T(8,128)S(1)} %shard_map.87.x0.x_ref), channel_id=1, source_target_pairs={{0,1},{1,0},{2,3},{3,2},{4,5},{5,4},{6,7},{7,6},{8,9},{9,8},{10,11... | collective-permute-start | bytes 786440 | tf_op jit(solution)/shard_map/ppermute | solution.py:337
  6.0 0.7 copy-start.6
  9.6 30.6 %copy-start = (bf16[1,256,256]{2,1,0:T(8,128)(2,1)S(1)}, bf16[1,256,256]{2,1,0:T(8,128)(2,1)}, u32[]{:S(2)}) copy-start(bf16[1,256,256]{2,1,0:T(8,128)(2,1)} %diag_ref.3) | copy-start | bytes 393220
  11.7 15.0 %all-to-all-start = ((f32[8,64,128]{2,1,0:T(8,128)}), f32[8,64,128]{2,1,0:T(8,128)S(1)}, u32[]{:S(2)}, u32[]{:S(2)}) async-start(f32[8,64,128]{2,1,0:T(8,128)} %get-tuple-element.21), calls=%async_computation | async-start | bytes 524288 | tf_op jit(solution)/shard_map/all_to_all | solution.py:375
  18.1 3.0 %collective-permute-start.4 = (f32[8,128]{1,0:T(8,128)S(1)}, f32[8,128]{1,0:T(8,128)S(1)}, u32[]{:S(2)}, u32[]{:S(2)}) collective-permute-start(f32[8,128]{1,0:T(8,128)S(1)} %get-tuple-element.22.mine), channel_id=1, source_target_pairs={{0,3},{1,2},{2,1},{3,0},{4,7},{5,6},{6,5},{7,4},{8,11},{9,10},{10,... | collective-permute-start | bytes 12296 | tf_op jit(solution)/shard_map/ppermute | solution.py:366
  18.1 3.7 %collective-permute-start.3 = (f32[8,128]{1,0:T(8,128)S(1)}, f32[8,128]{1,0:T(8,128)S(1)}, u32[]{:S(2)}, u32[]{:S(2)}) collective-permute-start(f32[8,128]{1,0:T(8,128)S(1)} %get-tuple-element.22.mine), channel_id=1, source_target_pairs={{0,2},{1,3},{2,0},{3,1},{4,6},{5,7},{6,4},{7,5},{8,10},{9,11},{10,... | collective-permute-start | bytes 12296 | tf_op jit(solution)/shard_map/ppermute | solution.py:366
  19.1 2.7 %collective-permute-start.2 = (f32[8,128]{1,0:T(8,128)S(1)}, f32[8,128]{1,0:T(8,128)S(1)}, u32[]{:S(2)}, u32[]{:S(2)}) collective-permute-start(f32[8,128]{1,0:T(8,128)S(1)} %get-tuple-element.22.mine), channel_id=1, source_target_pairs={{0,1},{1,0},{2,3},{3,2},{4,5},{5,4},{6,7},{7,6},{8,9},{9,8},{10,11... | collective-permute-start | bytes 12296 | tf_op jit(solution)/shard_map/ppermute | solution.py:366
  40.5 6.4 %collective-permute-start.6 = (f32[8,64,128]{2,1,0:T(8,128)S(1)}, f32[8,64,128]{2,1,0:T(8,128)S(1)}, u32[]{:S(2)}, u32[]{:S(2)}) collective-permute-start(f32[8,64,128]{2,1,0:T(8,128)S(1)} %get-tuple-element.23.r0.r_in), channel_id=1, source_target_pairs={{1,2},{2,1},{0,4},{3,7},{5,6},{6,5},{4,0},{7,3},{9,10},{10,9},{8,1... | collective-permute-start | bytes 786440 | tf_op jit(solution)/shard_map/ppermute | solution.py:348
  41.2 5.7 %collective-permute-start.5 = (f32[8,64,128]{2,1,0:T(8,128)S(1)}, f32[8,64,128]{2,1,0:T(8,128)S(1)}, u32[]{:S(2)}, u32[]{:S(2)}) collective-permute-start(f32[8,64,128]{2,1,0:T(8,128)S(1)} %get-tuple-element.23.r0.r_in), channel_id=1, source_target_pairs={{0,1},{1,0},{2,3},{3,2},{4,5},{5,4},{6,7},{7,6},{8,9},{9,8},{10,11... | collective-permute-start | bytes 786440 | tf_op jit(solution)/shard_map/ppermute | solution.py:337
  49.1 11.8 %all-to-all-start.2 = ((f32[8,64,128]{2,1,0:T(8,128)}), f32[8,64,128]{2,1,0:T(8,128)S(1)}, u32[]{:S(2)}, u32[]{:S(2)}) async-start(f32[8,64,128]{2,1,0:T(8,128)} %get-tuple-element.24), calls=%async_computation.2 | async-start | bytes 524288 | tf_op jit(solution)/shard_map/all_to_all | solution.py:375
  52.5 3.1 %collective-permute-start.9 = (f32[8,128]{1,0:T(8,128)S(1)}, f32[8,128]{1,0:T(8,128)S(1)}, u32[]{:S(2)}, u32[]{:S(2)}) collective-permute-start(f32[8,128]{1,0:T(8,128)S(1)} %get-tuple-element.25.mine), channel_id=1, source_target_pairs={{0,3},{1,2},{2,1},{3,0},{4,7},{5,6},{6,5},{7,4},{8,11},{9,10},{10,... | collective-permute-start | bytes 12296 | tf_op jit(solution)/shard_map/ppermute | solution.py:366
  52.6 3.7 %collective-permute-start.8 = (f32[8,128]{1,0:T(8,128)S(1)}, f32[8,128]{1,0:T(8,128)S(1)}, u32[]{:S(2)}, u32[]{:S(2)}) collective-permute-start(f32[8,128]{1,0:T(8,128)S(1)} %get-tuple-element.25.mine), channel_id=1, source_target_pairs={{0,2},{1,3},{2,0},{3,1},{4,6},{5,7},{6,4},{7,5},{8,10},{9,11},{10,... | collective-permute-start | bytes 12296 | tf_op jit(solution)/shard_map/ppermute | solution.py:366
  53.2 3.1 %collective-permute-start.7 = (f32[8,128]{1,0:T(8,128)S(1)}, f32[8,128]{1,0:T(8,128)S(1)}, u32[]{:S(2)}, u32[]{:S(2)}) collective-permute-start(f32[8,128]{1,0:T(8,128)S(1)} %get-tuple-element.25.mine), channel_id=1, source_target_pairs={{0,1},{1,0},{2,3},{3,2},{4,5},{5,4},{6,7},{7,6},{8,9},{9,8},{10,11... | collective-permute-start | bytes 12296 | tf_op jit(solution)/shard_map/ppermute | solution.py:366
  60.9 15.4 %copy-start.2 = (f32[2,256,256]{2,1,0:T(8,128)S(1)}, f32[2,256,256]{2,1,0:T(8,128)}, u32[]{:S(2)}) copy-start(f32[2,256,256]{2,1,0:T(8,128)} %get-tuple-element.32.b_ref) | copy-start | bytes 1572868
  74.6 3.0 %collective-permute-start.11 = (f32[8,64,128]{2,1,0:T(8,128)S(1)}, f32[8,64,128]{2,1,0:T(8,128)S(1)}, u32[]{:S(2)}, u32[]{:S(2)}) collective-permute-start(f32[8,64,128]{2,1,0:T(8,128)S(1)} %get-tuple-element.27.r0.s_ref.s0), channel_id=1, source_target_pairs={{1,2},{2,1},{5,6},{6,5},{9,10},{10,9},{13,14},{14,13},{17,18},{18,... | collective-permute-start | bytes 786440 | tf_op jit(solution)/shard_map/ppermute | solution.py:348
  75.3 2.3 %collective-permute-start.10 = (f32[8,64,128]{2,1,0:T(8,128)S(1)}, f32[8,64,128]{2,1,0:T(8,128)S(1)}, u32[]{:S(2)}, u32[]{:S(2)}) collective-permute-start(f32[8,64,128]{2,1,0:T(8,128)S(1)} %get-tuple-element.27.r0.s_ref.s0), channel_id=1, source_target_pairs={{0,1},{1,0},{2,3},{3,2},{4,5},{5,4},{6,7},{7,6},{8,9},{9,8},{10,11... | collective-permute-start | bytes 786440 | tf_op jit(solution)/shard_map/ppermute | solution.py:337
  76.3 1.0 %copy-start.1 = (f32[2,256,256]{2,1,0:T(8,128)S(1)}, f32[2,256,256]{2,1,0:T(8,128)}, u32[]{:S(2)}) copy-start(f32[2,256,256]{2,1,0:T(8,128)} %get-tuple-element.31.a_ref) | copy-start | bytes 1572868
  77.5 8.9 %collective-permute-start.12 = (f32[3,256,256]{2,1,0:T(8,128)S(1)}, f32[3,256,256]{2,1,0:T(8,128)}, u32[]{:S(2)}, u32[]{:S(2)}) collective-permute-start(f32[3,256,256]{2,1,0:T(8,128)S(1)} %shard_map.97.b_ref), channel_id=1, source_target_pairs={{0,1},{1,0},{2,3},{3,2},{4,5},{5,4},{6,7},{7,6},{8,9},{9,8},{10,11... | collective-permute-start | bytes 2359304 | tf_op jit(solution)/shard_map/ppermute | solution.py:337
  78.1 7.5 %collective-permute-start.13 = (f32[2,256,256]{2,1,0:T(8,128)S(1)}, f32[2,256,256]{2,1,0:T(8,128)S(1)}, u32[]{:S(2)}, u32[]{:S(2)}) collective-permute-start(f32[2,256,256]{2,1,0:T(8,128)S(1)} %shard_map.94.m_ref), channel_id=1, source_target_pairs={{0,1},{1,0},{2,3},{3,2},{4,5},{5,4},{6,7},{7,6},{8,9},{9,8},{10,11... | collective-permute-start | bytes 1572872 | tf_op jit(solution)/shard_map/ppermute | solution.py:337
  82.3 10.4 %all-to-all-start.4 = ((f32[32,1,128]{2,1,0:T(1,128)}), f32[32,1,128]{2,1,0:T(1,128)S(1)}, u32[]{:S(2)}, u32[]{:S(2)}) async-start(f32[32,1,128]{2,1,0:T(1,128)} %bitcast.2), calls=%async_computation.4 | async-start | bytes 32768 | tf_op jit(solution)/shard_map/all_to_all | solution.py:449
  85.6 0.8 copy-start.3
  86.4 1.0 %copy-start.4 = (f32[2,256,256]{2,1,0:T(8,128)S(1)}, f32[2,256,256]{2,1,0:T(8,128)}, u32[]{:S(2)}) copy-start(f32[2,256,256]{2,1,0:T(8,128)} %copy-done.3) | copy-start | bytes 1572868
